TPU v7x, 128 devices: a whole 4x4x4 slice. The times are simulated.
128 devices in a mesh: shot: 16 (over y, x_lo, core), brick: 8 (over z, x_hi).
Axes of the slice: x: 4 (x_hi: 2, x_lo: 2; x = x_hi * 2 + x_lo), y: 4, z: 4, core: 2. Of those that a mesh axis runs over, the one named last changes fastest.
Arguments:
- latent: bfloat16 [16, 256, 32, 128], P(None, 'brick', 'shot'), may hold values from -6 to 6
- conv_in: bfloat16 [27, 16, 16], replicated, may hold values from -0.3125 to 0.3125
- conv_out: bfloat16 [27, 2, 16], replicated, may hold values from -0.3125 to 0.3125
- source_field: float32 [16, 256, 16, 128], P('shot', 'brick'), may hold values from -6 to 6
- observed: float32 [16, 3, 2048], P('shot'), may hold values from -6 to 6
- aperture: int32 [16], P('shot'), may hold values from 0 to 16, as said below
- receivers: int32 [16, 3, 2048], P('shot'), may hold values from 0 to 255, as said below
Outputs:
- grad_latent: float32 [16, 256, 32, 128], P(None, 'brick', 'shot')
- grad_first: float32 [27, 16, 16], replicated
- grad_second: float32 [27, 2, 16], replicated
Inputs may be any that keep to these rules, and one draw needn't show every extreme that they name: Every shot's aperture lies inside the grid; some shot starts at 0 and some at 16. `receivers`: each receiver's first index is below 256, its third below 128, and its second lies inside its shot's aperture.
All inputs are finite; a program needn't handle non-finite values.
Results may differ from a plain program's by a relative error of at most 0.0023.
The roundings to bfloat16 on the way count: a program that leaves them out, or rounds other values in their place, can miss the bound.
Values may be sent and summed in bfloat16 or wider, within the bound.
No kernel may reach another device: no remote copies, remote signals or barrier semaphores. Data moves between devices by JAX's collectives and lax.ppermute only.
A program may use at most 128 MiB of HBM per device.

v0:
```python
import jax
import jax.numpy as jnp
from jax import lax
from jax.sharding import PartitionSpec as P

stencil_taps = (1225.0 / 1024.0, -245.0 / 3072.0, 49.0 / 5120.0, -5.0 / 7168.0)
misfit_weight = 16.0
wave_rim = 8


def with_halo(block, sides, width):
    for axis, dim in sides:
        count = lax.axis_size(axis)
        forward = [(i, i + 1) for i in range(count - 1)]
        backward = [(target, source) for source, target in forward]
        low = lax.ppermute(
            lax.slice_in_dim(block, block.shape[dim] - width, None, axis=dim), axis, forward
        )
        high = lax.ppermute(lax.slice_in_dim(block, 0, width, axis=dim), axis, backward)
        block = jnp.concatenate([low, block, high], axis=dim)
    return block


def take_slab(array, first_index, length, which_axis):
    return lax.slice_in_dim(array, first_index, first_index + length, axis=which_axis)


def inner_part(array, which_axis):
    for other_axis in range(3):
        if other_axis != which_axis:
            array = take_slab(array, wave_rim, array.shape[other_axis] - 2 * wave_rim, other_axis)
    return array


def face_slope(array, which_axis):
    length = array.shape[which_axis] - 2 * wave_rim
    summed = jnp.zeros_like(take_slab(array, 0, length + 8, which_axis))
    for tap_index in range(1, 5):
        upper = take_slab(array, 3 + tap_index, length + 8, which_axis)
        lower = take_slab(array, 4 - tap_index, length + 8, which_axis)
        summed = summed + stencil_taps[tap_index - 1] * (upper - lower)
    return summed


def operate(wavefield_pad, buoyancy_pad):
    summed = 0.0
    for which_axis in range(3):
        field_part = inner_part(wavefield_pad, which_axis)
        weight_part = inner_part(buoyancy_pad, which_axis)
        length = field_part.shape[which_axis] - 2 * wave_rim
        face_weight = 0.5 * (
            take_slab(weight_part, 3, length + 8, which_axis)
            + take_slab(weight_part, 4, length + 8, which_axis)
        )
        face_flux = face_weight * face_slope(field_part, which_axis)
        for tap_index in range(1, 5):
            upper = take_slab(face_flux, 4 + tap_index, length, which_axis)
            lower = take_slab(face_flux, 5 - tap_index, length, which_axis)
            summed = summed + stencil_taps[tap_index - 1] * (upper - lower)
    return summed


def buoyancy_slope(scaled_pad, wavefield_pad):
    summed = 0.0
    for which_axis in range(3):
        scaled_part = inner_part(scaled_pad, which_axis)
        length = scaled_part.shape[which_axis] - 2 * wave_rim
        face_product = -face_slope(scaled_part, which_axis) * face_slope(
            inner_part(wavefield_pad, which_axis), which_axis
        )
        summed = summed + 0.5 * (
            take_slab(face_product, 4, length, which_axis)
            + take_slab(face_product, 5, length, which_axis)
        )
    return summed


def brick_rims(stacked):
    widened = with_halo(stacked, (("brick", 1),), 8)
    return jnp.pad(widened, ((0, 0), (0, 0), (wave_rim, wave_rim), (wave_rim, wave_rim)))


def tile_rims(array):
    widened = with_halo(array, (("shot", 2), ("brick", 1)), 1)
    return jnp.pad(widened, ((0, 0), (0, 0), (0, 0), (1, 1)))


def kernel_shifts():
    listed = []
    for shift_x in range(3):
        for shift_y in range(3):
            for shift_z in range(3):
                listed.append((9 * shift_x + 3 * shift_y + shift_z, shift_x, shift_y, shift_z))
    return listed


def conv_forward(padded, weights):
    extent = [padded.shape[dim_index] - 2 for dim_index in range(1, 4)]
    summed = 0.0
    for kernel_index, shift_x, shift_y, shift_z in kernel_shifts():
        window = padded[
            :,
            shift_x : shift_x + extent[0],
            shift_y : shift_y + extent[1],
            shift_z : shift_z + extent[2],
        ]
        summed = summed + jnp.einsum(
            "oc,cxyz->oxyz", weights[kernel_index], window, preferred_element_type=jnp.float32
        )
    return summed


def conv_back(grad_pad, weights):
    extent = [grad_pad.shape[dim_index] - 2 for dim_index in range(1, 4)]
    summed = 0.0
    for kernel_index, shift_x, shift_y, shift_z in kernel_shifts():
        window = grad_pad[
            :,
            2 - shift_x : 2 - shift_x + extent[0],
            2 - shift_y : 2 - shift_y + extent[1],
            2 - shift_z : 2 - shift_z + extent[2],
        ]
        summed = summed + jnp.einsum(
            "oc,oxyz->cxyz", weights[kernel_index], window, preferred_element_type=jnp.float32
        )
    return summed


def weight_grad(grads, padded):
    extent = grads.shape[1:]
    listed = []
    for kernel_index, shift_x, shift_y, shift_z in kernel_shifts():
        window = padded[
            :,
            shift_x : shift_x + extent[0],
            shift_y : shift_y + extent[1],
            shift_z : shift_z + extent[2],
        ]
        listed.append(
            jnp.einsum("oxyz,cxyz->oc", grads, window, preferred_element_type=jnp.float32)
        )
    return jnp.stack(listed)


def per_device(latent, conv_in, conv_out, source_field, observed, aperture, receivers):
    latent_pad = tile_rims(latent)
    hidden = jnp.tanh(conv_forward(latent_pad, conv_in)).astype(jnp.bfloat16)
    hidden_pad = tile_rims(hidden)
    output = conv_forward(hidden_pad, conv_out)
    squashed = jax.nn.sigmoid(output[0])
    modulus = 0.03 + 0.09 * squashed
    bent_part = jnp.tanh(output[1])
    buoyancy = jnp.exp(0.35 * bent_part)
    column = lax.all_gather(jnp.stack([modulus, buoyancy]), "shot", axis=2, tiled=True)
    first_row = aperture[0]
    window_rows = source_field.shape[2]
    window = lax.dynamic_slice_in_dim(column, first_row, window_rows, 2)
    brick_width = latent.shape[1]
    receiver_cells = receivers[0]
    local_x = receiver_cells[0] - lax.axis_index("brick") * brick_width
    owned_here = (local_x >= 0) & (local_x < brick_width)
    cell_x = jnp.clip(local_x, 0, brick_width - 1)
    cell_y = receiver_cells[1] - first_row
    cell_z = receiver_cells[2]
    recorded = observed[0]
    source = source_field[0]
    sections = recorded.shape[0]

    def inject(values):
        return jnp.zeros(source.shape, jnp.float32).at[cell_x, cell_y, cell_z].add(values)

    fields = []
    images = []
    residuals = []
    coefficient_pad = brick_rims(window)
    modulus_pad = coefficient_pad[0]
    buoyancy_pad = coefficient_pad[1]
    modulus_window = window[0]
    earlier = jnp.zeros_like(source)
    current = source
    for section_index in range(sections):
        wavefield_pad = brick_rims(current[None])[0]
        operated = operate(wavefield_pad, buoyancy_pad)
        following = 2.0 * current - earlier + modulus_window * operated
        fields.append(wavefield_pad)
        images.append(operated)
        misfit = misfit_weight * (following[cell_x, cell_y, cell_z] - recorded[len(residuals)])
        residuals.append(jnp.where(owned_here, misfit, 0.0))
        earlier = current
        current = following
    adjoint = inject(residuals[sections - 1])
    adjoint_later = jnp.zeros_like(source)
    grad_modulus = jnp.zeros_like(source)
    grad_buoyancy = jnp.zeros_like(source)
    for section_index in reversed(range(sections)):
        scaled_pad = modulus_pad * brick_rims(adjoint[None])[0]
        grad_modulus = grad_modulus + adjoint * images[section_index]
        grad_buoyancy = grad_buoyancy + buoyancy_slope(scaled_pad, fields[section_index])
        if section_index > 0:
            earlier_adjoint = (
                inject(residuals[section_index - 1])
                + 2.0 * adjoint
                + operate(scaled_pad, buoyancy_pad)
                - adjoint_later
            )
            adjoint_later = adjoint
            adjoint = earlier_adjoint
    column_grad = lax.dynamic_update_slice_in_dim(
        jnp.zeros(column.shape, jnp.float32), jnp.stack([grad_modulus, grad_buoyancy]), first_row, 2
    )
    tile_grad = lax.psum_scatter(column_grad, "shot", scatter_dimension=2, tiled=True)
    grad_output = jnp.stack(
        [
            tile_grad[0] * 0.09 * squashed * (1.0 - squashed),
            tile_grad[1] * buoyancy * 0.35 * (1.0 - bent_part * bent_part),
        ]
    ).astype(jnp.bfloat16)
    grad_hidden = conv_back(tile_rims(grad_output), conv_out)
    hidden_wide = hidden.astype(jnp.float32)
    grad_inner = (grad_hidden * (1.0 - hidden_wide * hidden_wide)).astype(jnp.bfloat16)
    grad_latent = conv_back(tile_rims(grad_inner), conv_in)
    grad_first = weight_grad(grad_inner, latent_pad)
    grad_second = weight_grad(grad_output, hidden_pad)
    grad_first, grad_second = lax.psum((grad_first, grad_second), ("shot", "brick"))
    return (grad_latent, grad_first, grad_second)


def solution(mesh):
    placed = (
        P(None, "brick", "shot", None),
        P(),
        P(),
        P("shot", "brick", None, None),
        P("shot", None, None),
        P("shot"),
        P("shot", None, None),
    )
    return jax.shard_map(
        per_device,
        mesh=mesh,
        in_specs=placed,
        out_specs=(P(None, "brick", "shot", None), P(), P()),
        check_vma=False,
    )
```

profile of v0, /device:TPU:32, one launch (start us, length us, event | category | flops | bytes accessed | tf_op | source)
XLA Modules:
  0.0 565.5 jit_solution(16717900112438961506)
XLA Ops:
  15.9 4.6 collective-permute-start.2
  20.5 3.6 collective-permute-start.3
  38.4 4.9 collective-permute-start.4
  44.8 2.0 collective-permute-done.5
  46.8 3.7 collective-permute-start.6
  50.5 4.7 collective-permute-start.7
  55.6 2.1 collective-permute-done.7
  79.7 5.9 %collective-permute-start.10 = (f32[1,8,16,128]{3,1,2,0:T(8,128)S(1)}, f32[1,8,16,128]{3,1,2,0:T(8,128)S(1)}, u32[]{:S(2)}, u32[]{:S(2)}) collective-permute-start(f32[1,8,16,128]{3,1,2,0:T(8,128)S(1)} %get-tuple-element.119), channel_id=1, source_target_pairs={{0,1},{1,2},{2,3},{3,4},{4,5},{5,6},{6,7},{8,9},{9,10},{10,11},{11... | collective-permute-start | bytes 196616 | tf_op jit(solution)/shard_map/ppermute | solution.py:16
  85.6 2.4 collective-permute-start.11
  93.2 2.2 fusion.772
  95.4 22.9 %all-gather.2.cloned.1.call-done = f32[2,32,32,128]{3,1,2,0:T(8,128)} async-done(((f32[2,32,2,128]{3,1,2,0:T(8,128)}), f32[2,32,32,128]{3,1,2,0:T(8,128)}) %all-gather.2.cloned.1.call-update) | async-done | bytes 1048592 | tf_op jit(solution)/shard_map/all_gather | solution.py:154
  119.3 4.7 collective-permute-start.8
  124.0 3.7 collective-permute-start.9
  129.3 3.4 collective-permute-done.9
  133.5 1.9 fusion.799
  135.3 2.1 fusion.802
  142.0 4.6 collective-permute-start.12
  146.7 4.0 collective-permute-start.13
  150.7 3.6 collective-permute-done.13
  161.2 4.6 collective-permute-start.14
  165.8 3.7 collective-permute-start.15
  170.7 24.9 %gather_fusion.2 = f32[2048]{0:T(1024)} fusion(f32[32,16,128]{2,0,1:T(8,128)S(1)} %get-tuple-element.78, s32[2048]{0:T(1024)S(1)} %bitcast.1233), kind=kCustom, calls=%fused_computation.2 | custom fusion | bytes 40960 | tf_op jit(solution)/shard_map/gather | solution.py:187
  195.7 25.0 %gather_fusion.1 = f32[2048]{0:T(1024)} fusion(f32[32,16,128]{2,0,1:T(8,128)S(1)} %get-tuple-element.70, s32[2048]{0:T(1024)S(1)} %bitcast.1234), kind=kCustom, calls=%fused_computation.1 | custom fusion | bytes 40960 | tf_op jit(solution)/shard_map/gather | solution.py:187
  223.7 1.8 fusion.786
  227.0 2.3 multiply_add_fusion
  229.3 16.2 %gather_fusion = f32[2048]{0:T(1024)S(1)} fusion(f32[32,16,128]{2,0,1:T(8,128)S(1)} %get-tuple-element.62, s32[2048]{0:T(1024)S(1)} %bitcast.1235), kind=kCustom, calls=%fused_computation | custom fusion | bytes 40960 | tf_op jit(solution)/shard_map/gather | solution.py:187
  245.6 11.3 %scatter_custom_fusion = f32[65536]{0:T(1024)S(1)} fusion(s32[2048]{0:T(1024)S(1)} %broadcast_select_fusion, f32[2048]{0:T(1024)S(1)} %get-tuple-element.195, f32[]{:T(128)} %constant.19.clone.1), kind=kCustom, calls=%fused_computation.892 | custom fusion | flops 2048 | bytes 262148
  257.0 3.7 collective-permute-start.16
  260.7 4.9 collective-permute-start.17
  265.6 2.9 collective-permute-done.17
  275.4 1.9 negate_multiply_fusion.1
  278.1 11.6 %scatter_fusion = f32[65536]{0:T(1024)S(1)} fusion(f32[65536]{0:T(1024)S(1)} %bitcast.1238, s32[2048]{0:T(1024)S(1)} %broadcast_select_fusion, f32[2048]{0:T(1024)S(1)} %get-tuple-element.194), kind=kCustom, calls=%fused_computation.4 | custom fusion | flops 2048 | bytes 32768
  289.9 5.3 collective-permute-start.18
  295.2 3.1 collective-permute-start.19
  298.5 4.5 collective-permute-done.19
  309.8 1.8 negate_multiply_fusion
  312.5 11.6 %scatter_fusion.1 = f32[65536]{0:T(1024)S(1)} fusion(f32[65536]{0:T(1024)S(1)} %bitcast.1244, s32[2048]{0:T(1024)S(1)} %broadcast_select_fusion, f32[2048]{0:T(1024)S(1)} %get-tuple-element.193), kind=kCustom, calls=%fused_computation.5 | custom fusion | flops 2048 | bytes 32768
  325.6 3.7 collective-permute-start.20
  329.3 4.9 collective-permute-start.21
  334.2 2.9 collective-permute-done.21
  344.9 60.9 %reduce-scatter.2.cloned.1.call-done = f32[2,32,2,128]{3,1,0,2:T(8,128)} async-done(((f32[2,32,32,128]{3,1,0,2:T(8,128)}), f32[2,32,2,128]{3,1,0,2:T(8,128)}) %reduce-scatter.2.cloned.1.call-update) | async-done | bytes 65552 | tf_op jit(solution)/shard_map/reduce_scatter | solution.py:211
  418.6 4.6 collective-permute-start.24
  423.2 3.9 collective-permute-start.25
  427.4 2.8 collective-permute-done.25
  462.1 69.3 %all-reduce.11 = (f32[27,16,16]{2,1,0:T(8,128)S(1)}, f32[27,2,16]{2,1,0:T(2,128)S(1)}) all-reduce(f32[27,16,16]{2,1,0:T(8,128)S(1)} %fusion.84, f32[27,2,16]{2,1,0:T(2,128)S(1)} %fusion.111), channel_id=1, replica_groups=mesh['shot'=16,'brick'=8] {'shot','brick'}, use_global_device_ids=true, to_apply=%region_4.5 | all-reduce | flops 7776 | bytes 62208 | tf_op jit(solution)/shard_map/psum | solution.py:224
  533.0 4.1 collective-permute-start.29
  537.1 3.5 collective-permute-start.28
  541.2 3.9 collective-permute-done.28
  (575 shorter events, 155.3 us)
Async XLA Ops:
  7.2 111.1 %all-gather.2.cloned.1.call-start = ((), (), s32[]{:S(2)}) async-start(), calls=%async_computation.1 | async-start | bytes 1114112 | tf_op jit(solution)/shard_map/all_gather | solution.py:154
  8.5 27.7 %copy-start.22 = (bf16[16,32,2,128]{3,0,2,1:T(8,128)(2,1)}, bf16[16,32,2,128]{3,0,2,1:T(8,128)(2,1)S(1)}, u32[]{:S(2)}) copy-start(bf16[16,32,2,128]{3,0,2,1:T(8,128)(2,1)S(1)} %copy.382) | copy-start | bytes 786436
  9.2 5.8 %collective-permute-start = (bf16[16,32,1,128]{3,0,2,1:T(8,128)(2,1)S(1)}, bf16[16,32,1,128]{3,0,2,1:T(8,128)(2,1)S(1)}, u32[]{:S(2)}, u32[]{:S(2)}) collective-permute-start(bf16[16,32,1,128]{3,0,2,1:T(8,128)(2,1)S(1)} %get-tuple-element.124), channel_id=1, source_target_pairs={{0,8},{8,16},{16,24},{24,32},{32,40},{40,48},{48,56},{56,64},{64,7... | collective-permute-start | bytes 393224 | tf_op jit(solution)/shard_map/ppermute | solution.py:16
  11.0 4.9 collective-permute-start.1
  15.0 29.6 %copy-start.124 = (bf16[2,16]{1,0:T(2,128)(2,1)}, bf16[2,16]{1,0:T(2,128)(2,1)S(1)}, u32[]{:S(2)}) copy-start(bf16[2,16]{1,0:T(2,128)(2,1)S(1)} %get-tuple-element.30) | copy-start | bytes 196
  15.0 40.5 %copy-start.126 = (bf16[2,16]{1,0:T(2,128)(2,1)}, bf16[2,16]{1,0:T(2,128)(2,1)S(1)}, u32[]{:S(2)}) copy-start(bf16[2,16]{1,0:T(2,128)(2,1)S(1)} %get-tuple-element.27) | copy-start | bytes 196
  15.0 52.6 %copy-start.120 = (bf16[2,16]{1,0:T(2,128)(2,1)}, bf16[2,16]{1,0:T(2,128)(2,1)S(1)}, u32[]{:S(2)}) copy-start(bf16[2,16]{1,0:T(2,128)(2,1)S(1)} %get-tuple-element.26) | copy-start | bytes 196
  15.0 52.8 %copy-start.122 = (bf16[2,16]{1,0:T(2,128)(2,1)}, bf16[2,16]{1,0:T(2,128)(2,1)S(1)}, u32[]{:S(2)}) copy-start(bf16[2,16]{1,0:T(2,128)(2,1)S(1)} %get-tuple-element.28) | copy-start | bytes 196
  15.0 20.2 %copy-start.51 = (bf16[16,32,1,128]{3,0,2,1:T(8,128)(2,1)}, bf16[16,32,1,128]{3,0,2,1:T(8,128)(2,1)S(1)}, u32[]{:S(2)}) copy-start(bf16[16,32,1,128]{3,0,2,1:T(8,128)(2,1)S(1)} %collective-permute-done) | copy-start | bytes 393220
  15.8 20.4 %copy-start.49 = (bf16[16,32,1,128]{3,0,2,1:T(8,128)(2,1)}, bf16[16,32,1,128]{3,0,2,1:T(8,128)(2,1)S(1)}, u32[]{:S(2)}) copy-start(bf16[16,32,1,128]{3,0,2,1:T(8,128)(2,1)S(1)} %collective-permute-done.1) | copy-start | bytes 393220
  15.9 15.5 %collective-permute-start.2 = (bf16[16,1,4,128]{3,0,2,1:T(8,128)(2,1)S(1)}, bf16[16,1,4,128]{3,0,2,1:T(8,128)(2,1)S(1)}, u32[]{:S(2)}, u32[]{:S(2)}) collective-permute-start(bf16[16,1,4,128]{3,0,2,1:T(8,128)(2,1)S(1)} %get-tuple-element.99), channel_id=1, source_target_pairs={{0,1},{1,2},{2,3},{3,4},{4,5},{5,6},{6,7},{8,9},{9,10},{10,11},{11... | collective-permute-start | bytes 49160 | tf_op jit(solution)/shard_map/ppermute | solution.py:16
  20.5 10.9 %collective-permute-start.3 = (bf16[16,1,4,128]{3,0,2,1:T(8,128)(2,1)S(1)}, bf16[16,1,4,128]{3,0,2,1:T(8,128)(2,1)S(1)}, u32[]{:S(2)}, u32[]{:S(2)}) collective-permute-start(bf16[16,1,4,128]{3,0,2,1:T(8,128)(2,1)S(1)} %get-tuple-element.100), channel_id=1, source_target_pairs={{1,0},{2,1},{3,2},{4,3},{5,4},{6,5},{7,6},{9,8},{10,9},{11,10},{12... | collective-permute-start | bytes 49160 | tf_op jit(solution)/shard_map/ppermute | solution.py:19
  38.4 24.4 %copy-start.6 = (bf16[16,32,2,128]{3,0,2,1:T(8,128)(2,1)}, bf16[16,32,2,128]{3,0,2,1:T(8,128)(2,1)S(1)}, u32[]{:S(2)}) copy-start(bf16[16,32,2,128]{3,0,2,1:T(8,128)(2,1)S(1)} %fusion.63) | copy-start | bytes 786436
  38.4 6.4 %collective-permute-start.4 = (bf16[16,32,1,128]{3,0,2,1:T(8,128)(2,1)S(1)}, bf16[16,32,1,128]{3,0,2,1:T(8,128)(2,1)S(1)}, u32[]{:S(2)}, u32[]{:S(2)}) collective-permute-start(bf16[16,32,1,128]{3,0,2,1:T(8,128)(2,1)S(1)} %get-tuple-element.121), channel_id=1, source_target_pairs={{0,8},{8,16},{16,24},{24,32},{32,40},{40,48},{48,56},{56,64},{64,7... | collective-permute-start | bytes 393224 | tf_op jit(solution)/shard_map/ppermute | solution.py:16
  43.3 3.5 collective-permute-start.5
  44.8 17.9 %copy-start.45 = (bf16[16,32,1,128]{3,0,2,1:T(8,128)(2,1)}, bf16[16,32,1,128]{3,0,2,1:T(8,128)(2,1)S(1)}, u32[]{:S(2)}) copy-start(bf16[16,32,1,128]{3,0,2,1:T(8,128)(2,1)S(1)} %collective-permute-done.4) | copy-start | bytes 393220
  46.8 8.8 %collective-permute-start.6 = (bf16[16,1,4,128]{3,0,2,1:T(8,128)(2,1)S(1)}, bf16[16,1,4,128]{3,0,2,1:T(8,128)(2,1)S(1)}, u32[]{:S(2)}, u32[]{:S(2)}) collective-permute-start(bf16[16,1,4,128]{3,0,2,1:T(8,128)(2,1)S(1)} %get-tuple-element.97), channel_id=1, source_target_pairs={{0,1},{1,2},{2,3},{3,4},{4,5},{5,6},{6,7},{8,9},{9,10},{10,11},{11... | collective-permute-start | bytes 49160 | tf_op jit(solution)/shard_map/ppermute | solution.py:16
  50.5 7.1 %collective-permute-start.7 = (bf16[16,1,4,128]{3,0,2,1:T(8,128)(2,1)S(1)}, bf16[16,1,4,128]{3,0,2,1:T(8,128)(2,1)S(1)}, u32[]{:S(2)}, u32[]{:S(2)}) collective-permute-start(bf16[16,1,4,128]{3,0,2,1:T(8,128)(2,1)S(1)} %get-tuple-element.98), channel_id=1, source_target_pairs={{1,0},{2,1},{3,2},{4,3},{5,4},{6,5},{7,6},{9,8},{10,9},{11,10},{12... | collective-permute-start | bytes 49160 | tf_op jit(solution)/shard_map/ppermute | solution.py:19
  79.5 326.4 %reduce-scatter.2.cloned.1.call-start = ((), (), s32[]{:S(2)}) async-start(), calls=%async_computation.2 | async-start | bytes 1114112 | tf_op jit(solution)/shard_map/reduce_scatter | solution.py:211
  79.7 12.4 %collective-permute-start.10 = (f32[1,8,16,128]{3,1,2,0:T(8,128)S(1)}, f32[1,8,16,128]{3,1,2,0:T(8,128)S(1)}, u32[]{:S(2)}, u32[]{:S(2)}) collective-permute-start(f32[1,8,16,128]{3,1,2,0:T(8,128)S(1)} %get-tuple-element.119), channel_id=1, source_target_pairs={{0,1},{1,2},{2,3},{3,4},{4,5},{5,6},{6,7},{8,9},{9,10},{10,11},{11... | collective-permute-start | bytes 196616 | tf_op jit(solution)/shard_map/ppermute | solution.py:16
  85.6 7.7 %collective-permute-start.11 = (f32[1,8,16,128]{3,1,2,0:T(8,128)S(1)}, f32[1,8,16,128]{3,1,2,0:T(8,128)S(1)}, u32[]{:S(2)}, u32[]{:S(2)}) collective-permute-start(f32[1,8,16,128]{3,1,2,0:T(8,128)S(1)} %get-tuple-element.120), channel_id=1, source_target_pairs={{1,0},{2,1},{3,2},{4,3},{5,4},{6,5},{7,6},{9,8},{10,9},{11,10},{12... | collective-permute-start | bytes 196616 | tf_op jit(solution)/shard_map/ppermute | solution.py:19
  119.3 10.1 %collective-permute-start.8 = (f32[2,8,16,128]{3,1,2,0:T(8,128)S(1)}, f32[2,8,16,128]{3,1,2,0:T(8,128)S(1)}, u32[]{:S(2)}, u32[]{:S(2)}) collective-permute-start(f32[2,8,16,128]{3,1,2,0:T(8,128)S(1)} %get-tuple-element.89), channel_id=1, source_target_pairs={{0,1},{1,2},{2,3},{3,4},{4,5},{5,6},{6,7},{8,9},{9,10},{10,11},{11... | collective-permute-start | bytes 393224 | tf_op jit(solution)/shard_map/ppermute | solution.py:16
  124.0 8.7 %collective-permute-start.9 = (f32[2,8,16,128]{3,1,2,0:T(8,128)S(1)}, f32[2,8,16,128]{3,1,2,0:T(8,128)S(1)}, u32[]{:S(2)}, u32[]{:S(2)}) collective-permute-start(f32[2,8,16,128]{3,1,2,0:T(8,128)S(1)} %get-tuple-element.90), channel_id=1, source_target_pairs={{1,0},{2,1},{3,2},{4,3},{5,4},{6,5},{7,6},{9,8},{10,9},{11,10},{12... | collective-permute-start | bytes 393224 | tf_op jit(solution)/shard_map/ppermute | solution.py:19
  135.3 19.5 %copy-start.9 = (f32[32,24,128]{2,0,1:T(8,128)}, f32[32,24,128]{2,0,1:T(8,128)S(1)}, u32[]{:S(2)}) copy-start(f32[32,24,128]{2,0,1:T(8,128)S(1)} %get-tuple-element.85) | copy-start | bytes 1179652
  137.4 19.1 %copy-start.2 = (f32[32,16,136]{2,0,1:T(8,128)}, f32[32,16,136]{2,0,1:T(8,128)S(1)}, u32[]{:S(2)}) copy-start(f32[32,16,136]{2,0,1:T(8,128)S(1)} %get-tuple-element.87) | copy-start | bytes 835588
  140.7 17.7 %copy-start.13 = (f32[40,16,128]{2,0,1:T(8,128)}, f32[40,16,128]{2,0,1:T(8,128)S(1)}, u32[]{:S(2)}) copy-start(f32[40,16,128]{2,0,1:T(8,128)S(1)} %get-tuple-element.82) | copy-start | bytes 983044
  142.0 8.7 %collective-permute-start.12 = (f32[1,8,16,128]{3,1,2,0:T(8,128)S(1)}, f32[1,8,16,128]{3,1,2,0:T(8,128)S(1)}, u32[]{:S(2)}, u32[]{:S(2)}) collective-permute-start(f32[1,8,16,128]{3,1,2,0:T(8,128)S(1)} %get-tuple-element.117), channel_id=1, source_target_pairs={{0,1},{1,2},{2,3},{3,4},{4,5},{5,6},{6,7},{8,9},{9,10},{10,11},{11... | collective-permute-start | bytes 196616 | tf_op jit(solution)/shard_map/ppermute | solution.py:16
  146.7 7.7 %collective-permute-start.13 = (f32[1,8,16,128]{3,1,2,0:T(8,128)S(1)}, f32[1,8,16,128]{3,1,2,0:T(8,128)S(1)}, u32[]{:S(2)}, u32[]{:S(2)}) collective-permute-start(f32[1,8,16,128]{3,1,2,0:T(8,128)S(1)} %get-tuple-element.118), channel_id=1, source_target_pairs={{1,0},{2,1},{3,2},{4,3},{5,4},{6,5},{7,6},{9,8},{10,9},{11,10},{12... | collective-permute-start | bytes 196616 | tf_op jit(solution)/shard_map/ppermute | solution.py:19
  161.2 59.5 %collective-permute-start.14 = (f32[1,8,16,128]{3,1,2,0:T(8,128)S(1)}, f32[1,8,16,128]{3,1,2,0:T(8,128)S(1)}, u32[]{:S(2)}, u32[]{:S(2)}) collective-permute-start(f32[1,8,16,128]{3,1,2,0:T(8,128)S(1)} %get-tuple-element.115), channel_id=1, source_target_pairs={{0,1},{1,2},{2,3},{3,4},{4,5},{5,6},{6,7},{8,9},{9,10},{10,11},{11... | collective-permute-start | bytes 196616 | tf_op jit(solution)/shard_map/ppermute | solution.py:16
  165.8 54.9 %collective-permute-start.15 = (f32[1,8,16,128]{3,1,2,0:T(8,128)S(1)}, f32[1,8,16,128]{3,1,2,0:T(8,128)S(1)}, u32[]{:S(2)}, u32[]{:S(2)}) collective-permute-start(f32[1,8,16,128]{3,1,2,0:T(8,128)S(1)} %get-tuple-element.116), channel_id=1, source_target_pairs={{1,0},{2,1},{3,2},{4,3},{5,4},{6,5},{7,6},{9,8},{10,9},{11,10},{12... | collective-permute-start | bytes 196616 | tf_op jit(solution)/shard_map/ppermute | solution.py:19
  257.0 8.6 %collective-permute-start.16 = (f32[1,8,16,128]{3,1,2,0:T(8,128)S(1)}, f32[1,8,16,128]{3,1,2,0:T(8,128)S(1)}, u32[]{:S(2)}, u32[]{:S(2)}) collective-permute-start(f32[1,8,16,128]{3,1,2,0:T(8,128)S(1)} %get-tuple-element.113), channel_id=1, source_target_pairs={{0,1},{1,2},{2,3},{3,4},{4,5},{5,6},{6,7},{8,9},{9,10},{10,11},{11... | collective-permute-start | bytes 196616 | tf_op jit(solution)/shard_map/ppermute | solution.py:16
  260.7 7.8 %collective-permute-start.17 = (f32[1,8,16,128]{3,1,2,0:T(8,128)S(1)}, f32[1,8,16,128]{3,1,2,0:T(8,128)S(1)}, u32[]{:S(2)}, u32[]{:S(2)}) collective-permute-start(f32[1,8,16,128]{3,1,2,0:T(8,128)S(1)} %get-tuple-element.114), channel_id=1, source_target_pairs={{1,0},{2,1},{3,2},{4,3},{5,4},{6,5},{7,6},{9,8},{10,9},{11,10},{12... | collective-permute-start | bytes 196616 | tf_op jit(solution)/shard_map/ppermute | solution.py:19
  289.9 8.6 %collective-permute-start.18 = (f32[1,8,16,128]{3,1,2,0:T(8,128)S(1)}, f32[1,8,16,128]{3,1,2,0:T(8,128)S(1)}, u32[]{:S(2)}, u32[]{:S(2)}) collective-permute-start(f32[1,8,16,128]{3,1,2,0:T(8,128)S(1)} %get-tuple-element.111), channel_id=1, source_target_pairs={{0,1},{1,2},{2,3},{3,4},{4,5},{5,6},{6,7},{8,9},{9,10},{10,11},{11... | collective-permute-start | bytes 196616 | tf_op jit(solution)/shard_map/ppermute | solution.py:16
  295.2 7.8 %collective-permute-start.19 = (f32[1,8,16,128]{3,1,2,0:T(8,128)S(1)}, f32[1,8,16,128]{3,1,2,0:T(8,128)S(1)}, u32[]{:S(2)}, u32[]{:S(2)}) collective-permute-start(f32[1,8,16,128]{3,1,2,0:T(8,128)S(1)} %get-tuple-element.112), channel_id=1, source_target_pairs={{1,0},{2,1},{3,2},{4,3},{5,4},{6,5},{7,6},{9,8},{10,9},{11,10},{12... | collective-permute-start | bytes 196616 | tf_op jit(solution)/shard_map/ppermute | solution.py:19
  325.6 8.6 %collective-permute-start.20 = (f32[1,8,16,128]{3,1,2,0:T(8,128)S(1)}, f32[1,8,16,128]{3,1,2,0:T(8,128)S(1)}, u32[]{:S(2)}, u32[]{:S(2)}) collective-permute-start(f32[1,8,16,128]{3,1,2,0:T(8,128)S(1)} %get-tuple-element.109), channel_id=1, source_target_pairs={{0,1},{1,2},{2,3},{3,4},{4,5},{5,6},{6,7},{8,9},{9,10},{10,11},{11... | collective-permute-start | bytes 196616 | tf_op jit(solution)/shard_map/ppermute | solution.py:16
  329.3 7.8 %collective-permute-start.21 = (f32[1,8,16,128]{3,1,2,0:T(8,128)S(1)}, f32[1,8,16,128]{3,1,2,0:T(8,128)S(1)}, u32[]{:S(2)}, u32[]{:S(2)}) collective-permute-start(f32[1,8,16,128]{3,1,2,0:T(8,128)S(1)} %get-tuple-element.110), channel_id=1, source_target_pairs={{1,0},{2,1},{3,2},{4,3},{5,4},{6,5},{7,6},{9,8},{10,9},{11,10},{12... | collective-permute-start | bytes 196616 | tf_op jit(solution)/shard_map/ppermute | solution.py:19
  344.1 61.8 %copy-start.48 = (f32[2,32,2,128]{3,1,2,0:T(8,128)S(1)}, f32[2,32,2,128]{3,1,2,0:T(8,128)}, u32[]{:S(2)}) copy-start(f32[2,32,2,128]{3,1,2,0:T(8,128)} %copy-done.47) | copy-start | bytes 196612
  344.9 66.4 %copy-start.21 = (bf16[16,33,4,128]{3,0,2,1:T(8,128)(2,1)S(1)}, bf16[16,33,4,128]{3,0,2,1:T(8,128)(2,1)}, u32[]{:S(2)}) copy-start(bf16[16,33,4,128]{3,0,2,1:T(8,128)(2,1)} %copy-done.20) | copy-start | bytes 1622020
  406.7 2.6 collective-permute-start.22
  408.0 3.1 collective-permute-start.23
  418.6 8.8 %collective-permute-start.24 = (bf16[2,1,4,128]{3,1,2,0:T(2,128)(2,1)S(1)}, bf16[2,1,4,128]{3,1,2,0:T(2,128)(2,1)S(1)}, u32[]{:S(2)}, u32[]{:S(2)}) collective-permute-start(bf16[2,1,4,128]{3,1,2,0:T(2,128)(2,1)S(1)} %get-tuple-element.153), channel_id=1, source_target_pairs={{0,1},{1,2},{2,3},{3,4},{4,5},{5,6},{6,7},{8,9},{9,10},{10,11},{11... | collective-permute-start | bytes 6152 | tf_op jit(solution)/shard_map/ppermute | solution.py:16
  423.2 7.0 %collective-permute-start.25 = (bf16[2,1,4,128]{3,1,2,0:T(2,128)(2,1)S(1)}, bf16[2,1,4,128]{3,1,2,0:T(2,128)(2,1)S(1)}, u32[]{:S(2)}, u32[]{:S(2)}) collective-permute-start(bf16[2,1,4,128]{3,1,2,0:T(2,128)(2,1)S(1)} %get-tuple-element.154), channel_id=1, source_target_pairs={{1,0},{2,1},{3,2},{4,3},{5,4},{6,5},{7,6},{9,8},{10,9},{11,10},{12... | collective-permute-start | bytes 6152 | tf_op jit(solution)/shard_map/ppermute | solution.py:19
  459.0 74.0 %collective-permute-start.26 = (bf16[16,32,1,128]{3,0,2,1:T(8,128)(2,1)S(1)}, bf16[16,32,1,128]{3,0,2,1:T(8,128)(2,1)S(1)}, u32[]{:S(2)}, u32[]{:S(2)}) collective-permute-start(bf16[16,32,1,128]{3,0,2,1:T(8,128)(2,1)S(1)} %get-tuple-element.107), channel_id=1, source_target_pairs={{0,8},{8,16},{16,24},{24,32},{32,40},{40,48},{48,56},{56,64},{64,7... | collective-permute-start | bytes 393224 | tf_op jit(solution)/shard_map/ppermute | solution.py:16
  460.3 80.3 %copy-start.97 = (bf16[1,16,16]{2,1,0:T(8,128)(2,1)S(1)}, bf16[1,16,16]{2,1,0:T(8,128)(2,1)}, u32[]{:S(2)}) copy-start(bf16[1,16,16]{2,1,0:T(8,128)(2,1)} %copy-done.96) | copy-start | bytes 1540
  460.3 72.7 %collective-permute-start.27 = (bf16[16,32,1,128]{3,0,2,1:T(8,128)(2,1)S(1)}, bf16[16,32,1,128]{3,0,2,1:T(8,128)(2,1)S(1)}, u32[]{:S(2)}, u32[]{:S(2)}) collective-permute-start(bf16[16,32,1,128]{3,0,2,1:T(8,128)(2,1)S(1)} %get-tuple-element.108), channel_id=1, source_target_pairs={{8,0},{16,8},{24,16},{32,24},{40,32},{48,40},{56,48},{64,56},{72,6... | collective-permute-start | bytes 393224 | tf_op jit(solution)/shard_map/ppermute | solution.py:19
  462.1 78.8 %copy-start.99 = (bf16[1,16,16]{2,1,0:T(8,128)(2,1)S(1)}, bf16[1,16,16]{2,1,0:T(8,128)(2,1)}, u32[]{:S(2)}) copy-start(bf16[1,16,16]{2,1,0:T(8,128)(2,1)} %copy-done.98) | copy-start | bytes 1540
  533.0 8.2 %collective-permute-start.29 = (bf16[16,1,4,128]{3,0,2,1:T(8,128)(2,1)S(1)}, bf16[16,1,4,128]{3,0,2,1:T(8,128)(2,1)S(1)}, u32[]{:S(2)}, u32[]{:S(2)}) collective-permute-start(bf16[16,1,4,128]{3,0,2,1:T(8,128)(2,1)S(1)} %get-tuple-element.92), channel_id=1, source_target_pairs={{1,0},{2,1},{3,2},{4,3},{5,4},{6,5},{7,6},{9,8},{10,9},{11,10},{12... | collective-permute-start | bytes 49160 | tf_op jit(solution)/shard_map/ppermute | solution.py:19
  537.1 8.0 %collective-permute-start.28 = (bf16[16,1,4,128]{3,0,2,1:T(8,128)(2,1)S(1)}, bf16[16,1,4,128]{3,0,2,1:T(8,128)(2,1)S(1)}, u32[]{:S(2)}, u32[]{:S(2)}) collective-permute-start(bf16[16,1,4,128]{3,0,2,1:T(8,128)(2,1)S(1)} %get-tuple-element.91), channel_id=1, source_target_pairs={{0,1},{1,2},{2,3},{3,4},{4,5},{5,6},{6,7},{8,9},{9,10},{10,11},{11... | collective-permute-start | bytes 49160 | tf_op jit(solution)/shard_map/ppermute | solution.py:16
  (116 other events, 501.1 us)
Sparse Core Ops, SparseCore 0:
  79.6 38.5 all-gather.1
  345.1 60.7 reduce-scatter.1
where the time goes:
time: 575 us; the launch traced here: 565 us
  waiting for transfers between devices  116 us (20%)
  starting transfers between devices  106 us (18%)
  local copies, waits for them, and re-layouts  98.6 us (17%)
  other arithmetic  88.4 us (15%)
  matrix products  69.4 us (12%)
  blocking collectives  69.3 us (12%)
  between operations  17.5 us (3%)
    psum x1, blocking collectives, per_device(): lax.psum((grad_first, grad_second), ('shot', 'brick'))  69.3 us
    gather x3, local copies, waits for them, and re-layouts, per_device(): following[cell_x, cell_y, cell_z] - recorded[len(residuals)]  66.2 us
    reduce_scatter x1, waiting for transfers between devices, per_device(): lax.psum_scatter(column_grad, 'shot', scatter_dimension=2, tiled=True)  60.9 us
    ppermute x15, starting transfers between devices, with_halo(): lax.ppermute(lax.slice_in_dim(block, block.shape[dim] - width, None, axis...  58.2 us
    ppermute x15, starting transfers between devices, with_halo(): lax.ppermute(lax.slice_in_dim(block, 0, width, axis=dim), axis, backward)  48.2 us
    unnamed x6, other arithmetic  35.9 us
    dot_general x54, matrix products, conv_back(): jnp.einsum('oc,oxyz->cxyz', weights[kernel_index], window, preferred_elem...  29.4 us
    ppermute x15, waiting for transfers between devices, with_halo(): lax.ppermute(lax.slice_in_dim(block, 0, width, axis=dim), axis, backward)  27.5 us
  transfers between devices with their start and end apart: 32, of which 16 were waited for; matrix products, arithmetic and copies ran while one was open for 13% of the time, Pallas kernels for 0%

commit v1 on v0

v1 whole, which is shorter than its diff:
```python
import functools

import jax
import jax.numpy as jnp
from jax import lax
from jax.experimental import pallas as pl
from jax.experimental.pallas import tpu as pltpu
from jax.sharding import PartitionSpec as P

F32 = jnp.float32
BF16 = jnp.bfloat16
stencil_taps = (1225.0 / 1024.0, -245.0 / 3072.0, 49.0 / 5120.0, -5.0 / 7168.0)
ratios = tuple(tap / stencil_taps[0] for tap in stencil_taps)
tap_square = stencil_taps[0] ** 2
misfit_weight = 16.0

bricks, shots = 8, 16
bx = 32
ay = 16
nz = 128
rim = 24
dom = bx + 2 * rim
lead = 8
xpad = dom + 24
ypad = ay + 8
gx = bx + 4
vmem = pltpu.CompilerParams(vmem_limit_bytes=40 * 1024 * 1024)


def whole(count):
    return [pl.BlockSpec(memory_space=pltpu.VMEM)] * count


scalars = pl.BlockSpec(memory_space=pltpu.SMEM)


def lane_index():
    return lax.broadcasted_iota(jnp.int32, (1, nz), 1)


def lane_shift(value, offset):
    if offset == 1:
        return value
    lane = lax.broadcasted_iota(jnp.int32, value.shape, 1)
    if offset == 0:
        return jnp.where(lane == 0, 0.0, pltpu.roll(value, 1, 1))
    return jnp.where(lane == nz - 1, 0.0, pltpu.roll(value, nz - 1, 1))


def generator_kernel(
    at_ref, lo_ref, mid_ref, hi_ref, w1_ref, w2_ref, coef_ref, out_ref, hid_ref, s1, s2
):
    shot, brick = at_ref[0], at_ref[1]
    y_fine = (shot > 0, True, shot < shots - 1)

    def spread(x, carry):
        x_fine = ((x >= 4) | (brick > 0)) & ((x < bx + 4) | (brick < bricks - 1))
        for part, ref in enumerate((lo_ref, mid_ref, hi_ref)):
            fine = x_fine & y_fine[part]
            for row in range(2):
                value = jnp.where(fine, ref[row, x].astype(F32), 0.0)
                for k in range(3):
                    s1[x, pl.ds((2 * part + row) * 48 + k * 16, 16), :] = lane_shift(
                        value, k
                    ).astype(BF16)
        return carry

    lax.fori_loop(0, bx + 8, spread, 0)

    def first_conv(block, carry):
        rows = s1[pl.ds(2 * block, 4)].reshape(4 * 288, nz)
        acc = jnp.tanh(jnp.dot(w1_ref[...], rows, preferred_element_type=F32))
        for xo in range(2):
            x = 2 * block + xo
            x_fine = ((x >= 3) | (brick > 0)) & ((x < bx + 3) | (brick < bricks - 1))
            for y in range(4):
                fine = x_fine
                if y == 0:
                    fine = fine & (shot > 0)
                if y == 3:
                    fine = fine & (shot < shots - 1)
                start = (xo * 4 + y) * 16
                value = jnp.where(fine, acc[start : start + 16], 0.0).astype(BF16)
                hid_ref[x, pl.ds(y * 16, 16), :] = value
                wide = value.astype(F32)
                for k in range(3):
                    s2[x, pl.ds(y * 48 + k * 16, 16), :] = lane_shift(wide, k).astype(BF16)
        return carry

    lax.fori_loop(0, (bx + 6) // 2, first_conv, 0)

    for block in range(gx // 6):
        rows = s2[pl.ds(6 * block, 8)].reshape(8 * 192, nz)
        acc = jnp.dot(w2_ref[...], rows, preferred_element_type=F32)
        for channel in range(2):
            for y in range(2):
                start = (channel * 2 + y) * 6
                out_ref[channel, y, pl.ds(6 * block, 6), :] = acc[start : start + 6]
    for y in range(2):
        modulus = 0.03 + 0.09 * jax.nn.sigmoid(out_ref[0, y, pl.ds(2, bx), :])
        buoyancy = jnp.exp(0.35 * jnp.tanh(out_ref[1, y, pl.ds(2, bx), :]))
        coef_ref[y, 0] = modulus
        coef_ref[y, 1] = buoyancy


def generator(at, lo, mid, hi, w1, w2):
    return pl.pallas_call(
        generator_kernel,
        out_shape=(
            jax.ShapeDtypeStruct((2, 2, bx, nz), F32),
            jax.ShapeDtypeStruct((2, 2, gx, nz), F32),
            jax.ShapeDtypeStruct((bx + 6, 64, nz), BF16),
        ),
        in_specs=[scalars] + whole(5),
        out_specs=tuple(whole(3)),
        scratch_shapes=[
            pltpu.VMEM((bx + 8, 288, nz), BF16),
            pltpu.VMEM((bx + 6, 192, nz), BF16),
        ],
        compiler_params=vmem,
        name="generator",
    )(at, lo, mid, hi, w1, w2)


def receiver_kernel(at_ref, cell_ref, seen_ref, out_ref, hot, spread):
    brick, first_row = at_ref[1], at_ref[2]
    count = cell_ref.shape[1]
    x = cell_ref[0:1] - brick * bx + rim
    row_of = jnp.where((x >= 0) & (x < dom), (cell_ref[1:2] - first_row) * dom + x, -1)
    z = cell_ref[2:3]

    def mark(chunk, carry):
        rows = chunk * 16 + lax.broadcasted_iota(jnp.int32, (16, count), 0)
        hot[pl.ds(chunk * 16, 16), :] = jnp.where(rows == row_of, 1.0, 0.0).astype(BF16)
        return carry

    lax.fori_loop(0, ay * dom // 16, mark, 0)
    parts = [jnp.ones((1, count), F32)]
    for step in range(3):
        value = seen_ref[step : step + 1]
        high = value.astype(BF16).astype(F32)
        parts += [high, value - high]

    def place(chunk, carry):
        same = chunk * 16 + lax.broadcasted_iota(jnp.int32, (16, count), 0) == z
        for index, part in enumerate(parts):
            spread[pl.ds(index * nz + chunk * 16, 16), :] = jnp.where(same, part, 0.0).astype(BF16)
        return carry

    lax.fori_loop(0, nz // 16, place, 0)
    size = 256

    def multiply(chunk, carry):
        left = hot[pl.ds(chunk * size, size), :]
        for field in range(4):
            first = 0 if field == 0 else (2 * field - 1) * nz
            right = spread[pl.ds(first, nz if field == 0 else 2 * nz), :]
            acc = lax.dot_general(
                left, right, (((1,), (1,)), ((), ())), preferred_element_type=F32
            )
            if field:
                acc = acc[:, :nz] + acc[:, nz:]
            out_ref[field, pl.ds(chunk * size, size), :] = acc
        return carry

    lax.fori_loop(0, ay * dom // size, multiply, 0)


def receiver_fields(at, cells, seen):
    count = cells.shape[1]
    return pl.pallas_call(
        receiver_kernel,
        out_shape=jax.ShapeDtypeStruct((4, ay * dom, nz), F32),
        in_specs=[scalars] + whole(2),
        out_specs=whole(1)[0],
        scratch_shapes=[
            pltpu.VMEM((ay * dom, count), BF16),
            pltpu.VMEM((7 * nz, count), BF16),
        ],
        compiler_params=vmem,
        cost_estimate=pl.CostEstimate(
            flops=2 * ay * dom * count * 7 * nz, bytes_accessed=4 * ay * dom * nz * 4, transcendentals=0
        ),
        name="receiver_fields",
    )(at, cells, seen)


def lane_factors():
    lane = lane_index()
    last = lane == nz - 1
    upper = [jnp.where((lane <= nz - 1 - t) | last, ratios[t - 1], 0.0) for t in range(1, 5)]
    lower = [jnp.where(lane >= t - 1, ratios[t - 1], 0.0) for t in range(1, 5)]
    above = [jnp.where(lane <= nz - t, ratios[t - 1], 0.0) for t in range(1, 5)]
    return last, upper, lower, above


def turn(value, shift):
    shift = shift % nz
    return value if shift == 0 else pltpu.roll(value, shift, 1)


def slope_z(value, factors):
    last, upper, lower, _ = factors
    up = sum(upper[t - 1] * turn(value, -t) for t in range(1, 5))
    low = sum(lower[t - 1] * turn(value, t - 1) for t in range(1, 5))
    slope = up - low
    return jnp.where(last, -low, slope), jnp.where(last, up, slope)


def differences(get):
    total = None
    for t in range(1, 5):
        upper, lower = get(t)
        term = upper - lower
        if t > 1:
            term = ratios[t - 1] * term
        total = term if total is None else total + term
    return total


def load_padded(ref, pieces):
    ref[...] = jnp.zeros(ref.shape, F32)

    def body(y, carry):
        for first, rows in pieces:
            value = rows(y)
            ref[y + 4, pl.ds(lead + first, value.shape[0]), :] = value
        return carry

    lax.fori_loop(0, ay, body, 0)


def face_weights(buoy, wx, wy, wz, wzl, factors):
    last = factors[0]
    half = 0.5 * tap_square

    def body(y, carry):
        value = buoy[y + 4, pl.ds(0, dom + 16), :]
        wx[y] = half * (value + buoy[y + 4, pl.ds(1, dom + 16), :])
        inner = buoy[y + 4, pl.ds(lead, dom), :]
        ahead = pltpu.roll(inner, nz - 1, 1)
        wz[y] = half * jnp.where(last, inner, inner + ahead)
        wzl[y] = half * jnp.where(last, ahead, inner + ahead)
        return carry

    lax.fori_loop(0, ay, body, 0)

    def faces(j, carry):
        wy[j] = half * (buoy[j + 3, pl.ds(lead, dom), :] + buoy[j + 4, pl.ds(lead, dom), :])
        return carry

    lax.fori_loop(0, ay + 1, faces, 0)


def slope_y(field, j, first, rows):
    return differences(
        lambda t: (
            field[j + 3 + t, pl.ds(lead + first, rows), :],
            field[j + 4 - t, pl.ds(lead + first, rows), :],
        )
    )


def apply_operator(field, weights, flux_y, flux_x, factors, first, rows, consume):
    wx, wy, wz, wzl = weights
    _, _, lower, above = factors

    def faces(j, carry):
        flux_y[j + 3, pl.ds(0, rows), :] = wy[j, pl.ds(first, rows), :] * slope_y(field, j, first, rows)
        return carry

    lax.fori_loop(0, ay + 1, faces, 0)
    base = lead + first - 4
    more = rows + 8

    def body(y, carry):
        flux_x[pl.ds(0, more), :] = wx[y, pl.ds(base, more), :] * differences(
            lambda t: (
                field[y + 4, pl.ds(base + t, more), :],
                field[y + 4, pl.ds(base + 1 - t, more), :],
            )
        )
        total = differences(
            lambda t: (
                flux_y[y + t + 3, pl.ds(0, rows), :],
                flux_y[y - t + 4, pl.ds(0, rows), :],
            )
        )
        here, before = slope_z(field[y + 4, pl.ds(lead + first, rows), :], factors)
        here = wz[y, pl.ds(first, rows), :] * here
        before = wzl[y, pl.ds(first, rows), :] * before
        total = total + sum(above[t - 1] * turn(here, 1 - t) for t in range(1, 5))
        total = total - sum(lower[t - 1] * turn(before, t) for t in range(1, 5))
        total = total + differences(
            lambda t: (flux_x[pl.ds(3 + t, rows), :], flux_x[pl.ds(4 - t, rows), :])
        )
        consume(y, total)
        return carry

    lax.fori_loop(0, ay, body, 0)


def clear_rims(flux_y):
    for j in (0, 1, 2, 20, 21, 22):
        flux_y[j] = jnp.zeros(flux_y.shape[1:], F32)


def halo_scale(at_ref):
    brick = at_ref[1]
    return (
        jnp.where(brick > 0, 1.0, 0.0).astype(F32),
        jnp.where(brick < bricks - 1, 1.0, 0.0).astype(F32),
    )


def load_window(at_ref, win_ref, clo_ref, chi_ref, modulus, buoy):
    low, high = halo_scale(at_ref)
    load_padded(
        buoy,
        (
            (0, lambda y: low * clo_ref[y, 1]),
            (rim, lambda y: win_ref[y, 1]),
            (rim + bx, lambda y: high * chi_ref[y, 1]),
        ),
    )

    def body(y, carry):
        modulus[y, pl.ds(0, rim), :] = low * clo_ref[y, 0]
        modulus[y, pl.ds(rim, bx), :] = win_ref[y, 0]
        modulus[y, pl.ds(rim + bx, rim), :] = high * chi_ref[y, 0]
        return carry

    lax.fori_loop(0, ay, body, 0)


weight_shapes = [
    pltpu.VMEM((ay, dom + 16, nz), F32),
    pltpu.VMEM((ay + 1, dom, nz), F32),
    pltpu.VMEM((ay, dom, nz), F32),
    pltpu.VMEM((ay, dom, nz), F32),
]
padded = pltpu.VMEM((ypad, xpad, nz), F32)


def forward_kernel(
    at_ref, win_ref, clo_ref, chi_ref, src_ref, plo_ref, phi_ref,
    p1_ref, p2_ref, p3_ref, p4_ref, image_ref, ahead_ref, behind_ref,
    modulus, buoy, f1, f2, f3, wx, wy, wz, wzl, flux_y, flux_x,
):
    factors = lane_factors()
    load_window(at_ref, win_ref, clo_ref, chi_ref, modulus, buoy)
    weights = (wx, wy, wz, wzl)
    face_weights(buoy, *weights, factors)
    clear_rims(flux_y)
    low, high = halo_scale(at_ref)
    load_padded(
        f1,
        (
            (0, lambda y: low * plo_ref[y]),
            (rim, lambda y: src_ref[y]),
            (rim + bx, lambda y: high * phi_ref[y]),
        ),
    )
    f2[...] = jnp.zeros(f2.shape, F32)
    f3[...] = jnp.zeros(f3.shape, F32)

    def first_step(y, image):
        f2[y + 4, pl.ds(lead + 8, 64), :] = (
            2.0 * f1[y + 4, pl.ds(lead + 8, 64), :] + modulus[y, pl.ds(8, 64), :] * image
        )
        image_ref[0, y] = image[8:56]

    def second_step(y, image):
        value = (
            2.0 * f2[y + 4, pl.ds(lead + 16, 48), :]
            - f1[y + 4, pl.ds(lead + 16, 48), :]
            + modulus[y, pl.ds(16, 48), :] * image
        )
        f3[y + 4, pl.ds(lead + 16, 48), :] = value
        image_ref[1, y] = image
        p3_ref[y] = value
        p1_ref[y] = f1[y + 4, pl.ds(lead + 8, 64), :]
        p2_ref[y] = f2[y + 4, pl.ds(lead + 8, 64), :]
        ahead_ref[y, pl.ds(rim, 8), :] = value[24:32]
        behind_ref[y, pl.ds(rim, 8), :] = value[16:24]

    def third_step(y, image):
        image_ref[2, y] = image
        value = (
            2.0 * f3[y + 4, pl.ds(lead + rim, bx), :]
            - f2[y + 4, pl.ds(lead + rim, bx), :]
            + modulus[y, pl.ds(rim, bx), :] * image[8:40]
        )
        p4_ref[y] = value
        ahead_ref[y, pl.ds(0, rim), :] = value[8:32]
        behind_ref[y, pl.ds(0, rim), :] = value[0:24]

    apply_operator(f1, weights, flux_y, flux_x, factors, 8, 64, first_step)
    apply_operator(f2, weights, flux_y, flux_x, factors, 16, 48, second_step)
    apply_operator(f3, weights, flux_y, flux_x, factors, 16, 48, third_step)


def forward_waves(at, window, clo, chi, source, plo, phi):
    shapes = [(ay, 64, nz), (ay, 64, nz), (ay, 48, nz), (ay, bx, nz), (3, ay, 48, nz), (ay, 32, nz), (ay, 32, nz)]
    return pl.pallas_call(
        forward_kernel,
        out_shape=tuple(jax.ShapeDtypeStruct(shape, F32) for shape in shapes),
        in_specs=[scalars] + whole(6),
        out_specs=tuple(whole(7)),
        scratch_shapes=[
            pltpu.VMEM((ay, dom, nz), F32),
            padded, padded, padded, padded,
            *weight_shapes,
            pltpu.VMEM((23, dom, nz), F32),
            pltpu.VMEM((dom + 16, nz), F32),
        ],
        compiler_params=vmem,
        name="forward_waves",
    )(at, window, clo, chi, source, plo, phi)


def adjoint_kernel(
    at_ref, win_ref, clo_ref, chi_ref, p1_ref, p2_ref, p3_ref, p4_ref, image_ref, back_ref, front_ref, seen_ref,
    column_ref,
    modulus, buoy, scaled, wave, later, late, grad_m, grad_b, wx, wy, wz, wzl, flux_y, flux_x, cross_y, cross_x,
):
    factors = lane_factors()
    load_window(at_ref, win_ref, clo_ref, chi_ref, modulus, buoy)
    weights = (wx, wy, wz, wzl)
    face_weights(buoy, *weights, factors)
    clear_rims(flux_y)
    low, high = halo_scale(at_ref)
    scaled[...] = jnp.zeros(scaled.shape, F32)
    wave[...] = jnp.zeros(wave.shape, F32)

    def residual(step, y, first, value):
        rows = value.shape[0]
        start = pl.multiple_of(y * dom + first, 8)
        count = seen_ref[0, pl.ds(start, rows), :]
        total = seen_ref[step, pl.ds(start, rows), :]
        return misfit_weight * (count * value - total)

    def seed(y, carry):
        for first, value in (
            (0, low * back_ref[y, pl.ds(0, rim), :]),
            (rim, p4_ref[y]),
            (rim + bx, high * front_ref[y, pl.ds(0, rim), :]),
        ):
            rows = value.shape[0]
            error = residual(3, y, first, value)
            later[y, pl.ds(first, rows), :] = error
            scaled[y + 4, pl.ds(lead + first, rows), :] = modulus[y, pl.ds(first, rows), :] * error
        return carry

    lax.fori_loop(0, ay, seed, 0)
    grad_m[...] = jnp.zeros(grad_m.shape, F32)
    grad_b[...] = jnp.zeros(grad_b.shape, F32)

    def set_wave(ref, first, offset):
        def body(y, carry):
            rows = ref.shape[1] - 2 * offset
            wave[y + 4, pl.ds(lead + first, rows), :] = ref[y, pl.ds(offset, rows), :]
            return carry

        lax.fori_loop(0, ay, body, 0)

    def gradients(adjoint_of, image):
        def faces(j, carry):
            cross_y[j] = slope_y(scaled, j, 16, 48) * slope_y(wave, j, 16, 48)
            return carry

        lax.fori_loop(0, ay + 1, faces, 0)
        base = lead + 8

        def body(y, carry):
            def slope_x(field):
                return differences(
                    lambda t: (
                        field[y + 4, pl.ds(base + t, 56), :],
                        field[y + 4, pl.ds(base + 1 - t, 56), :],
                    )
                )

            cross_x[...] = slope_x(scaled) * slope_x(wave)
            here_s, before_s = slope_z(scaled[y + 4, pl.ds(lead + 16, 48), :], factors)
            here_w, before_w = slope_z(wave[y + 4, pl.ds(lead + 16, 48), :], factors)
            total = here_s * here_w + pltpu.roll(before_s * before_w, 1, 1)
            total = total + cross_y[y] + cross_y[y + 1]
            total = total + cross_x[pl.ds(7, 48), :] + cross_x[pl.ds(8, 48), :]
            grad_b[y] = grad_b[y] - (0.5 * tap_square) * total
            grad_m[y] = grad_m[y] + adjoint_of(y) * image_ref[image, y]
            return carry

        lax.fori_loop(0, ay, body, 0)

    set_wave(p3_ref, 16, 0)
    gradients(lambda y: later[y, pl.ds(16, 48), :], 2)

    def step_three(y, image):
        value = jnp.concatenate(
            [
                low * back_ref[y, pl.ds(rim, 8), :],
                p3_ref[y],
                high * front_ref[y, pl.ds(rim, 8), :],
            ],
            axis=0,
        )
        late[y] = residual(2, y, 8, value) + 2.0 * later[y, pl.ds(8, 64), :] + image

    apply_operator(scaled, weights, flux_y, flux_x, factors, 8, 64, step_three)

    def rescale(y, carry):
        scaled[y + 4, pl.ds(lead + 8, 64), :] = modulus[y, pl.ds(8, 64), :] * late[y]
        return carry

    lax.fori_loop(0, ay, rescale, 0)
    set_wave(p2_ref, 8, 0)
    gradients(lambda y: late[y, pl.ds(8, 48), :], 1)

    def step_two(y, image):
        value = (
            residual(1, y, 16, p2_ref[y, pl.ds(8, 48), :])
            + 2.0 * late[y, pl.ds(8, 48), :]
            + image
            - later[y, pl.ds(16, 48), :]
        )
        later[y, pl.ds(16, 48), :] = value

    apply_operator(scaled, weights, flux_y, flux_x, factors, 16, 48, step_two)

    def rescale_last(y, carry):
        scaled[y + 4, pl.ds(lead + 16, 48), :] = modulus[y, pl.ds(16, 48), :] * later[y, pl.ds(16, 48), :]
        return carry

    lax.fori_loop(0, ay, rescale_last, 0)
    set_wave(p1_ref, 8, 0)
    gradients(lambda y: later[y, pl.ds(16, 48), :], 0)

    column_ref[...] = jnp.zeros(column_ref.shape, F32)
    first_row = at_ref[2]

    def place(y, carry):
        column_ref[first_row + y, pl.ds(0, gx), :] = grad_m[y, pl.ds(6, gx), :]
        column_ref[first_row + y, pl.ds(gx, gx), :] = grad_b[y, pl.ds(6, gx), :]
        return carry

    lax.fori_loop(0, ay, place, 0)


def adjoint_waves(at, window, clo, chi, fields, back, front, seen):
    return pl.pallas_call(
        adjoint_kernel,
        out_shape=jax.ShapeDtypeStruct((2 * shots, 2 * gx, nz), F32),
        in_specs=[scalars] + whole(11),
        out_specs=whole(1)[0],
        scratch_shapes=[
            pltpu.VMEM((ay, dom, nz), F32),
            padded, padded, padded,
            pltpu.VMEM((ay, dom, nz), F32),
            pltpu.VMEM((ay, 64, nz), F32),
            pltpu.VMEM((ay, 48, nz), F32),
            pltpu.VMEM((ay, 48, nz), F32),
            *weight_shapes,
            pltpu.VMEM((23, dom, nz), F32),
            pltpu.VMEM((dom + 16, nz), F32),
            pltpu.VMEM((ay + 1, 48, nz), F32),
            pltpu.VMEM((56, nz), F32),
        ],
        compiler_params=vmem,
        name="adjoint_waves",
    )(at, window, clo, chi, *fields, back, front, seen)


def chain_kernel(at_ref, got_ref, out_ref, grad_ref):
    brick = at_ref[1]
    row = lax.broadcasted_iota(jnp.int32, (gx, nz), 0)
    fine = ((row >= 2) | (brick > 0)) & ((row < gx - 2) | (brick < bricks - 1))
    for y in range(2):
        total = got_ref[0, y]
        for shot in range(1, shots):
            total = total + got_ref[shot, y]
        squashed = jax.nn.sigmoid(out_ref[0, y])
        bent = jnp.tanh(out_ref[1, y])
        buoyancy = jnp.exp(0.35 * bent)
        first = total[:gx] * 0.09 * squashed * (1.0 - squashed)
        second = total[gx:] * buoyancy * 0.35 * (1.0 - bent * bent)
        grad_ref[y, 0] = jnp.where(fine, first, 0.0).astype(BF16)
        grad_ref[y, 1] = jnp.where(fine, second, 0.0).astype(BF16)


def chain(at, got, output):
    return pl.pallas_call(
        chain_kernel,
        out_shape=jax.ShapeDtypeStruct((2, 2, gx, nz), BF16),
        in_specs=[scalars] + whole(2),
        out_specs=whole(1)[0],
        compiler_params=vmem,
        name="chain",
    )(at, got, output)


def backward_kernel(
    at_ref, glo_ref, gmid_ref, ghi_ref, hid_ref, lo_ref, mid_ref, hi_ref, w3_ref, w4_ref,
    latent_ref, kernel_ref,
    grads, own, s1, s2, s3, s4, inner,
):
    shot, brick = at_ref[0], at_ref[1]
    y_fine = (shot > 0, True, shot < shots - 1)
    grads[...] = jnp.zeros(grads.shape, F32)
    own[...] = jnp.zeros(own.shape, F32)
    for part, ref in enumerate((glo_ref, gmid_ref, ghi_ref)):
        for row in range(2):
            for channel in range(2):
                value = jnp.where(y_fine[part], ref[row, channel].astype(F32), 0.0)
                grads[(2 * part + row) * 2 + channel, pl.ds(0, gx), :] = value
                if part == 1:
                    own[:, channel * 2 + row, :] = value[2 : bx + 2]

    def hidden_grad(block, carry):
        for plane in range(12):
            value = grads[plane, pl.ds(8 * block, 16), :]
            for k in range(3):
                s3[pl.ds((plane * 3 + k) * 16, 16), :] = lane_shift(value, k).astype(BF16)
        acc = jnp.dot(w3_ref[...], s3[...], preferred_element_type=F32)
        for xo in range(8):
            x = 8 * block + xo
            x_fine = ((x >= 1) | (brick > 0)) & ((x < bx + 1) | (brick < bricks - 1))
            for y in range(4):
                fine = x_fine
                if y == 0:
                    fine = fine & (shot > 0)
                if y == 3:
                    fine = fine & (shot < shots - 1)
                hidden = hid_ref[jnp.minimum(x + 2, bx + 5), pl.ds(y * 16, 16), :].astype(F32)
                start = (xo * 4 + y) * 16
                value = acc[start : start + 16] * (1.0 - hidden * hidden)
                value = jnp.where(fine, value, 0.0).astype(BF16)
                if y in (1, 2):
                    inner[x, pl.ds((y - 1) * 16, 16), :] = value
                wide = value.astype(F32)
                for k in range(3):
                    s4[x, pl.ds(y * 48 + k * 16, 16), :] = lane_shift(wide, k).astype(BF16)
        return carry

    lax.fori_loop(0, 5, hidden_grad, 0)

    def latent_grad(block, carry):
        rows = s4[pl.ds(4 * block, 6)].reshape(6 * 192, nz)
        acc = jnp.dot(w4_ref[...], rows, preferred_element_type=F32)
        latent_ref[pl.ds(4 * block, 4)] = acc.reshape(4, 32, nz)
        return carry

    lax.fori_loop(0, bx // 4, latent_grad, 0)

    def spread(x, carry):
        x_fine = ((x >= 1) | (brick > 0)) & ((x < bx + 1) | (brick < bricks - 1))
        for y, (ref, row, part) in enumerate(((lo_ref, 1, 0), (mid_ref, 0, 1), (mid_ref, 1, 1), (hi_ref, 0, 2))):
            value = jnp.where(x_fine & y_fine[part], ref[row, x + 3].astype(F32), 0.0)
            hidden = hid_ref[x + 2, pl.ds(y * 16, 16), :].astype(F32)
            for k in range(3):
                s1[x, pl.ds(y * 48 + k * 16, 16), :] = lane_shift(value, k).astype(BF16)
                s2[x, pl.ds(y * 48 + k * 16, 16), :] = lane_shift(hidden, k).astype(BF16)
        return carry

    lax.fori_loop(0, bx + 2, spread, 0)

    def kernel_grad(x, carry):
        first, second = carry
        contract = (((1,), (1,)), ((), ()))
        first = first + lax.dot_general(
            inner[x + 1], s1[pl.ds(x, 3)].reshape(576, nz), contract, preferred_element_type=F32
        )
        second = second + lax.dot_general(
            own[x].astype(BF16), s2[pl.ds(x, 3)].reshape(576, nz), contract, preferred_element_type=F32
        )
        return first, second

    first, second = lax.fori_loop(
        0, bx, kernel_grad, (jnp.zeros((32, 576), F32), jnp.zeros((8, 576), F32))
    )
    kernel_ref[...] = jnp.zeros(kernel_ref.shape, F32)
    for dx in range(3):
        start = dx * 192
        one = first[:16, start : start + 144] + first[16:, start + 48 : start + 192]
        for channel in range(2):
            row = channel * 2
            two = (
                second[row : row + 1, start : start + 144]
                + second[row + 1 : row + 2, start + 48 : start + 192]
            )
            place = dx * 2 * 18 + 16 + channel
            kernel_ref[pl.ds(place, 1), :] = two[:, :128]
            kernel_ref[pl.ds(place + 18, 1), pl.ds(0, 16)] = two[:, 128:]
        kernel_ref[pl.ds(dx * 36, 16), :] = one[:, :128]
        kernel_ref[pl.ds(dx * 36 + 18, 16), pl.ds(0, 16)] = one[:, 128:]


def backward(at, glo, gmid, ghi, hidden, lo, mid, hi, w3, w4):
    return pl.pallas_call(
        backward_kernel,
        out_shape=(
            jax.ShapeDtypeStruct((bx, 32, nz), F32),
            jax.ShapeDtypeStruct((128, nz), F32),
        ),
        in_specs=[scalars] + whole(9),
        out_specs=tuple(whole(2)),
        scratch_shapes=[
            pltpu.VMEM((12, 48, nz), F32),
            pltpu.VMEM((bx, 8, nz), F32),
            pltpu.VMEM((bx + 2, 192, nz), BF16),
            pltpu.VMEM((bx + 2, 192, nz), BF16),
            pltpu.VMEM((576, nz), BF16),
            pltpu.VMEM((40, 192, nz), BF16),
            pltpu.VMEM((40, 32, nz), BF16),
        ],
        compiler_params=vmem,
        name="backward",
    )(at, glo, gmid, ghi, hidden, lo, mid, hi, w3, w4)


def both_ways(ahead, behind, axis):
    count = lax.axis_size(axis)
    forward = [(i, (i + 1) % count) for i in range(count)]
    backward_ = [(target, source) for source, target in forward]
    return lax.ppermute(ahead, axis, forward), lax.ppermute(behind, axis, backward_)


def banded(outputs, inputs):
    step = jnp.arange(inputs)[None, :] - jnp.arange(outputs)[:, None]
    return (step[:, :, None] == jnp.arange(3)[None, None, :]).astype(BF16)


def band_matrix(weights, x_out, y_out, form):
    rows = jnp.einsum("yjb,abkoc->yjakoc", banded(y_out, y_out + 2), weights)
    x_in = 16 if x_out == 8 else x_out + 2
    full = jnp.einsum("xia,yjakoc->" + form, banded(x_out, x_in), rows)
    return full


def per_device(latent, conv_in, conv_out, source_field, observed, aperture, receivers):
    shot = lax.axis_index("shot")
    brick = lax.axis_index("brick")
    at = jnp.stack([shot, brick, aperture[0]]).astype(jnp.int32)
    taps_in = conv_in.reshape(3, 3, 3, 16, 16)
    taps_out = conv_out.reshape(3, 3, 3, 2, 16)
    w1 = band_matrix(taps_in, 2, 4, "xyoijkc").reshape(128, 1152)
    w2 = band_matrix(taps_out, 6, 2, "oyxijkc").reshape(24, 1536)
    w3 = band_matrix(taps_out[::-1, ::-1, ::-1], 8, 4, "xycjoki").reshape(512, 576)
    w4 = band_matrix(taps_in[::-1, ::-1, ::-1], 4, 2, "xycijko").reshape(128, 1152)

    tile = jnp.transpose(latent, (2, 1, 0, 3))
    from_low, from_high = both_ways(tile[:, bx - 4 :], tile[:, :4], "brick")
    mid = jnp.concatenate([from_low, tile, from_high], axis=1)
    lo, hi = both_ways(mid, mid, "shot")
    source = jnp.transpose(source_field[0], (1, 0, 2))
    plo, phi = both_ways(source[:, bx - rim :], source[:, :rim], "brick")
    seen = receiver_fields(at, receivers[0], observed[0])

    coefficients, output, hidden = generator(at, lo, mid, hi, w1, w2)
    sent = jnp.broadcast_to(coefficients[None], (shots, 2, 2, bx, nz))
    column = lax.all_to_all(sent, "shot", 0, 0, tiled=True).reshape(2 * shots, 2, bx, nz)
    window = lax.dynamic_slice_in_dim(column, aperture[0], ay, 0)
    clo, chi = both_ways(window[:, :, bx - rim :], window[:, :, :rim], "brick")
    p1, p2, p3, p4, images, ahead, behind = forward_waves(at, window, clo, chi, source, plo, phi)
    back, front = both_ways(ahead, behind, "brick")
    grads = adjoint_waves(at, window, clo, chi, (p1, p2, p3, p4, images), back, front, seen)
    got = lax.all_to_all(grads, "shot", 0, 0, tiled=True).reshape(shots, 2, 2 * gx, nz)
    grad_output = chain(at, got, output)
    glo, ghi = both_ways(grad_output, grad_output, "shot")
    grad_latent, kernels = backward(at, glo, grad_output, ghi, hidden, lo, mid, hi, w3, w4)
    grad_latent = jnp.transpose(grad_latent.reshape(bx, 2, 16, nz), (2, 0, 1, 3))

    everyone = ("shot", "brick")
    slices = lax.all_to_all(kernels, everyone, 0, 0, tiled=True)
    mine = jnp.sum(slices, axis=0, keepdims=True)
    summed = lax.all_to_all(jnp.broadcast_to(mine, (128, nz)), everyone, 0, 0, tiled=True)
    folded = summed[:108].reshape(3, 2, 18, nz).transpose(0, 2, 1, 3).reshape(3, 18, 256)[:, :, :144]
    folded = folded.reshape(3, 18, 9, 16).transpose(0, 2, 1, 3).reshape(27, 18, 16)
    return (grad_latent, folded[:, :16], folded[:, 16:])


def solution(mesh):
    placed = (
        P(None, "brick", "shot", None),
        P(),
        P(),
        P("shot", "brick", None, None),
        P("shot", None, None),
        P("shot"),
        P("shot", None, None),
    )
    return jax.shard_map(
        per_device,
        mesh=mesh,
        in_specs=placed,
        out_specs=(P(None, "brick", "shot", None), P(), P()),
        check_vma=False,
    )
```

time: 575 us -> 262 us (0.46); the launches traced: 565 us -> 259 us
  other arithmetic: 88.4 us -> 0.29 us
  Pallas kernels: 0 us -> 76.6 us
  starting transfers between devices: 106 us -> 39.7 us
  matrix products: 69.4 us -> 9.17 us
  blocking collectives: 69.3 us -> 16 us
  waiting for transfers between devices: 116 us -> 65.6 us
  local copies, waits for them, and re-layouts: 98.6 us -> 50 us
  between operations: 17.5 us -> 1.65 us
    ppermute x30 -> x12, starting transfers between devices: 106 us -> 24.9 us  [the longest x6 13.6 us: both_ways(): lax.ppermute(behind, axis, backward_)]
    pallas_call x0 -> x6, Pallas kernels: none -> 76.6 us  [the longest x1 25.7 us: adjoint_waves(): pl.pallas_call(adjoint_kernel, out_shape=jax.ShapeDtypeStruct((2 * shots,...]
    psum x1 -> x0, blocking collectives: 69.3 us -> none  [per_device(): lax.psum((grad_first, grad_second), ('shot', 'brick'))]
    gather x3 -> x0, local copies, waits for them, and re-layouts: 66.2 us -> none  [per_device(): following[cell_x, cell_y, cell_z] - recorded[len(residuals)]]
    reduce_scatter x1 -> x0, waiting for transfers between devices: 60.9 us -> none  [per_device(): lax.psum_scatter(column_grad, 'shot', scatter_dimension=2, tiled=True)]
    dot_general x162 -> x8, matrix products: 69.4 us -> 9.17 us  [the longest x4 7.91 us: band_matrix(): full = jnp.einsum('xia,yjakoc->' + form, banded(x_out, x_in), rows)]
    all_to_all x0 -> x3, waiting for transfers between devices: none -> 38.4 us  [the longest x1 16.4 us: per_device(): lax.all_to_all(sent, 'shot', 0, 0, tiled=True).reshape(2 * shots, 2, bx, nz)]
    unnamed x6 -> x0, other arithmetic: 35.9 us -> none
  transfers between devices with their start and end apart: 32 -> 15, of which waited for: 16 -> 7; matrix products, arithmetic and copies ran while one was open for 13% -> 21% of each run, Pallas kernels for 0% -> 4%
where the time goes in v1:
time: 262 us; the launch traced here: 259 us
  Pallas kernels  76.6 us (29%)
  waiting for transfers between devices  65.6 us (25%)
  local copies, waits for them, and re-layouts  50 us (19%)
  starting transfers between devices  39.7 us (15%)
  blocking collectives  16 us (6%)
  matrix products  9.17 us (4%)
    pallas_call x1, Pallas kernels, adjoint_waves(): pl.pallas_call(adjoint_kernel, out_shape=jax.ShapeDtypeStruct((2 * shots,...  25.7 us
    ppermute x6, waiting for transfers between devices, both_ways(): lax.ppermute(ahead, axis, forward)  22.5 us
    transpose x4, local copies, waits for them, and re-layouts, band_matrix(): full = jnp.einsum('xia,yjakoc->' + form, banded(x_out, x_in), rows)  20.5 us
    all_to_all x1, waiting for transfers between devices, per_device(): lax.all_to_all(sent, 'shot', 0, 0, tiled=True).reshape(2 * shots, 2, bx, nz)  16.4 us
    all_to_all x1, blocking collectives, per_device(): slices = lax.all_to_all(kernels, everyone, 0, 0, tiled=True)  16 us
    pallas_call x1, Pallas kernels, forward_waves(): pl.pallas_call(forward_kernel, out_shape=tuple((jax.ShapeDtypeStruct(shap...  15.3 us
    pallas_call x1, Pallas kernels, backward(): pl.pallas_call(backward_kernel, out_shape=(jax.ShapeDtypeStruct((bx, 32,...  15.1 us
    all_to_all x1, waiting for transfers between devices, per_device(): lax.all_to_all(grads, 'shot', 0, 0, tiled=True)  14.2 us
  transfers between devices with their start and end apart: 15, of which 7 were waited for; matrix products, arithmetic and copies ran while one was open for 21% of the time, Pallas kernels for 4%

profile of v1, /device:TPU:32, one launch (start us, length us, event | category | flops | bytes accessed | tf_op | source)
XLA Modules:
  0.0 259.1 jit_solution(7645027033626918525)
XLA Ops:
  0.6 1.1 copy.110
  1.8 2.6 %collective-permute-start.1 = (bf16[2,4,16,128]{3,2,1,0:T(8,128)(2,1)S(1)}, bf16[2,4,16,128]{3,2,1,0:T(8,128)(2,1)S(1)}, u32[]{:S(2)}, u32[]{:S(2)}) collective-permute-start(bf16[2,4,16,128]{3,2,1,0:T(8,128)(2,1)S(1)} %get-tuple-element.38), channel_id=1, source_target_pairs={{1,0},{2,1},{3,2},{4,3},{5,4},{6,5},{7,6},{0,7},{9,8},{10,9},{11,1... | collective-permute-start | bytes 98312 | tf_op jit(solution)/shard_map/ppermute | solution.py:725
  4.4 1.0 collective-permute-start
  5.4 1.0 copy.34
  6.4 0.8 copy.38
  7.2 0.5 convolution_bitcast_fusion.3
  7.7 1.7 convolution_bitcast_fusion.2
  10.3 3.7 %copy.37 = bf16[2,4,16,4,6,3,16]{2,1,0,6,5,4,3:T(4,128)(2,1)} copy(bf16[2,4,16,4,6,3,16]{6,3,0,2,5,4,1:T(4,128)(2,1)S(1)} %convolution_bitcast_fusion.2) | data formatting | bytes 589824 | tf_op jit(solution)/shard_map/xia,yjakoc->xyoijkc/transpose | solution.py:736
  14.1 3.8 %reshape.105 = bf16[128,1152]{0,1:T(8,128)(2,1)S(1)} reshape(bf16[2,4,16,4,6,3,16]{2,1,0,6,5,4,3:T(4,128)(2,1)} %copy.37) | data formatting | bytes 589824 | tf_op jit(solution)/shard_map/reshape | solution.py:746
  18.3 3.8 %collective-permute-start.3 = (bf16[2,40,16,128]{3,2,1,0:T(8,128)(2,1)S(1)}, bf16[2,40,16,128]{3,2,1,0:T(8,128)(2,1)S(1)}, u32[]{:S(2)}, u32[]{:S(2)}) collective-permute-start(bf16[2,40,16,128]{3,2,1,0:T(8,128)(2,1)S(1)} %pad_maximum_fusion.mid_ref), channel_id=1, source_target_pairs={{8,0},{16,8},{24,16},{32,24},{40,32},{48,40},{56,48},{64,56},{72,6... | collective-permute-start | bytes 983048 | tf_op jit(solution)/shard_map/ppermute | solution.py:725
  22.1 0.4 convolution_bitcast_fusion.4
  22.5 0.4 copy.41
  22.9 0.7 reshape.107.w2_ref
  23.7 4.6 %collective-permute-done.2.lo_ref = bf16[2,40,16,128]{3,2,1,0:T(8,128)(2,1)S(1)} collective-permute-done((bf16[2,40,16,128]{3,2,1,0:T(8,128)(2,1)S(1)}, bf16[2,40,16,128]{3,2,1,0:T(8,128)(2,1)S(1)}, u32[]{:S(2)}, u32[]{:S(2)}) %collective-permute-start.2) | collective-permute-done | bytes 327712 | tf_op jit(solution)/shard_map/ppermute | solution.py:725
  28.2 10.6 %generator.1 = (f32[2,2,32,128]{3,2,1,0:T(8,128)S(1)}, f32[2,2,36,128]{3,2,1,0:T(8,128)S(1)}, bf16[38,64,128]{2,1,0:T(8,128)(2,1)S(1)}) custom-call(s32[3]{0:T(128)S(1)} %pad_add_fusion.at_ref, bf16[2,40,16,128]{3,2,1,0:T(8,128)(2,1)S(1)} %collective-permute-done.2.lo_ref, bf16[2,40,16,128]{3,2,1,0:T(8,128)(2,1)S(1)} %pad_maximum_fusion.mid_ref, ...), custom_call_target="tpu_custom_call" | custom-call | tf_op jit(solution)/shard_map/generator/pallas_call | solution.py:107
  38.9 1.1 broadcast_in_dim.4
  40.0 5.8 %all-to-all-start = ((f32[16,2,2,32,128]{4,3,2,1,0:T(8,128)}), f32[16,2,2,32,128]{4,3,2,1,0:T(8,128)S(1)}, u32[]{:S(2)}, u32[]{:S(2)}) async-start(f32[16,2,2,32,128]{4,3,2,1,0:T(8,128)} %broadcast_in_dim.4), calls=%async_computation | async-start | bytes 2097152 | tf_op jit(solution)/shard_map/all_to_all | solution.py:761
  45.9 16.4 %all-to-all-done = f32[16,2,2,32,128]{4,3,2,1,0:T(8,128)S(1)} async-done(((f32[16,2,2,32,128]{4,3,2,1,0:T(8,128)}), f32[16,2,2,32,128]{4,3,2,1,0:T(8,128)S(1)}, u32[]{:S(2)}, u32[]{:S(2)}) %all-to-all-start) | async-done | bytes 1048608 | tf_op jit(solution)/shard_map/all_to_all | solution.py:761
  62.4 3.7 %collective-permute-start.4 = (f32[16,2,24,128]{3,2,1,0:T(8,128)S(1)}, f32[16,2,24,128]{3,2,1,0:T(8,128)S(1)}, u32[]{:S(2)}, u32[]{:S(2)}) collective-permute-start(f32[16,2,24,128]{3,2,1,0:T(8,128)S(1)} %get-tuple-element.34), channel_id=1, source_target_pairs={{0,1},{1,2},{2,3},{3,4},{4,5},{5,6},{6,7},{7,0},{8,9},{9,10},{10,1... | collective-permute-start | bytes 1179656 | tf_op jit(solution)/shard_map/ppermute | solution.py:725
  66.1 0.8 collective-permute-start.5
  66.9 2.8 %collective-permute-start.6 = (f32[16,24,128]{2,1,0:T(8,128)S(1)}, f32[16,24,128]{2,1,0:T(8,128)S(1)}, u32[]{:S(2)}, u32[]{:S(2)}) collective-permute-start(f32[16,24,128]{2,1,0:T(8,128)S(1)} %get-tuple-element.36), channel_id=1, source_target_pairs={{0,1},{1,2},{2,3},{3,4},{4,5},{5,6},{6,7},{7,0},{8,9},{9,10},{10,1... | collective-permute-start | bytes 589832 | tf_op jit(solution)/shard_map/ppermute | solution.py:725
  69.7 1.7 collective-permute-start.7
  71.5 18.0 %collective-permute-done.6.plo_ref = f32[16,24,128]{2,1,0:T(8,128)S(1)} collective-permute-done((f32[16,24,128]{2,1,0:T(8,128)S(1)}, f32[16,24,128]{2,1,0:T(8,128)S(1)}, u32[]{:S(2)}, u32[]{:S(2)}) %collective-permute-start.6) | collective-permute-done | bytes 196640 | tf_op jit(solution)/shard_map/ppermute | solution.py:725
  89.5 3.2 %collective-permute-done.7.phi_ref = f32[16,24,128]{2,1,0:T(8,128)S(1)} collective-permute-done((f32[16,24,128]{2,1,0:T(8,128)S(1)}, f32[16,24,128]{2,1,0:T(8,128)S(1)}, u32[]{:S(2)}, u32[]{:S(2)}) %collective-permute-start.7) | collective-permute-done | bytes 196640 | tf_op jit(solution)/shard_map/ppermute | solution.py:725
  92.7 15.3 %forward_waves.1 = (f32[16,64,128]{2,1,0:T(8,128)S(1)}, f32[16,64,128]{2,1,0:T(8,128)S(1)}, f32[16,48,128]{2,1,0:T(8,128)S(1)}, f32[16,32,128]{2,1,0:T(8,128)S(1...) custom-call(s32[3]{0:T(128)S(1)} %pad_add_fusion.at_ref, ...), custom_call_target="tpu_custom_call" | custom-call | tf_op jit(solution)/shard_map/forward_waves/pallas_call | solution.py:405
  108.1 3.7 %collective-permute-start.8 = (f32[16,32,128]{2,1,0:T(8,128)S(1)}, f32[16,32,128]{2,1,0:T(8,128)S(1)}, u32[]{:S(2)}, u32[]{:S(2)}) collective-permute-start(f32[16,32,128]{2,1,0:T(8,128)S(1)} %get-tuple-element.21), channel_id=1, source_target_pairs={{0,1},{1,2},{2,3},{3,4},{4,5},{5,6},{6,7},{7,0},{8,9},{9,10},{10,1... | collective-permute-start | bytes 786440 | tf_op jit(solution)/shard_map/ppermute | solution.py:725
  111.8 0.8 collective-permute-start.9
  112.6 9.3 %receiver_fields.1.seen_ref = f32[4,1280,128]{2,1,0:T(8,128)S(1)} custom-call(s32[3]{0:T(128)S(1)} %pad_add_fusion.at_ref, s32[3,2048]{1,0:T(4,128)S(1)} %bitcast.110, f32[3,2048]{1,0:T(4,128)S(1)} %bitcast.111), custom_call_target="tpu_custom_call" | custom-call | flops 4697620480 | bytes 2621440 | tf_op jit(solution)/shard_map/receiver_fields/pallas_call | solution.py:171
  121.9 1.4 collective-permute-done.9.front_ref
  123.3 25.7 %adjoint_waves.1 = f32[32,72,128]{2,1,0:T(8,128)} custom-call(s32[3]{0:T(128)S(1)} %pad_add_fusion.at_ref, f32[16,2,32,128]{3,2,1,0:T(8,128)S(1)} %constant_dynamic-slice_fusion.2.win_ref, f32[16,2,24,128]{3,2,1,0:T(8,128)S(1)} %collective-permute-done.4.clo_ref, f32[16,2,24,128]{3,2,1,0:T(8,128)S(1)} %collective-permute-done.5.chi_ref, ...), custom_call_target="tpu_custom_call" | custom-call | tf_op jit(solution)/shard_map/adjoint_waves/pallas_call | solution.py:551
  149.0 3.8 %all-to-all-start.1 = ((f32[32,72,128]{2,1,0:T(8,128)}), f32[32,72,128]{2,1,0:T(8,128)S(1)}, u32[]{:S(2)}, u32[]{:S(2)}) async-start(f32[32,72,128]{2,1,0:T(8,128)} %adjoint_waves.1), calls=%async_computation.1 | async-start | bytes 2359296 | tf_op jit(solution)/shard_map/all_to_all | solution.py:767
  153.4 3.2 %convolution_bitcast_fusion = bf16[8,4,16,6,2,3,16]{6,2,0,4,5,3,1:T(8,128)(2,1)} fusion(bf16[4,6,3,3,2,16,1]{5,1,4,3,2,0,6:T(8,128)(2,1)S(1)} %convolution_bitcast_fusion.6, s32[8,16]{1,0:T(8,128)S(1)} %iota_subtract_fusion), kind=kOutput, calls=%fused_computation | convolution fusion | flops 1769856 | bytes 604160 | tf_op jit(solution)/shard_map/xia,yjakoc->xycjoki/dot_general | solution.py:736
  156.6 14.2 %all-to-all-done.1 = f32[32,72,128]{2,1,0:T(8,128)S(1)} async-done(((f32[32,72,128]{2,1,0:T(8,128)}), f32[32,72,128]{2,1,0:T(8,128)S(1)}, u32[]{:S(2)}, u32[]{:S(2)}) %all-to-all-start.1) | async-done | bytes 1179680 | tf_op jit(solution)/shard_map/all_to_all | solution.py:767
  170.8 0.6 chain.1.gmid_ref
  171.5 3.8 %collective-permute-start.11 = (bf16[2,2,36,128]{3,2,1,0:T(8,128)(2,1)S(1)}, bf16[2,2,36,128]{3,2,1,0:T(8,128)(2,1)S(1)}, u32[]{:S(2)}, u32[]{:S(2)}) collective-permute-start(bf16[2,2,36,128]{3,2,1,0:T(8,128)(2,1)S(1)} %chain.1.gmid_ref), channel_id=1, source_target_pairs={{8,0},{16,8},{24,16},{32,24},{40,32},{48,40},{56,48},{64,56},{72,6... | collective-permute-start | bytes 110600 | tf_op jit(solution)/shard_map/ppermute | solution.py:725
  175.4 2.7 %convolution_bitcast_fusion.1 = bf16[4,2,16,6,4,3,16]{2,3,0,6,5,4,1:T(8,128)(2,1)} fusion(bf16[2,4,3,3,16,16,1]{5,1,4,3,2,0,6:T(4,128)(2,1)S(1)} %convolution_bitcast_fusion.5, s32[4,6]{1,0:T(4,128)S(1)} %iota_subtract_fusion.2), kind=kOutput, calls=%fused_computation.1 | convolution fusion | flops 884808 | bytes 331872 | tf_op jit(solution)/shard_map/xia,yjakoc->xycijko/dot_general | solution.py:736
  178.0 10.6 %copy.46 = bf16[8,4,16,6,2,3,16]{2,1,0,6,5,4,3:T(4,128)(2,1)} copy(bf16[8,4,16,6,2,3,16]{6,2,0,4,5,3,1:T(8,128)(2,1)} %convolution_bitcast_fusion) | data formatting | bytes 1179648 | tf_op jit(solution)/shard_map/xia,yjakoc->xycjoki/transpose | solution.py:736
  188.6 8.9 %reshape.110 = bf16[512,576]{0,1:T(8,128)(2,1)S(1)} reshape(bf16[8,4,16,6,2,3,16]{2,1,0,6,5,4,3:T(4,128)(2,1)} %copy.46) | data formatting | bytes 1179648 | tf_op jit(solution)/shard_map/reshape | solution.py:748
  197.9 5.8 %copy.49 = bf16[4,2,16,6,4,3,16]{2,1,0,6,5,4,3:T(2,128)(2,1)} copy(bf16[4,2,16,6,4,3,16]{2,3,0,6,5,4,1:T(8,128)(2,1)} %convolution_bitcast_fusion.1) | data formatting | bytes 589824 | tf_op jit(solution)/shard_map/xia,yjakoc->xycijko/transpose | solution.py:736
  203.7 7.1 %reshape.111 = bf16[128,1152]{0,1:T(8,128)(2,1)S(1)} reshape(bf16[4,2,16,6,4,3,16]{2,1,0,6,5,4,3:T(2,128)(2,1)} %copy.49) | data formatting | bytes 589824 | tf_op jit(solution)/shard_map/reshape | solution.py:749
  211.0 15.1 %backward.1 = (f32[32,32,128]{2,1,0:T(8,128)S(1)}, f32[128,128]{1,0:T(8,128)S(1)}) custom-call(s32[3]{0:T(128)S(1)} %pad_add_fusion.at_ref, bf16[2,2,36,128]{3,2,1,0:T(8,128)(2,1)S(1)} %collective-permute-done.10.glo_ref, bf16[2,2,36,128]{3,2,1,0:T(8,128)(2,1)S(1)} %chain.1.gmid_ref, bf16[2,2,36,128]{3,2,1,0:T(8,128)(2,1)S(1)} %collective-permute-done.11.ghi_ref, ...), custom_call_target="tpu_custom_call" | custom-call | tf_op jit(solution)/shard_map/backward/pallas_call | solution.py:699
  226.1 16.0 %all_to_all.25 = f32[128,1,128]{2,1,0:T(1,128)S(1)} all-to-all(f32[128,1,128]{2,1,0:T(1,128)S(1)} %bitcast.109), channel_id=1, replica_groups=mesh['shot'=16,'brick'=8] {'shot','brick'}, dimensions={0} | all-to-all | bytes 131072 | tf_op jit(solution)/shard_map/all_to_all | solution.py:774
  242.2 0.7 broadcast_in_dim.5
  242.9 5.2 %all-to-all-start.3 = ((f32[128,1,128]{2,1,0:T(1,128)}), f32[128,1,128]{2,1,0:T(1,128)S(1)}, u32[]{:S(2)}, u32[]{:S(2)}) async-start(f32[128,1,128]{2,1,0:T(1,128)} %broadcast_in_dim.5), calls=%async_computation.3 | async-start | bytes 131072 | tf_op jit(solution)/shard_map/all_to_all | solution.py:776
  248.0 1.1 copy.108
  249.1 7.8 %all-to-all-done.3 = f32[128,1,128]{2,1,0:T(1,128)S(1)} async-done(((f32[128,1,128]{2,1,0:T(1,128)}), f32[128,1,128]{2,1,0:T(1,128)S(1)}, u32[]{:S(2)}, u32[]{:S(2)}) %all-to-all-start.3) | async-done | bytes 65568 | tf_op jit(solution)/shard_map/all_to_all | solution.py:776
  257.4 0.8 copy.56
  258.2 0.8 copy.57
  (44 shorter events, 2.7 us)
Async XLA Ops:
  1.8 16.3 %collective-permute-start.1 = (bf16[2,4,16,128]{3,2,1,0:T(8,128)(2,1)S(1)}, bf16[2,4,16,128]{3,2,1,0:T(8,128)(2,1)S(1)}, u32[]{:S(2)}, u32[]{:S(2)}) collective-permute-start(bf16[2,4,16,128]{3,2,1,0:T(8,128)(2,1)S(1)} %get-tuple-element.38), channel_id=1, source_target_pairs={{1,0},{2,1},{3,2},{4,3},{5,4},{6,5},{7,6},{0,7},{9,8},{10,9},{11,1... | collective-permute-start | bytes 98312 | tf_op jit(solution)/shard_map/ppermute | solution.py:725
  4.4 13.7 %collective-permute-start = (bf16[2,4,16,128]{3,2,1,0:T(8,128)(2,1)S(1)}, bf16[2,4,16,128]{3,2,1,0:T(8,128)(2,1)S(1)}, u32[]{:S(2)}, u32[]{:S(2)}) collective-permute-start(bf16[2,4,16,128]{3,2,1,0:T(8,128)(2,1)S(1)} %get-tuple-element.37), channel_id=1, source_target_pairs={{0,1},{1,2},{2,3},{3,4},{4,5},{5,6},{6,7},{7,0},{8,9},{9,10},{10,1... | collective-permute-start | bytes 98312 | tf_op jit(solution)/shard_map/ppermute | solution.py:725
  18.2 10.1 %collective-permute-start.2 = (bf16[2,40,16,128]{3,2,1,0:T(8,128)(2,1)S(1)}, bf16[2,40,16,128]{3,2,1,0:T(8,128)(2,1)S(1)}, u32[]{:S(2)}, u32[]{:S(2)}) collective-permute-start(bf16[2,40,16,128]{3,2,1,0:T(8,128)(2,1)S(1)} %pad_maximum_fusion.mid_ref), channel_id=1, source_target_pairs={{0,8},{8,16},{16,24},{24,32},{32,40},{40,48},{48,56},{56,64},{64,7... | collective-permute-start | bytes 983048 | tf_op jit(solution)/shard_map/ppermute | solution.py:725
  18.3 10.0 %collective-permute-start.3 = (bf16[2,40,16,128]{3,2,1,0:T(8,128)(2,1)S(1)}, bf16[2,40,16,128]{3,2,1,0:T(8,128)(2,1)S(1)}, u32[]{:S(2)}, u32[]{:S(2)}) collective-permute-start(bf16[2,40,16,128]{3,2,1,0:T(8,128)(2,1)S(1)} %pad_maximum_fusion.mid_ref), channel_id=1, source_target_pairs={{8,0},{16,8},{24,16},{32,24},{40,32},{48,40},{56,48},{64,56},{72,6... | collective-permute-start | bytes 983048 | tf_op jit(solution)/shard_map/ppermute | solution.py:725
  23.6 22.2 %copy-start = (f32[1,32,16,128]{3,2,1,0:T(8,128)S(1)}, f32[1,32,16,128]{3,2,1,0:T(8,128)}, u32[]{:S(2)}) copy-start(f32[1,32,16,128]{3,2,1,0:T(8,128)} %param.10) | copy-start | bytes 786436
  40.0 31.5 %copy-start.1 = (s32[1,3,2048]{2,0,1:T(1,128)S(1)}, s32[1,3,2048]{2,0,1:T(1,128)}, u32[]{:S(2)}) copy-start(s32[1,3,2048]{2,0,1:T(1,128)} %param.13) | copy-start | bytes 73732
  40.0 31.5 %copy-start.2 = (f32[1,3,2048]{2,0,1:T(1,128)S(1)}, f32[1,3,2048]{2,0,1:T(1,128)}, u32[]{:S(2)}) copy-start(f32[1,3,2048]{2,0,1:T(1,128)} %param.11) | copy-start | bytes 73732
  40.0 22.3 %all-to-all-start = ((f32[16,2,2,32,128]{4,3,2,1,0:T(8,128)}), f32[16,2,2,32,128]{4,3,2,1,0:T(8,128)S(1)}, u32[]{:S(2)}, u32[]{:S(2)}) async-start(f32[16,2,2,32,128]{4,3,2,1,0:T(8,128)} %broadcast_in_dim.4), calls=%async_computation | async-start | bytes 2097152 | tf_op jit(solution)/shard_map/all_to_all | solution.py:761
  62.4 30.3 %collective-permute-start.4 = (f32[16,2,24,128]{3,2,1,0:T(8,128)S(1)}, f32[16,2,24,128]{3,2,1,0:T(8,128)S(1)}, u32[]{:S(2)}, u32[]{:S(2)}) collective-permute-start(f32[16,2,24,128]{3,2,1,0:T(8,128)S(1)} %get-tuple-element.34), channel_id=1, source_target_pairs={{0,1},{1,2},{2,3},{3,4},{4,5},{5,6},{6,7},{7,0},{8,9},{9,10},{10,1... | collective-permute-start | bytes 1179656 | tf_op jit(solution)/shard_map/ppermute | solution.py:725
  66.1 26.7 %collective-permute-start.5 = (f32[16,2,24,128]{3,2,1,0:T(8,128)S(1)}, f32[16,2,24,128]{3,2,1,0:T(8,128)S(1)}, u32[]{:S(2)}, u32[]{:S(2)}) collective-permute-start(f32[16,2,24,128]{3,2,1,0:T(8,128)S(1)} %get-tuple-element.33), channel_id=1, source_target_pairs={{1,0},{2,1},{3,2},{4,3},{5,4},{6,5},{7,6},{0,7},{9,8},{10,9},{11,1... | collective-permute-start | bytes 1179656 | tf_op jit(solution)/shard_map/ppermute | solution.py:725
  66.9 22.6 %collective-permute-start.6 = (f32[16,24,128]{2,1,0:T(8,128)S(1)}, f32[16,24,128]{2,1,0:T(8,128)S(1)}, u32[]{:S(2)}, u32[]{:S(2)}) collective-permute-start(f32[16,24,128]{2,1,0:T(8,128)S(1)} %get-tuple-element.36), channel_id=1, source_target_pairs={{0,1},{1,2},{2,3},{3,4},{4,5},{5,6},{6,7},{7,0},{8,9},{9,10},{10,1... | collective-permute-start | bytes 589832 | tf_op jit(solution)/shard_map/ppermute | solution.py:725
  69.7 23.0 %collective-permute-start.7 = (f32[16,24,128]{2,1,0:T(8,128)S(1)}, f32[16,24,128]{2,1,0:T(8,128)S(1)}, u32[]{:S(2)}, u32[]{:S(2)}) collective-permute-start(f32[16,24,128]{2,1,0:T(8,128)S(1)} %get-tuple-element.35), channel_id=1, source_target_pairs={{1,0},{2,1},{3,2},{4,3},{5,4},{6,5},{7,6},{0,7},{9,8},{10,9},{11,1... | collective-permute-start | bytes 589832 | tf_op jit(solution)/shard_map/ppermute | solution.py:725
  108.1 13.8 %collective-permute-start.8 = (f32[16,32,128]{2,1,0:T(8,128)S(1)}, f32[16,32,128]{2,1,0:T(8,128)S(1)}, u32[]{:S(2)}, u32[]{:S(2)}) collective-permute-start(f32[16,32,128]{2,1,0:T(8,128)S(1)} %get-tuple-element.21), channel_id=1, source_target_pairs={{0,1},{1,2},{2,3},{3,4},{4,5},{5,6},{6,7},{7,0},{8,9},{9,10},{10,1... | collective-permute-start | bytes 786440 | tf_op jit(solution)/shard_map/ppermute | solution.py:725
  111.8 11.5 %collective-permute-start.9 = (f32[16,32,128]{2,1,0:T(8,128)S(1)}, f32[16,32,128]{2,1,0:T(8,128)S(1)}, u32[]{:S(2)}, u32[]{:S(2)}) collective-permute-start(f32[16,32,128]{2,1,0:T(8,128)S(1)} %get-tuple-element.22), channel_id=1, source_target_pairs={{1,0},{2,1},{3,2},{4,3},{5,4},{6,5},{7,6},{0,7},{9,8},{10,9},{11,1... | collective-permute-start | bytes 786440 | tf_op jit(solution)/shard_map/ppermute | solution.py:725
  149.0 21.8 %all-to-all-start.1 = ((f32[32,72,128]{2,1,0:T(8,128)}), f32[32,72,128]{2,1,0:T(8,128)S(1)}, u32[]{:S(2)}, u32[]{:S(2)}) async-start(f32[32,72,128]{2,1,0:T(8,128)} %adjoint_waves.1), calls=%async_computation.1 | async-start | bytes 2359296 | tf_op jit(solution)/shard_map/all_to_all | solution.py:767
  171.4 39.5 %collective-permute-start.10 = (bf16[2,2,36,128]{3,2,1,0:T(8,128)(2,1)S(1)}, bf16[2,2,36,128]{3,2,1,0:T(8,128)(2,1)S(1)}, u32[]{:S(2)}, u32[]{:S(2)}) collective-permute-start(bf16[2,2,36,128]{3,2,1,0:T(8,128)(2,1)S(1)} %chain.1.gmid_ref), channel_id=1, source_target_pairs={{0,8},{8,16},{16,24},{24,32},{32,40},{40,48},{48,56},{56,64},{64,7... | collective-permute-start | bytes 110600 | tf_op jit(solution)/shard_map/ppermute | solution.py:725
  171.5 39.5 %collective-permute-start.11 = (bf16[2,2,36,128]{3,2,1,0:T(8,128)(2,1)S(1)}, bf16[2,2,36,128]{3,2,1,0:T(8,128)(2,1)S(1)}, u32[]{:S(2)}, u32[]{:S(2)}) collective-permute-start(bf16[2,2,36,128]{3,2,1,0:T(8,128)(2,1)S(1)} %chain.1.gmid_ref), channel_id=1, source_target_pairs={{8,0},{16,8},{24,16},{32,24},{40,32},{48,40},{56,48},{64,56},{72,6... | collective-permute-start | bytes 110600 | tf_op jit(solution)/shard_map/ppermute | solution.py:725
  242.9 14.0 %all-to-all-start.3 = ((f32[128,1,128]{2,1,0:T(1,128)}), f32[128,1,128]{2,1,0:T(1,128)S(1)}, u32[]{:S(2)}, u32[]{:S(2)}) async-start(f32[128,1,128]{2,1,0:T(1,128)} %broadcast_in_dim.5), calls=%async_computation.3 | async-start | bytes 131072 | tf_op jit(solution)/shard_map/all_to_all | solution.py:776

commit v2 on v1

--- a/solution.py
+++ b/solution.py
@@ -1,7 +1,6 @@
-import functools
-
 import jax
 import jax.numpy as jnp
+import numpy as np
 from jax import lax
 from jax.experimental import pallas as pl
 from jax.experimental.pallas import tpu as pltpu
@@ -25,6 +24,10 @@
 ypad = ay + 8
 gx = bx + 4
 vmem = pltpu.CompilerParams(vmem_limit_bytes=40 * 1024 * 1024)
+
+
+def cost(microseconds):
+    return pl.CostEstimate(flops=0, bytes_accessed=int(microseconds * 3e6), transcendentals=0)
 
 
 def whole(count):
@@ -178,9 +181,7 @@
             pltpu.VMEM((7 * nz, count), BF16),
         ],
         compiler_params=vmem,
-        cost_estimate=pl.CostEstimate(
-            flops=2 * ay * dom * count * 7 * nz, bytes_accessed=4 * ay * dom * nz * 4, transcendentals=0
-        ),
+        cost_estimate=cost(9),
         name="receiver_fields",
     )(at, cells, seen)
 
@@ -599,14 +600,42 @@
     )(at, got, output)
 
 
-def backward_kernel(
-    at_ref, glo_ref, gmid_ref, ghi_ref, hid_ref, lo_ref, mid_ref, hi_ref, w3_ref, w4_ref,
-    latent_ref, kernel_ref,
-    grads, own, s1, s2, s3, s4, inner,
+def spread_kernel(at_ref, lo_ref, mid_ref, hi_ref, hid_ref, s1, s2):
+    shot, brick = at_ref[0], at_ref[1]
+    y_fine = (shot > 0, True, shot < shots - 1)
+
+    def spread(x, carry):
+        x_fine = ((x >= 1) | (brick > 0)) & ((x < bx + 1) | (brick < bricks - 1))
+        for y, (ref, row, part) in enumerate(((lo_ref, 1, 0), (mid_ref, 0, 1), (mid_ref, 1, 1), (hi_ref, 0, 2))):
+            value = jnp.where(x_fine & y_fine[part], ref[row, x + 3].astype(F32), 0.0)
+            hidden = hid_ref[x + 2, pl.ds(y * 16, 16), :].astype(F32)
+            for k in range(3):
+                s1[x, pl.ds(y * 48 + k * 16, 16), :] = lane_shift(value, k).astype(BF16)
+                s2[x, pl.ds(y * 48 + k * 16, 16), :] = lane_shift(hidden, k).astype(BF16)
+        return carry
+
+    lax.fori_loop(0, bx + 2, spread, 0, unroll=2)
+
+
+def spread_fields(at, lo, mid, hi, hidden):
+    shape = jax.ShapeDtypeStruct((bx + 2, 192, nz), BF16)
+    return pl.pallas_call(
+        spread_kernel,
+        out_shape=(shape, shape),
+        in_specs=[scalars] + whole(4),
+        out_specs=tuple(whole(2)),
+        compiler_params=vmem,
+        cost_estimate=cost(3),
+        name="spread_fields",
+    )(at, lo, mid, hi, hidden)
+
+
+def kernel_grads_kernel(
+    at_ref, glo_ref, gmid_ref, ghi_ref, hid_ref, s1, s2, w3_ref, s4, kernel_ref, grads, own, s3, inner
 ):
     shot, brick = at_ref[0], at_ref[1]
     y_fine = (shot > 0, True, shot < shots - 1)
-    grads[...] = jnp.zeros(grads.shape, F32)
+    grads[:, pl.ds(gx, 12), :] = jnp.zeros((12, 12, nz), F32)
     own[...] = jnp.zeros(own.shape, F32)
     for part, ref in enumerate((glo_ref, gmid_ref, ghi_ref)):
         for row in range(2):
@@ -644,26 +673,6 @@
 
     lax.fori_loop(0, 5, hidden_grad, 0)
 
-    def latent_grad(block, carry):
-        rows = s4[pl.ds(4 * block, 6)].reshape(6 * 192, nz)
-        acc = jnp.dot(w4_ref[...], rows, preferred_element_type=F32)
-        latent_ref[pl.ds(4 * block, 4)] = acc.reshape(4, 32, nz)
-        return carry
-
-    lax.fori_loop(0, bx // 4, latent_grad, 0)
-
-    def spread(x, carry):
-        x_fine = ((x >= 1) | (brick > 0)) & ((x < bx + 1) | (brick < bricks - 1))
-        for y, (ref, row, part) in enumerate(((lo_ref, 1, 0), (mid_ref, 0, 1), (mid_ref, 1, 1), (hi_ref, 0, 2))):
-            value = jnp.where(x_fine & y_fine[part], ref[row, x + 3].astype(F32), 0.0)
-            hidden = hid_ref[x + 2, pl.ds(y * 16, 16), :].astype(F32)
-            for k in range(3):
-                s1[x, pl.ds(y * 48 + k * 16, 16), :] = lane_shift(value, k).astype(BF16)
-                s2[x, pl.ds(y * 48 + k * 16, 16), :] = lane_shift(hidden, k).astype(BF16)
-        return carry
-
-    lax.fori_loop(0, bx + 2, spread, 0)
-
     def kernel_grad(x, carry):
         first, second = carry
         contract = (((1,), (1,)), ((), ()))
@@ -676,7 +685,7 @@
         return first, second
 
     first, second = lax.fori_loop(
-        0, bx, kernel_grad, (jnp.zeros((32, 576), F32), jnp.zeros((8, 576), F32))
+        0, bx, kernel_grad, (jnp.zeros((32, 576), F32), jnp.zeros((8, 576), F32)), unroll=4
     )
     kernel_ref[...] = jnp.zeros(kernel_ref.shape, F32)
     for dx in range(3):
@@ -695,27 +704,142 @@
         kernel_ref[pl.ds(dx * 36 + 18, 16), pl.ds(0, 16)] = one[:, 128:]
 
 
-def backward(at, glo, gmid, ghi, hidden, lo, mid, hi, w3, w4):
+def kernel_grads(at, glo, gmid, ghi, hidden, s1, s2, w3):
     return pl.pallas_call(
-        backward_kernel,
+        kernel_grads_kernel,
         out_shape=(
-            jax.ShapeDtypeStruct((bx, 32, nz), F32),
+            jax.ShapeDtypeStruct((40, 192, nz), BF16),
             jax.ShapeDtypeStruct((128, nz), F32),
         ),
-        in_specs=[scalars] + whole(9),
+        in_specs=[scalars] + whole(7),
         out_specs=tuple(whole(2)),
         scratch_shapes=[
             pltpu.VMEM((12, 48, nz), F32),
             pltpu.VMEM((bx, 8, nz), F32),
-            pltpu.VMEM((bx + 2, 192, nz), BF16),
-            pltpu.VMEM((bx + 2, 192, nz), BF16),
             pltpu.VMEM((576, nz), BF16),
-            pltpu.VMEM((40, 192, nz), BF16),
             pltpu.VMEM((40, 32, nz), BF16),
         ],
         compiler_params=vmem,
-        name="backward",
-    )(at, glo, gmid, ghi, hidden, lo, mid, hi, w3, w4)
+        name="kernel_grads",
+    )(at, glo, gmid, ghi, hidden, s1, s2, w3)
+
+
+def latent_grad_kernel(s4, w4_ref, latent_ref):
+    def latent_grad(block, carry):
+        rows = s4[pl.ds(4 * block, 6)].reshape(6 * 192, nz)
+        acc = jnp.dot(w4_ref[...], rows, preferred_element_type=F32)
+        latent_ref[pl.ds(4 * block, 4)] = acc.reshape(4, 32, nz)
+        return carry
+
+    lax.fori_loop(0, bx // 4, latent_grad, 0)
+
+
+def latent_grads(s4, w4):
+    return pl.pallas_call(
+        latent_grad_kernel,
+        out_shape=jax.ShapeDtypeStruct((bx, 32, nz), F32),
+        in_specs=whole(2),
+        out_specs=whole(1)[0],
+        compiler_params=vmem,
+        cost_estimate=cost(4),
+        name="latent_grads",
+    )(s4, w4)
+
+
+def column_codes(x_in, y_in, order):
+    if order == "xykc":
+        x, y, k, c = np.meshgrid(*map(np.arange, (x_in, y_in, 3, 16)), indexing="ij")
+    else:
+        y, c, k, x = np.meshgrid(*map(np.arange, (y_in, 2, 3, x_in)), indexing="ij")
+    return np.stack([(8 * x + y).ravel(), (16 * k + c).ravel()]).astype(np.int32)
+
+
+codes_1 = column_codes(4, 6, "xykc")
+codes_2 = column_codes(8, 4, "xykc")
+codes_3 = column_codes(16, 6, "yckx")
+codes_4 = column_codes(6, 4, "xykc")
+
+
+def expand(taps_ref, codes_ref, spare, flip):
+    place = codes_ref[1:2]
+    size = place.shape[1]
+    rows = lax.broadcasted_iota(jnp.int32, (16, size), 0)
+    picks = [jnp.where(place == rows + 16 * k, 1.0, 0.0).astype(BF16) for k in range(3)]
+    for pair in range(9):
+        total = None
+        for k in range(3):
+            q = 3 * pair + k
+            term = jnp.dot(taps_ref[26 - q if flip else q], picks[k], preferred_element_type=F32)
+            total = term if total is None else total + term
+        spare[pair, :, pl.ds(0, size)] = total
+
+
+def fill_blocks(out_ref, codes_ref, spare, x_out, y_out):
+    code = codes_ref[0:1]
+    size = code.shape[1]
+    same = lax.broadcasted_iota(jnp.int32, (16, size), 0) * 0 + code
+    for xo in range(x_out):
+        for y in range(y_out):
+            block = jnp.zeros((16, size), F32)
+            for pair in range(9):
+                wanted = (xo + pair // 3) * 8 + y + pair % 3
+                block = jnp.where(same == wanted, spare[pair, :, pl.ds(0, size)], block)
+            out_ref[pl.ds((xo * y_out + y) * 16, 16), :] = block.astype(BF16)
+
+
+def forward_bands_kernel(in_ref, out_taps_ref, codes_1_ref, codes_2_ref, w1_ref, w2_ref, spare, rows):
+    expand(in_ref, codes_1_ref, spare, False)
+    fill_blocks(w1_ref, codes_1_ref, spare, 2, 4)
+    expand(out_taps_ref, codes_2_ref, spare, False)
+    size = codes_2_ref.shape[1]
+    code = codes_2_ref[0:1] - 8 * lax.broadcasted_iota(jnp.int32, (6, size), 0)
+    for channel in range(2):
+        for y in range(2):
+            block = jnp.zeros((6, size), F32)
+            for pair in range(9):
+                wanted = (pair // 3) * 8 + y + pair % 3
+                block = jnp.where(code == wanted, spare[pair, channel : channel + 1, :], block)
+            rows[pl.ds((channel * 2 + y) * 6, 6), :] = block
+    w2_ref[...] = rows[...].astype(BF16)
+
+
+def backward_bands_kernel(in_ref, out_taps_ref, codes_3_ref, codes_4_ref, w3_ref, w4_ref, spare):
+    expand(out_taps_ref, codes_3_ref, spare, True)
+    fill_blocks(w3_ref, codes_3_ref, spare, 8, 4)
+    expand(in_ref, codes_4_ref, spare, True)
+    fill_blocks(w4_ref, codes_4_ref, spare, 4, 2)
+
+
+def forward_bands(taps_in, taps_out):
+    return pl.pallas_call(
+        forward_bands_kernel,
+        out_shape=(
+            jax.ShapeDtypeStruct((128, 1152), BF16),
+            jax.ShapeDtypeStruct((24, 1536), BF16),
+        ),
+        in_specs=whole(4),
+        out_specs=tuple(whole(2)),
+        scratch_shapes=[pltpu.VMEM((9, 16, 1536), F32), pltpu.VMEM((24, 1536), F32)],
+        compiler_params=vmem,
+        cost_estimate=cost(3),
+        name="forward_bands",
+    )(taps_in, taps_out, codes_1, codes_2)
+
+
+def backward_bands(taps_in, taps_out):
+    return pl.pallas_call(
+        backward_bands_kernel,
+        out_shape=(
+            jax.ShapeDtypeStruct((512, 576), BF16),
+            jax.ShapeDtypeStruct((128, 1152), BF16),
+        ),
+        in_specs=whole(4),
+        out_specs=tuple(whole(2)),
+        scratch_shapes=[pltpu.VMEM((9, 16, 1152), F32)],
+        compiler_params=vmem,
+        cost_estimate=cost(4),
+        name="backward_bands",
+    )(taps_in, taps_out, codes_3, codes_4)
 
 
 def both_ways(ahead, behind, axis):
@@ -725,28 +849,13 @@
     return lax.ppermute(ahead, axis, forward), lax.ppermute(behind, axis, backward_)
 
 
-def banded(outputs, inputs):
-    step = jnp.arange(inputs)[None, :] - jnp.arange(outputs)[:, None]
-    return (step[:, :, None] == jnp.arange(3)[None, None, :]).astype(BF16)
-
-
-def band_matrix(weights, x_out, y_out, form):
-    rows = jnp.einsum("yjb,abkoc->yjakoc", banded(y_out, y_out + 2), weights)
-    x_in = 16 if x_out == 8 else x_out + 2
-    full = jnp.einsum("xia,yjakoc->" + form, banded(x_out, x_in), rows)
-    return full
-
-
 def per_device(latent, conv_in, conv_out, source_field, observed, aperture, receivers):
     shot = lax.axis_index("shot")
     brick = lax.axis_index("brick")
     at = jnp.stack([shot, brick, aperture[0]]).astype(jnp.int32)
-    taps_in = conv_in.reshape(3, 3, 3, 16, 16)
-    taps_out = conv_out.reshape(3, 3, 3, 2, 16)
-    w1 = band_matrix(taps_in, 2, 4, "xyoijkc").reshape(128, 1152)
-    w2 = band_matrix(taps_out, 6, 2, "oyxijkc").reshape(24, 1536)
-    w3 = band_matrix(taps_out[::-1, ::-1, ::-1], 8, 4, "xycjoki").reshape(512, 576)
-    w4 = band_matrix(taps_in[::-1, ::-1, ::-1], 4, 2, "xycijko").reshape(128, 1152)
+    taps_out = jnp.pad(conv_out, ((0, 0), (0, 14), (0, 0)))
+    w1, w2 = forward_bands(conv_in, taps_out)
+    w3, w4 = backward_bands(conv_in.transpose(0, 2, 1), taps_out.transpose(0, 2, 1))
 
     tile = jnp.transpose(latent, (2, 1, 0, 3))
     from_low, from_high = both_ways(tile[:, bx - 4 :], tile[:, :4], "brick")
@@ -757,17 +866,24 @@
     seen = receiver_fields(at, receivers[0], observed[0])
 
     coefficients, output, hidden = generator(at, lo, mid, hi, w1, w2)
+    coefficients, plo, phi = lax.optimization_barrier((coefficients, plo, phi))
     sent = jnp.broadcast_to(coefficients[None], (shots, 2, 2, bx, nz))
-    column = lax.all_to_all(sent, "shot", 0, 0, tiled=True).reshape(2 * shots, 2, bx, nz)
+    column = lax.all_to_all(sent, "shot", 0, 0, tiled=True)
+    column, seen, w3, w4 = lax.optimization_barrier((column, seen, w3, w4))
+    column = column.reshape(2 * shots, 2, bx, nz)
     window = lax.dynamic_slice_in_dim(column, aperture[0], ay, 0)
     clo, chi = both_ways(window[:, :, bx - rim :], window[:, :, :rim], "brick")
     p1, p2, p3, p4, images, ahead, behind = forward_waves(at, window, clo, chi, source, plo, phi)
     back, front = both_ways(ahead, behind, "brick")
     grads = adjoint_waves(at, window, clo, chi, (p1, p2, p3, p4, images), back, front, seen)
-    got = lax.all_to_all(grads, "shot", 0, 0, tiled=True).reshape(shots, 2, 2 * gx, nz)
+    got = lax.all_to_all(grads, "shot", 0, 0, tiled=True)
+    s1, s2 = spread_fields(at, lo, mid, hi, hidden)
+    got, s1, s2 = lax.optimization_barrier((got, s1, s2))
+    got = got.reshape(shots, 2, 2 * gx, nz)
     grad_output = chain(at, got, output)
     glo, ghi = both_ways(grad_output, grad_output, "shot")
-    grad_latent, kernels = backward(at, glo, grad_output, ghi, hidden, lo, mid, hi, w3, w4)
+    s4, kernels = kernel_grads(at, glo, grad_output, ghi, hidden, s1, s2, w3)
+    grad_latent = latent_grads(s4, w4)
     grad_latent = jnp.transpose(grad_latent.reshape(bx, 2, 16, nz), (2, 0, 1, 3))
 
     everyone = ("shot", "brick")

time: 262 us -> 217 us (0.83)
  local copies, waits for them, and re-layouts: 50 us -> 28.5 us
  waiting for transfers between devices: 65.6 us -> 51 us
  matrix products: 9.17 us -> 0 us
    reshape x7 -> x0, local copies, waits for them, and re-layouts: 21.2 us -> none  [the longest x2 9.24 us: per_device(): band_matrix(taps_out[::-1, ::-1, ::-1], 8, 4, 'xycjoki').reshape(512, 576)]
    transpose x4 -> x1, local copies, waits for them, and re-layouts: 20.5 us -> 0.92 us  [per_device(): taps_out.transpose(0, 2, 1)]
    all_to_all x2, waiting for transfers between devices: 30.6 us -> 13.2 us  [the longest x1 13.2 us: per_device(): got = lax.all_to_all(grads, 'shot', 0, 0, tiled=True)]
    unnamed x14 -> x76, local copies, waits for them, and re-layouts: 4.73 us -> 21.9 us
    ppermute x6, waiting for transfers between devices: 4.63 us -> 14.8 us  [both_ways(): lax.ppermute(behind, axis, backward_)]
    dot_general x8 -> x0, matrix products: 9.17 us -> none  [the longest x4 7.91 us: band_matrix(): full = jnp.einsum('xia,yjakoc->' + form, banded(x_out, x_in), rows)]
    ppermute x6, waiting for transfers between devices: 22.5 us -> 18.7 us  [both_ways(): lax.ppermute(ahead, axis, forward)]
    all_to_all x1, waiting for transfers between devices: 7.77 us -> 4.38 us  [per_device(): lax.all_to_all(jnp.broadcast_to(mine, (128, nz)), everyone, 0, 0, tiled=T...]
  transfers between devices with their start and end apart: 15 -> 15, of which waited for: 7 -> 10; matrix products, arithmetic and copies ran while one was open for 21% -> 3% of each run, Pallas kernels for 4% -> 12%
where the time goes in v2:
time: 217 us; the launch traced here: 214 us
  Pallas kernels  74.2 us (34%)
  waiting for transfers between devices  51 us (24%)
  starting transfers between devices  42 us (19%)
  local copies, waits for them, and re-layouts  28.5 us (13%)
  blocking collectives  16.3 us (8%)
    pallas_call x1, Pallas kernels, adjoint_waves(): pl.pallas_call(adjoint_kernel, out_shape=jax.ShapeDtypeStruct((2 * shots,...  24.7 us
    unnamed x76, local copies, waits for them, and re-layouts  21.9 us
    ppermute x6, waiting for transfers between devices, both_ways(): lax.ppermute(ahead, axis, forward)  18.7 us
    all_to_all x1, blocking collectives, per_device(): slices = lax.all_to_all(kernels, everyone, 0, 0, tiled=True)  16.3 us
    pallas_call x1, Pallas kernels, forward_waves(): pl.pallas_call(forward_kernel, out_shape=tuple((jax.ShapeDtypeStruct(shap...  15.4 us
    ppermute x6, waiting for transfers between devices, both_ways(): lax.ppermute(behind, axis, backward_)  14.8 us
    ppermute x6, starting transfers between devices, both_ways(): lax.ppermute(behind, axis, backward_)  13.8 us
    all_to_all x1, waiting for transfers between devices, per_device(): got = lax.all_to_all(grads, 'shot', 0, 0, tiled=True)  13.2 us
  transfers between devices with their start and end apart: 15, of which 10 were waited for; matrix products, arithmetic and copies ran while one was open for 3% of the time, Pallas kernels for 12%

profile of v2, /device:TPU:32, one launch (start us, length us, event | category | flops | bytes accessed | tf_op | source)
XLA Modules:
  0.0 214.0 jit_solution(8910796202470244842)
XLA Ops:
  0.7 1.2 copy.55
  1.8 3.1 %collective-permute-start = (bf16[2,4,16,128]{3,2,1,0:T(8,128)(2,1)S(1)}, bf16[2,4,16,128]{3,2,1,0:T(8,128)(2,1)S(1)}, u32[]{:S(2)}, u32[]{:S(2)}) collective-permute-start(bf16[2,4,16,128]{3,2,1,0:T(8,128)(2,1)S(1)} %get-tuple-element.69), channel_id=1, source_target_pairs={{0,1},{1,2},{2,3},{3,4},{4,5},{5,6},{6,7},{7,0},{8,9},{9,10},{10,1... | collective-permute-start | bytes 98312 | tf_op jit(solution)/shard_map/ppermute | solution.py:849
  4.9 1.4 collective-permute-start.1
  6.3 1.0 copy.54
  7.4 0.9 collective-permute-done
  8.3 2.0 collective-permute-done.1
  10.5 3.8 %collective-permute-start.3 = (bf16[2,40,16,128]{3,2,1,0:T(8,128)(2,1)S(1)}, bf16[2,40,16,128]{3,2,1,0:T(8,128)(2,1)S(1)}, u32[]{:S(2)}, u32[]{:S(2)}) collective-permute-start(bf16[2,40,16,128]{3,2,1,0:T(8,128)(2,1)S(1)} %pad_maximum_fusion.mid_ref), channel_id=1, source_target_pairs={{8,0},{16,8},{24,16},{32,24},{40,32},{48,40},{56,48},{64,56},{72,6... | collective-permute-start | bytes 983048 | tf_op jit(solution)/shard_map/ppermute | solution.py:849
  14.4 2.8 %collective-permute-start.4 = (f32[16,24,128]{2,1,0:T(8,128)S(1)}, f32[16,24,128]{2,1,0:T(8,128)S(1)}, u32[]{:S(2)}, u32[]{:S(2)}) collective-permute-start(f32[16,24,128]{2,1,0:T(8,128)S(1)} %get-tuple-element.68), channel_id=1, source_target_pairs={{0,1},{1,2},{2,3},{3,4},{4,5},{5,6},{6,7},{7,0},{8,9},{9,10},{10,1... | collective-permute-start | bytes 589832 | tf_op jit(solution)/shard_map/ppermute | solution.py:849
  17.2 1.7 collective-permute-start.5
  20.9 1.1 forward_bands.1
  22.2 10.6 %generator.1 = (f32[2,2,32,128]{3,2,1,0:T(8,128)S(1)}, f32[2,2,36,128]{3,2,1,0:T(8,128)S(1)}, bf16[38,64,128]{2,1,0:T(8,128)(2,1)S(1)}) custom-call(s32[3]{0:T(128)S(1)} %pad_add_fusion.at_ref, bf16[2,40,16,128]{3,2,1,0:T(8,128)(2,1)S(1)} %collective-permute-done.2.lo_ref, bf16[2,40,16,128]{3,2,1,0:T(8,128)(2,1)S(1)} %pad_maximum_fusion.mid_ref, ...), custom_call_target="tpu_custom_call" | custom-call | tf_op jit(solution)/shard_map/generator/pallas_call | solution.py:110
  33.7 1.1 broadcast_in_dim.4
  34.8 5.7 %all-to-all-start = ((f32[16,2,2,32,128]{4,3,2,1,0:T(8,128)}), f32[16,2,2,32,128]{4,3,2,1,0:T(8,128)}, u32[]{:S(2)}, u32[]{:S(2)}) async-start(f32[16,2,2,32,128]{4,3,2,1,0:T(8,128)} %broadcast_in_dim.4), calls=%async_computation | async-start | bytes 2097152 | tf_op jit(solution)/shard_map/all_to_all | solution.py:871
  44.2 9.1 %receiver_fields.1.seen_ref = f32[4,1280,128]{2,1,0:T(8,128)S(1)} custom-call(s32[3]{0:T(128)S(1)} %pad_add_fusion.at_ref, s32[3,2048]{1,0:T(4,128)S(1)} %bitcast.46, f32[3,2048]{1,0:T(4,128)S(1)} %bitcast.45), custom_call_target="tpu_custom_call" | custom-call | bytes 27000000 | tf_op jit(solution)/shard_map/receiver_fields/pallas_call | solution.py:174
  53.3 0.9 pad_bitcast_fusion.out_taps_ref
  54.2 0.9 copy-done.13
  55.8 1.3 backward_bands.1
  57.2 0.9 copy-done.11
  58.8 1.2 constant_dynamic-slice_fusion
  60.0 3.1 %collective-permute-start.6 = (f32[16,2,24,128]{3,2,1,0:T(8,128)S(1)}, f32[16,2,24,128]{3,2,1,0:T(8,128)S(1)}, u32[]{:S(2)}, u32[]{:S(2)}) collective-permute-start(f32[16,2,24,128]{3,2,1,0:T(8,128)S(1)} %get-tuple-element.66), channel_id=1, source_target_pairs={{0,1},{1,2},{2,3},{3,4},{4,5},{5,6},{6,7},{7,0},{8,9},{9,10},{10,1... | collective-permute-start | bytes 1179656 | tf_op jit(solution)/shard_map/ppermute | solution.py:849
  63.1 1.4 collective-permute-start.7
  64.5 1.1 constant_dynamic-slice_fusion.2.win_ref
  65.6 8.9 %collective-permute-done.6.clo_ref = f32[16,2,24,128]{3,2,1,0:T(8,128)S(1)} collective-permute-done((f32[16,2,24,128]{3,2,1,0:T(8,128)S(1)}, f32[16,2,24,128]{3,2,1,0:T(8,128)S(1)}, u32[]{:S(2)}, u32[]{:S(2)}) %collective-permute-start.6) | collective-permute-done | bytes 393248 | tf_op jit(solution)/shard_map/ppermute | solution.py:849
  74.5 8.3 %collective-permute-done.7.chi_ref = f32[16,2,24,128]{3,2,1,0:T(8,128)S(1)} collective-permute-done((f32[16,2,24,128]{3,2,1,0:T(8,128)S(1)}, f32[16,2,24,128]{3,2,1,0:T(8,128)S(1)}, u32[]{:S(2)}, u32[]{:S(2)}) %collective-permute-start.7) | collective-permute-done | bytes 393248 | tf_op jit(solution)/shard_map/ppermute | solution.py:849
  82.8 15.4 %forward_waves.1 = (f32[16,64,128]{2,1,0:T(8,128)S(1)}, f32[16,64,128]{2,1,0:T(8,128)S(1)}, f32[16,48,128]{2,1,0:T(8,128)S(1)}, f32[16,32,128]{2,1,0:T(8,128)S(1...) custom-call(s32[3]{0:T(128)S(1)} %pad_add_fusion.at_ref, ...), custom_call_target="tpu_custom_call" | custom-call | tf_op jit(solution)/shard_map/forward_waves/pallas_call | solution.py:406
  98.1 2.8 %collective-permute-start.8 = (f32[16,32,128]{2,1,0:T(8,128)S(1)}, f32[16,32,128]{2,1,0:T(8,128)S(1)}, u32[]{:S(2)}, u32[]{:S(2)}) collective-permute-start(f32[16,32,128]{2,1,0:T(8,128)S(1)} %get-tuple-element.45), channel_id=1, source_target_pairs={{0,1},{1,2},{2,3},{3,4},{4,5},{5,6},{6,7},{7,0},{8,9},{9,10},{10,1... | collective-permute-start | bytes 786440 | tf_op jit(solution)/shard_map/ppermute | solution.py:849
  100.9 1.7 collective-permute-start.9
  102.6 7.2 %collective-permute-done.8.back_ref = f32[16,32,128]{2,1,0:T(8,128)S(1)} collective-permute-done((f32[16,32,128]{2,1,0:T(8,128)S(1)}, f32[16,32,128]{2,1,0:T(8,128)S(1)}, u32[]{:S(2)}, u32[]{:S(2)}) %collective-permute-start.8) | collective-permute-done | bytes 262176 | tf_op jit(solution)/shard_map/ppermute | solution.py:849
  109.8 4.3 %collective-permute-done.9.front_ref = f32[16,32,128]{2,1,0:T(8,128)S(1)} collective-permute-done((f32[16,32,128]{2,1,0:T(8,128)S(1)}, f32[16,32,128]{2,1,0:T(8,128)S(1)}, u32[]{:S(2)}, u32[]{:S(2)}) %collective-permute-start.9) | collective-permute-done | bytes 262176 | tf_op jit(solution)/shard_map/ppermute | solution.py:849
  114.1 24.7 %adjoint_waves.1 = f32[32,72,128]{2,1,0:T(8,128)S(1)} custom-call(s32[3]{0:T(128)S(1)} %pad_add_fusion.at_ref, f32[16,2,32,128]{3,2,1,0:T(8,128)S(1)} %constant_dynamic-slice_fusion.2.win_ref, f32[16,2,24,128]{3,2,1,0:T(8,128)S(1)} %collective-permute-done.6.clo_ref, f32[16,2,24,128]{3,2,1,0:T(8,128)S(1)} %collective-permute-done.7.chi_ref, ...), custom_call_target="tpu_custom_call" | custom-call | tf_op jit(solution)/shard_map/adjoint_waves/pallas_call | solution.py:552
  138.8 1.0 copy-done
  139.8 5.3 %all-to-all-start.1 = ((f32[32,72,128]{2,1,0:T(8,128)}), f32[32,72,128]{2,1,0:T(8,128)S(1)}, u32[]{:S(2)}, u32[]{:S(2)}) async-start(f32[32,72,128]{2,1,0:T(8,128)} %copy-done), calls=%async_computation.1 | async-start | bytes 2359296 | tf_op jit(solution)/shard_map/all_to_all | solution.py:879
  145.1 2.4 %spread_fields.1 = (bf16[34,192,128]{2,1,0:T(8,128)(2,1)S(1)}, bf16[34,192,128]{2,1,0:T(8,128)(2,1)S(1)}) custom-call(s32[3]{0:T(128)S(1)} %pad_add_fusion.at_ref, bf16[2,40,16,128]{3,2,1,0:T(8,128)(2,1)S(1)} %collective-permute-done.2.lo_ref, bf16[2,40,16,128]{3,2,1,0:T(8,128)(2,1)S(1)} %pad_maximum_fusion.mid_ref, bf16[2,40,16,128]{3,2,1,0:T(8,128)(2,1)S(1)} %copy-done.10, ...), custom_call_target="tpu_custom_call" | custom-call | bytes 9000000 | tf_op jit(solution)/shard_map/spread_fields/pallas_call | solution.py:622
  147.6 1.2 copy-done.5
  148.8 1.2 copy-done.7
  149.9 13.2 %all-to-all-done.1 = f32[32,72,128]{2,1,0:T(8,128)S(1)} async-done(((f32[32,72,128]{2,1,0:T(8,128)}), f32[32,72,128]{2,1,0:T(8,128)S(1)}, u32[]{:S(2)}, u32[]{:S(2)}) %all-to-all-start.1) | async-done | bytes 1179680 | tf_op jit(solution)/shard_map/all_to_all | solution.py:879
  163.8 3.8 %collective-permute-start.11 = (bf16[2,2,36,128]{3,2,1,0:T(8,128)(2,1)S(1)}, bf16[2,2,36,128]{3,2,1,0:T(8,128)(2,1)S(1)}, u32[]{:S(2)}, u32[]{:S(2)}) collective-permute-start(bf16[2,2,36,128]{3,2,1,0:T(8,128)(2,1)S(1)} %chain.1.gmid_ref), channel_id=1, source_target_pairs={{8,0},{16,8},{24,16},{32,24},{40,32},{48,40},{56,48},{64,56},{72,6... | collective-permute-start | bytes 110600 | tf_op jit(solution)/shard_map/ppermute | solution.py:849
  167.6 1.7 collective-permute-done.10.glo_ref
  169.3 1.4 copy-done.6
  170.8 1.4 copy-done.8
  172.2 7.2 %kernel_grads.1 = (bf16[40,192,128]{2,1,0:T(8,128)(2,1)S(1)}, f32[128,128]{1,0:T(8,128)S(1)}) custom-call(s32[3]{0:T(128)S(1)} %pad_add_fusion.at_ref, bf16[2,2,36,128]{3,2,1,0:T(8,128)(2,1)S(1)} %collective-permute-done.10.glo_ref, bf16[2,2,36,128]{3,2,1,0:T(8,128)(2,1)S(1)} %chain.1.gmid_ref, bf16[2,2,36,128]{3,2,1,0:T(8,128)(2,1)S(1)} %collective-permute-done.11.ghi_ref, ...), custom_call_target="tpu_custom_call" | custom-call | tf_op jit(solution)/shard_map/kernel_grads/pallas_call | solution.py:708
  179.4 1.3 copy-done.3
  180.7 16.3 %all_to_all.25 = f32[128,1,128]{2,1,0:T(1,128)S(1)} all-to-all(f32[128,1,128]{2,1,0:T(1,128)S(1)} %bitcast.47), channel_id=1, replica_groups=mesh['shot'=16,'brick'=8] {'shot','brick'}, dimensions={0} | all-to-all | bytes 131072 | tf_op jit(solution)/shard_map/all_to_all | solution.py:890
  197.8 5.2 %all-to-all-start.3 = ((f32[128,1,128]{2,1,0:T(1,128)}), f32[128,1,128]{2,1,0:T(1,128)S(1)}, u32[]{:S(2)}, u32[]{:S(2)}) async-start(f32[128,1,128]{2,1,0:T(1,128)} %broadcast_in_dim.5), calls=%async_computation.3 | async-start | bytes 131072 | tf_op jit(solution)/shard_map/all_to_all | solution.py:892
  203.0 1.5 copy-done.4
  204.5 1.8 latent_grads.1
  206.4 1.1 copy.53
  207.4 4.4 %all-to-all-done.3 = f32[128,1,128]{2,1,0:T(1,128)S(1)} async-done(((f32[128,1,128]{2,1,0:T(1,128)}), f32[128,1,128]{2,1,0:T(1,128)S(1)}, u32[]{:S(2)}, u32[]{:S(2)}) %all-to-all-start.3) | async-done | bytes 65568 | tf_op jit(solution)/shard_map/all_to_all | solution.py:892
  (87 shorter events, 11.3 us)
Async XLA Ops:
  0.6 20.3 %copy-start.26 = (s32[2,1152]{1,0:T(2,128)S(1)}, s32[2,1152]{1,0:T(2,128)}, u32[]{:S(2)}) copy-start(s32[2,1152]{1,0:T(2,128)} %constant.25.clone.codes_1_ref) | copy-start | bytes 27652
  0.6 20.3 %copy-start.24 = (s32[2,1536]{1,0:T(2,128)S(1)}, s32[2,1536]{1,0:T(2,128)}, u32[]{:S(2)}) copy-start(s32[2,1536]{1,0:T(2,128)} %constant.26.clone.codes_2_ref) | copy-start | bytes 36868
  0.7 18.9 %copy-start.32 = (bf16[27,2,16]{0,2,1:T(8,128)(2,1)S(1)}, bf16[27,2,16]{0,2,1:T(8,128)(2,1)}, u32[]{:S(2)}) copy-start(bf16[27,2,16]{0,2,1:T(8,128)(2,1)} %param.13) | copy-start | bytes 5188
  0.7 20.0 %copy-start.29 = (bf16[27,16,16]{0,2,1:T(8,128)(2,1)S(1)}, bf16[27,16,16]{0,2,1:T(8,128)(2,1)}, u32[]{:S(2)}) copy-start(bf16[27,16,16]{0,2,1:T(8,128)(2,1)} %param.12) | copy-start | bytes 41476
  1.8 6.5 %collective-permute-start = (bf16[2,4,16,128]{3,2,1,0:T(8,128)(2,1)S(1)}, bf16[2,4,16,128]{3,2,1,0:T(8,128)(2,1)S(1)}, u32[]{:S(2)}, u32[]{:S(2)}) collective-permute-start(bf16[2,4,16,128]{3,2,1,0:T(8,128)(2,1)S(1)} %get-tuple-element.69), channel_id=1, source_target_pairs={{0,1},{1,2},{2,3},{3,4},{4,5},{5,6},{6,7},{7,0},{8,9},{9,10},{10,1... | collective-permute-start | bytes 98312 | tf_op jit(solution)/shard_map/ppermute | solution.py:849
  4.9 5.4 %collective-permute-start.1 = (bf16[2,4,16,128]{3,2,1,0:T(8,128)(2,1)S(1)}, bf16[2,4,16,128]{3,2,1,0:T(8,128)(2,1)S(1)}, u32[]{:S(2)}, u32[]{:S(2)}) collective-permute-start(bf16[2,4,16,128]{3,2,1,0:T(8,128)(2,1)S(1)} %get-tuple-element.70), channel_id=1, source_target_pairs={{1,0},{2,1},{3,2},{4,3},{5,4},{6,5},{7,6},{0,7},{9,8},{10,9},{11,1... | collective-permute-start | bytes 98312 | tf_op jit(solution)/shard_map/ppermute | solution.py:849
  10.4 11.6 %collective-permute-start.2 = (bf16[2,40,16,128]{3,2,1,0:T(8,128)(2,1)S(1)}, bf16[2,40,16,128]{3,2,1,0:T(8,128)(2,1)S(1)}, u32[]{:S(2)}, u32[]{:S(2)}) collective-permute-start(bf16[2,40,16,128]{3,2,1,0:T(8,128)(2,1)S(1)} %pad_maximum_fusion.mid_ref), channel_id=1, source_target_pairs={{0,8},{8,16},{16,24},{24,32},{32,40},{40,48},{48,56},{56,64},{64,7... | collective-permute-start | bytes 983048 | tf_op jit(solution)/shard_map/ppermute | solution.py:849
  10.5 11.7 %collective-permute-start.3 = (bf16[2,40,16,128]{3,2,1,0:T(8,128)(2,1)S(1)}, bf16[2,40,16,128]{3,2,1,0:T(8,128)(2,1)S(1)}, u32[]{:S(2)}, u32[]{:S(2)}) collective-permute-start(bf16[2,40,16,128]{3,2,1,0:T(8,128)(2,1)S(1)} %pad_maximum_fusion.mid_ref), channel_id=1, source_target_pairs={{8,0},{16,8},{24,16},{32,24},{40,32},{48,40},{56,48},{64,56},{72,6... | collective-permute-start | bytes 983048 | tf_op jit(solution)/shard_map/ppermute | solution.py:849
  14.4 19.3 %collective-permute-start.4 = (f32[16,24,128]{2,1,0:T(8,128)S(1)}, f32[16,24,128]{2,1,0:T(8,128)S(1)}, u32[]{:S(2)}, u32[]{:S(2)}) collective-permute-start(f32[16,24,128]{2,1,0:T(8,128)S(1)} %get-tuple-element.68), channel_id=1, source_target_pairs={{0,1},{1,2},{2,3},{3,4},{4,5},{5,6},{6,7},{7,0},{8,9},{9,10},{10,1... | collective-permute-start | bytes 589832 | tf_op jit(solution)/shard_map/ppermute | solution.py:849
  17.2 16.5 %collective-permute-start.5 = (f32[16,24,128]{2,1,0:T(8,128)S(1)}, f32[16,24,128]{2,1,0:T(8,128)S(1)}, u32[]{:S(2)}, u32[]{:S(2)}) collective-permute-start(f32[16,24,128]{2,1,0:T(8,128)S(1)} %get-tuple-element.67), channel_id=1, source_target_pairs={{1,0},{2,1},{3,2},{4,3},{5,4},{6,5},{7,6},{0,7},{9,8},{10,9},{11,1... | collective-permute-start | bytes 589832 | tf_op jit(solution)/shard_map/ppermute | solution.py:849
  19.8 0.7 copy-start.28
  22.2 12.6 %copy-start.9 = (bf16[2,40,16,128]{3,2,1,0:T(8,128)(2,1)}, bf16[2,40,16,128]{3,2,1,0:T(8,128)(2,1)S(1)}, u32[]{:S(2)}) copy-start(bf16[2,40,16,128]{3,2,1,0:T(8,128)(2,1)S(1)} %collective-permute-done.3.hi_ref) | copy-start | bytes 983044
  32.8 0.8 copy-start.1
  33.6 7.8 %copy-start.22 = (f32[2,2,36,128]{3,2,1,0:T(8,128)}, f32[2,2,36,128]{3,2,1,0:T(8,128)S(1)}, u32[]{:S(2)}) copy-start(f32[2,2,36,128]{3,2,1,0:T(8,128)S(1)} %get-tuple-element.52.out_ref) | copy-start | bytes 221188
  33.6 7.8 %copy-start.16 = (f32[16,24,128]{2,1,0:T(8,128)}, f32[16,24,128]{2,1,0:T(8,128)S(1)}, u32[]{:S(2)}) copy-start(f32[16,24,128]{2,1,0:T(8,128)S(1)} %collective-permute-done.4.plo_ref) | copy-start | bytes 589828
  33.7 7.8 %copy-start.18 = (f32[16,24,128]{2,1,0:T(8,128)}, f32[16,24,128]{2,1,0:T(8,128)S(1)}, u32[]{:S(2)}) copy-start(f32[16,24,128]{2,1,0:T(8,128)S(1)} %collective-permute-done.5.phi_ref) | copy-start | bytes 589828
  33.7 7.7 %copy-start.30 = (f32[1,3,2048]{2,0,1:T(1,128)S(1)}, f32[1,3,2048]{2,0,1:T(1,128)}, u32[]{:S(2)}) copy-start(f32[1,3,2048]{2,0,1:T(1,128)} %param.15) | copy-start | bytes 73732
  33.7 8.4 %copy-start.31 = (s32[1,3,2048]{2,0,1:T(1,128)S(1)}, s32[1,3,2048]{2,0,1:T(1,128)}, u32[]{:S(2)}) copy-start(s32[1,3,2048]{2,0,1:T(1,128)} %param.17) | copy-start | bytes 73732
  34.8 24.0 %all-to-all-start = ((f32[16,2,2,32,128]{4,3,2,1,0:T(8,128)}), f32[16,2,2,32,128]{4,3,2,1,0:T(8,128)}, u32[]{:S(2)}, u32[]{:S(2)}) async-start(f32[16,2,2,32,128]{4,3,2,1,0:T(8,128)} %broadcast_in_dim.4), calls=%async_computation | async-start | bytes 2097152 | tf_op jit(solution)/shard_map/all_to_all | solution.py:871
  40.5 13.7 %copy-start.25 = (s32[2,1152]{1,0:T(2,128)S(1)}, s32[2,1152]{1,0:T(2,128)}, u32[]{:S(2)}) copy-start(s32[2,1152]{1,0:T(2,128)} %constant.28.clone.codes_4_ref) | copy-start | bytes 27652
  42.6 0.8 copy-start.20
  43.4 0.8 copy-start.21
  54.2 0.9 copy-start.13
  55.1 0.7 copy-start.27
  57.2 0.9 copy-start.11
  58.1 0.7 copy-start.14
  58.8 24.0 %copy-start.17 = (f32[16,24,128]{2,1,0:T(8,128)S(1)}, f32[16,24,128]{2,1,0:T(8,128)}, u32[]{:S(2)}) copy-start(f32[16,24,128]{2,1,0:T(8,128)} %copy-done.16) | copy-start | bytes 589828
  58.8 24.0 %copy-start.19 = (f32[16,24,128]{2,1,0:T(8,128)S(1)}, f32[16,24,128]{2,1,0:T(8,128)}, u32[]{:S(2)}) copy-start(f32[16,24,128]{2,1,0:T(8,128)} %copy-done.18) | copy-start | bytes 589828
  60.0 14.5 %collective-permute-start.6 = (f32[16,2,24,128]{3,2,1,0:T(8,128)S(1)}, f32[16,2,24,128]{3,2,1,0:T(8,128)S(1)}, u32[]{:S(2)}, u32[]{:S(2)}) collective-permute-start(f32[16,2,24,128]{3,2,1,0:T(8,128)S(1)} %get-tuple-element.66), channel_id=1, source_target_pairs={{0,1},{1,2},{2,3},{3,4},{4,5},{5,6},{6,7},{7,0},{8,9},{9,10},{10,1... | collective-permute-start | bytes 1179656 | tf_op jit(solution)/shard_map/ppermute | solution.py:849
  63.1 19.6 %collective-permute-start.7 = (f32[16,2,24,128]{3,2,1,0:T(8,128)S(1)}, f32[16,2,24,128]{3,2,1,0:T(8,128)S(1)}, u32[]{:S(2)}, u32[]{:S(2)}) collective-permute-start(f32[16,2,24,128]{3,2,1,0:T(8,128)S(1)} %get-tuple-element.65), channel_id=1, source_target_pairs={{1,0},{2,1},{3,2},{4,3},{5,4},{6,5},{7,6},{0,7},{9,8},{10,9},{11,1... | collective-permute-start | bytes 1179656 | tf_op jit(solution)/shard_map/ppermute | solution.py:849
  98.1 11.6 %collective-permute-start.8 = (f32[16,32,128]{2,1,0:T(8,128)S(1)}, f32[16,32,128]{2,1,0:T(8,128)S(1)}, u32[]{:S(2)}, u32[]{:S(2)}) collective-permute-start(f32[16,32,128]{2,1,0:T(8,128)S(1)} %get-tuple-element.45), channel_id=1, source_target_pairs={{0,1},{1,2},{2,3},{3,4},{4,5},{5,6},{6,7},{7,0},{8,9},{9,10},{10,1... | collective-permute-start | bytes 786440 | tf_op jit(solution)/shard_map/ppermute | solution.py:849
  100.9 13.1 %collective-permute-start.9 = (f32[16,32,128]{2,1,0:T(8,128)S(1)}, f32[16,32,128]{2,1,0:T(8,128)S(1)}, u32[]{:S(2)}, u32[]{:S(2)}) collective-permute-start(f32[16,32,128]{2,1,0:T(8,128)S(1)} %get-tuple-element.46), channel_id=1, source_target_pairs={{1,0},{2,1},{3,2},{4,3},{5,4},{6,5},{7,6},{0,7},{9,8},{10,9},{11,1... | collective-permute-start | bytes 786440 | tf_op jit(solution)/shard_map/ppermute | solution.py:849
  138.8 1.0 copy-start
  139.8 5.3 %copy-start.2 = (bf16[38,64,128]{2,1,0:T(8,128)(2,1)S(1)}, bf16[38,64,128]{2,1,0:T(8,128)(2,1)}, u32[]{:S(2)}) copy-start(bf16[38,64,128]{2,1,0:T(8,128)(2,1)} %copy-done.1) | copy-start | bytes 1867780
  139.8 5.3 %copy-start.10 = (bf16[2,40,16,128]{3,2,1,0:T(8,128)(2,1)S(1)}, bf16[2,40,16,128]{3,2,1,0:T(8,128)(2,1)}, u32[]{:S(2)}) copy-start(bf16[2,40,16,128]{3,2,1,0:T(8,128)(2,1)} %copy-done.9) | copy-start | bytes 983044
  139.8 23.3 %copy-start.23 = (f32[2,2,36,128]{3,2,1,0:T(8,128)S(1)}, f32[2,2,36,128]{3,2,1,0:T(8,128)}, u32[]{:S(2)}) copy-start(f32[2,2,36,128]{3,2,1,0:T(8,128)} %copy-done.22) | copy-start | bytes 221188
  139.8 23.3 %all-to-all-start.1 = ((f32[32,72,128]{2,1,0:T(8,128)}), f32[32,72,128]{2,1,0:T(8,128)S(1)}, u32[]{:S(2)}, u32[]{:S(2)}) async-start(f32[32,72,128]{2,1,0:T(8,128)} %copy-done), calls=%async_computation.1 | async-start | bytes 2359296 | tf_op jit(solution)/shard_map/all_to_all | solution.py:879
  145.1 24.2 %copy-start.12 = (bf16[512,576]{1,0:T(8,128)(2,1)S(1)}, bf16[512,576]{1,0:T(8,128)(2,1)}, u32[]{:S(2)}) copy-start(bf16[512,576]{1,0:T(8,128)(2,1)} %copy-done.11) | copy-start | bytes 1769476
  147.5 1.2 copy-start.5
  148.8 1.2 copy-start.7
  163.1 39.9 %copy-start.15 = (bf16[128,1152]{1,0:T(8,128)(2,1)S(1)}, bf16[128,1152]{1,0:T(8,128)(2,1)}, u32[]{:S(2)}) copy-start(bf16[128,1152]{1,0:T(8,128)(2,1)} %copy-done.14) | copy-start | bytes 884740
  163.7 5.6 %collective-permute-start.10 = (bf16[2,2,36,128]{3,2,1,0:T(8,128)(2,1)S(1)}, bf16[2,2,36,128]{3,2,1,0:T(8,128)(2,1)S(1)}, u32[]{:S(2)}, u32[]{:S(2)}) collective-permute-start(bf16[2,2,36,128]{3,2,1,0:T(8,128)(2,1)S(1)} %chain.1.gmid_ref), channel_id=1, source_target_pairs={{0,8},{8,16},{16,24},{24,32},{32,40},{40,48},{48,56},{56,64},{64,7... | collective-permute-start | bytes 110600 | tf_op jit(solution)/shard_map/ppermute | solution.py:849
  163.8 5.5 %collective-permute-start.11 = (bf16[2,2,36,128]{3,2,1,0:T(8,128)(2,1)S(1)}, bf16[2,2,36,128]{3,2,1,0:T(8,128)(2,1)S(1)}, u32[]{:S(2)}, u32[]{:S(2)}) collective-permute-start(bf16[2,2,36,128]{3,2,1,0:T(8,128)(2,1)S(1)} %chain.1.gmid_ref), channel_id=1, source_target_pairs={{8,0},{16,8},{24,16},{32,24},{40,32},{48,40},{56,48},{64,56},{72,6... | collective-permute-start | bytes 110600 | tf_op jit(solution)/shard_map/ppermute | solution.py:849
  169.3 1.4 copy-start.6
  170.8 1.4 copy-start.8
  179.4 1.3 copy-start.3
  197.8 14.0 %all-to-all-start.3 = ((f32[128,1,128]{2,1,0:T(1,128)}), f32[128,1,128]{2,1,0:T(1,128)S(1)}, u32[]{:S(2)}, u32[]{:S(2)}) async-start(f32[128,1,128]{2,1,0:T(1,128)} %broadcast_in_dim.5), calls=%async_computation.3 | async-start | bytes 131072 | tf_op jit(solution)/shard_map/all_to_all | solution.py:892
  203.0 1.5 copy-start.4

commit v3 on v2

--- a/solution.py
+++ b/solution.py
@@ -23,7 +23,7 @@
 xpad = dom + 24
 ypad = ay + 8
 gx = bx + 4
-vmem = pltpu.CompilerParams(vmem_limit_bytes=40 * 1024 * 1024)
+vmem = pltpu.CompilerParams(vmem_limit_bytes=24 * 1024 * 1024)
 
 
 def cost(microseconds):
@@ -200,14 +200,6 @@
     return value if shift == 0 else pltpu.roll(value, shift, 1)
 
 
-def slope_z(value, factors):
-    last, upper, lower, _ = factors
-    up = sum(upper[t - 1] * turn(value, -t) for t in range(1, 5))
-    low = sum(lower[t - 1] * turn(value, t - 1) for t in range(1, 5))
-    slope = up - low
-    return jnp.where(last, -low, slope), jnp.where(last, up, slope)
-
-
 def differences(get):
     total = None
     for t in range(1, 5):
@@ -219,38 +211,63 @@
     return total
 
 
-def load_padded(ref, pieces):
-    ref[...] = jnp.zeros(ref.shape, F32)
+def split_rows(value):
+    high = value.astype(BF16).astype(F32)
+    return jnp.concatenate([high, value - high], axis=0).astype(BF16)
+
+
+def joined(rows):
+    wide = rows.astype(F32)
+    return wide[:8] + wide[8:]
+
+
+def clear_sides(field):
+    for y in (0, 1, 2, 3, ay + 4, ay + 5, ay + 6, ay + 7):
+        field[y] = jnp.zeros(field.shape[1:], F32)
+
+
+def clear_rims(flux_y):
+    for j in (0, 1, 2, 20, 21, 22):
+        flux_y[j] = jnp.zeros(flux_y.shape[1:], F32)
+
+
+def halo_scale(at_ref):
+    brick = at_ref[1]
+    return (
+        jnp.where(brick > 0, 1.0, 0.0).astype(F32),
+        jnp.where(brick < bricks - 1, 1.0, 0.0).astype(F32),
+    )
+
+
+def window_kernel(at_ref, column_ref, win_ref, ahead_ref, behind_ref):
+    first_row = at_ref[2]
 
     def body(y, carry):
-        for first, rows in pieces:
-            value = rows(y)
-            ref[y + 4, pl.ds(lead + first, value.shape[0]), :] = value
-        return carry
-
-    lax.fori_loop(0, ay, body, 0)
-
-
-def face_weights(buoy, wx, wy, wz, wzl, factors):
-    last = factors[0]
-    half = 0.5 * tap_square
-
-    def body(y, carry):
-        value = buoy[y + 4, pl.ds(0, dom + 16), :]
-        wx[y] = half * (value + buoy[y + 4, pl.ds(1, dom + 16), :])
-        inner = buoy[y + 4, pl.ds(lead, dom), :]
-        ahead = pltpu.roll(inner, nz - 1, 1)
-        wz[y] = half * jnp.where(last, inner, inner + ahead)
-        wzl[y] = half * jnp.where(last, ahead, inner + ahead)
-        return carry
-
-    lax.fori_loop(0, ay, body, 0)
-
-    def faces(j, carry):
-        wy[j] = half * (buoy[j + 3, pl.ds(lead, dom), :] + buoy[j + 4, pl.ds(lead, dom), :])
-        return carry
-
-    lax.fori_loop(0, ay + 1, faces, 0)
+        for channel in range(2):
+            value = column_ref[first_row + y, channel]
+            win_ref[y, channel] = value
+            ahead_ref[y, channel, pl.ds(0, 16), :] = split_rows(value[24:])
+            ahead_ref[y, channel, pl.ds(16, 16), :] = value[8:24].astype(BF16)
+            behind_ref[y, channel, pl.ds(0, 16), :] = split_rows(value[:8])
+            behind_ref[y, channel, pl.ds(16, 16), :] = value[8:24].astype(BF16)
+        return carry
+
+    lax.fori_loop(0, ay, body, 0, unroll=2)
+
+
+def take_window(at, column):
+    return pl.pallas_call(
+        window_kernel,
+        out_shape=(
+            jax.ShapeDtypeStruct((ay, 2, bx, nz), F32),
+            jax.ShapeDtypeStruct((ay, 2, bx, nz), BF16),
+            jax.ShapeDtypeStruct((ay, 2, bx, nz), BF16),
+        ),
+        in_specs=[scalars] + whole(1),
+        out_specs=tuple(whole(3)),
+        compiler_params=vmem,
+        name="take_window",
+    )(at, column)
 
 
 def slope_y(field, j, first, rows):
@@ -262,108 +279,123 @@
     )
 
 
-def apply_operator(field, weights, flux_y, flux_x, factors, first, rows, consume):
+def slopes_at(field, y, first, rows, factors):
+    value = field[y + 4, pl.ds(lead + first, rows), :]
+    turned_up = [turn(value, -t) for t in range(1, 5)]
+    turned_low = [turn(value, t - 1) for t in range(1, 5)]
+    base, more = lead + first - 4, rows + 8
+    sx = differences(
+        lambda t: (
+            field[y + 4, pl.ds(base + t, more), :],
+            field[y + 4, pl.ds(base + 1 - t, more), :],
+        )
+    )
+    sy = slope_y(field, y, first, rows)
+    last, upper, lower, _ = factors
+    up = sum(upper[t] * turned_up[t] for t in range(4))
+    low = sum(lower[t] * turned_low[t] for t in range(4))
+    slope = up - low
+    return sx, sy, jnp.where(last, -low, slope), jnp.where(last, up, slope)
+
+
+def flux_pass(field, weights, fluxes, first, rows, factors, also=None):
     wx, wy, wz, wzl = weights
+    fx, fy, fh, fb = fluxes
+    base, more = lead + first - 4, rows + 8
+
+    def body(y, carry):
+        sx, sy, here, before = slopes_at(field, y, first, rows, factors)
+        fx[y, pl.ds(0, more), :] = wx[y, pl.ds(base, more), :] * sx
+        fy[y + 3, pl.ds(0, rows), :] = wy[y, pl.ds(first, rows), :] * sy
+        fh[y, pl.ds(0, rows), :] = wz[y, pl.ds(first, rows), :] * here
+        fb[y, pl.ds(0, rows), :] = wzl[y, pl.ds(first, rows), :] * before
+        if also is not None:
+            also(y, sx, sy, here, before)
+        return carry
+
+    lax.fori_loop(0, ay, body, 0, unroll=2)
+    sy = slope_y(field, ay, first, rows)
+    fy[ay + 3, pl.ds(0, rows), :] = wy[ay, pl.ds(first, rows), :] * sy
+    return sy
+
+
+def divergence_pass(fluxes, rows, factors, consume):
+    fx, fy, fh, fb = fluxes
     _, _, lower, above = factors
 
-    def faces(j, carry):
-        flux_y[j + 3, pl.ds(0, rows), :] = wy[j, pl.ds(first, rows), :] * slope_y(field, j, first, rows)
-        return carry
-
-    lax.fori_loop(0, ay + 1, faces, 0)
-    base = lead + first - 4
-    more = rows + 8
-
     def body(y, carry):
-        flux_x[pl.ds(0, more), :] = wx[y, pl.ds(base, more), :] * differences(
+        here = fh[y, pl.ds(0, rows), :]
+        before = fb[y, pl.ds(0, rows), :]
+        turned_here = [turn(here, 1 - t) for t in range(1, 5)]
+        turned_before = [turn(before, t) for t in range(1, 5)]
+        total = differences(
+            lambda t: (fx[y, pl.ds(3 + t, rows), :], fx[y, pl.ds(4 - t, rows), :])
+        )
+        total = total + differences(
             lambda t: (
-                field[y + 4, pl.ds(base + t, more), :],
-                field[y + 4, pl.ds(base + 1 - t, more), :],
+                fy[y + t + 3, pl.ds(0, rows), :],
+                fy[y - t + 4, pl.ds(0, rows), :],
             )
         )
-        total = differences(
-            lambda t: (
-                flux_y[y + t + 3, pl.ds(0, rows), :],
-                flux_y[y - t + 4, pl.ds(0, rows), :],
-            )
-        )
-        here, before = slope_z(field[y + 4, pl.ds(lead + first, rows), :], factors)
-        here = wz[y, pl.ds(first, rows), :] * here
-        before = wzl[y, pl.ds(first, rows), :] * before
-        total = total + sum(above[t - 1] * turn(here, 1 - t) for t in range(1, 5))
-        total = total - sum(lower[t - 1] * turn(before, t) for t in range(1, 5))
-        total = total + differences(
-            lambda t: (flux_x[pl.ds(3 + t, rows), :], flux_x[pl.ds(4 - t, rows), :])
-        )
+        total = total + sum(above[t] * turned_here[t] for t in range(4))
+        total = total - sum(lower[t] * turned_before[t] for t in range(4))
         consume(y, total)
         return carry
 
-    lax.fori_loop(0, ay, body, 0)
-
-
-def clear_rims(flux_y):
-    for j in (0, 1, 2, 20, 21, 22):
-        flux_y[j] = jnp.zeros(flux_y.shape[1:], F32)
-
-
-def halo_scale(at_ref):
-    brick = at_ref[1]
-    return (
-        jnp.where(brick > 0, 1.0, 0.0).astype(F32),
-        jnp.where(brick < bricks - 1, 1.0, 0.0).astype(F32),
-    )
-
-
-def load_window(at_ref, win_ref, clo_ref, chi_ref, modulus, buoy):
-    low, high = halo_scale(at_ref)
-    load_padded(
-        buoy,
-        (
-            (0, lambda y: low * clo_ref[y, 1]),
-            (rim, lambda y: win_ref[y, 1]),
-            (rim + bx, lambda y: high * chi_ref[y, 1]),
-        ),
-    )
-
-    def body(y, carry):
-        modulus[y, pl.ds(0, rim), :] = low * clo_ref[y, 0]
-        modulus[y, pl.ds(rim, bx), :] = win_ref[y, 0]
-        modulus[y, pl.ds(rim + bx, rim), :] = high * chi_ref[y, 0]
-        return carry
-
-    lax.fori_loop(0, ay, body, 0)
-
-
-weight_shapes = [
-    pltpu.VMEM((ay, dom + 16, nz), F32),
-    pltpu.VMEM((ay + 1, dom, nz), F32),
-    pltpu.VMEM((ay, dom, nz), F32),
-    pltpu.VMEM((ay, dom, nz), F32),
+    lax.fori_loop(0, ay, body, 0, unroll=2)
+
+
+weight_sizes = ((ay, dom + 16, nz), (ay + 1, dom, nz), (ay, dom, nz), (ay, dom, nz))
+padded = pltpu.VMEM((ypad, xpad, nz), F32)
+flux_shapes = [
+    pltpu.VMEM((ay, 72, nz), F32),
+    pltpu.VMEM((23, 64, nz), F32),
+    pltpu.VMEM((ay, 64, nz), F32),
+    pltpu.VMEM((ay, 64, nz), F32),
 ]
-padded = pltpu.VMEM((ypad, xpad, nz), F32)
 
 
 def forward_kernel(
     at_ref, win_ref, clo_ref, chi_ref, src_ref, plo_ref, phi_ref,
-    p1_ref, p2_ref, p3_ref, p4_ref, image_ref, ahead_ref, behind_ref,
-    modulus, buoy, f1, f2, f3, wx, wy, wz, wzl, flux_y, flux_x,
+    p1_ref, p2_ref, p3_ref, p4_ref, image_ref, ahead_ref, behind_ref, modulus, wx, wy, wz, wzl,
+    buoy, f1, f2, f3, fx, fy, fh, fb, message,
 ):
     factors = lane_factors()
-    load_window(at_ref, win_ref, clo_ref, chi_ref, modulus, buoy)
+    last = factors[0]
     weights = (wx, wy, wz, wzl)
-    face_weights(buoy, *weights, factors)
-    clear_rims(flux_y)
+    fluxes = (fx, fy, fh, fb)
+    clear_rims(fy)
+    for field in (buoy, f1, f2, f3):
+        clear_sides(field)
     low, high = halo_scale(at_ref)
-    load_padded(
-        f1,
-        (
-            (0, lambda y: low * plo_ref[y]),
-            (rim, lambda y: src_ref[y]),
-            (rim + bx, lambda y: high * phi_ref[y]),
-        ),
-    )
-    f2[...] = jnp.zeros(f2.shape, F32)
-    f3[...] = jnp.zeros(f3.shape, F32)
+    half = 0.5 * tap_square
+
+    def load(y, carry):
+        for channel, ref, row, skip in ((0, modulus, y, 0), (1, buoy, y + 4, lead)):
+            ref[row, pl.ds(skip, 16), :] = low * clo_ref[y, channel, pl.ds(16, 16), :].astype(F32)
+            ref[row, pl.ds(skip + 16, 8), :] = low * joined(clo_ref[y, channel, pl.ds(0, 16), :])
+            ref[row, pl.ds(skip + rim, bx), :] = win_ref[y, channel]
+            ref[row, pl.ds(skip + rim + bx, 8), :] = high * joined(chi_ref[y, channel, pl.ds(0, 16), :])
+            ref[row, pl.ds(skip + rim + bx + 8, 16), :] = high * chi_ref[y, channel, pl.ds(16, 16), :].astype(F32)
+        f1[y + 4, pl.ds(lead, rim), :] = low * plo_ref[y]
+        f1[y + 4, pl.ds(lead + rim, bx), :] = src_ref[y]
+        f1[y + 4, pl.ds(lead + rim + bx, rim), :] = high * phi_ref[y]
+        return carry
+
+    lax.fori_loop(0, ay, load, 0)
+
+    def weigh(y, carry):
+        inner = buoy[y + 4, pl.ds(lead, dom), :]
+        ahead = pltpu.roll(inner, nz - 1, 1)
+        value = buoy[y + 4, pl.ds(0, dom + 16), :]
+        wx[y] = half * (value + buoy[y + 4, pl.ds(1, dom + 16), :])
+        wy[y] = half * (buoy[y + 3, pl.ds(lead, dom), :] + inner)
+        wz[y] = half * jnp.where(last, inner, inner + ahead)
+        wzl[y] = half * jnp.where(last, ahead, inner + ahead)
+        return carry
+
+    lax.fori_loop(0, ay, weigh, 0, unroll=2)
+    wy[ay] = half * buoy[ay + 3, pl.ds(lead, dom), :]
 
     def first_step(y, image):
         f2[y + 4, pl.ds(lead + 8, 64), :] = (
@@ -373,17 +405,15 @@
 
     def second_step(y, image):
         value = (
-            2.0 * f2[y + 4, pl.ds(lead + 16, 48), :]
-            - f1[y + 4, pl.ds(lead + 16, 48), :]
-            + modulus[y, pl.ds(16, 48), :] * image
+            2.0 * f2[y + 4, pl.ds(lead + 12, 56), :]
+            - f1[y + 4, pl.ds(lead + 12, 56), :]
+            + modulus[y, pl.ds(12, 56), :] * image
         )
-        f3[y + 4, pl.ds(lead + 16, 48), :] = value
-        image_ref[1, y] = image
-        p3_ref[y] = value
+        f3[y + 4, pl.ds(lead + 12, 56), :] = value
+        image_ref[1, y] = image[4:52]
+        p3_ref[y] = value[4:52]
         p1_ref[y] = f1[y + 4, pl.ds(lead + 8, 64), :]
         p2_ref[y] = f2[y + 4, pl.ds(lead + 8, 64), :]
-        ahead_ref[y, pl.ds(rim, 8), :] = value[24:32]
-        behind_ref[y, pl.ds(rim, 8), :] = value[16:24]
 
     def third_step(y, image):
         image_ref[2, y] = image
@@ -393,46 +423,96 @@
             + modulus[y, pl.ds(rim, bx), :] * image[8:40]
         )
         p4_ref[y] = value
-        ahead_ref[y, pl.ds(0, rim), :] = value[8:32]
-        behind_ref[y, pl.ds(0, rim), :] = value[0:24]
-
-    apply_operator(f1, weights, flux_y, flux_x, factors, 8, 64, first_step)
-    apply_operator(f2, weights, flux_y, flux_x, factors, 16, 48, second_step)
-    apply_operator(f3, weights, flux_y, flux_x, factors, 16, 48, third_step)
+
+    def pack(y, ref, near, further, third):
+        value = p4_ref[y, pl.ds(near, 7), :]
+        rounded = value.astype(BF16).astype(F32)
+        message[pl.ds(0, 7), :] = rounded
+        message[pl.ds(7, 7), :] = value - rounded
+        message[pl.ds(14, 13), :] = p4_ref[y, pl.ds(further, 13), :]
+        message[pl.ds(27, 5), :] = f3[y + 4, pl.ds(lead + rim + third, 5), :]
+        ref[y] = message[...].astype(BF16)
+
+    def send(y, carry):
+        pack(y, ahead_ref, 25, 12, 19)
+        pack(y, behind_ref, 0, 7, 8)
+        return carry
+
+    flux_pass(f1, weights, fluxes, 8, 64, factors)
+    divergence_pass(fluxes, 64, factors, first_step)
+    flux_pass(f2, weights, fluxes, 12, 56, factors)
+    divergence_pass(fluxes, 56, factors, second_step)
+    flux_pass(f3, weights, fluxes, 16, 48, factors)
+    divergence_pass(fluxes, 48, factors, third_step)
+    lax.fori_loop(0, ay, send, 0)
 
 
 def forward_waves(at, window, clo, chi, source, plo, phi):
-    shapes = [(ay, 64, nz), (ay, 64, nz), (ay, 48, nz), (ay, bx, nz), (3, ay, 48, nz), (ay, 32, nz), (ay, 32, nz)]
+    shapes = [(ay, 64, nz), (ay, 64, nz), (ay, 48, nz), (ay, bx, nz), (3, ay, 48, nz)]
     return pl.pallas_call(
         forward_kernel,
-        out_shape=tuple(jax.ShapeDtypeStruct(shape, F32) for shape in shapes),
+        out_shape=tuple(jax.ShapeDtypeStruct(shape, F32) for shape in shapes)
+        + (jax.ShapeDtypeStruct((ay, 32, nz), BF16),) * 2
+        + (jax.ShapeDtypeStruct((ay, dom, nz), F32),)
+        + tuple(jax.ShapeDtypeStruct(shape, F32) for shape in weight_sizes),
         in_specs=[scalars] + whole(6),
-        out_specs=tuple(whole(7)),
-        scratch_shapes=[
-            pltpu.VMEM((ay, dom, nz), F32),
-            padded, padded, padded, padded,
-            *weight_shapes,
-            pltpu.VMEM((23, dom, nz), F32),
-            pltpu.VMEM((dom + 16, nz), F32),
-        ],
+        out_specs=tuple(whole(12)),
+        scratch_shapes=[padded, padded, padded, padded, *flux_shapes, pltpu.VMEM((32, nz), F32)],
         compiler_params=vmem,
         name="forward_waves",
     )(at, window, clo, chi, source, plo, phi)
 
 
+def slopes_kernel(p1_ref, p2_ref, p3_ref, sx_ref, sy_ref, sh_ref, sb_ref, field):
+    factors = lane_factors()
+    clear_sides(field)
+    for index, (ref, first) in enumerate(((p1_ref, 8), (p2_ref, 8), (p3_ref, 16))):
+        rows = ref.shape[1]
+
+        def load(y, carry):
+            field[y + 4, pl.ds(lead + first, rows), :] = ref[y]
+            return carry
+
+        lax.fori_loop(0, ay, load, 0)
+
+        def body(y, carry):
+            sx, sy, here, before = slopes_at(field, y, 16, 48, factors)
+            sx_ref[index, y] = sx[:48]
+            sy_ref[index, y] = sy
+            sh_ref[index, y] = here
+            sb_ref[index, y] = before
+            return carry
+
+        lax.fori_loop(0, ay, body, 0, unroll=2)
+        sy_ref[index, ay] = slope_y(field, ay, 16, 48)
+
+
+def wave_slopes(p1, p2, p3):
+    shapes = [(3, ay, 48, nz), (3, ay + 1, 48, nz), (3, ay, 48, nz), (3, ay, 48, nz)]
+    return pl.pallas_call(
+        slopes_kernel,
+        out_shape=tuple(jax.ShapeDtypeStruct(shape, F32) for shape in shapes),
+        in_specs=whole(3),
+        out_specs=tuple(whole(4)),
+        scratch_shapes=[padded],
+        compiler_params=vmem,
+        cost_estimate=cost(6),
+        name="wave_slopes",
+    )(p1, p2, p3)
+
+
 def adjoint_kernel(
-    at_ref, win_ref, clo_ref, chi_ref, p1_ref, p2_ref, p3_ref, p4_ref, image_ref, back_ref, front_ref, seen_ref,
+    at_ref, p2_ref, p3_ref, p4_ref, image_ref, back_ref, front_ref, seen_ref,
+    modulus, wx, wy, wz, wzl, px_ref, py_ref, ph_ref, pb_ref,
     column_ref,
-    modulus, buoy, scaled, wave, later, late, grad_m, grad_b, wx, wy, wz, wzl, flux_y, flux_x, cross_y, cross_x,
+    scaled, later, late, grad_m, fx, fy, fh, fb, qx, qy, qh, qb, far,
 ):
     factors = lane_factors()
-    load_window(at_ref, win_ref, clo_ref, chi_ref, modulus, buoy)
     weights = (wx, wy, wz, wzl)
-    face_weights(buoy, *weights, factors)
-    clear_rims(flux_y)
+    fluxes = (fx, fy, fh, fb)
+    clear_rims(fy)
+    clear_sides(scaled)
     low, high = halo_scale(at_ref)
-    scaled[...] = jnp.zeros(scaled.shape, F32)
-    wave[...] = jnp.zeros(wave.shape, F32)
 
     def residual(step, y, first, value):
         rows = value.shape[0]
@@ -441,82 +521,49 @@
         total = seen_ref[step, pl.ds(start, rows), :]
         return misfit_weight * (count * value - total)
 
+    far[...] = jnp.zeros(far.shape, F32)
+
     def seed(y, carry):
-        for first, value in (
-            (0, low * back_ref[y, pl.ds(0, rim), :]),
-            (rim, p4_ref[y]),
-            (rim + bx, high * front_ref[y, pl.ds(0, rim), :]),
-        ):
-            rows = value.shape[0]
-            error = residual(3, y, first, value)
-            later[y, pl.ds(first, rows), :] = error
-            scaled[y + 4, pl.ds(lead + first, rows), :] = modulus[y, pl.ds(first, rows), :] * error
+        late[y, pl.ds(8, 48), :] = p3_ref[y]
+        received = low * back_ref[y].astype(F32)
+        far[pl.ds(4, 13), :] = received[14:27]
+        far[pl.ds(17, 7), :] = received[:7] + received[7:14]
+        late[y, pl.ds(3, 5), :] = received[27:]
+        far[pl.ds(rim, bx), :] = p4_ref[y]
+        received = high * front_ref[y].astype(F32)
+        far[pl.ds(rim + bx, 7), :] = received[:7] + received[7:14]
+        far[pl.ds(rim + bx + 7, 13), :] = received[14:27]
+        late[y, pl.ds(56, 5), :] = received[27:]
+        error = residual(3, y, 0, far[...])
+        later[y] = error
+        scaled[y + 4, pl.ds(lead, dom), :] = modulus[y] * error
+        grad_m[y] = error[16:64] * image_ref[2, y]
         return carry
 
     lax.fori_loop(0, ay, seed, 0)
-    grad_m[...] = jnp.zeros(grad_m.shape, F32)
-    grad_b[...] = jnp.zeros(grad_b.shape, F32)
-
-    def set_wave(ref, first, offset):
-        def body(y, carry):
-            rows = ref.shape[1] - 2 * offset
-            wave[y + 4, pl.ds(lead + first, rows), :] = ref[y, pl.ds(offset, rows), :]
-            return carry
-
-        lax.fori_loop(0, ay, body, 0)
-
-    def gradients(adjoint_of, image):
-        def faces(j, carry):
-            cross_y[j] = slope_y(scaled, j, 16, 48) * slope_y(wave, j, 16, 48)
-            return carry
-
-        lax.fori_loop(0, ay + 1, faces, 0)
-        base = lead + 8
-
-        def body(y, carry):
-            def slope_x(field):
-                return differences(
-                    lambda t: (
-                        field[y + 4, pl.ds(base + t, 56), :],
-                        field[y + 4, pl.ds(base + 1 - t, 56), :],
-                    )
-                )
-
-            cross_x[...] = slope_x(scaled) * slope_x(wave)
-            here_s, before_s = slope_z(scaled[y + 4, pl.ds(lead + 16, 48), :], factors)
-            here_w, before_w = slope_z(wave[y + 4, pl.ds(lead + 16, 48), :], factors)
-            total = here_s * here_w + pltpu.roll(before_s * before_w, 1, 1)
-            total = total + cross_y[y] + cross_y[y + 1]
-            total = total + cross_x[pl.ds(7, 48), :] + cross_x[pl.ds(8, 48), :]
-            grad_b[y] = grad_b[y] - (0.5 * tap_square) * total
-            grad_m[y] = grad_m[y] + adjoint_of(y) * image_ref[image, y]
-            return carry
-
-        lax.fori_loop(0, ay, body, 0)
-
-    set_wave(p3_ref, 16, 0)
-    gradients(lambda y: later[y, pl.ds(16, 48), :], 2)
+
+    def cross(index, offset):
+        def also(y, sx, sy, here, before):
+            products = (
+                (qx, sx[offset : offset + 48] * px_ref[index, y]),
+                (qy, sy[offset : offset + 48] * py_ref[index, y]),
+                (qh, here[offset : offset + 48] * ph_ref[index, y]),
+                (qb, before[offset : offset + 48] * pb_ref[index, y]),
+            )
+            for ref, product in products:
+                ref[y] = product if index == 2 else ref[y] + product
+
+        return also
+
+    def cross_last(index, offset, sy):
+        product = sy[offset : offset + 48] * py_ref[index, ay]
+        qy[ay] = product if index == 2 else qy[ay] + product
 
     def step_three(y, image):
-        value = jnp.concatenate(
-            [
-                low * back_ref[y, pl.ds(rim, 8), :],
-                p3_ref[y],
-                high * front_ref[y, pl.ds(rim, 8), :],
-            ],
-            axis=0,
-        )
-        late[y] = residual(2, y, 8, value) + 2.0 * later[y, pl.ds(8, 64), :] + image
-
-    apply_operator(scaled, weights, flux_y, flux_x, factors, 8, 64, step_three)
-
-    def rescale(y, carry):
-        scaled[y + 4, pl.ds(lead + 8, 64), :] = modulus[y, pl.ds(8, 64), :] * late[y]
-        return carry
-
-    lax.fori_loop(0, ay, rescale, 0)
-    set_wave(p2_ref, 8, 0)
-    gradients(lambda y: late[y, pl.ds(8, 48), :], 1)
+        value = late[y]
+        value = residual(2, y, 8, value) + 2.0 * later[y, pl.ds(8, 64), :] + image
+        late[y] = value
+        grad_m[y] = grad_m[y] + value[8:56] * image_ref[1, y]
 
     def step_two(y, image):
         value = (
@@ -525,51 +572,78 @@
             + image
             - later[y, pl.ds(16, 48), :]
         )
+        grad_m[y] = grad_m[y] + value * image_ref[0, y]
         later[y, pl.ds(16, 48), :] = value
 
-    apply_operator(scaled, weights, flux_y, flux_x, factors, 16, 48, step_two)
+    sy = flux_pass(scaled, weights, fluxes, 8, 64, factors, cross(2, 8))
+    cross_last(2, 8, sy)
+    divergence_pass(fluxes, 64, factors, step_three)
+
+    def rescale(y, carry):
+        scaled[y + 4, pl.ds(lead + 8, 64), :] = modulus[y, pl.ds(8, 64), :] * late[y]
+        return carry
+
+    lax.fori_loop(0, ay, rescale, 0, unroll=2)
+    sy = flux_pass(scaled, weights, fluxes, 16, 48, factors, cross(1, 0))
+    cross_last(1, 0, sy)
+    divergence_pass(fluxes, 48, factors, step_two)
 
     def rescale_last(y, carry):
         scaled[y + 4, pl.ds(lead + 16, 48), :] = modulus[y, pl.ds(16, 48), :] * later[y, pl.ds(16, 48), :]
         return carry
 
-    lax.fori_loop(0, ay, rescale_last, 0)
-    set_wave(p1_ref, 8, 0)
-    gradients(lambda y: later[y, pl.ds(16, 48), :], 0)
-
-    column_ref[...] = jnp.zeros(column_ref.shape, F32)
+    lax.fori_loop(0, ay, rescale_last, 0, unroll=2)
+
+    def last_slopes(y, carry):
+        cross(0, 0)(y, *slopes_at(scaled, y, 16, 48, factors))
+        return carry
+
+    lax.fori_loop(0, ay, last_slopes, 0, unroll=2)
+    cross_last(0, 0, slope_y(scaled, ay, 16, 48))
+
     first_row = at_ref[2]
 
+    def blank(row, carry):
+        column_ref[row] = jnp.zeros(column_ref.shape[1:], F32)
+        return carry
+
+    lax.fori_loop(0, first_row, blank, 0)
+    lax.fori_loop(first_row + ay, 2 * shots, blank, 0)
+
     def place(y, carry):
+        before = pltpu.roll(qb[y, pl.ds(6, gx), :], 1, 1)
+        total = qh[y, pl.ds(6, gx), :] + before
+        total = total + qy[y, pl.ds(6, gx), :] + qy[y + 1, pl.ds(6, gx), :]
+        total = total + qx[y, pl.ds(9, gx), :] + qx[y, pl.ds(10, gx), :]
         column_ref[first_row + y, pl.ds(0, gx), :] = grad_m[y, pl.ds(6, gx), :]
-        column_ref[first_row + y, pl.ds(gx, gx), :] = grad_b[y, pl.ds(6, gx), :]
-        return carry
-
-    lax.fori_loop(0, ay, place, 0)
-
-
-def adjoint_waves(at, window, clo, chi, fields, back, front, seen):
+        column_ref[first_row + y, pl.ds(gx, gx), :] = (-0.5 * tap_square) * total
+        return carry
+
+    lax.fori_loop(0, ay, place, 0, unroll=2)
+
+
+def adjoint_waves(at, fields, images, back, front, seen, modulus, weights, slopes):
+    near = pltpu.VMEM((ay, 48, nz), F32)
     return pl.pallas_call(
         adjoint_kernel,
         out_shape=jax.ShapeDtypeStruct((2 * shots, 2 * gx, nz), F32),
-        in_specs=[scalars] + whole(11),
+        in_specs=[scalars] + whole(16),
         out_specs=whole(1)[0],
         scratch_shapes=[
-            pltpu.VMEM((ay, dom, nz), F32),
-            padded, padded, padded,
+            padded,
             pltpu.VMEM((ay, dom, nz), F32),
             pltpu.VMEM((ay, 64, nz), F32),
-            pltpu.VMEM((ay, 48, nz), F32),
-            pltpu.VMEM((ay, 48, nz), F32),
-            *weight_shapes,
-            pltpu.VMEM((23, dom, nz), F32),
-            pltpu.VMEM((dom + 16, nz), F32),
+            near,
+            *flux_shapes,
+            near,
             pltpu.VMEM((ay + 1, 48, nz), F32),
-            pltpu.VMEM((56, nz), F32),
+            near,
+            near,
+            pltpu.VMEM((dom, nz), F32),
         ],
         compiler_params=vmem,
         name="adjoint_waves",
-    )(at, window, clo, chi, *fields, back, front, seen)
+    )(at, *fields, images, back, front, seen, modulus, *weights, *slopes)
 
 
 def chain_kernel(at_ref, got_ref, out_ref, grad_ref):
@@ -870,12 +944,15 @@
     sent = jnp.broadcast_to(coefficients[None], (shots, 2, 2, bx, nz))
     column = lax.all_to_all(sent, "shot", 0, 0, tiled=True)
     column, seen, w3, w4 = lax.optimization_barrier((column, seen, w3, w4))
-    column = column.reshape(2 * shots, 2, bx, nz)
-    window = lax.dynamic_slice_in_dim(column, aperture[0], ay, 0)
-    clo, chi = both_ways(window[:, :, bx - rim :], window[:, :, :rim], "brick")
-    p1, p2, p3, p4, images, ahead, behind = forward_waves(at, window, clo, chi, source, plo, phi)
+    window, ahead, behind = take_window(at, column.reshape(2 * shots, 2, bx, nz))
+    clo, chi = both_ways(ahead, behind, "brick")
+    p1, p2, p3, p4, images, ahead, behind, modulus, *weights = forward_waves(
+        at, window, clo, chi, source, plo, phi
+    )
     back, front = both_ways(ahead, behind, "brick")
-    grads = adjoint_waves(at, window, clo, chi, (p1, p2, p3, p4, images), back, front, seen)
+    slopes = wave_slopes(p1, p2, p3)
+    back, front, slopes = lax.optimization_barrier((back, front, slopes))
+    grads = adjoint_waves(at, (p2, p3, p4), images, back, front, seen, modulus, weights, slopes)
     got = lax.all_to_all(grads, "shot", 0, 0, tiled=True)
     s1, s2 = spread_fields(at, lo, mid, hi, hidden)
     got, s1, s2 = lax.optimization_barrier((got, s1, s2))

time: 217 us -> 183 us (0.84)
  Pallas kernels: 74.2 us -> 60.9 us
  waiting for transfers between devices: 51 us -> 38.5 us
  local copies, waits for them, and re-layouts: 28.5 us -> 21 us
    pallas_call x1, Pallas kernels: 24.7 us -> 9.98 us  [adjoint_waves(): pl.pallas_call(adjoint_kernel, out_shape=jax.ShapeDtypeStruct((2 * shots,...]
    ppermute x6, waiting for transfers between devices: 18.7 us -> 9.77 us  [both_ways(): lax.ppermute(ahead, axis, forward)]
    ppermute x6, waiting for transfers between devices: 14.8 us -> 7.7 us  [both_ways(): lax.ppermute(behind, axis, backward_)]
    pallas_call x0 -> x2, Pallas kernels: none -> 5.55 us  [the longest x1 4.16 us: wave_slopes(): pl.pallas_call(slopes_kernel, out_shape=tuple((jax.ShapeDtypeStruct(shape...]
    unnamed x76 -> x74, local copies, waits for them, and re-layouts: 21.9 us -> 17.6 us
    pallas_call x1, Pallas kernels: 15.4 us -> 11.3 us  [forward_waves(): pl.pallas_call(forward_kernel, out_shape=tuple((jax.ShapeDtypeStruct(shap...]
    all_to_all x1, waiting for transfers between devices: 0.01 us -> 3.48 us  [per_device(): column = lax.all_to_all(sent, 'shot', 0, 0, tiled=True)]
  transfers between devices with their start and end apart: 15 -> 15, of which waited for: 10 -> 10; matrix products, arithmetic and copies ran while one was open for 3% -> 2% of each run, Pallas kernels for 12% -> 17%
where the time goes in v3:
time: 183 us; the launch traced here: 180 us
  Pallas kernels  60.9 us (33%)
  starting transfers between devices  40.7 us (22%)
  waiting for transfers between devices  38.5 us (21%)
  local copies, waits for them, and re-layouts  21 us (11%)
  blocking collectives  17 us (9%)
    unnamed x74, local copies, waits for them, and re-layouts  17.6 us
    all_to_all x1, blocking collectives, per_device(): slices = lax.all_to_all(kernels, everyone, 0, 0, tiled=True)  17 us
    ppermute x6, starting transfers between devices, both_ways(): lax.ppermute(behind, axis, backward_)  13.8 us
    all_to_all x1, waiting for transfers between devices, per_device(): got = lax.all_to_all(grads, 'shot', 0, 0, tiled=True)  13.1 us
    ppermute x6, starting transfers between devices, both_ways(): lax.ppermute(ahead, axis, forward)  12 us
    pallas_call x1, Pallas kernels, forward_waves(): pl.pallas_call(forward_kernel, out_shape=tuple((jax.ShapeDtypeStruct(shap...  11.3 us
    pallas_call x1, Pallas kernels, generator(): pl.pallas_call(generator_kernel, out_shape=(jax.ShapeDtypeStruct((2, 2, b...  10.6 us
    pallas_call x1, Pallas kernels, adjoint_waves(): pl.pallas_call(adjoint_kernel, out_shape=jax.ShapeDtypeStruct((2 * shots,...  9.98 us
  transfers between devices with their start and end apart: 15, of which 10 were waited for; matrix products, arithmetic and copies ran while one was open for 2% of the time, Pallas kernels for 17%

profile of v3, /device:TPU:32, one launch (start us, length us, event | category | flops | bytes accessed | tf_op | source)
XLA Modules:
  0.0 180.2 jit_solution(4406055192336007530)
XLA Ops:
  0.6 1.1 copy.55
  1.8 3.1 %collective-permute-start = (bf16[2,4,16,128]{3,2,1,0:T(8,128)(2,1)S(1)}, bf16[2,4,16,128]{3,2,1,0:T(8,128)(2,1)S(1)}, u32[]{:S(2)}, u32[]{:S(2)}) collective-permute-start(bf16[2,4,16,128]{3,2,1,0:T(8,128)(2,1)S(1)} %get-tuple-element.103), channel_id=1, source_target_pairs={{0,1},{1,2},{2,3},{3,4},{4,5},{5,6},{6,7},{7,0},{8,9},{9,10},{10,1... | collective-permute-start | bytes 98312 | tf_op jit(solution)/shard_map/ppermute | solution.py:923
  4.9 1.4 collective-permute-start.1
  6.3 1.0 copy.54
  7.3 0.9 collective-permute-done
  8.3 2.0 %collective-permute-done.1 = bf16[2,4,16,128]{3,2,1,0:T(8,128)(2,1)S(1)} collective-permute-done((bf16[2,4,16,128]{3,2,1,0:T(8,128)(2,1)S(1)}, bf16[2,4,16,128]{3,2,1,0:T(8,128)(2,1)S(1)}, u32[]{:S(2)}, u32[]{:S(2)}) %collective-permute-start.1) | collective-permute-done | bytes 32800 | tf_op jit(solution)/shard_map/ppermute | solution.py:923
  10.4 3.8 %collective-permute-start.3 = (bf16[2,40,16,128]{3,2,1,0:T(8,128)(2,1)S(1)}, bf16[2,40,16,128]{3,2,1,0:T(8,128)(2,1)S(1)}, u32[]{:S(2)}, u32[]{:S(2)}) collective-permute-start(bf16[2,40,16,128]{3,2,1,0:T(8,128)(2,1)S(1)} %pad_maximum_fusion.mid_ref), channel_id=1, source_target_pairs={{8,0},{16,8},{24,16},{32,24},{40,32},{48,40},{56,48},{64,56},{72,6... | collective-permute-start | bytes 983048 | tf_op jit(solution)/shard_map/ppermute | solution.py:923
  14.3 2.8 %collective-permute-start.4 = (f32[16,24,128]{2,1,0:T(8,128)S(1)}, f32[16,24,128]{2,1,0:T(8,128)S(1)}, u32[]{:S(2)}, u32[]{:S(2)}) collective-permute-start(f32[16,24,128]{2,1,0:T(8,128)S(1)} %get-tuple-element.102), channel_id=1, source_target_pairs={{0,1},{1,2},{2,3},{3,4},{4,5},{5,6},{6,7},{7,0},{8,9},{9,10},{10,1... | collective-permute-start | bytes 589832 | tf_op jit(solution)/shard_map/ppermute | solution.py:923
  17.1 1.7 collective-permute-start.5
  20.9 1.1 forward_bands.1
  22.1 10.6 %generator.1 = (f32[2,2,32,128]{3,2,1,0:T(8,128)S(1)}, f32[2,2,36,128]{3,2,1,0:T(8,128)S(1)}, bf16[38,64,128]{2,1,0:T(8,128)(2,1)S(1)}) custom-call(s32[3]{0:T(128)S(1)} %pad_add_fusion.at_ref, bf16[2,40,16,128]{3,2,1,0:T(8,128)(2,1)S(1)} %collective-permute-done.2.lo_ref, bf16[2,40,16,128]{3,2,1,0:T(8,128)(2,1)S(1)} %pad_maximum_fusion.mid_ref, ...), custom_call_target="tpu_custom_call" | custom-call | tf_op jit(solution)/shard_map/generator/pallas_call | solution.py:110
  33.6 1.1 broadcast_in_dim.4
  34.8 5.7 %all-to-all-start = ((f32[16,2,2,32,128]{4,3,2,1,0:T(8,128)}), f32[16,2,2,32,128]{4,3,2,1,0:T(8,128)}, u32[]{:S(2)}, u32[]{:S(2)}) async-start(f32[16,2,2,32,128]{4,3,2,1,0:T(8,128)} %broadcast_in_dim.4), calls=%async_computation | async-start | bytes 2097152 | tf_op jit(solution)/shard_map/all_to_all | solution.py:945
  40.5 0.8 copy.37
  41.5 9.1 %receiver_fields.1.seen_ref = f32[4,1280,128]{2,1,0:T(8,128)S(1)} custom-call(s32[3]{0:T(128)S(1)} %pad_add_fusion.at_ref, s32[3,2048]{1,0:T(4,128)S(1)} %bitcast.42, f32[3,2048]{1,0:T(4,128)S(1)} %bitcast.41), custom_call_target="tpu_custom_call" | custom-call | bytes 27000000 | tf_op jit(solution)/shard_map/receiver_fields/pallas_call | solution.py:174
  50.7 1.4 backward_bands.1
  52.0 0.9 copy-done.11
  53.6 3.5 %all-to-all-done = f32[16,2,2,32,128]{4,3,2,1,0:T(8,128)} async-done(((f32[16,2,2,32,128]{4,3,2,1,0:T(8,128)}), f32[16,2,2,32,128]{4,3,2,1,0:T(8,128)}, u32[]{:S(2)}, u32[]{:S(2)}) %all-to-all-start) | async-done | bytes 1048608 | tf_op jit(solution)/shard_map/all_to_all | solution.py:945
  57.1 1.4 take_window.1
  58.5 3.1 %collective-permute-start.6 = (bf16[16,2,32,128]{3,2,1,0:T(8,128)(2,1)S(1)}, bf16[16,2,32,128]{3,2,1,0:T(8,128)(2,1)S(1)}, u32[]{:S(2)}, u32[]{:S(2)}) collective-permute-start(bf16[16,2,32,128]{3,2,1,0:T(8,128)(2,1)S(1)} %get-tuple-element.57), channel_id=1, source_target_pairs={{0,1},{1,2},{2,3},{3,4},{4,5},{5,6},{6,7},{7,0},{8,9},{9,10},{10,1... | collective-permute-start | bytes 786440 | tf_op jit(solution)/shard_map/ppermute | solution.py:923
  61.6 1.4 collective-permute-start.7
  63.0 7.1 %collective-permute-done.6.clo_ref = bf16[16,2,32,128]{3,2,1,0:T(8,128)(2,1)S(1)} collective-permute-done((bf16[16,2,32,128]{3,2,1,0:T(8,128)(2,1)S(1)}, bf16[16,2,32,128]{3,2,1,0:T(8,128)(2,1)S(1)}, u32[]{:S(2)}, u32[]{:S(2)}) %collective-permute-start.6) | collective-permute-done | bytes 262176 | tf_op jit(solution)/shard_map/ppermute | solution.py:923
  70.1 4.7 %collective-permute-done.7.chi_ref = bf16[16,2,32,128]{3,2,1,0:T(8,128)(2,1)S(1)} collective-permute-done((bf16[16,2,32,128]{3,2,1,0:T(8,128)(2,1)S(1)}, bf16[16,2,32,128]{3,2,1,0:T(8,128)(2,1)S(1)}, u32[]{:S(2)}, u32[]{:S(2)}) %collective-permute-start.7) | collective-permute-done | bytes 262176 | tf_op jit(solution)/shard_map/ppermute | solution.py:923
  74.8 11.3 %forward_waves.1 = (f32[16,64,128]{2,1,0:T(8,128)S(1)}, f32[16,64,128]{2,1,0:T(8,128)S(1)}, f32[16,48,128]{2,1,0:T(8,128)S(1)}, f32[16,32,128]{2,1,0:T(8,128)S(1...) custom-call(s32[3]{0:T(128)S(1)} %pad_add_fusion.at_ref, ...), custom_call_target="tpu_custom_call" | custom-call | tf_op jit(solution)/shard_map/forward_waves/pallas_call | solution.py:452
  86.1 2.8 %collective-permute-start.8 = (bf16[16,32,128]{2,1,0:T(8,128)(2,1)S(1)}, bf16[16,32,128]{2,1,0:T(8,128)(2,1)S(1)}, u32[]{:S(2)}, u32[]{:S(2)}) collective-permute-start(bf16[16,32,128]{2,1,0:T(8,128)(2,1)S(1)} %get-tuple-element.65), channel_id=1, source_target_pairs={{0,1},{1,2},{2,3},{3,4},{4,5},{5,6},{6,7},{7,0},{8,9},{9,10},{10,1... | collective-permute-start | bytes 393224 | tf_op jit(solution)/shard_map/ppermute | solution.py:923
  88.9 1.7 collective-permute-start.9
  90.6 4.2 %wave_slopes.1 = (f32[3,16,48,128]{3,2,1,0:T(8,128)S(1)}, f32[3,17,48,128]{3,2,1,0:T(8,128)S(1)}, f32[3,16,48,128]{3,2,1,0:T(8,128)S(1)}, f32[3,16,48,128]{3,2,1,0:T(8,128)S(1)}) custom-call(f32[16,64,128]{2,1,0:T(8,128)S(1)} %get-tuple-element.67.p1_ref, f32[16,64,128]{2,1,0:T(8,128)S(1)} %get-tuple-element.61.p2_ref, ...), custom_call_target="tpu_custom_call" | custom-call | bytes 18000000 | tf_op jit(solution)/shard_map/wave_slopes/pallas_call | solution.py:492
  94.8 0.9 collective-permute-done.9.front_ref
  95.6 10.0 %adjoint_waves.1 = f32[32,72,128]{2,1,0:T(8,128)S(1)} custom-call(s32[3]{0:T(128)S(1)} %pad_add_fusion.at_ref, f32[16,64,128]{2,1,0:T(8,128)S(1)} %get-tuple-element.61.p2_ref, f32[16,48,128]{2,1,0:T(8,128)S(1)} %get-tuple-element.62.p3_ref, f32[16,32,128]{2,1,0:T(8,128)S(1)} %get-tuple-element.63.p4_ref, ...), custom_call_target="tpu_custom_call" | custom-call | tf_op jit(solution)/shard_map/adjoint_waves/pallas_call | solution.py:627
  105.6 1.0 copy-done
  106.6 4.0 %all-to-all-start.1 = ((f32[32,72,128]{2,1,0:T(8,128)}), f32[32,72,128]{2,1,0:T(8,128)S(1)}, u32[]{:S(2)}, u32[]{:S(2)}) async-start(f32[32,72,128]{2,1,0:T(8,128)} %copy-done), calls=%async_computation.1 | async-start | bytes 2359296 | tf_op jit(solution)/shard_map/all_to_all | solution.py:956
  110.6 2.4 %spread_fields.1 = (bf16[34,192,128]{2,1,0:T(8,128)(2,1)S(1)}, bf16[34,192,128]{2,1,0:T(8,128)(2,1)S(1)}) custom-call(s32[3]{0:T(128)S(1)} %pad_add_fusion.at_ref, bf16[2,40,16,128]{3,2,1,0:T(8,128)(2,1)S(1)} %collective-permute-done.2.lo_ref, bf16[2,40,16,128]{3,2,1,0:T(8,128)(2,1)S(1)} %pad_maximum_fusion.mid_ref, bf16[2,40,16,128]{3,2,1,0:T(8,128)(2,1)S(1)} %copy-done.10, ...), custom_call_target="tpu_custom_call" | custom-call | bytes 9000000 | tf_op jit(solution)/shard_map/spread_fields/pallas_call | solution.py:696
  113.0 1.2 copy-done.5
  114.2 1.2 copy-done.7
  115.4 13.1 %all-to-all-done.1 = f32[32,72,128]{2,1,0:T(8,128)S(1)} async-done(((f32[32,72,128]{2,1,0:T(8,128)}), f32[32,72,128]{2,1,0:T(8,128)S(1)}, u32[]{:S(2)}, u32[]{:S(2)}) %all-to-all-start.1) | async-done | bytes 1179680 | tf_op jit(solution)/shard_map/all_to_all | solution.py:956
  129.3 3.8 %collective-permute-start.11 = (bf16[2,2,36,128]{3,2,1,0:T(8,128)(2,1)S(1)}, bf16[2,2,36,128]{3,2,1,0:T(8,128)(2,1)S(1)}, u32[]{:S(2)}, u32[]{:S(2)}) collective-permute-start(bf16[2,2,36,128]{3,2,1,0:T(8,128)(2,1)S(1)} %chain.1.gmid_ref), channel_id=1, source_target_pairs={{8,0},{16,8},{24,16},{32,24},{40,32},{48,40},{56,48},{64,56},{72,6... | collective-permute-start | bytes 110600 | tf_op jit(solution)/shard_map/ppermute | solution.py:923
  133.1 1.7 collective-permute-done.10.glo_ref
  134.8 1.4 copy-done.6
  136.3 1.4 copy-done.8
  137.7 7.1 %kernel_grads.1 = (bf16[40,192,128]{2,1,0:T(8,128)(2,1)S(1)}, f32[128,128]{1,0:T(8,128)S(1)}) custom-call(s32[3]{0:T(128)S(1)} %pad_add_fusion.at_ref, bf16[2,2,36,128]{3,2,1,0:T(8,128)(2,1)S(1)} %collective-permute-done.10.glo_ref, bf16[2,2,36,128]{3,2,1,0:T(8,128)(2,1)S(1)} %chain.1.gmid_ref, bf16[2,2,36,128]{3,2,1,0:T(8,128)(2,1)S(1)} %collective-permute-done.11.ghi_ref, ...), custom_call_target="tpu_custom_call" | custom-call | tf_op jit(solution)/shard_map/kernel_grads/pallas_call | solution.py:782
  144.8 1.3 copy-done.3
  146.2 17.0 %all_to_all.25 = f32[128,1,128]{2,1,0:T(1,128)S(1)} all-to-all(f32[128,1,128]{2,1,0:T(1,128)S(1)} %bitcast.43), channel_id=1, replica_groups=mesh['shot'=16,'brick'=8] {'shot','brick'}, dimensions={0} | all-to-all | bytes 131072 | tf_op jit(solution)/shard_map/all_to_all | solution.py:967
  164.0 5.2 %all-to-all-start.3 = ((f32[128,1,128]{2,1,0:T(1,128)}), f32[128,1,128]{2,1,0:T(1,128)S(1)}, u32[]{:S(2)}, u32[]{:S(2)}) async-start(f32[128,1,128]{2,1,0:T(1,128)} %broadcast_in_dim.5), calls=%async_computation.3 | async-start | bytes 131072 | tf_op jit(solution)/shard_map/all_to_all | solution.py:969
  169.2 1.5 copy-done.4
  170.7 1.8 %latent_grads.1 = f32[32,32,128]{2,1,0:T(8,128)S(1)} custom-call(bf16[40,192,128]{2,1,0:T(8,128)(2,1)S(1)} %copy-done.4, bf16[128,1152]{1,0:T(8,128)(2,1)S(1)} %copy-done.15), custom_call_target="tpu_custom_call" | custom-call | bytes 12000000 | tf_op jit(solution)/shard_map/latent_grads/pallas_call | solution.py:812
  172.5 1.1 copy.53
  173.6 4.4 %all-to-all-done.3 = f32[128,1,128]{2,1,0:T(1,128)S(1)} async-done(((f32[128,1,128]{2,1,0:T(1,128)}), f32[128,1,128]{2,1,0:T(1,128)S(1)}, u32[]{:S(2)}, u32[]{:S(2)}) %all-to-all-start.3) | async-done | bytes 65568 | tf_op jit(solution)/shard_map/all_to_all | solution.py:969
  179.3 0.8 copy.42
  (85 shorter events, 6.2 us)
Async XLA Ops:
  1.8 17.7 %copy-start.31 = (bf16[27,2,16]{0,2,1:T(8,128)(2,1)S(1)}, bf16[27,2,16]{0,2,1:T(8,128)(2,1)}, u32[]{:S(2)}) copy-start(bf16[27,2,16]{0,2,1:T(8,128)(2,1)} %param.13) | copy-start | bytes 5188
  1.8 18.8 %copy-start.28 = (bf16[27,16,16]{0,2,1:T(8,128)(2,1)S(1)}, bf16[27,16,16]{0,2,1:T(8,128)(2,1)}, u32[]{:S(2)}) copy-start(bf16[27,16,16]{0,2,1:T(8,128)(2,1)} %param.12) | copy-start | bytes 41476
  1.8 6.5 %collective-permute-start = (bf16[2,4,16,128]{3,2,1,0:T(8,128)(2,1)S(1)}, bf16[2,4,16,128]{3,2,1,0:T(8,128)(2,1)S(1)}, u32[]{:S(2)}, u32[]{:S(2)}) collective-permute-start(bf16[2,4,16,128]{3,2,1,0:T(8,128)(2,1)S(1)} %get-tuple-element.103), channel_id=1, source_target_pairs={{0,1},{1,2},{2,3},{3,4},{4,5},{5,6},{6,7},{7,0},{8,9},{9,10},{10,1... | collective-permute-start | bytes 98312 | tf_op jit(solution)/shard_map/ppermute | solution.py:923
  4.9 16.0 %copy-start.22 = (s32[2,1536]{1,0:T(2,128)S(1)}, s32[2,1536]{1,0:T(2,128)}, u32[]{:S(2)}) copy-start(s32[2,1536]{1,0:T(2,128)} %constant.23.clone.codes_2_ref) | copy-start | bytes 36868
  4.9 16.0 %copy-start.24 = (s32[2,1152]{1,0:T(2,128)S(1)}, s32[2,1152]{1,0:T(2,128)}, u32[]{:S(2)}) copy-start(s32[2,1152]{1,0:T(2,128)} %constant.22.clone.codes_1_ref) | copy-start | bytes 27652
  4.9 5.4 %collective-permute-start.1 = (bf16[2,4,16,128]{3,2,1,0:T(8,128)(2,1)S(1)}, bf16[2,4,16,128]{3,2,1,0:T(8,128)(2,1)S(1)}, u32[]{:S(2)}, u32[]{:S(2)}) collective-permute-start(bf16[2,4,16,128]{3,2,1,0:T(8,128)(2,1)S(1)} %get-tuple-element.104), channel_id=1, source_target_pairs={{1,0},{2,1},{3,2},{4,3},{5,4},{6,5},{7,6},{0,7},{9,8},{10,9},{11,1... | collective-permute-start | bytes 98312 | tf_op jit(solution)/shard_map/ppermute | solution.py:923
  10.4 11.6 %collective-permute-start.2 = (bf16[2,40,16,128]{3,2,1,0:T(8,128)(2,1)S(1)}, bf16[2,40,16,128]{3,2,1,0:T(8,128)(2,1)S(1)}, u32[]{:S(2)}, u32[]{:S(2)}) collective-permute-start(bf16[2,40,16,128]{3,2,1,0:T(8,128)(2,1)S(1)} %pad_maximum_fusion.mid_ref), channel_id=1, source_target_pairs={{0,8},{8,16},{16,24},{24,32},{32,40},{40,48},{48,56},{56,64},{64,7... | collective-permute-start | bytes 983048 | tf_op jit(solution)/shard_map/ppermute | solution.py:923
  10.4 11.7 %collective-permute-start.3 = (bf16[2,40,16,128]{3,2,1,0:T(8,128)(2,1)S(1)}, bf16[2,40,16,128]{3,2,1,0:T(8,128)(2,1)S(1)}, u32[]{:S(2)}, u32[]{:S(2)}) collective-permute-start(bf16[2,40,16,128]{3,2,1,0:T(8,128)(2,1)S(1)} %pad_maximum_fusion.mid_ref), channel_id=1, source_target_pairs={{8,0},{16,8},{24,16},{32,24},{40,32},{48,40},{56,48},{64,56},{72,6... | collective-permute-start | bytes 983048 | tf_op jit(solution)/shard_map/ppermute | solution.py:923
  14.3 19.3 %collective-permute-start.4 = (f32[16,24,128]{2,1,0:T(8,128)S(1)}, f32[16,24,128]{2,1,0:T(8,128)S(1)}, u32[]{:S(2)}, u32[]{:S(2)}) collective-permute-start(f32[16,24,128]{2,1,0:T(8,128)S(1)} %get-tuple-element.102), channel_id=1, source_target_pairs={{0,1},{1,2},{2,3},{3,4},{4,5},{5,6},{6,7},{7,0},{8,9},{9,10},{10,1... | collective-permute-start | bytes 589832 | tf_op jit(solution)/shard_map/ppermute | solution.py:923
  17.1 16.5 %collective-permute-start.5 = (f32[16,24,128]{2,1,0:T(8,128)S(1)}, f32[16,24,128]{2,1,0:T(8,128)S(1)}, u32[]{:S(2)}, u32[]{:S(2)}) collective-permute-start(f32[16,24,128]{2,1,0:T(8,128)S(1)} %get-tuple-element.101), channel_id=1, source_target_pairs={{1,0},{2,1},{3,2},{4,3},{5,4},{6,5},{7,6},{0,7},{9,8},{10,9},{11,1... | collective-permute-start | bytes 589832 | tf_op jit(solution)/shard_map/ppermute | solution.py:923
  19.7 0.7 copy-start.26
  22.1 12.6 %copy-start.9 = (bf16[2,40,16,128]{3,2,1,0:T(8,128)(2,1)}, bf16[2,40,16,128]{3,2,1,0:T(8,128)(2,1)S(1)}, u32[]{:S(2)}) copy-start(bf16[2,40,16,128]{3,2,1,0:T(8,128)(2,1)S(1)} %collective-permute-done.3.hi_ref) | copy-start | bytes 983044
  32.8 0.8 copy-start.1
  33.6 1.1 copy-start.20
  33.6 1.1 copy-start.16
  33.6 1.1 copy-start.18
  34.7 6.6 %copy-start.29 = (f32[1,3,2048]{2,0,1:T(1,128)S(1)}, f32[1,3,2048]{2,0,1:T(1,128)}, u32[]{:S(2)}) copy-start(f32[1,3,2048]{2,0,1:T(1,128)} %param.15) | copy-start | bytes 73732
  34.7 6.7 %copy-start.30 = (s32[1,3,2048]{2,0,1:T(1,128)S(1)}, s32[1,3,2048]{2,0,1:T(1,128)}, u32[]{:S(2)}) copy-start(s32[1,3,2048]{2,0,1:T(1,128)} %param.17) | copy-start | bytes 73732
  34.8 22.3 %all-to-all-start = ((f32[16,2,2,32,128]{4,3,2,1,0:T(8,128)}), f32[16,2,2,32,128]{4,3,2,1,0:T(8,128)}, u32[]{:S(2)}, u32[]{:S(2)}) async-start(f32[16,2,2,32,128]{4,3,2,1,0:T(8,128)} %broadcast_in_dim.4), calls=%async_computation | async-start | bytes 2097152 | tf_op jit(solution)/shard_map/all_to_all | solution.py:945
  41.4 9.2 %copy-start.27 = (bf16[27,2,16]{1,2,0:T(8,128)(2,1)S(1)}, bf16[27,2,16]{1,2,0:T(8,128)(2,1)}, u32[]{:S(2)}) copy-start(bf16[27,2,16]{1,2,0:T(8,128)(2,1)} %copy-done.26) | copy-start | bytes 5188
  41.4 9.2 %copy-start.13 = (bf16[27,16,16]{1,2,0:T(8,128)(2,1)S(1)}, bf16[27,16,16]{1,2,0:T(8,128)(2,1)}, u32[]{:S(2)}) copy-start(bf16[27,16,16]{1,2,0:T(8,128)(2,1)} %copy.37) | copy-start | bytes 41476
  41.4 9.2 %copy-start.23 = (s32[2,1152]{1,0:T(2,128)S(1)}, s32[2,1152]{1,0:T(2,128)}, u32[]{:S(2)}) copy-start(s32[2,1152]{1,0:T(2,128)} %constant.25.clone.codes_4_ref) | copy-start | bytes 27652
  41.4 9.2 %copy-start.25 = (s32[2,576]{1,0:T(2,128)S(1)}, s32[2,576]{1,0:T(2,128)}, u32[]{:S(2)}) copy-start(s32[2,576]{1,0:T(2,128)} %constant.24.clone.codes_3_ref) | copy-start | bytes 13828
  52.0 0.9 copy-start.11
  52.9 0.7 copy-start.14
  57.1 17.7 %copy-start.17 = (f32[16,24,128]{2,1,0:T(8,128)S(1)}, f32[16,24,128]{2,1,0:T(8,128)}, u32[]{:S(2)}) copy-start(f32[16,24,128]{2,1,0:T(8,128)} %copy-done.16) | copy-start | bytes 589828
  57.1 17.7 %copy-start.19 = (f32[16,24,128]{2,1,0:T(8,128)S(1)}, f32[16,24,128]{2,1,0:T(8,128)}, u32[]{:S(2)}) copy-start(f32[16,24,128]{2,1,0:T(8,128)} %copy-done.18) | copy-start | bytes 589828
  58.5 11.6 %collective-permute-start.6 = (bf16[16,2,32,128]{3,2,1,0:T(8,128)(2,1)S(1)}, bf16[16,2,32,128]{3,2,1,0:T(8,128)(2,1)S(1)}, u32[]{:S(2)}, u32[]{:S(2)}) collective-permute-start(bf16[16,2,32,128]{3,2,1,0:T(8,128)(2,1)S(1)} %get-tuple-element.57), channel_id=1, source_target_pairs={{0,1},{1,2},{2,3},{3,4},{4,5},{5,6},{6,7},{7,0},{8,9},{9,10},{10,1... | collective-permute-start | bytes 786440 | tf_op jit(solution)/shard_map/ppermute | solution.py:923
  61.6 13.2 %collective-permute-start.7 = (bf16[16,2,32,128]{3,2,1,0:T(8,128)(2,1)S(1)}, bf16[16,2,32,128]{3,2,1,0:T(8,128)(2,1)S(1)}, u32[]{:S(2)}, u32[]{:S(2)}) collective-permute-start(bf16[16,2,32,128]{3,2,1,0:T(8,128)(2,1)S(1)} %get-tuple-element.58), channel_id=1, source_target_pairs={{1,0},{2,1},{3,2},{4,3},{5,4},{6,5},{7,6},{0,7},{9,8},{10,9},{11,1... | collective-permute-start | bytes 786440 | tf_op jit(solution)/shard_map/ppermute | solution.py:923
  86.1 8.7 %collective-permute-start.8 = (bf16[16,32,128]{2,1,0:T(8,128)(2,1)S(1)}, bf16[16,32,128]{2,1,0:T(8,128)(2,1)S(1)}, u32[]{:S(2)}, u32[]{:S(2)}) collective-permute-start(bf16[16,32,128]{2,1,0:T(8,128)(2,1)S(1)} %get-tuple-element.65), channel_id=1, source_target_pairs={{0,1},{1,2},{2,3},{3,4},{4,5},{5,6},{6,7},{7,0},{8,9},{9,10},{10,1... | collective-permute-start | bytes 393224 | tf_op jit(solution)/shard_map/ppermute | solution.py:923
  88.9 6.7 %collective-permute-start.9 = (bf16[16,32,128]{2,1,0:T(8,128)(2,1)S(1)}, bf16[16,32,128]{2,1,0:T(8,128)(2,1)S(1)}, u32[]{:S(2)}, u32[]{:S(2)}) collective-permute-start(bf16[16,32,128]{2,1,0:T(8,128)(2,1)S(1)} %get-tuple-element.66), channel_id=1, source_target_pairs={{1,0},{2,1},{3,2},{4,3},{5,4},{6,5},{7,6},{0,7},{9,8},{10,9},{11,1... | collective-permute-start | bytes 393224 | tf_op jit(solution)/shard_map/ppermute | solution.py:923
  105.6 1.0 copy-start
  106.6 4.0 %copy-start.2 = (bf16[38,64,128]{2,1,0:T(8,128)(2,1)S(1)}, bf16[38,64,128]{2,1,0:T(8,128)(2,1)}, u32[]{:S(2)}) copy-start(bf16[38,64,128]{2,1,0:T(8,128)(2,1)} %copy-done.1) | copy-start | bytes 1867780
  106.6 4.0 %copy-start.10 = (bf16[2,40,16,128]{3,2,1,0:T(8,128)(2,1)S(1)}, bf16[2,40,16,128]{3,2,1,0:T(8,128)(2,1)}, u32[]{:S(2)}) copy-start(bf16[2,40,16,128]{3,2,1,0:T(8,128)(2,1)} %copy-done.9) | copy-start | bytes 983044
  106.6 21.9 %all-to-all-start.1 = ((f32[32,72,128]{2,1,0:T(8,128)}), f32[32,72,128]{2,1,0:T(8,128)S(1)}, u32[]{:S(2)}, u32[]{:S(2)}) async-start(f32[32,72,128]{2,1,0:T(8,128)} %copy-done), calls=%async_computation.1 | async-start | bytes 2359296 | tf_op jit(solution)/shard_map/all_to_all | solution.py:956
  110.6 18.0 %copy-start.21 = (f32[2,2,36,128]{3,2,1,0:T(8,128)S(1)}, f32[2,2,36,128]{3,2,1,0:T(8,128)}, u32[]{:S(2)}) copy-start(f32[2,2,36,128]{3,2,1,0:T(8,128)} %copy-done.20) | copy-start | bytes 221188
  110.6 24.2 %copy-start.12 = (bf16[512,576]{1,0:T(8,128)(2,1)S(1)}, bf16[512,576]{1,0:T(8,128)(2,1)}, u32[]{:S(2)}) copy-start(bf16[512,576]{1,0:T(8,128)(2,1)} %copy-done.11) | copy-start | bytes 1769476
  113.0 1.2 copy-start.5
  114.2 1.2 copy-start.7
  128.6 40.6 %copy-start.15 = (bf16[128,1152]{1,0:T(8,128)(2,1)S(1)}, bf16[128,1152]{1,0:T(8,128)(2,1)}, u32[]{:S(2)}) copy-start(bf16[128,1152]{1,0:T(8,128)(2,1)} %copy-done.14) | copy-start | bytes 884740
  129.2 5.6 %collective-permute-start.10 = (bf16[2,2,36,128]{3,2,1,0:T(8,128)(2,1)S(1)}, bf16[2,2,36,128]{3,2,1,0:T(8,128)(2,1)S(1)}, u32[]{:S(2)}, u32[]{:S(2)}) collective-permute-start(bf16[2,2,36,128]{3,2,1,0:T(8,128)(2,1)S(1)} %chain.1.gmid_ref), channel_id=1, source_target_pairs={{0,8},{8,16},{16,24},{24,32},{32,40},{40,48},{48,56},{56,64},{64,7... | collective-permute-start | bytes 110600 | tf_op jit(solution)/shard_map/ppermute | solution.py:923
  129.3 5.5 %collective-permute-start.11 = (bf16[2,2,36,128]{3,2,1,0:T(8,128)(2,1)S(1)}, bf16[2,2,36,128]{3,2,1,0:T(8,128)(2,1)S(1)}, u32[]{:S(2)}, u32[]{:S(2)}) collective-permute-start(bf16[2,2,36,128]{3,2,1,0:T(8,128)(2,1)S(1)} %chain.1.gmid_ref), channel_id=1, source_target_pairs={{8,0},{16,8},{24,16},{32,24},{40,32},{48,40},{56,48},{64,56},{72,6... | collective-permute-start | bytes 110600 | tf_op jit(solution)/shard_map/ppermute | solution.py:923
  134.8 1.4 copy-start.6
  136.3 1.4 copy-start.8
  144.8 1.3 copy-start.3
  164.0 14.0 %all-to-all-start.3 = ((f32[128,1,128]{2,1,0:T(1,128)}), f32[128,1,128]{2,1,0:T(1,128)S(1)}, u32[]{:S(2)}, u32[]{:S(2)}) async-start(f32[128,1,128]{2,1,0:T(1,128)} %broadcast_in_dim.5), calls=%async_computation.3 | async-start | bytes 131072 | tf_op jit(solution)/shard_map/all_to_all | solution.py:969
  169.2 1.5 copy-start.4

commit v4 on v3

--- a/solution.py
+++ b/solution.py
@@ -68,13 +68,13 @@
                     ).astype(BF16)
         return carry
 
-    lax.fori_loop(0, bx + 8, spread, 0)
-
-    def first_conv(block, carry):
-        rows = s1[pl.ds(2 * block, 4)].reshape(4 * 288, nz)
-        acc = jnp.tanh(jnp.dot(w1_ref[...], rows, preferred_element_type=F32))
+    lax.fori_loop(0, bx + 8, spread, 0, unroll=4)
+    last_block = (bx + 6) // 2 - 1
+
+    def first_conv(block, before):
+        before = jnp.tanh(before)
         for xo in range(2):
-            x = 2 * block + xo
+            x = jnp.maximum(2 * block - 2, 0) + xo
             x_fine = ((x >= 3) | (brick > 0)) & ((x < bx + 3) | (brick < bricks - 1))
             for y in range(4):
                 fine = x_fine
@@ -83,14 +83,15 @@
                 if y == 3:
                     fine = fine & (shot < shots - 1)
                 start = (xo * 4 + y) * 16
-                value = jnp.where(fine, acc[start : start + 16], 0.0).astype(BF16)
+                value = jnp.where(fine, before[start : start + 16], 0.0).astype(BF16)
                 hid_ref[x, pl.ds(y * 16, 16), :] = value
                 wide = value.astype(F32)
                 for k in range(3):
                     s2[x, pl.ds(y * 48 + k * 16, 16), :] = lane_shift(wide, k).astype(BF16)
-        return carry
-
-    lax.fori_loop(0, (bx + 6) // 2, first_conv, 0)
+        rows = s1[pl.ds(2 * jnp.minimum(block, last_block), 4)].reshape(4 * 288, nz)
+        return jnp.dot(w1_ref[...], rows, preferred_element_type=F32)
+
+    lax.fori_loop(0, last_block + 2, first_conv, jnp.zeros((128, nz), F32))
 
     for block in range(gx // 6):
         rows = s2[pl.ds(6 * block, 8)].reshape(8 * 192, nz)
@@ -211,16 +212,6 @@
     return total
 
 
-def split_rows(value):
-    high = value.astype(BF16).astype(F32)
-    return jnp.concatenate([high, value - high], axis=0).astype(BF16)
-
-
-def joined(rows):
-    wide = rows.astype(F32)
-    return wide[:8] + wide[8:]
-
-
 def clear_sides(field):
     for y in (0, 1, 2, 3, ay + 4, ay + 5, ay + 6, ay + 7):
         field[y] = jnp.zeros(field.shape[1:], F32)
@@ -239,17 +230,21 @@
     )
 
 
-def window_kernel(at_ref, column_ref, win_ref, ahead_ref, behind_ref):
+def window_kernel(at_ref, column_ref, win_ref, ahead_ref, behind_ref, message):
     first_row = at_ref[2]
 
     def body(y, carry):
         for channel in range(2):
             value = column_ref[first_row + y, channel]
             win_ref[y, channel] = value
-            ahead_ref[y, channel, pl.ds(0, 16), :] = split_rows(value[24:])
-            ahead_ref[y, channel, pl.ds(16, 16), :] = value[8:24].astype(BF16)
-            behind_ref[y, channel, pl.ds(0, 16), :] = split_rows(value[:8])
-            behind_ref[y, channel, pl.ds(16, 16), :] = value[8:24].astype(BF16)
+            rounded = value.astype(BF16).astype(F32)
+            rest = value - rounded
+            for slot, (ref, near, further) in enumerate(((ahead_ref, 28, 12), (behind_ref, 0, 4))):
+                place = (channel * 2 + slot) * 24
+                message[pl.ds(place, 4), :] = rounded[near : near + 4]
+                message[pl.ds(place + 4, 4), :] = rest[near : near + 4]
+                message[pl.ds(place + 8, 16), :] = value[further : further + 16]
+                ref[y, channel] = message[pl.ds(place, 24), :].astype(BF16)
         return carry
 
     lax.fori_loop(0, ay, body, 0, unroll=2)
@@ -260,11 +255,12 @@
         window_kernel,
         out_shape=(
             jax.ShapeDtypeStruct((ay, 2, bx, nz), F32),
-            jax.ShapeDtypeStruct((ay, 2, bx, nz), BF16),
-            jax.ShapeDtypeStruct((ay, 2, bx, nz), BF16),
+            jax.ShapeDtypeStruct((ay, 2, 24, nz), BF16),
+            jax.ShapeDtypeStruct((ay, 2, 24, nz), BF16),
         ),
         in_specs=[scalars] + whole(1),
         out_specs=tuple(whole(3)),
+        scratch_shapes=[pltpu.VMEM((96, nz), F32)],
         compiler_params=vmem,
         name="take_window",
     )(at, column)
@@ -372,11 +368,13 @@
 
     def load(y, carry):
         for channel, ref, row, skip in ((0, modulus, y, 0), (1, buoy, y + 4, lead)):
-            ref[row, pl.ds(skip, 16), :] = low * clo_ref[y, channel, pl.ds(16, 16), :].astype(F32)
-            ref[row, pl.ds(skip + 16, 8), :] = low * joined(clo_ref[y, channel, pl.ds(0, 16), :])
+            received = low * clo_ref[y, channel].astype(F32)
+            ref[row, pl.ds(skip + 4, 16), :] = received[8:]
+            ref[row, pl.ds(skip + 20, 4), :] = received[:4] + received[4:8]
             ref[row, pl.ds(skip + rim, bx), :] = win_ref[y, channel]
-            ref[row, pl.ds(skip + rim + bx, 8), :] = high * joined(chi_ref[y, channel, pl.ds(0, 16), :])
-            ref[row, pl.ds(skip + rim + bx + 8, 16), :] = high * chi_ref[y, channel, pl.ds(16, 16), :].astype(F32)
+            received = high * chi_ref[y, channel].astype(F32)
+            ref[row, pl.ds(skip + rim + bx, 4), :] = received[:4] + received[4:8]
+            ref[row, pl.ds(skip + rim + bx + 4, 16), :] = received[8:]
         f1[y + 4, pl.ds(lead, rim), :] = low * plo_ref[y]
         f1[y + 4, pl.ds(lead + rim, bx), :] = src_ref[y]
         f1[y + 4, pl.ds(lead + rim + bx, rim), :] = high * phi_ref[y]
@@ -704,63 +702,84 @@
     )(at, lo, mid, hi, hidden)
 
 
-def kernel_grads_kernel(
-    at_ref, glo_ref, gmid_ref, ghi_ref, hid_ref, s1, s2, w3_ref, s4, kernel_ref, grads, own, s3, inner
+contract_lanes = (((1,), (1,)), ((), ()))
+
+
+def second_grads_kernel(gmid_ref, s2, second_ref, own):
+    own[...] = jnp.zeros(own.shape, F32)
+    for row in range(2):
+        for channel in range(2):
+            own[:, channel * 2 + row, :] = gmid_ref[row, channel].astype(F32)[2 : bx + 2]
+
+    def kernel_grad(x, second):
+        return second + lax.dot_general(
+            own[x].astype(BF16), s2[pl.ds(x, 3)].reshape(576, nz), contract_lanes, preferred_element_type=F32
+        )
+
+    second_ref[...] = lax.fori_loop(0, bx, kernel_grad, jnp.zeros((8, 576), F32), unroll=4)
+
+
+def second_grads(grad_output, s2):
+    return pl.pallas_call(
+        second_grads_kernel,
+        out_shape=jax.ShapeDtypeStruct((8, 576), F32),
+        in_specs=whole(2),
+        out_specs=whole(1)[0],
+        scratch_shapes=[pltpu.VMEM((bx, 8, nz), F32)],
+        compiler_params=vmem,
+        cost_estimate=cost(3),
+        name="second_grads",
+    )(grad_output, s2)
+
+
+def first_grads_kernel(
+    at_ref, glo_ref, gmid_ref, ghi_ref, hid_ref, second_ref, w3_ref, s1_any, inner_ref, kernel_ref, turned, s1, ready
 ):
+    fetch = pltpu.make_async_copy(s1_any, s1, ready)
+    fetch.start()
     shot, brick = at_ref[0], at_ref[1]
     y_fine = (shot > 0, True, shot < shots - 1)
-    grads[:, pl.ds(gx, 12), :] = jnp.zeros((12, 12, nz), F32)
-    own[...] = jnp.zeros(own.shape, F32)
     for part, ref in enumerate((glo_ref, gmid_ref, ghi_ref)):
         for row in range(2):
             for channel in range(2):
                 value = jnp.where(y_fine[part], ref[row, channel].astype(F32), 0.0)
-                grads[(2 * part + row) * 2 + channel, pl.ds(0, gx), :] = value
-                if part == 1:
-                    own[:, channel * 2 + row, :] = value[2 : bx + 2]
+                value = jnp.concatenate([value, jnp.zeros((12, nz), F32)], axis=0)
+                plane = (2 * part + row) * 2 + channel
+                for k in range(3):
+                    turned[plane * 3 + k] = lane_shift(value, k)
 
     def hidden_grad(block, carry):
-        for plane in range(12):
-            value = grads[plane, pl.ds(8 * block, 16), :]
-            for k in range(3):
-                s3[pl.ds((plane * 3 + k) * 16, 16), :] = lane_shift(value, k).astype(BF16)
-        acc = jnp.dot(w3_ref[...], s3[...], preferred_element_type=F32)
+        rows = turned[:, pl.ds(8 * block, 16), :].astype(BF16).reshape(576, nz)
+        acc = jnp.dot(w3_ref[...], rows, preferred_element_type=F32)
         for xo in range(8):
             x = 8 * block + xo
             x_fine = ((x >= 1) | (brick > 0)) & ((x < bx + 1) | (brick < bricks - 1))
+            hidden = hid_ref[jnp.minimum(x + 2, bx + 5)].astype(F32)
+            value = acc[xo * 64 : xo * 64 + 64] * (1.0 - hidden * hidden)
             for y in range(4):
                 fine = x_fine
                 if y == 0:
                     fine = fine & (shot > 0)
                 if y == 3:
                     fine = fine & (shot < shots - 1)
-                hidden = hid_ref[jnp.minimum(x + 2, bx + 5), pl.ds(y * 16, 16), :].astype(F32)
-                start = (xo * 4 + y) * 16
-                value = acc[start : start + 16] * (1.0 - hidden * hidden)
-                value = jnp.where(fine, value, 0.0).astype(BF16)
-                if y in (1, 2):
-                    inner[x, pl.ds((y - 1) * 16, 16), :] = value
-                wide = value.astype(F32)
-                for k in range(3):
-                    s4[x, pl.ds(y * 48 + k * 16, 16), :] = lane_shift(wide, k).astype(BF16)
+                inner_ref[x, pl.ds(y * 16, 16), :] = jnp.where(
+                    fine, value[y * 16 : y * 16 + 16], 0.0
+                ).astype(BF16)
         return carry
 
     lax.fori_loop(0, 5, hidden_grad, 0)
-
-    def kernel_grad(x, carry):
-        first, second = carry
-        contract = (((1,), (1,)), ((), ()))
-        first = first + lax.dot_general(
-            inner[x + 1], s1[pl.ds(x, 3)].reshape(576, nz), contract, preferred_element_type=F32
+    fetch.wait()
+
+    def kernel_grad(x, first):
+        return first + lax.dot_general(
+            inner_ref[x + 1, pl.ds(16, 32), :],
+            s1[pl.ds(x, 3)].reshape(576, nz),
+            contract_lanes,
+            preferred_element_type=F32,
         )
-        second = second + lax.dot_general(
-            own[x].astype(BF16), s2[pl.ds(x, 3)].reshape(576, nz), contract, preferred_element_type=F32
-        )
-        return first, second
-
-    first, second = lax.fori_loop(
-        0, bx, kernel_grad, (jnp.zeros((32, 576), F32), jnp.zeros((8, 576), F32)), unroll=4
-    )
+
+    first = lax.fori_loop(0, bx, kernel_grad, jnp.zeros((32, 576), F32), unroll=4)
+    second = second_ref[...]
     kernel_ref[...] = jnp.zeros(kernel_ref.shape, F32)
     for dx in range(3):
         start = dx * 192
@@ -778,27 +797,35 @@
         kernel_ref[pl.ds(dx * 36 + 18, 16), pl.ds(0, 16)] = one[:, 128:]
 
 
-def kernel_grads(at, glo, gmid, ghi, hidden, s1, s2, w3):
-    return pl.pallas_call(
-        kernel_grads_kernel,
+def first_grads(at, glo, gmid, ghi, hidden, second, w3, s1):
+    return pl.pallas_call(
+        first_grads_kernel,
         out_shape=(
-            jax.ShapeDtypeStruct((40, 192, nz), BF16),
+            jax.ShapeDtypeStruct((40, 64, nz), BF16),
             jax.ShapeDtypeStruct((128, nz), F32),
         ),
-        in_specs=[scalars] + whole(7),
+        in_specs=[scalars] + whole(6) + [pl.BlockSpec(memory_space=pl.ANY)],
         out_specs=tuple(whole(2)),
         scratch_shapes=[
-            pltpu.VMEM((12, 48, nz), F32),
-            pltpu.VMEM((bx, 8, nz), F32),
-            pltpu.VMEM((576, nz), BF16),
-            pltpu.VMEM((40, 32, nz), BF16),
+            pltpu.VMEM((36, 48, nz), F32),
+            pltpu.VMEM((bx + 2, 192, nz), BF16),
+            pltpu.SemaphoreType.DMA,
         ],
         compiler_params=vmem,
-        name="kernel_grads",
-    )(at, glo, gmid, ghi, hidden, s1, s2, w3)
-
-
-def latent_grad_kernel(s4, w4_ref, latent_ref):
+        name="first_grads",
+    )(at, glo, gmid, ghi, hidden, second, w3, s1)
+
+
+def latent_grad_kernel(inner_ref, w4_ref, latent_ref, s4):
+    def spread(x, carry):
+        for y in range(4):
+            value = inner_ref[x, pl.ds(y * 16, 16), :].astype(F32)
+            for k in range(3):
+                s4[x, pl.ds(y * 48 + k * 16, 16), :] = lane_shift(value, k).astype(BF16)
+        return carry
+
+    lax.fori_loop(0, bx + 2, spread, 0, unroll=2)
+
     def latent_grad(block, carry):
         rows = s4[pl.ds(4 * block, 6)].reshape(6 * 192, nz)
         acc = jnp.dot(w4_ref[...], rows, preferred_element_type=F32)
@@ -808,16 +835,17 @@
     lax.fori_loop(0, bx // 4, latent_grad, 0)
 
 
-def latent_grads(s4, w4):
+def latent_grads(inner, w4):
     return pl.pallas_call(
         latent_grad_kernel,
         out_shape=jax.ShapeDtypeStruct((bx, 32, nz), F32),
         in_specs=whole(2),
         out_specs=whole(1)[0],
+        scratch_shapes=[pltpu.VMEM((bx + 2, 192, nz), BF16)],
         compiler_params=vmem,
         cost_estimate=cost(4),
         name="latent_grads",
-    )(s4, w4)
+    )(inner, w4)
 
 
 def column_codes(x_in, y_in, order):
@@ -959,8 +987,9 @@
     got = got.reshape(shots, 2, 2 * gx, nz)
     grad_output = chain(at, got, output)
     glo, ghi = both_ways(grad_output, grad_output, "shot")
-    s4, kernels = kernel_grads(at, glo, grad_output, ghi, hidden, s1, s2, w3)
-    grad_latent = latent_grads(s4, w4)
+    second = second_grads(grad_output, s2)
+    inner, kernels = first_grads(at, glo, grad_output, ghi, hidden, second, w3, s1)
+    grad_latent = latent_grads(inner, w4)
     grad_latent = jnp.transpose(grad_latent.reshape(bx, 2, 16, nz), (2, 0, 1, 3))
 
     everyone = ("shot", "brick")

time: 183 us -> 171 us (0.934)
  local copies, waits for them, and re-layouts: 21 us -> 16.7 us
  waiting for transfers between devices: 38.5 us -> 35.6 us
  blocking collectives: 17 us -> 15.1 us
    unnamed x74 -> x70, local copies, waits for them, and re-layouts: 17.6 us -> 13.3 us
    pallas_call x1, Pallas kernels: 10.6 us -> 6.84 us  [generator(): pl.pallas_call(generator_kernel, out_shape=(jax.ShapeDtypeStruct((2, 2, b...]
    ppermute x6, waiting for transfers between devices: 9.77 us -> 6.69 us  [both_ways(): lax.ppermute(ahead, axis, forward)]
    all_to_all x1, blocking collectives: 17 us -> 15.1 us  [per_device(): slices = lax.all_to_all(kernels, everyone, 0, 0, tiled=True)]
    pallas_call x1 -> x2, Pallas kernels: 7.15 us -> 7.51 us  [the longest x1 5.18 us: first_grads(): pl.pallas_call(first_grads_kernel, out_shape=(jax.ShapeDtypeStruct((40, 6...]
  transfers between devices with their start and end apart: 15 -> 15, of which waited for: 10 -> 10; matrix products, arithmetic and copies ran while one was open for 2% -> 2% of each run, Pallas kernels for 17% -> 18%
where the time goes in v4:
time: 171 us; the launch traced here: 168 us
  Pallas kernels  59.2 us (35%)
  starting transfers between devices  39.4 us (23%)
  waiting for transfers between devices  35.6 us (21%)
  local copies, waits for them, and re-layouts  16.7 us (10%)
  blocking collectives  15.1 us (9%)
  between operations  1.76 us (1%)
    all_to_all x1, blocking collectives, per_device(): slices = lax.all_to_all(kernels, everyone, 0, 0, tiled=True)  15.1 us
    ppermute x6, starting transfers between devices, both_ways(): lax.ppermute(behind, axis, backward_)  14 us
    unnamed x70, local copies, waits for them, and re-layouts  13.3 us
    all_to_all x1, waiting for transfers between devices, per_device(): got = lax.all_to_all(grads, 'shot', 0, 0, tiled=True)  13.1 us
    ppermute x6, starting transfers between devices, both_ways(): lax.ppermute(ahead, axis, forward)  11.8 us
    pallas_call x1, Pallas kernels, forward_waves(): pl.pallas_call(forward_kernel, out_shape=tuple((jax.ShapeDtypeStruct(shap...  11.3 us
    pallas_call x1, Pallas kernels, adjoint_waves(): pl.pallas_call(adjoint_kernel, out_shape=jax.ShapeDtypeStruct((2 * shots,...  9.98 us
    pallas_call x1, Pallas kernels, receiver_fields(): pl.pallas_call(receiver_kernel, out_shape=jax.ShapeDtypeStruct((4, ay * d...  9.12 us
  transfers between devices with their start and end apart: 15, of which 10 were waited for; matrix products, arithmetic and copies ran while one was open for 2% of the time, Pallas kernels for 18%

profile of v4, /device:TPU:32, one launch (start us, length us, event | category | flops | bytes accessed | tf_op | source)
XLA Modules:
  0.0 168.1 jit_solution(14826761193582530495)
XLA Ops:
  0.6 1.1 copy.55
  1.8 3.1 %collective-permute-start = (bf16[2,4,16,128]{3,2,1,0:T(8,128)(2,1)S(1)}, bf16[2,4,16,128]{3,2,1,0:T(8,128)(2,1)S(1)}, u32[]{:S(2)}, u32[]{:S(2)}) collective-permute-start(bf16[2,4,16,128]{3,2,1,0:T(8,128)(2,1)S(1)} %get-tuple-element.103), channel_id=1, source_target_pairs={{0,1},{1,2},{2,3},{3,4},{4,5},{5,6},{6,7},{7,0},{8,9},{9,10},{10,1... | collective-permute-start | bytes 98312 | tf_op jit(solution)/shard_map/ppermute | solution.py:951
  4.9 1.4 collective-permute-start.1
  6.3 1.0 copy.54
  7.3 0.9 collective-permute-done
  8.3 2.0 %collective-permute-done.1 = bf16[2,4,16,128]{3,2,1,0:T(8,128)(2,1)S(1)} collective-permute-done((bf16[2,4,16,128]{3,2,1,0:T(8,128)(2,1)S(1)}, bf16[2,4,16,128]{3,2,1,0:T(8,128)(2,1)S(1)}, u32[]{:S(2)}, u32[]{:S(2)}) %collective-permute-start.1) | collective-permute-done | bytes 32800 | tf_op jit(solution)/shard_map/ppermute | solution.py:951
  10.4 3.8 %collective-permute-start.3 = (bf16[2,40,16,128]{3,2,1,0:T(8,128)(2,1)S(1)}, bf16[2,40,16,128]{3,2,1,0:T(8,128)(2,1)S(1)}, u32[]{:S(2)}, u32[]{:S(2)}) collective-permute-start(bf16[2,40,16,128]{3,2,1,0:T(8,128)(2,1)S(1)} %pad_maximum_fusion.mid_ref), channel_id=1, source_target_pairs={{8,0},{16,8},{24,16},{32,24},{40,32},{48,40},{56,48},{64,56},{72,6... | collective-permute-start | bytes 983048 | tf_op jit(solution)/shard_map/ppermute | solution.py:951
  14.3 2.8 %collective-permute-start.4 = (f32[16,24,128]{2,1,0:T(8,128)S(1)}, f32[16,24,128]{2,1,0:T(8,128)S(1)}, u32[]{:S(2)}, u32[]{:S(2)}) collective-permute-start(f32[16,24,128]{2,1,0:T(8,128)S(1)} %get-tuple-element.102), channel_id=1, source_target_pairs={{0,1},{1,2},{2,3},{3,4},{4,5},{5,6},{6,7},{7,0},{8,9},{9,10},{10,1... | collective-permute-start | bytes 589832 | tf_op jit(solution)/shard_map/ppermute | solution.py:951
  17.1 1.7 collective-permute-start.5
  20.9 1.1 forward_bands.1
  22.1 6.8 %generator.1 = (f32[2,2,32,128]{3,2,1,0:T(8,128)S(1)}, f32[2,2,36,128]{3,2,1,0:T(8,128)S(1)}, bf16[38,64,128]{2,1,0:T(8,128)(2,1)S(1)}) custom-call(s32[3]{0:T(128)S(1)} %pad_add_fusion.at_ref, bf16[2,40,16,128]{3,2,1,0:T(8,128)(2,1)S(1)} %collective-permute-done.2.lo_ref, bf16[2,40,16,128]{3,2,1,0:T(8,128)(2,1)S(1)} %pad_maximum_fusion.mid_ref, ...), custom_call_target="tpu_custom_call" | custom-call | tf_op jit(solution)/shard_map/generator/pallas_call | solution.py:111
  29.0 0.8 copy-done.1
  29.8 1.9 %collective-permute-done.5.phi_ref = f32[16,24,128]{2,1,0:T(8,128)S(1)} collective-permute-done((f32[16,24,128]{2,1,0:T(8,128)S(1)}, f32[16,24,128]{2,1,0:T(8,128)S(1)}, u32[]{:S(2)}, u32[]{:S(2)}) %collective-permute-start.5) | collective-permute-done | bytes 196640 | tf_op jit(solution)/shard_map/ppermute | solution.py:951
  31.7 1.1 broadcast_in_dim.4
  32.8 4.6 %all-to-all-start = ((f32[16,2,2,32,128]{4,3,2,1,0:T(8,128)}), f32[16,2,2,32,128]{4,3,2,1,0:T(8,128)}, u32[]{:S(2)}, u32[]{:S(2)}) async-start(f32[16,2,2,32,128]{4,3,2,1,0:T(8,128)} %broadcast_in_dim.4), calls=%async_computation | async-start | bytes 2097152 | tf_op jit(solution)/shard_map/all_to_all | solution.py:973
  37.5 0.8 copy.37
  38.4 9.1 %receiver_fields.1.seen_ref = f32[4,1280,128]{2,1,0:T(8,128)S(1)} custom-call(s32[3]{0:T(128)S(1)} %pad_add_fusion.at_ref, s32[3,2048]{1,0:T(4,128)S(1)} %bitcast.42, f32[3,2048]{1,0:T(4,128)S(1)} %bitcast.41), custom_call_target="tpu_custom_call" | custom-call | bytes 27000000 | tf_op jit(solution)/shard_map/receiver_fields/pallas_call | solution.py:175
  47.6 1.4 backward_bands.1
  49.0 0.9 copy-done.9
  50.6 3.5 %all-to-all-done = f32[16,2,2,32,128]{4,3,2,1,0:T(8,128)} async-done(((f32[16,2,2,32,128]{4,3,2,1,0:T(8,128)}), f32[16,2,2,32,128]{4,3,2,1,0:T(8,128)}, u32[]{:S(2)}, u32[]{:S(2)}) %all-to-all-start) | async-done | bytes 1048608 | tf_op jit(solution)/shard_map/all_to_all | solution.py:973
  54.1 1.5 take_window.1
  55.6 2.9 %collective-permute-start.6 = (bf16[16,2,24,128]{3,2,1,0:T(8,128)(2,1)S(1)}, bf16[16,2,24,128]{3,2,1,0:T(8,128)(2,1)S(1)}, u32[]{:S(2)}, u32[]{:S(2)}) collective-permute-start(bf16[16,2,24,128]{3,2,1,0:T(8,128)(2,1)S(1)} %get-tuple-element.57), channel_id=1, source_target_pairs={{0,1},{1,2},{2,3},{3,4},{4,5},{5,6},{6,7},{7,0},{8,9},{9,10},{10,1... | collective-permute-start | bytes 589832 | tf_op jit(solution)/shard_map/ppermute | solution.py:951
  58.5 1.6 collective-permute-start.7
  60.1 5.7 %collective-permute-done.6.clo_ref = bf16[16,2,24,128]{3,2,1,0:T(8,128)(2,1)S(1)} collective-permute-done((bf16[16,2,24,128]{3,2,1,0:T(8,128)(2,1)S(1)}, bf16[16,2,24,128]{3,2,1,0:T(8,128)(2,1)S(1)}, u32[]{:S(2)}, u32[]{:S(2)}) %collective-permute-start.6) | collective-permute-done | bytes 196640 | tf_op jit(solution)/shard_map/ppermute | solution.py:951
  65.8 2.9 %collective-permute-done.7.chi_ref = bf16[16,2,24,128]{3,2,1,0:T(8,128)(2,1)S(1)} collective-permute-done((bf16[16,2,24,128]{3,2,1,0:T(8,128)(2,1)S(1)}, bf16[16,2,24,128]{3,2,1,0:T(8,128)(2,1)S(1)}, u32[]{:S(2)}, u32[]{:S(2)}) %collective-permute-start.7) | collective-permute-done | bytes 196640 | tf_op jit(solution)/shard_map/ppermute | solution.py:951
  68.8 11.3 %forward_waves.1 = (f32[16,64,128]{2,1,0:T(8,128)S(1)}, f32[16,64,128]{2,1,0:T(8,128)S(1)}, f32[16,48,128]{2,1,0:T(8,128)S(1)}, f32[16,32,128]{2,1,0:T(8,128)S(1...) custom-call(s32[3]{0:T(128)S(1)} %pad_add_fusion.at_ref, ...), custom_call_target="tpu_custom_call" | custom-call | tf_op jit(solution)/shard_map/forward_waves/pallas_call | solution.py:450
  80.1 2.9 %collective-permute-start.8 = (bf16[16,32,128]{2,1,0:T(8,128)(2,1)S(1)}, bf16[16,32,128]{2,1,0:T(8,128)(2,1)S(1)}, u32[]{:S(2)}, u32[]{:S(2)}) collective-permute-start(bf16[16,32,128]{2,1,0:T(8,128)(2,1)S(1)} %get-tuple-element.65), channel_id=1, source_target_pairs={{0,1},{1,2},{2,3},{3,4},{4,5},{5,6},{6,7},{7,0},{8,9},{9,10},{10,1... | collective-permute-start | bytes 393224 | tf_op jit(solution)/shard_map/ppermute | solution.py:951
  83.0 1.6 collective-permute-start.9
  84.6 4.2 %wave_slopes.1 = (f32[3,16,48,128]{3,2,1,0:T(8,128)S(1)}, f32[3,17,48,128]{3,2,1,0:T(8,128)S(1)}, f32[3,16,48,128]{3,2,1,0:T(8,128)S(1)}, f32[3,16,48,128]{3,2,1,0:T(8,128)S(1)}) custom-call(f32[16,64,128]{2,1,0:T(8,128)S(1)} %get-tuple-element.67.p1_ref, f32[16,64,128]{2,1,0:T(8,128)S(1)} %get-tuple-element.61.p2_ref, ...), custom_call_target="tpu_custom_call" | custom-call | bytes 18000000 | tf_op jit(solution)/shard_map/wave_slopes/pallas_call | solution.py:490
  88.8 0.9 collective-permute-done.9.front_ref
  89.7 10.0 %adjoint_waves.1 = f32[32,72,128]{2,1,0:T(8,128)S(1)} custom-call(s32[3]{0:T(128)S(1)} %pad_add_fusion.at_ref, f32[16,64,128]{2,1,0:T(8,128)S(1)} %get-tuple-element.61.p2_ref, f32[16,48,128]{2,1,0:T(8,128)S(1)} %get-tuple-element.62.p3_ref, f32[16,32,128]{2,1,0:T(8,128)S(1)} %get-tuple-element.63.p4_ref, ...), custom_call_target="tpu_custom_call" | custom-call | tf_op jit(solution)/shard_map/adjoint_waves/pallas_call | solution.py:625
  99.7 1.0 copy-done
  100.7 3.8 %all-to-all-start.1 = ((f32[32,72,128]{2,1,0:T(8,128)}), f32[32,72,128]{2,1,0:T(8,128)S(1)}, u32[]{:S(2)}, u32[]{:S(2)}) async-start(f32[32,72,128]{2,1,0:T(8,128)} %copy-done), calls=%async_computation.1 | async-start | bytes 2359296 | tf_op jit(solution)/shard_map/all_to_all | solution.py:984
  104.6 2.4 %spread_fields.1 = (bf16[34,192,128]{2,1,0:T(8,128)(2,1)S(1)}, bf16[34,192,128]{2,1,0:T(8,128)(2,1)S(1)}) custom-call(s32[3]{0:T(128)S(1)} %pad_add_fusion.at_ref, bf16[2,40,16,128]{3,2,1,0:T(8,128)(2,1)S(1)} %collective-permute-done.2.lo_ref, bf16[2,40,16,128]{3,2,1,0:T(8,128)(2,1)S(1)} %pad_maximum_fusion.mid_ref, bf16[2,40,16,128]{3,2,1,0:T(8,128)(2,1)S(1)} %copy-done.8, ...), custom_call_target="tpu_custom_call" | custom-call | bytes 9000000 | tf_op jit(solution)/shard_map/spread_fields/pallas_call | solution.py:694
  107.0 1.2 copy-done.3
  108.2 1.2 copy-done.5
  109.3 13.1 %all-to-all-done.1 = f32[32,72,128]{2,1,0:T(8,128)S(1)} async-done(((f32[32,72,128]{2,1,0:T(8,128)}), f32[32,72,128]{2,1,0:T(8,128)S(1)}, u32[]{:S(2)}, u32[]{:S(2)}) %all-to-all-start.1) | async-done | bytes 1179680 | tf_op jit(solution)/shard_map/all_to_all | solution.py:984
  123.2 3.8 %collective-permute-start.11 = (bf16[2,2,36,128]{3,2,1,0:T(8,128)(2,1)S(1)}, bf16[2,2,36,128]{3,2,1,0:T(8,128)(2,1)S(1)}, u32[]{:S(2)}, u32[]{:S(2)}) collective-permute-start(bf16[2,2,36,128]{3,2,1,0:T(8,128)(2,1)S(1)} %chain.1.gmid_ref), channel_id=1, source_target_pairs={{8,0},{16,8},{24,16},{32,24},{40,32},{48,40},{56,48},{64,56},{72,6... | collective-permute-start | bytes 110600 | tf_op jit(solution)/shard_map/ppermute | solution.py:951
  127.1 1.4 copy-done.6
  128.5 2.3 %second_grads.1.second_ref = f32[8,576]{1,0:T(8,128)S(1)} custom-call(bf16[2,2,36,128]{3,2,1,0:T(8,128)(2,1)S(1)} %chain.1.gmid_ref, bf16[34,192,128]{2,1,0:T(8,128)(2,1)S(1)} %copy-done.6), custom_call_target="tpu_custom_call" | custom-call | bytes 9000000 | tf_op jit(solution)/shard_map/second_grads/pallas_call | solution.py:723
  130.9 5.2 %first_grads.1 = (bf16[40,64,128]{2,1,0:T(8,128)(2,1)S(1)}, f32[128,128]{1,0:T(8,128)S(1)}) custom-call(s32[3]{0:T(128)S(1)} %pad_add_fusion.at_ref, bf16[2,2,36,128]{3,2,1,0:T(8,128)(2,1)S(1)} %collective-permute-done.10.glo_ref, bf16[2,2,36,128]{3,2,1,0:T(8,128)(2,1)S(1)} %chain.1.gmid_ref, bf16[2,2,36,128]{3,2,1,0:T(8,128)(2,1)S(1)} %collective-permute-done.11.ghi_ref, ...), custom_call_target="tpu_custom_call" | custom-call | tf_op jit(solution)/shard_map/first_grads/pallas_call | solution.py:801
  136.1 15.1 %all_to_all.25 = f32[128,1,128]{2,1,0:T(1,128)S(1)} all-to-all(f32[128,1,128]{2,1,0:T(1,128)S(1)} %bitcast.43), channel_id=1, replica_groups=mesh['shot'=16,'brick'=8] {'shot','brick'}, dimensions={0} | all-to-all | bytes 131072 | tf_op jit(solution)/shard_map/all_to_all | solution.py:996
  151.9 5.2 %all-to-all-start.3 = ((f32[128,1,128]{2,1,0:T(1,128)}), f32[128,1,128]{2,1,0:T(1,128)S(1)}, u32[]{:S(2)}, u32[]{:S(2)}) async-start(f32[128,1,128]{2,1,0:T(1,128)} %broadcast_in_dim.5), calls=%async_computation.3 | async-start | bytes 131072 | tf_op jit(solution)/shard_map/all_to_all | solution.py:998
  157.1 3.4 %latent_grads.1 = f32[32,32,128]{2,1,0:T(8,128)S(1)} custom-call(bf16[40,64,128]{2,1,0:T(8,128)(2,1)S(1)} %get-tuple-element.92.inner_ref, bf16[128,1152]{1,0:T(8,128)(2,1)S(1)} %copy-done.13), custom_call_target="tpu_custom_call" | custom-call | bytes 12000000 | tf_op jit(solution)/shard_map/latent_grads/pallas_call | solution.py:839
  160.5 1.1 copy.53
  161.5 4.4 %all-to-all-done.3 = f32[128,1,128]{2,1,0:T(1,128)S(1)} async-done(((f32[128,1,128]{2,1,0:T(1,128)}), f32[128,1,128]{2,1,0:T(1,128)S(1)}, u32[]{:S(2)}, u32[]{:S(2)}) %all-to-all-start.3) | async-done | bytes 65568 | tf_op jit(solution)/shard_map/all_to_all | solution.py:998
  166.5 0.8 copy.43
  167.3 0.8 copy.42
  (82 shorter events, 4.6 us)
Async XLA Ops:
  1.8 17.7 %copy-start.29 = (bf16[27,2,16]{0,2,1:T(8,128)(2,1)S(1)}, bf16[27,2,16]{0,2,1:T(8,128)(2,1)}, u32[]{:S(2)}) copy-start(bf16[27,2,16]{0,2,1:T(8,128)(2,1)} %param.13) | copy-start | bytes 5188
  1.8 18.8 %copy-start.26 = (bf16[27,16,16]{0,2,1:T(8,128)(2,1)S(1)}, bf16[27,16,16]{0,2,1:T(8,128)(2,1)}, u32[]{:S(2)}) copy-start(bf16[27,16,16]{0,2,1:T(8,128)(2,1)} %param.12) | copy-start | bytes 41476
  1.8 6.5 %collective-permute-start = (bf16[2,4,16,128]{3,2,1,0:T(8,128)(2,1)S(1)}, bf16[2,4,16,128]{3,2,1,0:T(8,128)(2,1)S(1)}, u32[]{:S(2)}, u32[]{:S(2)}) collective-permute-start(bf16[2,4,16,128]{3,2,1,0:T(8,128)(2,1)S(1)} %get-tuple-element.103), channel_id=1, source_target_pairs={{0,1},{1,2},{2,3},{3,4},{4,5},{5,6},{6,7},{7,0},{8,9},{9,10},{10,1... | collective-permute-start | bytes 98312 | tf_op jit(solution)/shard_map/ppermute | solution.py:951
  4.9 15.9 %copy-start.20 = (s32[2,1536]{1,0:T(2,128)S(1)}, s32[2,1536]{1,0:T(2,128)}, u32[]{:S(2)}) copy-start(s32[2,1536]{1,0:T(2,128)} %constant.23.clone.codes_2_ref) | copy-start | bytes 36868
  4.9 16.0 %copy-start.22 = (s32[2,1152]{1,0:T(2,128)S(1)}, s32[2,1152]{1,0:T(2,128)}, u32[]{:S(2)}) copy-start(s32[2,1152]{1,0:T(2,128)} %constant.22.clone.codes_1_ref) | copy-start | bytes 27652
  4.9 5.4 %collective-permute-start.1 = (bf16[2,4,16,128]{3,2,1,0:T(8,128)(2,1)S(1)}, bf16[2,4,16,128]{3,2,1,0:T(8,128)(2,1)S(1)}, u32[]{:S(2)}, u32[]{:S(2)}) collective-permute-start(bf16[2,4,16,128]{3,2,1,0:T(8,128)(2,1)S(1)} %get-tuple-element.104), channel_id=1, source_target_pairs={{1,0},{2,1},{3,2},{4,3},{5,4},{6,5},{7,6},{0,7},{9,8},{10,9},{11,1... | collective-permute-start | bytes 98312 | tf_op jit(solution)/shard_map/ppermute | solution.py:951
  10.4 11.6 %collective-permute-start.2 = (bf16[2,40,16,128]{3,2,1,0:T(8,128)(2,1)S(1)}, bf16[2,40,16,128]{3,2,1,0:T(8,128)(2,1)S(1)}, u32[]{:S(2)}, u32[]{:S(2)}) collective-permute-start(bf16[2,40,16,128]{3,2,1,0:T(8,128)(2,1)S(1)} %pad_maximum_fusion.mid_ref), channel_id=1, source_target_pairs={{0,8},{8,16},{16,24},{24,32},{32,40},{40,48},{48,56},{56,64},{64,7... | collective-permute-start | bytes 983048 | tf_op jit(solution)/shard_map/ppermute | solution.py:951
  10.4 11.7 %collective-permute-start.3 = (bf16[2,40,16,128]{3,2,1,0:T(8,128)(2,1)S(1)}, bf16[2,40,16,128]{3,2,1,0:T(8,128)(2,1)S(1)}, u32[]{:S(2)}, u32[]{:S(2)}) collective-permute-start(bf16[2,40,16,128]{3,2,1,0:T(8,128)(2,1)S(1)} %pad_maximum_fusion.mid_ref), channel_id=1, source_target_pairs={{8,0},{16,8},{24,16},{32,24},{40,32},{48,40},{56,48},{64,56},{72,6... | collective-permute-start | bytes 983048 | tf_op jit(solution)/shard_map/ppermute | solution.py:951
  14.3 15.5 %collective-permute-start.4 = (f32[16,24,128]{2,1,0:T(8,128)S(1)}, f32[16,24,128]{2,1,0:T(8,128)S(1)}, u32[]{:S(2)}, u32[]{:S(2)}) collective-permute-start(f32[16,24,128]{2,1,0:T(8,128)S(1)} %get-tuple-element.102), channel_id=1, source_target_pairs={{0,1},{1,2},{2,3},{3,4},{4,5},{5,6},{6,7},{7,0},{8,9},{9,10},{10,1... | collective-permute-start | bytes 589832 | tf_op jit(solution)/shard_map/ppermute | solution.py:951
  17.1 14.6 %collective-permute-start.5 = (f32[16,24,128]{2,1,0:T(8,128)S(1)}, f32[16,24,128]{2,1,0:T(8,128)S(1)}, u32[]{:S(2)}, u32[]{:S(2)}) collective-permute-start(f32[16,24,128]{2,1,0:T(8,128)S(1)} %get-tuple-element.101), channel_id=1, source_target_pairs={{1,0},{2,1},{3,2},{4,3},{5,4},{6,5},{7,6},{0,7},{9,8},{10,9},{11,1... | collective-permute-start | bytes 589832 | tf_op jit(solution)/shard_map/ppermute | solution.py:951
  19.7 0.6 copy-start.24
  22.1 10.7 %copy-start.7 = (bf16[2,40,16,128]{3,2,1,0:T(8,128)(2,1)}, bf16[2,40,16,128]{3,2,1,0:T(8,128)(2,1)S(1)}, u32[]{:S(2)}) copy-start(bf16[2,40,16,128]{3,2,1,0:T(8,128)(2,1)S(1)} %collective-permute-done.3.hi_ref) | copy-start | bytes 983044
  29.0 0.8 copy-start.1
  29.8 3.0 %copy-start.18 = (f32[2,2,36,128]{3,2,1,0:T(8,128)}, f32[2,2,36,128]{3,2,1,0:T(8,128)S(1)}, u32[]{:S(2)}) copy-start(f32[2,2,36,128]{3,2,1,0:T(8,128)S(1)} %get-tuple-element.88.out_ref) | copy-start | bytes 221188
  29.8 3.0 %copy-start.14 = (f32[16,24,128]{2,1,0:T(8,128)}, f32[16,24,128]{2,1,0:T(8,128)S(1)}, u32[]{:S(2)}) copy-start(f32[16,24,128]{2,1,0:T(8,128)S(1)} %collective-permute-done.4.plo_ref) | copy-start | bytes 589828
  31.7 1.1 copy-start.16
  32.8 5.5 %copy-start.27 = (f32[1,3,2048]{2,0,1:T(1,128)S(1)}, f32[1,3,2048]{2,0,1:T(1,128)}, u32[]{:S(2)}) copy-start(f32[1,3,2048]{2,0,1:T(1,128)} %param.15) | copy-start | bytes 73732
  32.8 5.5 %copy-start.28 = (s32[1,3,2048]{2,0,1:T(1,128)S(1)}, s32[1,3,2048]{2,0,1:T(1,128)}, u32[]{:S(2)}) copy-start(s32[1,3,2048]{2,0,1:T(1,128)} %param.17) | copy-start | bytes 73732
  32.8 21.2 %all-to-all-start = ((f32[16,2,2,32,128]{4,3,2,1,0:T(8,128)}), f32[16,2,2,32,128]{4,3,2,1,0:T(8,128)}, u32[]{:S(2)}, u32[]{:S(2)}) async-start(f32[16,2,2,32,128]{4,3,2,1,0:T(8,128)} %broadcast_in_dim.4), calls=%async_computation | async-start | bytes 2097152 | tf_op jit(solution)/shard_map/all_to_all | solution.py:973
  38.4 9.2 %copy-start.25 = (bf16[27,2,16]{1,2,0:T(8,128)(2,1)S(1)}, bf16[27,2,16]{1,2,0:T(8,128)(2,1)}, u32[]{:S(2)}) copy-start(bf16[27,2,16]{1,2,0:T(8,128)(2,1)} %copy-done.24) | copy-start | bytes 5188
  38.4 9.2 %copy-start.11 = (bf16[27,16,16]{1,2,0:T(8,128)(2,1)S(1)}, bf16[27,16,16]{1,2,0:T(8,128)(2,1)}, u32[]{:S(2)}) copy-start(bf16[27,16,16]{1,2,0:T(8,128)(2,1)} %copy.37) | copy-start | bytes 41476
  38.4 9.2 %copy-start.21 = (s32[2,1152]{1,0:T(2,128)S(1)}, s32[2,1152]{1,0:T(2,128)}, u32[]{:S(2)}) copy-start(s32[2,1152]{1,0:T(2,128)} %constant.25.clone.codes_4_ref) | copy-start | bytes 27652
  38.4 9.2 %copy-start.23 = (s32[2,576]{1,0:T(2,128)S(1)}, s32[2,576]{1,0:T(2,128)}, u32[]{:S(2)}) copy-start(s32[2,576]{1,0:T(2,128)} %constant.24.clone.codes_3_ref) | copy-start | bytes 13828
  49.0 0.9 copy-start.9
  49.9 0.7 copy-start.12
  54.1 14.7 %copy-start.15 = (f32[16,24,128]{2,1,0:T(8,128)S(1)}, f32[16,24,128]{2,1,0:T(8,128)}, u32[]{:S(2)}) copy-start(f32[16,24,128]{2,1,0:T(8,128)} %copy-done.14) | copy-start | bytes 589828
  54.1 14.7 %copy-start.17 = (f32[16,24,128]{2,1,0:T(8,128)S(1)}, f32[16,24,128]{2,1,0:T(8,128)}, u32[]{:S(2)}) copy-start(f32[16,24,128]{2,1,0:T(8,128)} %copy-done.16) | copy-start | bytes 589828
  55.6 10.2 %collective-permute-start.6 = (bf16[16,2,24,128]{3,2,1,0:T(8,128)(2,1)S(1)}, bf16[16,2,24,128]{3,2,1,0:T(8,128)(2,1)S(1)}, u32[]{:S(2)}, u32[]{:S(2)}) collective-permute-start(bf16[16,2,24,128]{3,2,1,0:T(8,128)(2,1)S(1)} %get-tuple-element.57), channel_id=1, source_target_pairs={{0,1},{1,2},{2,3},{3,4},{4,5},{5,6},{6,7},{7,0},{8,9},{9,10},{10,1... | collective-permute-start | bytes 589832 | tf_op jit(solution)/shard_map/ppermute | solution.py:951
  58.5 10.3 %collective-permute-start.7 = (bf16[16,2,24,128]{3,2,1,0:T(8,128)(2,1)S(1)}, bf16[16,2,24,128]{3,2,1,0:T(8,128)(2,1)S(1)}, u32[]{:S(2)}, u32[]{:S(2)}) collective-permute-start(bf16[16,2,24,128]{3,2,1,0:T(8,128)(2,1)S(1)} %get-tuple-element.58), channel_id=1, source_target_pairs={{1,0},{2,1},{3,2},{4,3},{5,4},{6,5},{7,6},{0,7},{9,8},{10,9},{11,1... | collective-permute-start | bytes 589832 | tf_op jit(solution)/shard_map/ppermute | solution.py:951
  80.1 8.7 %collective-permute-start.8 = (bf16[16,32,128]{2,1,0:T(8,128)(2,1)S(1)}, bf16[16,32,128]{2,1,0:T(8,128)(2,1)S(1)}, u32[]{:S(2)}, u32[]{:S(2)}) collective-permute-start(bf16[16,32,128]{2,1,0:T(8,128)(2,1)S(1)} %get-tuple-element.65), channel_id=1, source_target_pairs={{0,1},{1,2},{2,3},{3,4},{4,5},{5,6},{6,7},{7,0},{8,9},{9,10},{10,1... | collective-permute-start | bytes 393224 | tf_op jit(solution)/shard_map/ppermute | solution.py:951
  83.0 6.7 %collective-permute-start.9 = (bf16[16,32,128]{2,1,0:T(8,128)(2,1)S(1)}, bf16[16,32,128]{2,1,0:T(8,128)(2,1)S(1)}, u32[]{:S(2)}, u32[]{:S(2)}) collective-permute-start(bf16[16,32,128]{2,1,0:T(8,128)(2,1)S(1)} %get-tuple-element.66), channel_id=1, source_target_pairs={{1,0},{2,1},{3,2},{4,3},{5,4},{6,5},{7,6},{0,7},{9,8},{10,9},{11,1... | collective-permute-start | bytes 393224 | tf_op jit(solution)/shard_map/ppermute | solution.py:951
  99.7 1.0 copy-start
  100.7 3.9 %copy-start.2 = (bf16[38,64,128]{2,1,0:T(8,128)(2,1)S(1)}, bf16[38,64,128]{2,1,0:T(8,128)(2,1)}, u32[]{:S(2)}) copy-start(bf16[38,64,128]{2,1,0:T(8,128)(2,1)} %copy-done.1) | copy-start | bytes 1867780
  100.7 3.9 %copy-start.8 = (bf16[2,40,16,128]{3,2,1,0:T(8,128)(2,1)S(1)}, bf16[2,40,16,128]{3,2,1,0:T(8,128)(2,1)}, u32[]{:S(2)}) copy-start(bf16[2,40,16,128]{3,2,1,0:T(8,128)(2,1)} %copy-done.7) | copy-start | bytes 983044
  100.7 21.8 %all-to-all-start.1 = ((f32[32,72,128]{2,1,0:T(8,128)}), f32[32,72,128]{2,1,0:T(8,128)S(1)}, u32[]{:S(2)}, u32[]{:S(2)}) async-start(f32[32,72,128]{2,1,0:T(8,128)} %copy-done), calls=%async_computation.1 | async-start | bytes 2359296 | tf_op jit(solution)/shard_map/all_to_all | solution.py:984
  104.5 18.0 %copy-start.19 = (f32[2,2,36,128]{3,2,1,0:T(8,128)S(1)}, f32[2,2,36,128]{3,2,1,0:T(8,128)}, u32[]{:S(2)}) copy-start(f32[2,2,36,128]{3,2,1,0:T(8,128)} %copy-done.18) | copy-start | bytes 221188
  107.0 1.2 copy-start.3
  108.2 1.2 copy-start.5
  122.5 8.4 %copy-start.10 = (bf16[512,576]{1,0:T(8,128)(2,1)S(1)}, bf16[512,576]{1,0:T(8,128)(2,1)}, u32[]{:S(2)}) copy-start(bf16[512,576]{1,0:T(8,128)(2,1)} %copy-done.9) | copy-start | bytes 1769476
  123.1 7.7 %copy-start.4 = (bf16[34,192,128]{2,1,0:T(8,128)(2,1)S(1)}, bf16[34,192,128]{2,1,0:T(8,128)(2,1)}, u32[]{:S(2)}) copy-start(bf16[34,192,128]{2,1,0:T(8,128)(2,1)} %copy-done.3) | copy-start | bytes 5013508
  123.1 7.7 %collective-permute-start.10 = (bf16[2,2,36,128]{3,2,1,0:T(8,128)(2,1)S(1)}, bf16[2,2,36,128]{3,2,1,0:T(8,128)(2,1)S(1)}, u32[]{:S(2)}, u32[]{:S(2)}) collective-permute-start(bf16[2,2,36,128]{3,2,1,0:T(8,128)(2,1)S(1)} %chain.1.gmid_ref), channel_id=1, source_target_pairs={{0,8},{8,16},{16,24},{24,32},{32,40},{40,48},{48,56},{56,64},{64,7... | collective-permute-start | bytes 110600 | tf_op jit(solution)/shard_map/ppermute | solution.py:951
  123.2 7.6 %collective-permute-start.11 = (bf16[2,2,36,128]{3,2,1,0:T(8,128)(2,1)S(1)}, bf16[2,2,36,128]{3,2,1,0:T(8,128)(2,1)S(1)}, u32[]{:S(2)}, u32[]{:S(2)}) collective-permute-start(bf16[2,2,36,128]{3,2,1,0:T(8,128)(2,1)S(1)} %chain.1.gmid_ref), channel_id=1, source_target_pairs={{8,0},{16,8},{24,16},{32,24},{40,32},{48,40},{56,48},{64,56},{72,6... | collective-permute-start | bytes 110600 | tf_op jit(solution)/shard_map/ppermute | solution.py:951
  127.1 1.4 copy-start.6
  130.8 26.3 %copy-start.13 = (bf16[128,1152]{1,0:T(8,128)(2,1)S(1)}, bf16[128,1152]{1,0:T(8,128)(2,1)}, u32[]{:S(2)}) copy-start(bf16[128,1152]{1,0:T(8,128)(2,1)} %copy-done.12) | copy-start | bytes 884740
  151.9 14.0 %all-to-all-start.3 = ((f32[128,1,128]{2,1,0:T(1,128)}), f32[128,1,128]{2,1,0:T(1,128)S(1)}, u32[]{:S(2)}, u32[]{:S(2)}) async-start(f32[128,1,128]{2,1,0:T(1,128)} %broadcast_in_dim.5), calls=%async_computation.3 | async-start | bytes 131072 | tf_op jit(solution)/shard_map/all_to_all | solution.py:998

commit v5 on v4

--- a/solution.py
+++ b/solution.py
@@ -187,18 +187,56 @@
     )(at, cells, seen)
 
 
-def lane_factors():
-    lane = lane_index()
-    last = lane == nz - 1
-    upper = [jnp.where((lane <= nz - 1 - t) | last, ratios[t - 1], 0.0) for t in range(1, 5)]
-    lower = [jnp.where(lane >= t - 1, ratios[t - 1], 0.0) for t in range(1, 5)]
-    above = [jnp.where(lane <= nz - t, ratios[t - 1], 0.0) for t in range(1, 5)]
-    return last, upper, lower, above
-
-
-def turn(value, shift):
-    shift = shift % nz
-    return value if shift == 0 else pltpu.roll(value, shift, 1)
+def third_dimension_matrices():
+    slope = np.zeros((nz, 2 * nz))
+    spread = np.zeros((2 * nz, nz))
+    for t, ratio in enumerate(ratios, 1):
+        for face in range(nz):
+            for column, at in ((face, face), (nz + face, face if face < nz - 1 else -1)):
+                if 0 <= at + t < nz:
+                    slope[at + t, column] += ratio
+                if 0 <= at + 1 - t < nz:
+                    slope[at + 1 - t, column] -= ratio
+        for cell in range(nz):
+            if cell + t - 1 < nz:
+                spread[cell + t - 1, cell] += ratio
+            if cell - t >= -1:
+                spread[nz + (cell - t) % nz, cell] -= ratio
+
+    def parts(matrix):
+        high = matrix.astype(jnp.bfloat16)
+        return high, (matrix - high.astype(np.float64)).astype(jnp.bfloat16)
+
+    high, low = parts(slope)
+    slope = np.concatenate([high, high, low])
+    blocks = []
+    for half in (spread[:nz], spread[nz:]):
+        high, low = parts(half)
+        blocks += [high, high, low]
+    return slope, np.concatenate(blocks)
+
+
+slope_matrix, spread_matrix = third_dimension_matrices()
+
+
+def halves(value):
+    high = value.astype(BF16)
+    return high, (value - high.astype(F32)).astype(BF16)
+
+
+def slopes_z(value, slope_ref):
+    high, low = halves(value)
+    both = jnp.dot(
+        jnp.concatenate([high, low, high], axis=1), slope_ref[...], preferred_element_type=F32
+    )
+    return both[:, :nz], both[:, nz:]
+
+
+def rows_of(ref, y, count, first, rows):
+    return ref[pl.ds(y, count), pl.ds(first, rows), :].reshape(count * rows, nz)
+
+
+group = 4
 
 
 def differences(get):
@@ -275,10 +313,7 @@
     )
 
 
-def slopes_at(field, y, first, rows, factors):
-    value = field[y + 4, pl.ds(lead + first, rows), :]
-    turned_up = [turn(value, -t) for t in range(1, 5)]
-    turned_low = [turn(value, t - 1) for t in range(1, 5)]
+def slopes_xy(field, y, first, rows):
     base, more = lead + first - 4, rows + 8
     sx = differences(
         lambda t: (
@@ -286,27 +321,42 @@
             field[y + 4, pl.ds(base + 1 - t, more), :],
         )
     )
-    sy = slope_y(field, y, first, rows)
-    last, upper, lower, _ = factors
-    up = sum(upper[t] * turned_up[t] for t in range(4))
-    low = sum(lower[t] * turned_low[t] for t in range(4))
-    slope = up - low
-    return sx, sy, jnp.where(last, -low, slope), jnp.where(last, up, slope)
-
-
-def flux_pass(field, weights, fluxes, first, rows, factors, also=None):
-    wx, wy, wz, wzl = weights
-    fx, fy, fh, fb = fluxes
+    return sx, slope_y(field, y, first, rows)
+
+
+def third_pass(field, weights, matrices, out, first, rows, also=None):
+    _, _, wz, wzl = weights
+    slope_ref, spread_ref = matrices
+
+    def body(index, carry):
+        y = index * group
+        here, before = slopes_z(rows_of(field, y + 4, group, lead + first, rows), slope_ref)
+        if also is not None:
+            also(y, here, before)
+        high_h, low_h = halves(rows_of(wz, y, group, first, rows) * here)
+        high_b, low_b = halves(rows_of(wzl, y, group, first, rows) * before)
+        total = jnp.dot(
+            jnp.concatenate([high_h, low_h, high_h, high_b, low_b, high_b], axis=1),
+            spread_ref[...],
+            preferred_element_type=F32,
+        )
+        out[pl.ds(y, group), pl.ds(0, rows), :] = total.reshape(group, rows, nz)
+        return carry
+
+    lax.fori_loop(0, ay // group, body, 0, unroll=2)
+
+
+def flux_pass(field, weights, fluxes, first, rows, also=None):
+    wx, wy, _, _ = weights
+    fx, fy, _ = fluxes
     base, more = lead + first - 4, rows + 8
 
     def body(y, carry):
-        sx, sy, here, before = slopes_at(field, y, first, rows, factors)
+        sx, sy = slopes_xy(field, y, first, rows)
         fx[y, pl.ds(0, more), :] = wx[y, pl.ds(base, more), :] * sx
         fy[y + 3, pl.ds(0, rows), :] = wy[y, pl.ds(first, rows), :] * sy
-        fh[y, pl.ds(0, rows), :] = wz[y, pl.ds(first, rows), :] * here
-        fb[y, pl.ds(0, rows), :] = wzl[y, pl.ds(first, rows), :] * before
         if also is not None:
-            also(y, sx, sy, here, before)
+            also(y, sx, sy)
         return carry
 
     lax.fori_loop(0, ay, body, 0, unroll=2)
@@ -315,16 +365,11 @@
     return sy
 
 
-def divergence_pass(fluxes, rows, factors, consume):
-    fx, fy, fh, fb = fluxes
-    _, _, lower, above = factors
+def divergence_pass(fluxes, rows, consume):
+    fx, fy, az = fluxes
 
     def body(y, carry):
-        here = fh[y, pl.ds(0, rows), :]
-        before = fb[y, pl.ds(0, rows), :]
-        turned_here = [turn(here, 1 - t) for t in range(1, 5)]
-        turned_before = [turn(before, t) for t in range(1, 5)]
-        total = differences(
+        total = az[y, pl.ds(0, rows), :] + differences(
             lambda t: (fx[y, pl.ds(3 + t, rows), :], fx[y, pl.ds(4 - t, rows), :])
         )
         total = total + differences(
@@ -333,8 +378,6 @@
                 fy[y - t + 4, pl.ds(0, rows), :],
             )
         )
-        total = total + sum(above[t] * turned_here[t] for t in range(4))
-        total = total - sum(lower[t] * turned_before[t] for t in range(4))
         consume(y, total)
         return carry
 
@@ -347,19 +390,18 @@
     pltpu.VMEM((ay, 72, nz), F32),
     pltpu.VMEM((23, 64, nz), F32),
     pltpu.VMEM((ay, 64, nz), F32),
-    pltpu.VMEM((ay, 64, nz), F32),
 ]
 
 
 def forward_kernel(
-    at_ref, win_ref, clo_ref, chi_ref, src_ref, plo_ref, phi_ref,
+    at_ref, win_ref, clo_ref, chi_ref, src_ref, plo_ref, phi_ref, slope_ref, spread_ref,
     p1_ref, p2_ref, p3_ref, p4_ref, image_ref, ahead_ref, behind_ref, modulus, wx, wy, wz, wzl,
-    buoy, f1, f2, f3, fx, fy, fh, fb, message,
+    buoy, f1, f2, f3, fx, fy, az, message,
 ):
-    factors = lane_factors()
-    last = factors[0]
+    last = lane_index() == nz - 1
     weights = (wx, wy, wz, wzl)
-    fluxes = (fx, fy, fh, fb)
+    fluxes = (fx, fy, az)
+    matrices = (slope_ref, spread_ref)
     clear_rims(fy)
     for field in (buoy, f1, f2, f3):
         clear_sides(field)
@@ -436,12 +478,14 @@
         pack(y, behind_ref, 0, 7, 8)
         return carry
 
-    flux_pass(f1, weights, fluxes, 8, 64, factors)
-    divergence_pass(fluxes, 64, factors, first_step)
-    flux_pass(f2, weights, fluxes, 12, 56, factors)
-    divergence_pass(fluxes, 56, factors, second_step)
-    flux_pass(f3, weights, fluxes, 16, 48, factors)
-    divergence_pass(fluxes, 48, factors, third_step)
+    for field, first, rows, consume in (
+        (f1, 8, 64, first_step),
+        (f2, 12, 56, second_step),
+        (f3, 16, 48, third_step),
+    ):
+        third_pass(field, weights, matrices, az, first, rows)
+        flux_pass(field, weights, fluxes, first, rows)
+        divergence_pass(fluxes, rows, consume)
     lax.fori_loop(0, ay, send, 0)
 
 
@@ -453,16 +497,15 @@
         + (jax.ShapeDtypeStruct((ay, 32, nz), BF16),) * 2
         + (jax.ShapeDtypeStruct((ay, dom, nz), F32),)
         + tuple(jax.ShapeDtypeStruct(shape, F32) for shape in weight_sizes),
-        in_specs=[scalars] + whole(6),
+        in_specs=[scalars] + whole(8),
         out_specs=tuple(whole(12)),
         scratch_shapes=[padded, padded, padded, padded, *flux_shapes, pltpu.VMEM((32, nz), F32)],
         compiler_params=vmem,
         name="forward_waves",
-    )(at, window, clo, chi, source, plo, phi)
-
-
-def slopes_kernel(p1_ref, p2_ref, p3_ref, sx_ref, sy_ref, sh_ref, sb_ref, field):
-    factors = lane_factors()
+    )(at, window, clo, chi, source, plo, phi, slope_matrix, spread_matrix)
+
+
+def slopes_kernel(p1_ref, p2_ref, p3_ref, slope_ref, sx_ref, sy_ref, sh_ref, sb_ref, field):
     clear_sides(field)
     for index, (ref, first) in enumerate(((p1_ref, 8), (p2_ref, 8), (p3_ref, 16))):
         rows = ref.shape[1]
@@ -474,40 +517,47 @@
         lax.fori_loop(0, ay, load, 0)
 
         def body(y, carry):
-            sx, sy, here, before = slopes_at(field, y, 16, 48, factors)
+            sx, sy = slopes_xy(field, y, 16, 48)
             sx_ref[index, y] = sx[:48]
             sy_ref[index, y] = sy
-            sh_ref[index, y] = here
-            sb_ref[index, y] = before
             return carry
 
         lax.fori_loop(0, ay, body, 0, unroll=2)
         sy_ref[index, ay] = slope_y(field, ay, 16, 48)
 
+        def third(part, carry):
+            y = part * group
+            here, before = slopes_z(rows_of(field, y + 4, group, lead + 16, 48), slope_ref)
+            sh_ref[index, pl.ds(y, group)] = here.reshape(group, 48, nz)
+            sb_ref[index, pl.ds(y, group)] = before.reshape(group, 48, nz)
+            return carry
+
+        lax.fori_loop(0, ay // group, third, 0)
+
 
 def wave_slopes(p1, p2, p3):
     shapes = [(3, ay, 48, nz), (3, ay + 1, 48, nz), (3, ay, 48, nz), (3, ay, 48, nz)]
     return pl.pallas_call(
         slopes_kernel,
         out_shape=tuple(jax.ShapeDtypeStruct(shape, F32) for shape in shapes),
-        in_specs=whole(3),
+        in_specs=whole(4),
         out_specs=tuple(whole(4)),
         scratch_shapes=[padded],
         compiler_params=vmem,
         cost_estimate=cost(6),
         name="wave_slopes",
-    )(p1, p2, p3)
+    )(p1, p2, p3, slope_matrix)
 
 
 def adjoint_kernel(
     at_ref, p2_ref, p3_ref, p4_ref, image_ref, back_ref, front_ref, seen_ref,
-    modulus, wx, wy, wz, wzl, px_ref, py_ref, ph_ref, pb_ref,
+    slope_ref, spread_ref, modulus, wx, wy, wz, wzl, px_ref, py_ref, ph_ref, pb_ref,
     column_ref,
-    scaled, later, late, grad_m, fx, fy, fh, fb, qx, qy, qh, qb, far,
+    scaled, later, late, grad_m, fx, fy, az, qx, qy, qh, qb, far,
 ):
-    factors = lane_factors()
     weights = (wx, wy, wz, wzl)
-    fluxes = (fx, fy, fh, fb)
+    fluxes = (fx, fy, az)
+    matrices = (slope_ref, spread_ref)
     clear_rims(fy)
     clear_sides(scaled)
     low, high = halo_scale(at_ref)
@@ -540,22 +590,27 @@
 
     lax.fori_loop(0, ay, seed, 0)
 
+    def add(ref, place, product, index):
+        ref[place] = product if index == 2 else ref[place] + product
+
     def cross(index, offset):
-        def also(y, sx, sy, here, before):
-            products = (
-                (qx, sx[offset : offset + 48] * px_ref[index, y]),
-                (qy, sy[offset : offset + 48] * py_ref[index, y]),
-                (qh, here[offset : offset + 48] * ph_ref[index, y]),
-                (qb, before[offset : offset + 48] * pb_ref[index, y]),
-            )
-            for ref, product in products:
-                ref[y] = product if index == 2 else ref[y] + product
+        def also(y, sx, sy):
+            add(qx, y, sx[offset : offset + 48] * px_ref[index, y], index)
+            add(qy, y, sy[offset : offset + 48] * py_ref[index, y], index)
 
         return also
 
+    def cross_third(index, offset):
+        def also(y, here, before):
+            for ref, slope, other in ((qh, here, ph_ref), (qb, before, pb_ref)):
+                rows = slope.shape[0] // group
+                near_rows = slope.reshape(group, rows, nz)[:, offset : offset + 48]
+                add(ref, pl.ds(y, group), near_rows * other[index, pl.ds(y, group)], index)
+
+        return also
+
     def cross_last(index, offset, sy):
-        product = sy[offset : offset + 48] * py_ref[index, ay]
-        qy[ay] = product if index == 2 else qy[ay] + product
+        add(qy, ay, sy[offset : offset + 48] * py_ref[index, ay], index)
 
     def step_three(y, image):
         value = late[y]
@@ -573,18 +628,20 @@
         grad_m[y] = grad_m[y] + value * image_ref[0, y]
         later[y, pl.ds(16, 48), :] = value
 
-    sy = flux_pass(scaled, weights, fluxes, 8, 64, factors, cross(2, 8))
+    third_pass(scaled, weights, matrices, az, 8, 64, cross_third(2, 8))
+    sy = flux_pass(scaled, weights, fluxes, 8, 64, cross(2, 8))
     cross_last(2, 8, sy)
-    divergence_pass(fluxes, 64, factors, step_three)
+    divergence_pass(fluxes, 64, step_three)
 
     def rescale(y, carry):
         scaled[y + 4, pl.ds(lead + 8, 64), :] = modulus[y, pl.ds(8, 64), :] * late[y]
         return carry
 
     lax.fori_loop(0, ay, rescale, 0, unroll=2)
-    sy = flux_pass(scaled, weights, fluxes, 16, 48, factors, cross(1, 0))
+    third_pass(scaled, weights, matrices, az, 16, 48, cross_third(1, 0))
+    sy = flux_pass(scaled, weights, fluxes, 16, 48, cross(1, 0))
     cross_last(1, 0, sy)
-    divergence_pass(fluxes, 48, factors, step_two)
+    divergence_pass(fluxes, 48, step_two)
 
     def rescale_last(y, carry):
         scaled[y + 4, pl.ds(lead + 16, 48), :] = modulus[y, pl.ds(16, 48), :] * later[y, pl.ds(16, 48), :]
@@ -592,8 +649,15 @@
 
     lax.fori_loop(0, ay, rescale_last, 0, unroll=2)
 
+    def last_third(part, carry):
+        y = part * group
+        cross_third(0, 0)(y, *slopes_z(rows_of(scaled, y + 4, group, lead + 16, 48), slope_ref))
+        return carry
+
+    lax.fori_loop(0, ay // group, last_third, 0)
+
     def last_slopes(y, carry):
-        cross(0, 0)(y, *slopes_at(scaled, y, 16, 48, factors))
+        cross(0, 0)(y, *slopes_xy(scaled, y, 16, 48))
         return carry
 
     lax.fori_loop(0, ay, last_slopes, 0, unroll=2)
@@ -625,7 +689,7 @@
     return pl.pallas_call(
         adjoint_kernel,
         out_shape=jax.ShapeDtypeStruct((2 * shots, 2 * gx, nz), F32),
-        in_specs=[scalars] + whole(16),
+        in_specs=[scalars] + whole(18),
         out_specs=whole(1)[0],
         scratch_shapes=[
             padded,
@@ -641,7 +705,7 @@
         ],
         compiler_params=vmem,
         name="adjoint_waves",
-    )(at, *fields, images, back, front, seen, modulus, *weights, *slopes)
+    )(at, *fields, images, back, front, seen, slope_matrix, spread_matrix, modulus, *weights, *slopes)
 
 
 def chain_kernel(at_ref, got_ref, out_ref, grad_ref):

time: 171 us -> 167 us (0.977)
  Pallas kernels: 59.2 us -> 55.3 us
    pallas_call x1, Pallas kernels: 11.3 us -> 9.31 us  [forward_waves(): pl.pallas_call(forward_kernel, out_shape=tuple((jax.ShapeDtypeStruct(shap...]
    unnamed x70 -> x76, local copies, waits for them, and re-layouts: 13.3 us -> 12.7 us
where the time goes in v5:
time: 167 us; the launch traced here: 165 us
  Pallas kernels  55.3 us (33%)
  starting transfers between devices  39.4 us (24%)
  waiting for transfers between devices  36.6 us (22%)
  local copies, waits for them, and re-layouts  16.1 us (10%)
  blocking collectives  15.1 us (9%)
  between operations  1.8 us (1%)
    all_to_all x1, blocking collectives, per_device(): slices = lax.all_to_all(kernels, everyone, 0, 0, tiled=True)  15.1 us
    ppermute x6, starting transfers between devices, both_ways(): lax.ppermute(behind, axis, backward_)  14 us
    all_to_all x1, waiting for transfers between devices, per_device(): got = lax.all_to_all(grads, 'shot', 0, 0, tiled=True)  13.1 us
    unnamed x76, local copies, waits for them, and re-layouts  12.7 us
    ppermute x6, starting transfers between devices, both_ways(): lax.ppermute(ahead, axis, forward)  11.8 us
    pallas_call x1, Pallas kernels, forward_waves(): pl.pallas_call(forward_kernel, out_shape=tuple((jax.ShapeDtypeStruct(shap...  9.31 us
    pallas_call x1, Pallas kernels, receiver_fields(): pl.pallas_call(receiver_kernel, out_shape=jax.ShapeDtypeStruct((4, ay * d...  9.12 us
    pallas_call x1, Pallas kernels, adjoint_waves(): pl.pallas_call(adjoint_kernel, out_shape=jax.ShapeDtypeStruct((2 * shots,...  8.42 us
  transfers between devices with their start and end apart: 15, of which 10 were waited for; matrix products, arithmetic and copies ran while one was open for 2% of the time, Pallas kernels for 18%

profile of v5, /device:TPU:32, one launch (start us, length us, event | category | flops | bytes accessed | tf_op | source)
XLA Modules:
  0.0 164.6 jit_solution(6559429754754762517)
XLA Ops:
  0.6 1.1 copy.57
  1.8 3.1 %collective-permute-start = (bf16[2,4,16,128]{3,2,1,0:T(8,128)(2,1)S(1)}, bf16[2,4,16,128]{3,2,1,0:T(8,128)(2,1)S(1)}, u32[]{:S(2)}, u32[]{:S(2)}) collective-permute-start(bf16[2,4,16,128]{3,2,1,0:T(8,128)(2,1)S(1)} %get-tuple-element.103), channel_id=1, source_target_pairs={{0,1},{1,2},{2,3},{3,4},{4,5},{5,6},{6,7},{7,0},{8,9},{9,10},{10,1... | collective-permute-start | bytes 98312 | tf_op jit(solution)/shard_map/ppermute | solution.py:1015
  4.9 1.4 collective-permute-start.1
  6.3 1.0 copy.56
  7.3 0.9 collective-permute-done
  8.3 2.0 %collective-permute-done.1 = bf16[2,4,16,128]{3,2,1,0:T(8,128)(2,1)S(1)} collective-permute-done((bf16[2,4,16,128]{3,2,1,0:T(8,128)(2,1)S(1)}, bf16[2,4,16,128]{3,2,1,0:T(8,128)(2,1)S(1)}, u32[]{:S(2)}, u32[]{:S(2)}) %collective-permute-start.1) | collective-permute-done | bytes 32800 | tf_op jit(solution)/shard_map/ppermute | solution.py:1015
  10.4 3.8 %collective-permute-start.3 = (bf16[2,40,16,128]{3,2,1,0:T(8,128)(2,1)S(1)}, bf16[2,40,16,128]{3,2,1,0:T(8,128)(2,1)S(1)}, u32[]{:S(2)}, u32[]{:S(2)}) collective-permute-start(bf16[2,40,16,128]{3,2,1,0:T(8,128)(2,1)S(1)} %pad_maximum_fusion.mid_ref), channel_id=1, source_target_pairs={{8,0},{16,8},{24,16},{32,24},{40,32},{48,40},{56,48},{64,56},{72,6... | collective-permute-start | bytes 983048 | tf_op jit(solution)/shard_map/ppermute | solution.py:1015
  14.3 2.8 %collective-permute-start.4 = (f32[16,24,128]{2,1,0:T(8,128)S(1)}, f32[16,24,128]{2,1,0:T(8,128)S(1)}, u32[]{:S(2)}, u32[]{:S(2)}) collective-permute-start(f32[16,24,128]{2,1,0:T(8,128)S(1)} %get-tuple-element.102), channel_id=1, source_target_pairs={{0,1},{1,2},{2,3},{3,4},{4,5},{5,6},{6,7},{7,0},{8,9},{9,10},{10,1... | collective-permute-start | bytes 589832 | tf_op jit(solution)/shard_map/ppermute | solution.py:1015
  17.1 1.7 %collective-permute-start.5 = (f32[16,24,128]{2,1,0:T(8,128)S(1)}, f32[16,24,128]{2,1,0:T(8,128)S(1)}, u32[]{:S(2)}, u32[]{:S(2)}) collective-permute-start(f32[16,24,128]{2,1,0:T(8,128)S(1)} %get-tuple-element.101), channel_id=1, source_target_pairs={{1,0},{2,1},{3,2},{4,3},{5,4},{6,5},{7,6},{0,7},{9,8},{10,9},{11,1... | collective-permute-start | bytes 589832 | tf_op jit(solution)/shard_map/ppermute | solution.py:1015
  20.9 1.1 forward_bands.1
  22.1 6.8 %generator.1 = (f32[2,2,32,128]{3,2,1,0:T(8,128)S(1)}, f32[2,2,36,128]{3,2,1,0:T(8,128)S(1)}, bf16[38,64,128]{2,1,0:T(8,128)(2,1)S(1)}) custom-call(s32[3]{0:T(128)S(1)} %pad_add_fusion.at_ref, bf16[2,40,16,128]{3,2,1,0:T(8,128)(2,1)S(1)} %collective-permute-done.2.lo_ref, bf16[2,40,16,128]{3,2,1,0:T(8,128)(2,1)S(1)} %pad_maximum_fusion.mid_ref, ...), custom_call_target="tpu_custom_call" | custom-call | tf_op jit(solution)/shard_map/generator/pallas_call | solution.py:111
  29.0 0.8 copy-done.1
  29.8 1.9 %collective-permute-done.5.phi_ref = f32[16,24,128]{2,1,0:T(8,128)S(1)} collective-permute-done((f32[16,24,128]{2,1,0:T(8,128)S(1)}, f32[16,24,128]{2,1,0:T(8,128)S(1)}, u32[]{:S(2)}, u32[]{:S(2)}) %collective-permute-start.5) | collective-permute-done | bytes 196640 | tf_op jit(solution)/shard_map/ppermute | solution.py:1015
  31.7 1.1 broadcast_in_dim.4
  32.8 4.6 %all-to-all-start = ((f32[16,2,2,32,128]{4,3,2,1,0:T(8,128)}), f32[16,2,2,32,128]{4,3,2,1,0:T(8,128)}, u32[]{:S(2)}, u32[]{:S(2)}) async-start(f32[16,2,2,32,128]{4,3,2,1,0:T(8,128)} %broadcast_in_dim.4), calls=%async_computation | async-start | bytes 2097152 | tf_op jit(solution)/shard_map/all_to_all | solution.py:1037
  37.8 9.1 %receiver_fields.1.seen_ref = f32[4,1280,128]{2,1,0:T(8,128)S(1)} custom-call(s32[3]{0:T(128)S(1)} %pad_add_fusion.at_ref, s32[3,2048]{1,0:T(4,128)S(1)} %bitcast.42, f32[3,2048]{1,0:T(4,128)S(1)} %bitcast.41), custom_call_target="tpu_custom_call" | custom-call | bytes 27000000 | tf_op jit(solution)/shard_map/receiver_fields/pallas_call | solution.py:175
  47.0 1.3 backward_bands.1
  48.4 0.9 copy-done.13
  49.2 0.7 copy-done.15
  49.9 4.1 %all-to-all-done = f32[16,2,2,32,128]{4,3,2,1,0:T(8,128)} async-done(((f32[16,2,2,32,128]{4,3,2,1,0:T(8,128)}), f32[16,2,2,32,128]{4,3,2,1,0:T(8,128)}, u32[]{:S(2)}, u32[]{:S(2)}) %all-to-all-start) | async-done | bytes 1048608 | tf_op jit(solution)/shard_map/all_to_all | solution.py:1037
  54.1 1.5 take_window.1
  55.6 2.9 %collective-permute-start.6 = (bf16[16,2,24,128]{3,2,1,0:T(8,128)(2,1)S(1)}, bf16[16,2,24,128]{3,2,1,0:T(8,128)(2,1)S(1)}, u32[]{:S(2)}, u32[]{:S(2)}) collective-permute-start(bf16[16,2,24,128]{3,2,1,0:T(8,128)(2,1)S(1)} %get-tuple-element.57), channel_id=1, source_target_pairs={{0,1},{1,2},{2,3},{3,4},{4,5},{5,6},{6,7},{7,0},{8,9},{9,10},{10,1... | collective-permute-start | bytes 589832 | tf_op jit(solution)/shard_map/ppermute | solution.py:1015
  58.5 1.6 collective-permute-start.7
  60.1 5.7 %collective-permute-done.6.clo_ref = bf16[16,2,24,128]{3,2,1,0:T(8,128)(2,1)S(1)} collective-permute-done((bf16[16,2,24,128]{3,2,1,0:T(8,128)(2,1)S(1)}, bf16[16,2,24,128]{3,2,1,0:T(8,128)(2,1)S(1)}, u32[]{:S(2)}, u32[]{:S(2)}) %collective-permute-start.6) | collective-permute-done | bytes 196640 | tf_op jit(solution)/shard_map/ppermute | solution.py:1015
  65.9 2.9 %collective-permute-done.7.chi_ref = bf16[16,2,24,128]{3,2,1,0:T(8,128)(2,1)S(1)} collective-permute-done((bf16[16,2,24,128]{3,2,1,0:T(8,128)(2,1)S(1)}, bf16[16,2,24,128]{3,2,1,0:T(8,128)(2,1)S(1)}, u32[]{:S(2)}, u32[]{:S(2)}) %collective-permute-start.7) | collective-permute-done | bytes 196640 | tf_op jit(solution)/shard_map/ppermute | solution.py:1015
  68.8 9.3 %forward_waves.1 = (f32[16,64,128]{2,1,0:T(8,128)S(1)}, f32[16,64,128]{2,1,0:T(8,128)S(1)}, f32[16,48,128]{2,1,0:T(8,128)S(1)}, f32[16,32,128]{2,1,0:T(8,128)S(1...) custom-call(s32[3]{0:T(128)S(1)} %pad_add_fusion.at_ref, ...), custom_call_target="tpu_custom_call" | custom-call | tf_op jit(solution)/shard_map/forward_waves/pallas_call | solution.py:494
  78.1 2.9 %collective-permute-start.8 = (bf16[16,32,128]{2,1,0:T(8,128)(2,1)S(1)}, bf16[16,32,128]{2,1,0:T(8,128)(2,1)S(1)}, u32[]{:S(2)}, u32[]{:S(2)}) collective-permute-start(bf16[16,32,128]{2,1,0:T(8,128)(2,1)S(1)} %get-tuple-element.65), channel_id=1, source_target_pairs={{0,1},{1,2},{2,3},{3,4},{4,5},{5,6},{6,7},{7,0},{8,9},{9,10},{10,1... | collective-permute-start | bytes 393224 | tf_op jit(solution)/shard_map/ppermute | solution.py:1015
  81.0 1.6 collective-permute-start.9
  82.6 3.8 %wave_slopes.1 = (f32[3,16,48,128]{3,2,1,0:T(8,128)S(1)}, f32[3,17,48,128]{3,2,1,0:T(8,128)S(1)}, f32[3,16,48,128]{3,2,1,0:T(8,128)S(1)}, f32[3,16,48,128]{3,2,1,0:T(8,128)S(1)}) custom-call(f32[16,64,128]{2,1,0:T(8,128)S(1)} %get-tuple-element.67.p1_ref, f32[16,64,128]{2,1,0:T(8,128)S(1)} %get-tuple-element.61.p2_ref, ...), custom_call_target="tpu_custom_call" | custom-call | bytes 18000000 | tf_op jit(solution)/shard_map/wave_slopes/pallas_call | solution.py:540
  86.5 1.3 collective-permute-done.9.front_ref
  87.7 8.4 %adjoint_waves.1 = f32[32,72,128]{2,1,0:T(8,128)S(1)} custom-call(s32[3]{0:T(128)S(1)} %pad_add_fusion.at_ref, f32[16,64,128]{2,1,0:T(8,128)S(1)} %get-tuple-element.61.p2_ref, f32[16,48,128]{2,1,0:T(8,128)S(1)} %get-tuple-element.62.p3_ref, f32[16,32,128]{2,1,0:T(8,128)S(1)} %get-tuple-element.63.p4_ref, ...), custom_call_target="tpu_custom_call" | custom-call | tf_op jit(solution)/shard_map/adjoint_waves/pallas_call | solution.py:689
  96.2 1.0 copy-done
  97.2 3.8 %all-to-all-start.1 = ((f32[32,72,128]{2,1,0:T(8,128)}), f32[32,72,128]{2,1,0:T(8,128)S(1)}, u32[]{:S(2)}, u32[]{:S(2)}) async-start(f32[32,72,128]{2,1,0:T(8,128)} %copy-done), calls=%async_computation.1 | async-start | bytes 2359296 | tf_op jit(solution)/shard_map/all_to_all | solution.py:1048
  101.1 2.4 %spread_fields.1 = (bf16[34,192,128]{2,1,0:T(8,128)(2,1)S(1)}, bf16[34,192,128]{2,1,0:T(8,128)(2,1)S(1)}) custom-call(s32[3]{0:T(128)S(1)} %pad_add_fusion.at_ref, bf16[2,40,16,128]{3,2,1,0:T(8,128)(2,1)S(1)} %copy-done.9, bf16[2,40,16,128]{3,2,1,0:T(8,128)(2,1)S(1)} %pad_maximum_fusion.mid_ref, bf16[2,40,16,128]{3,2,1,0:T(8,128)(2,1)S(1)} %copy-done.11, ...), custom_call_target="tpu_custom_call" | custom-call | bytes 9000000 | tf_op jit(solution)/shard_map/spread_fields/pallas_call | solution.py:758
  103.5 1.2 copy-done.4
  104.7 1.2 copy-done.6
  105.8 13.1 %all-to-all-done.1 = f32[32,72,128]{2,1,0:T(8,128)S(1)} async-done(((f32[32,72,128]{2,1,0:T(8,128)}), f32[32,72,128]{2,1,0:T(8,128)S(1)}, u32[]{:S(2)}, u32[]{:S(2)}) %all-to-all-start.1) | async-done | bytes 1179680 | tf_op jit(solution)/shard_map/all_to_all | solution.py:1048
  119.7 3.8 %collective-permute-start.11 = (bf16[2,2,36,128]{3,2,1,0:T(8,128)(2,1)S(1)}, bf16[2,2,36,128]{3,2,1,0:T(8,128)(2,1)S(1)}, u32[]{:S(2)}, u32[]{:S(2)}) collective-permute-start(bf16[2,2,36,128]{3,2,1,0:T(8,128)(2,1)S(1)} %chain.1.gmid_ref), channel_id=1, source_target_pairs={{8,0},{16,8},{24,16},{32,24},{40,32},{48,40},{56,48},{64,56},{72,6... | collective-permute-start | bytes 110600 | tf_op jit(solution)/shard_map/ppermute | solution.py:1015
  123.5 1.4 copy-done.7
  125.0 2.3 %second_grads.1.second_ref = f32[8,576]{1,0:T(8,128)S(1)} custom-call(bf16[2,2,36,128]{3,2,1,0:T(8,128)(2,1)S(1)} %chain.1.gmid_ref, bf16[34,192,128]{2,1,0:T(8,128)(2,1)S(1)} %copy-done.7), custom_call_target="tpu_custom_call" | custom-call | bytes 9000000 | tf_op jit(solution)/shard_map/second_grads/pallas_call | solution.py:787
  127.4 5.2 %first_grads.1 = (bf16[40,64,128]{2,1,0:T(8,128)(2,1)S(1)}, f32[128,128]{1,0:T(8,128)S(1)}) custom-call(s32[3]{0:T(128)S(1)} %pad_add_fusion.at_ref, bf16[2,2,36,128]{3,2,1,0:T(8,128)(2,1)S(1)} %collective-permute-done.10.glo_ref, bf16[2,2,36,128]{3,2,1,0:T(8,128)(2,1)S(1)} %chain.1.gmid_ref, bf16[2,2,36,128]{3,2,1,0:T(8,128)(2,1)S(1)} %collective-permute-done.11.ghi_ref, ...), custom_call_target="tpu_custom_call" | custom-call | tf_op jit(solution)/shard_map/first_grads/pallas_call | solution.py:865
  132.5 15.1 %all_to_all.25 = f32[128,1,128]{2,1,0:T(1,128)S(1)} all-to-all(f32[128,1,128]{2,1,0:T(1,128)S(1)} %bitcast.43), channel_id=1, replica_groups=mesh['shot'=16,'brick'=8] {'shot','brick'}, dimensions={0} | all-to-all | bytes 131072 | tf_op jit(solution)/shard_map/all_to_all | solution.py:1060
  148.4 5.2 %all-to-all-start.3 = ((f32[128,1,128]{2,1,0:T(1,128)}), f32[128,1,128]{2,1,0:T(1,128)S(1)}, u32[]{:S(2)}, u32[]{:S(2)}) async-start(f32[128,1,128]{2,1,0:T(1,128)} %broadcast_in_dim.5), calls=%async_computation.3 | async-start | bytes 131072 | tf_op jit(solution)/shard_map/all_to_all | solution.py:1062
  153.6 3.4 %latent_grads.1 = f32[32,32,128]{2,1,0:T(8,128)S(1)} custom-call(bf16[40,64,128]{2,1,0:T(8,128)(2,1)S(1)} %get-tuple-element.92.inner_ref, bf16[128,1152]{1,0:T(8,128)(2,1)S(1)} %copy-done.16), custom_call_target="tpu_custom_call" | custom-call | bytes 12000000 | tf_op jit(solution)/shard_map/latent_grads/pallas_call | solution.py:903
  157.0 1.1 copy.55
  158.0 4.4 %all-to-all-done.3 = f32[128,1,128]{2,1,0:T(1,128)S(1)} async-done(((f32[128,1,128]{2,1,0:T(1,128)}), f32[128,1,128]{2,1,0:T(1,128)S(1)}, u32[]{:S(2)}, u32[]{:S(2)}) %all-to-all-start.3) | async-done | bytes 65568 | tf_op jit(solution)/shard_map/all_to_all | solution.py:1062
  163.0 0.8 copy.45
  163.8 0.8 copy.44
  (88 shorter events, 4.1 us)
Async XLA Ops:
  1.8 17.7 %copy-start.32 = (bf16[27,2,16]{0,2,1:T(8,128)(2,1)S(1)}, bf16[27,2,16]{0,2,1:T(8,128)(2,1)}, u32[]{:S(2)}) copy-start(bf16[27,2,16]{0,2,1:T(8,128)(2,1)} %param.15) | copy-start | bytes 5188
  1.8 18.8 %copy-start.29 = (bf16[27,16,16]{0,2,1:T(8,128)(2,1)S(1)}, bf16[27,16,16]{0,2,1:T(8,128)(2,1)}, u32[]{:S(2)}) copy-start(bf16[27,16,16]{0,2,1:T(8,128)(2,1)} %param.14) | copy-start | bytes 41476
  1.8 6.5 %collective-permute-start = (bf16[2,4,16,128]{3,2,1,0:T(8,128)(2,1)S(1)}, bf16[2,4,16,128]{3,2,1,0:T(8,128)(2,1)S(1)}, u32[]{:S(2)}, u32[]{:S(2)}) collective-permute-start(bf16[2,4,16,128]{3,2,1,0:T(8,128)(2,1)S(1)} %get-tuple-element.103), channel_id=1, source_target_pairs={{0,1},{1,2},{2,3},{3,4},{4,5},{5,6},{6,7},{7,0},{8,9},{9,10},{10,1... | collective-permute-start | bytes 98312 | tf_op jit(solution)/shard_map/ppermute | solution.py:1015
  4.9 15.9 %copy-start.23 = (s32[2,1536]{1,0:T(2,128)S(1)}, s32[2,1536]{1,0:T(2,128)}, u32[]{:S(2)}) copy-start(s32[2,1536]{1,0:T(2,128)} %constant.27.clone.codes_2_ref) | copy-start | bytes 36868
  4.9 16.0 %copy-start.25 = (s32[2,1152]{1,0:T(2,128)S(1)}, s32[2,1152]{1,0:T(2,128)}, u32[]{:S(2)}) copy-start(s32[2,1152]{1,0:T(2,128)} %constant.26.clone.codes_1_ref) | copy-start | bytes 27652
  4.9 5.4 %collective-permute-start.1 = (bf16[2,4,16,128]{3,2,1,0:T(8,128)(2,1)S(1)}, bf16[2,4,16,128]{3,2,1,0:T(8,128)(2,1)S(1)}, u32[]{:S(2)}, u32[]{:S(2)}) collective-permute-start(bf16[2,4,16,128]{3,2,1,0:T(8,128)(2,1)S(1)} %get-tuple-element.104), channel_id=1, source_target_pairs={{1,0},{2,1},{3,2},{4,3},{5,4},{6,5},{7,6},{0,7},{9,8},{10,9},{11,1... | collective-permute-start | bytes 98312 | tf_op jit(solution)/shard_map/ppermute | solution.py:1015
  10.4 11.6 %collective-permute-start.2 = (bf16[2,40,16,128]{3,2,1,0:T(8,128)(2,1)S(1)}, bf16[2,40,16,128]{3,2,1,0:T(8,128)(2,1)S(1)}, u32[]{:S(2)}, u32[]{:S(2)}) collective-permute-start(bf16[2,40,16,128]{3,2,1,0:T(8,128)(2,1)S(1)} %pad_maximum_fusion.mid_ref), channel_id=1, source_target_pairs={{0,8},{8,16},{16,24},{24,32},{32,40},{40,48},{48,56},{56,64},{64,7... | collective-permute-start | bytes 983048 | tf_op jit(solution)/shard_map/ppermute | solution.py:1015
  10.4 11.7 %collective-permute-start.3 = (bf16[2,40,16,128]{3,2,1,0:T(8,128)(2,1)S(1)}, bf16[2,40,16,128]{3,2,1,0:T(8,128)(2,1)S(1)}, u32[]{:S(2)}, u32[]{:S(2)}) collective-permute-start(bf16[2,40,16,128]{3,2,1,0:T(8,128)(2,1)S(1)} %pad_maximum_fusion.mid_ref), channel_id=1, source_target_pairs={{8,0},{16,8},{24,16},{32,24},{40,32},{48,40},{56,48},{64,56},{72,6... | collective-permute-start | bytes 983048 | tf_op jit(solution)/shard_map/ppermute | solution.py:1015
  14.3 15.5 %collective-permute-start.4 = (f32[16,24,128]{2,1,0:T(8,128)S(1)}, f32[16,24,128]{2,1,0:T(8,128)S(1)}, u32[]{:S(2)}, u32[]{:S(2)}) collective-permute-start(f32[16,24,128]{2,1,0:T(8,128)S(1)} %get-tuple-element.102), channel_id=1, source_target_pairs={{0,1},{1,2},{2,3},{3,4},{4,5},{5,6},{6,7},{7,0},{8,9},{9,10},{10,1... | collective-permute-start | bytes 589832 | tf_op jit(solution)/shard_map/ppermute | solution.py:1015
  17.1 14.6 %collective-permute-start.5 = (f32[16,24,128]{2,1,0:T(8,128)S(1)}, f32[16,24,128]{2,1,0:T(8,128)S(1)}, u32[]{:S(2)}, u32[]{:S(2)}) collective-permute-start(f32[16,24,128]{2,1,0:T(8,128)S(1)} %get-tuple-element.101), channel_id=1, source_target_pairs={{1,0},{2,1},{3,2},{4,3},{5,4},{6,5},{7,6},{0,7},{9,8},{10,9},{11,1... | collective-permute-start | bytes 589832 | tf_op jit(solution)/shard_map/ppermute | solution.py:1015
  19.7 0.6 copy-start.27
  22.0 10.8 %copy-start.8 = (bf16[2,40,16,128]{3,2,1,0:T(8,128)(2,1)}, bf16[2,40,16,128]{3,2,1,0:T(8,128)(2,1)S(1)}, u32[]{:S(2)}) copy-start(bf16[2,40,16,128]{3,2,1,0:T(8,128)(2,1)S(1)} %collective-permute-done.2.lo_ref) | copy-start | bytes 983044
  22.1 10.7 %copy-start.10 = (bf16[2,40,16,128]{3,2,1,0:T(8,128)(2,1)}, bf16[2,40,16,128]{3,2,1,0:T(8,128)(2,1)S(1)}, u32[]{:S(2)}) copy-start(bf16[2,40,16,128]{3,2,1,0:T(8,128)(2,1)S(1)} %collective-permute-done.3.hi_ref) | copy-start | bytes 983044
  29.0 0.8 copy-start.1
  29.8 3.0 %copy-start.21 = (f32[2,2,36,128]{3,2,1,0:T(8,128)}, f32[2,2,36,128]{3,2,1,0:T(8,128)S(1)}, u32[]{:S(2)}) copy-start(f32[2,2,36,128]{3,2,1,0:T(8,128)S(1)} %get-tuple-element.88.out_ref) | copy-start | bytes 221188
  29.8 3.0 %copy-start.17 = (f32[16,24,128]{2,1,0:T(8,128)}, f32[16,24,128]{2,1,0:T(8,128)S(1)}, u32[]{:S(2)}) copy-start(f32[16,24,128]{2,1,0:T(8,128)S(1)} %collective-permute-done.4.plo_ref) | copy-start | bytes 589828
  31.7 1.1 copy-start.19
  32.8 4.9 %copy-start.30 = (f32[1,3,2048]{2,0,1:T(1,128)S(1)}, f32[1,3,2048]{2,0,1:T(1,128)}, u32[]{:S(2)}) copy-start(f32[1,3,2048]{2,0,1:T(1,128)} %param.17) | copy-start | bytes 73732
  32.8 4.9 %copy-start.31 = (s32[1,3,2048]{2,0,1:T(1,128)S(1)}, s32[1,3,2048]{2,0,1:T(1,128)}, u32[]{:S(2)}) copy-start(s32[1,3,2048]{2,0,1:T(1,128)} %param.19) | copy-start | bytes 73732
  32.8 21.2 %all-to-all-start = ((f32[16,2,2,32,128]{4,3,2,1,0:T(8,128)}), f32[16,2,2,32,128]{4,3,2,1,0:T(8,128)}, u32[]{:S(2)}, u32[]{:S(2)}) async-start(f32[16,2,2,32,128]{4,3,2,1,0:T(8,128)} %broadcast_in_dim.4), calls=%async_computation | async-start | bytes 2097152 | tf_op jit(solution)/shard_map/all_to_all | solution.py:1037
  37.8 9.2 %copy-start.28 = (bf16[27,2,16]{1,2,0:T(8,128)(2,1)S(1)}, bf16[27,2,16]{1,2,0:T(8,128)(2,1)}, u32[]{:S(2)}) copy-start(bf16[27,2,16]{1,2,0:T(8,128)(2,1)} %copy-done.27) | copy-start | bytes 5188
  37.8 9.2 %copy-start.24 = (s32[2,1152]{1,0:T(2,128)S(1)}, s32[2,1152]{1,0:T(2,128)}, u32[]{:S(2)}) copy-start(s32[2,1152]{1,0:T(2,128)} %constant.29.clone.codes_4_ref) | copy-start | bytes 27652
  37.8 9.2 %copy-start.26 = (s32[2,576]{1,0:T(2,128)S(1)}, s32[2,576]{1,0:T(2,128)}, u32[]{:S(2)}) copy-start(s32[2,576]{1,0:T(2,128)} %constant.28.clone.codes_3_ref) | copy-start | bytes 13828
  46.9 21.9 %copy-start.3 = (bf16[384,256]{1,0:T(8,128)(2,1)S(1)}, bf16[384,256]{1,0:T(8,128)(2,1)}, u32[]{:S(2)}) copy-start(bf16[384,256]{1,0:T(8,128)(2,1)} %constant.30.clone.slope_ref) | copy-start | bytes 589828
  48.3 0.9 copy-start.13
  49.2 0.7 copy-start.15
  54.1 14.7 %copy-start.12 = (bf16[768,128]{1,0:T(8,128)(2,1)S(1)}, bf16[768,128]{1,0:T(8,128)(2,1)}, u32[]{:S(2)}) copy-start(bf16[768,128]{1,0:T(8,128)(2,1)} %constant.31.clone.spread_ref) | copy-start | bytes 589828
  54.1 14.7 %copy-start.18 = (f32[16,24,128]{2,1,0:T(8,128)S(1)}, f32[16,24,128]{2,1,0:T(8,128)}, u32[]{:S(2)}) copy-start(f32[16,24,128]{2,1,0:T(8,128)} %copy-done.17) | copy-start | bytes 589828
  54.1 14.7 %copy-start.20 = (f32[16,24,128]{2,1,0:T(8,128)S(1)}, f32[16,24,128]{2,1,0:T(8,128)}, u32[]{:S(2)}) copy-start(f32[16,24,128]{2,1,0:T(8,128)} %copy-done.19) | copy-start | bytes 589828
  55.6 10.2 %collective-permute-start.6 = (bf16[16,2,24,128]{3,2,1,0:T(8,128)(2,1)S(1)}, bf16[16,2,24,128]{3,2,1,0:T(8,128)(2,1)S(1)}, u32[]{:S(2)}, u32[]{:S(2)}) collective-permute-start(bf16[16,2,24,128]{3,2,1,0:T(8,128)(2,1)S(1)} %get-tuple-element.57), channel_id=1, source_target_pairs={{0,1},{1,2},{2,3},{3,4},{4,5},{5,6},{6,7},{7,0},{8,9},{9,10},{10,1... | collective-permute-start | bytes 589832 | tf_op jit(solution)/shard_map/ppermute | solution.py:1015
  58.5 10.3 %collective-permute-start.7 = (bf16[16,2,24,128]{3,2,1,0:T(8,128)(2,1)S(1)}, bf16[16,2,24,128]{3,2,1,0:T(8,128)(2,1)S(1)}, u32[]{:S(2)}, u32[]{:S(2)}) collective-permute-start(bf16[16,2,24,128]{3,2,1,0:T(8,128)(2,1)S(1)} %get-tuple-element.58), channel_id=1, source_target_pairs={{1,0},{2,1},{3,2},{4,3},{5,4},{6,5},{7,6},{0,7},{9,8},{10,9},{11,1... | collective-permute-start | bytes 589832 | tf_op jit(solution)/shard_map/ppermute | solution.py:1015
  78.1 8.3 %collective-permute-start.8 = (bf16[16,32,128]{2,1,0:T(8,128)(2,1)S(1)}, bf16[16,32,128]{2,1,0:T(8,128)(2,1)S(1)}, u32[]{:S(2)}, u32[]{:S(2)}) collective-permute-start(bf16[16,32,128]{2,1,0:T(8,128)(2,1)S(1)} %get-tuple-element.65), channel_id=1, source_target_pairs={{0,1},{1,2},{2,3},{3,4},{4,5},{5,6},{6,7},{7,0},{8,9},{9,10},{10,1... | collective-permute-start | bytes 393224 | tf_op jit(solution)/shard_map/ppermute | solution.py:1015
  81.0 6.7 %collective-permute-start.9 = (bf16[16,32,128]{2,1,0:T(8,128)(2,1)S(1)}, bf16[16,32,128]{2,1,0:T(8,128)(2,1)S(1)}, u32[]{:S(2)}, u32[]{:S(2)}) collective-permute-start(bf16[16,32,128]{2,1,0:T(8,128)(2,1)S(1)} %get-tuple-element.66), channel_id=1, source_target_pairs={{1,0},{2,1},{3,2},{4,3},{5,4},{6,5},{7,6},{0,7},{9,8},{10,9},{11,1... | collective-permute-start | bytes 393224 | tf_op jit(solution)/shard_map/ppermute | solution.py:1015
  96.2 1.0 copy-start
  97.2 3.9 %copy-start.2 = (bf16[38,64,128]{2,1,0:T(8,128)(2,1)S(1)}, bf16[38,64,128]{2,1,0:T(8,128)(2,1)}, u32[]{:S(2)}) copy-start(bf16[38,64,128]{2,1,0:T(8,128)(2,1)} %copy-done.1) | copy-start | bytes 1867780
  97.2 3.9 %copy-start.9 = (bf16[2,40,16,128]{3,2,1,0:T(8,128)(2,1)S(1)}, bf16[2,40,16,128]{3,2,1,0:T(8,128)(2,1)}, u32[]{:S(2)}) copy-start(bf16[2,40,16,128]{3,2,1,0:T(8,128)(2,1)} %copy-done.8) | copy-start | bytes 983044
  97.2 3.9 %copy-start.11 = (bf16[2,40,16,128]{3,2,1,0:T(8,128)(2,1)S(1)}, bf16[2,40,16,128]{3,2,1,0:T(8,128)(2,1)}, u32[]{:S(2)}) copy-start(bf16[2,40,16,128]{3,2,1,0:T(8,128)(2,1)} %copy-done.10) | copy-start | bytes 983044
  97.2 21.8 %all-to-all-start.1 = ((f32[32,72,128]{2,1,0:T(8,128)}), f32[32,72,128]{2,1,0:T(8,128)S(1)}, u32[]{:S(2)}, u32[]{:S(2)}) async-start(f32[32,72,128]{2,1,0:T(8,128)} %copy-done), calls=%async_computation.1 | async-start | bytes 2359296 | tf_op jit(solution)/shard_map/all_to_all | solution.py:1048
  101.0 18.0 %copy-start.22 = (f32[2,2,36,128]{3,2,1,0:T(8,128)S(1)}, f32[2,2,36,128]{3,2,1,0:T(8,128)}, u32[]{:S(2)}) copy-start(f32[2,2,36,128]{3,2,1,0:T(8,128)} %copy-done.21) | copy-start | bytes 221188
  103.5 1.2 copy-start.4
  104.7 1.2 copy-start.6
  119.0 8.4 %copy-start.14 = (bf16[512,576]{1,0:T(8,128)(2,1)S(1)}, bf16[512,576]{1,0:T(8,128)(2,1)}, u32[]{:S(2)}) copy-start(bf16[512,576]{1,0:T(8,128)(2,1)} %copy-done.13) | copy-start | bytes 1769476
  119.6 7.7 %copy-start.5 = (bf16[34,192,128]{2,1,0:T(8,128)(2,1)S(1)}, bf16[34,192,128]{2,1,0:T(8,128)(2,1)}, u32[]{:S(2)}) copy-start(bf16[34,192,128]{2,1,0:T(8,128)(2,1)} %copy-done.4) | copy-start | bytes 5013508
  119.6 7.7 %collective-permute-start.10 = (bf16[2,2,36,128]{3,2,1,0:T(8,128)(2,1)S(1)}, bf16[2,2,36,128]{3,2,1,0:T(8,128)(2,1)S(1)}, u32[]{:S(2)}, u32[]{:S(2)}) collective-permute-start(bf16[2,2,36,128]{3,2,1,0:T(8,128)(2,1)S(1)} %chain.1.gmid_ref), channel_id=1, source_target_pairs={{0,8},{8,16},{16,24},{24,32},{32,40},{40,48},{48,56},{56,64},{64,7... | collective-permute-start | bytes 110600 | tf_op jit(solution)/shard_map/ppermute | solution.py:1015
  119.7 7.6 %collective-permute-start.11 = (bf16[2,2,36,128]{3,2,1,0:T(8,128)(2,1)S(1)}, bf16[2,2,36,128]{3,2,1,0:T(8,128)(2,1)S(1)}, u32[]{:S(2)}, u32[]{:S(2)}) collective-permute-start(bf16[2,2,36,128]{3,2,1,0:T(8,128)(2,1)S(1)} %chain.1.gmid_ref), channel_id=1, source_target_pairs={{8,0},{16,8},{24,16},{32,24},{40,32},{48,40},{56,48},{64,56},{72,6... | collective-permute-start | bytes 110600 | tf_op jit(solution)/shard_map/ppermute | solution.py:1015
  123.5 1.4 copy-start.7
  127.3 26.3 %copy-start.16 = (bf16[128,1152]{1,0:T(8,128)(2,1)S(1)}, bf16[128,1152]{1,0:T(8,128)(2,1)}, u32[]{:S(2)}) copy-start(bf16[128,1152]{1,0:T(8,128)(2,1)} %copy-done.15) | copy-start | bytes 884740
  148.4 14.0 %all-to-all-start.3 = ((f32[128,1,128]{2,1,0:T(1,128)}), f32[128,1,128]{2,1,0:T(1,128)S(1)}, u32[]{:S(2)}, u32[]{:S(2)}) async-start(f32[128,1,128]{2,1,0:T(1,128)} %broadcast_in_dim.5), calls=%async_computation.3 | async-start | bytes 131072 | tf_op jit(solution)/shard_map/all_to_all | solution.py:1062

commit v6 on v5

--- a/solution.py
+++ b/solution.py
@@ -232,6 +232,16 @@
     return both[:, :nz], both[:, nz:]
 
 
+def divergence_z(here, before, spread_ref):
+    high_h, low_h = halves(here)
+    high_b, low_b = halves(before)
+    return jnp.dot(
+        jnp.concatenate([high_h, low_h, high_h, high_b, low_b, high_b], axis=1),
+        spread_ref[...],
+        preferred_element_type=F32,
+    )
+
+
 def rows_of(ref, y, count, first, rows):
     return ref[pl.ds(y, count), pl.ds(first, rows), :].reshape(count * rows, nz)
 
@@ -333,12 +343,10 @@
         here, before = slopes_z(rows_of(field, y + 4, group, lead + first, rows), slope_ref)
         if also is not None:
             also(y, here, before)
-        high_h, low_h = halves(rows_of(wz, y, group, first, rows) * here)
-        high_b, low_b = halves(rows_of(wzl, y, group, first, rows) * before)
-        total = jnp.dot(
-            jnp.concatenate([high_h, low_h, high_h, high_b, low_b, high_b], axis=1),
-            spread_ref[...],
-            preferred_element_type=F32,
+        total = divergence_z(
+            rows_of(wz, y, group, first, rows) * here,
+            rows_of(wzl, y, group, first, rows) * before,
+            spread_ref,
         )
         out[pl.ds(y, group), pl.ds(0, rows), :] = total.reshape(group, rows, nz)
         return carry
@@ -393,17 +401,63 @@
 ]
 
 
+def source_slopes_kernel(
+    at_ref, src_ref, plo_ref, phi_ref, slope_ref, p1_ref, sx_ref, sy_ref, sh_ref, sb_ref, f1
+):
+    clear_sides(f1)
+    low, high = halo_scale(at_ref)
+
+    def load(y, carry):
+        f1[y + 4, pl.ds(lead, rim), :] = low * plo_ref[y]
+        f1[y + 4, pl.ds(lead + rim, bx), :] = src_ref[y]
+        f1[y + 4, pl.ds(lead + rim + bx, rim), :] = high * phi_ref[y]
+        p1_ref[y] = f1[y + 4, pl.ds(lead + 8, 64), :]
+        return carry
+
+    lax.fori_loop(0, ay, load, 0)
+
+    def body(y, carry):
+        sx_ref[y], sy_ref[y] = slopes_xy(f1, y, 8, 64)
+        return carry
+
+    lax.fori_loop(0, ay, body, 0, unroll=2)
+    sy_ref[ay] = slope_y(f1, ay, 8, 64)
+
+    def third(part, carry):
+        y = part * group
+        here, before = slopes_z(rows_of(f1, y + 4, group, lead + 8, 64), slope_ref)
+        sh_ref[pl.ds(y, group)] = here.reshape(group, 64, nz)
+        sb_ref[pl.ds(y, group)] = before.reshape(group, 64, nz)
+        return carry
+
+    lax.fori_loop(0, ay // group, third, 0)
+
+
+def source_slopes(at, source, plo, phi):
+    shapes = [(ay, 64, nz), (ay, 72, nz), (ay + 1, 64, nz), (ay, 64, nz), (ay, 64, nz)]
+    return pl.pallas_call(
+        source_slopes_kernel,
+        out_shape=tuple(jax.ShapeDtypeStruct(shape, F32) for shape in shapes),
+        in_specs=[scalars] + whole(4),
+        out_specs=tuple(whole(5)),
+        scratch_shapes=[padded],
+        compiler_params=vmem,
+        cost_estimate=cost(3),
+        name="source_slopes",
+    )(at, source, plo, phi, slope_matrix)
+
+
 def forward_kernel(
-    at_ref, win_ref, clo_ref, chi_ref, src_ref, plo_ref, phi_ref, slope_ref, spread_ref,
-    p1_ref, p2_ref, p3_ref, p4_ref, image_ref, ahead_ref, behind_ref, modulus, wx, wy, wz, wzl,
-    buoy, f1, f2, f3, fx, fy, az, message,
+    at_ref, win_ref, clo_ref, chi_ref, p1_ref, sx_ref, sy_ref, sh_ref, sb_ref, slope_ref, spread_ref,
+    p2_ref, p3_ref, p4_ref, image_ref, ahead_ref, behind_ref, modulus, wx, wy, wz, wzl,
+    buoy, f2, f3, fx, fy, az, message,
 ):
     last = lane_index() == nz - 1
     weights = (wx, wy, wz, wzl)
     fluxes = (fx, fy, az)
     matrices = (slope_ref, spread_ref)
     clear_rims(fy)
-    for field in (buoy, f1, f2, f3):
+    for field in (buoy, f2, f3):
         clear_sides(field)
     low, high = halo_scale(at_ref)
     half = 0.5 * tap_square
@@ -417,9 +471,6 @@
             received = high * chi_ref[y, channel].astype(F32)
             ref[row, pl.ds(skip + rim + bx, 4), :] = received[:4] + received[4:8]
             ref[row, pl.ds(skip + rim + bx + 4, 16), :] = received[8:]
-        f1[y + 4, pl.ds(lead, rim), :] = low * plo_ref[y]
-        f1[y + 4, pl.ds(lead + rim, bx), :] = src_ref[y]
-        f1[y + 4, pl.ds(lead + rim + bx, rim), :] = high * phi_ref[y]
         return carry
 
     lax.fori_loop(0, ay, load, 0)
@@ -439,20 +490,19 @@
 
     def first_step(y, image):
         f2[y + 4, pl.ds(lead + 8, 64), :] = (
-            2.0 * f1[y + 4, pl.ds(lead + 8, 64), :] + modulus[y, pl.ds(8, 64), :] * image
+            2.0 * p1_ref[y] + modulus[y, pl.ds(8, 64), :] * image
         )
         image_ref[0, y] = image[8:56]
 
     def second_step(y, image):
         value = (
             2.0 * f2[y + 4, pl.ds(lead + 12, 56), :]
-            - f1[y + 4, pl.ds(lead + 12, 56), :]
+            - p1_ref[y, pl.ds(4, 56), :]
             + modulus[y, pl.ds(12, 56), :] * image
         )
         f3[y + 4, pl.ds(lead + 12, 56), :] = value
         image_ref[1, y] = image[4:52]
         p3_ref[y] = value[4:52]
-        p1_ref[y] = f1[y + 4, pl.ds(lead + 8, 64), :]
         p2_ref[y] = f2[y + 4, pl.ds(lead + 8, 64), :]
 
     def third_step(y, image):
@@ -478,8 +528,27 @@
         pack(y, behind_ref, 0, 7, 8)
         return carry
 
+    def first_third(part, carry):
+        y = part * group
+        total = divergence_z(
+            rows_of(wz, y, group, 8, 64) * rows_of(sh_ref, y, group, 0, 64),
+            rows_of(wzl, y, group, 8, 64) * rows_of(sb_ref, y, group, 0, 64),
+            spread_ref,
+        )
+        az[pl.ds(y, group), pl.ds(0, 64), :] = total.reshape(group, 64, nz)
+        return carry
+
+    lax.fori_loop(0, ay // group, first_third, 0, unroll=2)
+
+    def first_flux(y, carry):
+        fx[y] = wx[y, pl.ds(lead + 4, 72), :] * sx_ref[y]
+        fy[y + 3] = wy[y, pl.ds(8, 64), :] * sy_ref[y]
+        return carry
+
+    lax.fori_loop(0, ay, first_flux, 0, unroll=2)
+    fy[ay + 3] = wy[ay, pl.ds(8, 64), :] * sy_ref[ay]
+    divergence_pass(fluxes, 64, first_step)
     for field, first, rows, consume in (
-        (f1, 8, 64, first_step),
         (f2, 12, 56, second_step),
         (f3, 16, 48, third_step),
     ):
@@ -489,20 +558,20 @@
     lax.fori_loop(0, ay, send, 0)
 
 
-def forward_waves(at, window, clo, chi, source, plo, phi):
-    shapes = [(ay, 64, nz), (ay, 64, nz), (ay, 48, nz), (ay, bx, nz), (3, ay, 48, nz)]
+def forward_waves(at, window, clo, chi, first_slopes):
+    shapes = [(ay, 64, nz), (ay, 48, nz), (ay, bx, nz), (3, ay, 48, nz)]
     return pl.pallas_call(
         forward_kernel,
         out_shape=tuple(jax.ShapeDtypeStruct(shape, F32) for shape in shapes)
         + (jax.ShapeDtypeStruct((ay, 32, nz), BF16),) * 2
         + (jax.ShapeDtypeStruct((ay, dom, nz), F32),)
         + tuple(jax.ShapeDtypeStruct(shape, F32) for shape in weight_sizes),
-        in_specs=[scalars] + whole(8),
-        out_specs=tuple(whole(12)),
-        scratch_shapes=[padded, padded, padded, padded, *flux_shapes, pltpu.VMEM((32, nz), F32)],
+        in_specs=[scalars] + whole(10),
+        out_specs=tuple(whole(11)),
+        scratch_shapes=[padded, padded, padded, *flux_shapes, pltpu.VMEM((32, nz), F32)],
         compiler_params=vmem,
         name="forward_waves",
-    )(at, window, clo, chi, source, plo, phi, slope_matrix, spread_matrix)
+    )(at, window, clo, chi, *first_slopes, slope_matrix, spread_matrix)
 
 
 def slopes_kernel(p1_ref, p2_ref, p3_ref, slope_ref, sx_ref, sy_ref, sh_ref, sb_ref, field):
@@ -1038,16 +1107,17 @@
     column, seen, w3, w4 = lax.optimization_barrier((column, seen, w3, w4))
     window, ahead, behind = take_window(at, column.reshape(2 * shots, 2, bx, nz))
     clo, chi = both_ways(ahead, behind, "brick")
-    p1, p2, p3, p4, images, ahead, behind, modulus, *weights = forward_waves(
-        at, window, clo, chi, source, plo, phi
+    s1, s2 = spread_fields(at, lo, mid, hi, hidden)
+    first_slopes = source_slopes(at, source, plo, phi)
+    clo, chi, s1, s2, first_slopes = lax.optimization_barrier((clo, chi, s1, s2, first_slopes))
+    p2, p3, p4, images, ahead, behind, modulus, *weights = forward_waves(
+        at, window, clo, chi, first_slopes
     )
     back, front = both_ways(ahead, behind, "brick")
-    slopes = wave_slopes(p1, p2, p3)
+    slopes = wave_slopes(first_slopes[0], p2, p3)
     back, front, slopes = lax.optimization_barrier((back, front, slopes))
     grads = adjoint_waves(at, (p2, p3, p4), images, back, front, seen, modulus, weights, slopes)
     got = lax.all_to_all(grads, "shot", 0, 0, tiled=True)
-    s1, s2 = spread_fields(at, lo, mid, hi, hidden)
-    got, s1, s2 = lax.optimization_barrier((got, s1, s2))
     got = got.reshape(shots, 2, 2 * gx, nz)
     grad_output = chain(at, got, output)
     glo, ghi = both_ways(grad_output, grad_output, "shot")

time: 167 us -> 164 us (0.982)
  blocking collectives: 15.1 us -> 35.7 us
  waiting for transfers between devices: 36.6 us -> 24.2 us
  starting transfers between devices: 39.4 us -> 29.3 us
  local copies, waits for them, and re-layouts: 16.1 us -> 13.8 us
    all_to_all x0 -> x1, blocking collectives: none -> 20.9 us  [per_device(): got = lax.all_to_all(grads, 'shot', 0, 0, tiled=True)]
    all_to_all x1 -> x0, waiting for transfers between devices: 13.1 us -> none  [per_device(): got = lax.all_to_all(grads, 'shot', 0, 0, tiled=True)]
    ppermute x6, starting transfers between devices: 14 us -> 8.35 us  [both_ways(): lax.ppermute(behind, axis, backward_)]
    all_to_all x1 -> x0, starting transfers between devices: 3.83 us -> none  [per_device(): got = lax.all_to_all(grads, 'shot', 0, 0, tiled=True)]
    unnamed x76 -> x66, local copies, waits for them, and re-layouts: 12.7 us -> 10.3 us
    pallas_call x0 -> x1, Pallas kernels: none -> 2.07 us  [source_slopes(): pl.pallas_call(source_slopes_kernel, out_shape=tuple((jax.ShapeDtypeStruc...]
    ppermute x6, waiting for transfers between devices: 6.69 us -> 8.59 us  [both_ways(): lax.ppermute(ahead, axis, forward)]
  transfers between devices with their start and end apart: 15 -> 14, of which waited for: 10 -> 10; matrix products, arithmetic and copies ran while one was open for 2% -> 2% of each run, Pallas kernels for 18% -> 20%
where the time goes in v6:
time: 164 us; the launch traced here: 161 us
  Pallas kernels  56.4 us (34%)
  blocking collectives  35.7 us (22%)
  starting transfers between devices  29.3 us (18%)
  waiting for transfers between devices  24.2 us (15%)
  local copies, waits for them, and re-layouts  13.8 us (8%)
  between operations  1.74 us (1%)
    all_to_all x1, blocking collectives, per_device(): got = lax.all_to_all(grads, 'shot', 0, 0, tiled=True)  20.9 us
    all_to_all x1, blocking collectives, per_device(): slices = lax.all_to_all(kernels, everyone, 0, 0, tiled=True)  14.8 us
    ppermute x6, starting transfers between devices, both_ways(): lax.ppermute(ahead, axis, forward)  11.4 us
    unnamed x66, local copies, waits for them, and re-layouts  10.3 us
    pallas_call x1, Pallas kernels, receiver_fields(): pl.pallas_call(receiver_kernel, out_shape=jax.ShapeDtypeStruct((4, ay * d...  9.12 us
    ppermute x6, waiting for transfers between devices, both_ways(): lax.ppermute(ahead, axis, forward)  8.59 us
    pallas_call x1, Pallas kernels, adjoint_waves(): pl.pallas_call(adjoint_kernel, out_shape=jax.ShapeDtypeStruct((2 * shots,...  8.48 us
    ppermute x6, starting transfers between devices, both_ways(): lax.ppermute(behind, axis, backward_)  8.35 us
  transfers between devices with their start and end apart: 14, of which 10 were waited for; matrix products, arithmetic and copies ran while one was open for 2% of the time, Pallas kernels for 20%

profile of v6, /device:TPU:32, one launch (start us, length us, event | category | flops | bytes accessed | tf_op | source)
XLA Modules:
  0.0 161.3 jit_solution(17482253179235282004)
XLA Ops:
  0.6 1.1 copy.57
  1.8 3.1 %collective-permute-start = (bf16[2,4,16,128]{3,2,1,0:T(8,128)(2,1)S(1)}, bf16[2,4,16,128]{3,2,1,0:T(8,128)(2,1)S(1)}, u32[]{:S(2)}, u32[]{:S(2)}) collective-permute-start(bf16[2,4,16,128]{3,2,1,0:T(8,128)(2,1)S(1)} %get-tuple-element.123), channel_id=1, source_target_pairs={{0,1},{1,2},{2,3},{3,4},{4,5},{5,6},{6,7},{7,0},{8,9},{9,10},{10,1... | collective-permute-start | bytes 98312 | tf_op jit(solution)/shard_map/ppermute | solution.py:1084
  4.9 1.4 collective-permute-start.1
  6.3 1.0 copy.56
  7.3 0.9 collective-permute-done
  8.3 2.0 %collective-permute-done.1 = bf16[2,4,16,128]{3,2,1,0:T(8,128)(2,1)S(1)} collective-permute-done((bf16[2,4,16,128]{3,2,1,0:T(8,128)(2,1)S(1)}, bf16[2,4,16,128]{3,2,1,0:T(8,128)(2,1)S(1)}, u32[]{:S(2)}, u32[]{:S(2)}) %collective-permute-start.1) | collective-permute-done | bytes 32800 | tf_op jit(solution)/shard_map/ppermute | solution.py:1084
  10.4 1.4 collective-permute-start.3
  11.8 3.6 %collective-permute-start.5 = (f32[16,24,128]{2,1,0:T(8,128)S(1)}, f32[16,24,128]{2,1,0:T(8,128)S(1)}, u32[]{:S(2)}, u32[]{:S(2)}) collective-permute-start(f32[16,24,128]{2,1,0:T(8,128)S(1)} %get-tuple-element.121), channel_id=1, source_target_pairs={{1,0},{2,1},{3,2},{4,3},{5,4},{6,5},{7,6},{0,7},{9,8},{10,9},{11,1... | collective-permute-start | bytes 589832 | tf_op jit(solution)/shard_map/ppermute | solution.py:1084
  16.8 0.6 copy-done.22
  18.0 1.0 forward_bands.1
  19.1 0.8 collective-permute-done.3.hi_ref
  19.9 4.0 %collective-permute-done.2.lo_ref = bf16[2,40,16,128]{3,2,1,0:T(8,128)(2,1)S(1)} collective-permute-done((bf16[2,40,16,128]{3,2,1,0:T(8,128)(2,1)S(1)}, bf16[2,40,16,128]{3,2,1,0:T(8,128)(2,1)S(1)}, u32[]{:S(2)}, u32[]{:S(2)}) %collective-permute-start.2) | collective-permute-done | bytes 327712 | tf_op jit(solution)/shard_map/ppermute | solution.py:1084
  23.9 6.9 %generator.1 = (f32[2,2,32,128]{3,2,1,0:T(8,128)S(1)}, f32[2,2,36,128]{3,2,1,0:T(8,128)S(1)}, bf16[38,64,128]{2,1,0:T(8,128)(2,1)S(1)}) custom-call(s32[3]{0:T(128)S(1)} %pad_add_fusion.at_ref, bf16[2,40,16,128]{3,2,1,0:T(8,128)(2,1)S(1)} %collective-permute-done.2.lo_ref, bf16[2,40,16,128]{3,2,1,0:T(8,128)(2,1)S(1)} %pad_maximum_fusion.mid_ref, ...), custom_call_target="tpu_custom_call" | custom-call | tf_op jit(solution)/shard_map/generator/pallas_call | solution.py:111
  30.9 0.8 copy-done.1
  31.7 0.6 copy-done.16
  32.3 1.1 broadcast_in_dim.4
  33.5 4.3 %all-to-all-start = ((f32[16,2,2,32,128]{4,3,2,1,0:T(8,128)}), f32[16,2,2,32,128]{4,3,2,1,0:T(8,128)}, u32[]{:S(2)}, u32[]{:S(2)}) async-start(f32[16,2,2,32,128]{4,3,2,1,0:T(8,128)} %broadcast_in_dim.4), calls=%async_computation | async-start | bytes 2097152 | tf_op jit(solution)/shard_map/all_to_all | solution.py:1106
  38.2 9.1 %receiver_fields.1.seen_ref = f32[4,1280,128]{2,1,0:T(8,128)S(1)} custom-call(s32[3]{0:T(128)S(1)} %pad_add_fusion.at_ref, s32[3,2048]{1,0:T(4,128)S(1)} %bitcast.42, f32[3,2048]{1,0:T(4,128)S(1)} %bitcast.41), custom_call_target="tpu_custom_call" | custom-call | bytes 27000000 | tf_op jit(solution)/shard_map/receiver_fields/pallas_call | solution.py:175
  47.4 1.3 backward_bands.1
  48.7 0.8 copy-done.8
  49.6 0.7 copy-done.10
  50.3 4.1 %all-to-all-done = f32[16,2,2,32,128]{4,3,2,1,0:T(8,128)} async-done(((f32[16,2,2,32,128]{4,3,2,1,0:T(8,128)}), f32[16,2,2,32,128]{4,3,2,1,0:T(8,128)}, u32[]{:S(2)}, u32[]{:S(2)}) %all-to-all-start) | async-done | bytes 1048608 | tf_op jit(solution)/shard_map/all_to_all | solution.py:1106
  54.4 1.6 take_window.1
  56.0 4.0 %collective-permute-start.6 = (bf16[16,2,24,128]{3,2,1,0:T(8,128)(2,1)S(1)}, bf16[16,2,24,128]{3,2,1,0:T(8,128)(2,1)S(1)}, u32[]{:S(2)}, u32[]{:S(2)}) collective-permute-start(bf16[16,2,24,128]{3,2,1,0:T(8,128)(2,1)S(1)} %get-tuple-element.67), channel_id=1, source_target_pairs={{0,1},{1,2},{2,3},{3,4},{4,5},{5,6},{6,7},{7,0},{8,9},{9,10},{10,1... | collective-permute-start | bytes 589832 | tf_op jit(solution)/shard_map/ppermute | solution.py:1084
  60.5 0.9 copy-done.13
  61.4 0.9 copy-done.15
  62.4 2.1 %source_slopes.1 = (f32[16,64,128]{2,1,0:T(8,128)S(1)}, f32[16,72,128]{2,1,0:T(8,128)S(1)}, f32[17,64,128]{2,1,0:T(8,128)S(1)}, f32[16,64,128]{2,1,0:T(8,128)S(1)}, f32[16,64,128]{2,1,0:T(8,128)S(1)}) custom-call(s32[3]{0:T(128)S(1)} %pad_add_fusion.at_ref, f32[16,32,128]{2,1,0:T(8,128)S(1)} %bitcast.38, f32[16,24,128]{2,1,0:T(8,128)S(1)} %copy-done.15, ...), custom_call_target="tpu_custom_call" | custom-call | bytes 9000000 | tf_op jit(solution)/shard_map/source_slopes/pallas_call | solution.py:438
  64.5 2.4 %spread_fields.1 = (bf16[34,192,128]{2,1,0:T(8,128)(2,1)S(1)}, bf16[34,192,128]{2,1,0:T(8,128)(2,1)S(1)}) custom-call(s32[3]{0:T(128)S(1)} %pad_add_fusion.at_ref, bf16[2,40,16,128]{3,2,1,0:T(8,128)(2,1)S(1)} %copy-done.6, bf16[2,40,16,128]{3,2,1,0:T(8,128)(2,1)S(1)} %pad_maximum_fusion.mid_ref, bf16[2,40,16,128]{3,2,1,0:T(8,128)(2,1)S(1)} %copy-done.4, ...), custom_call_target="tpu_custom_call" | custom-call | bytes 9000000 | tf_op jit(solution)/shard_map/spread_fields/pallas_call | solution.py:827
  66.9 2.6 %collective-permute-done.7.chi_ref = bf16[16,2,24,128]{3,2,1,0:T(8,128)(2,1)S(1)} collective-permute-done((bf16[16,2,24,128]{3,2,1,0:T(8,128)(2,1)S(1)}, bf16[16,2,24,128]{3,2,1,0:T(8,128)(2,1)S(1)}, u32[]{:S(2)}, u32[]{:S(2)}) %collective-permute-start.7) | collective-permute-done | bytes 196640 | tf_op jit(solution)/shard_map/ppermute | solution.py:1084
  69.5 8.1 %forward_waves.1 = (f32[16,64,128]{2,1,0:T(8,128)S(1)}, f32[16,48,128]{2,1,0:T(8,128)S(1)}, f32[16,32,128]{2,1,0:T(8,128)S(1)}, f32[3,16,48,128]{3,2,1,0:T(8,128...) custom-call(s32[3]{0:T(128)S(1)} %pad_add_fusion.at_ref, ...), custom_call_target="tpu_custom_call" | custom-call | tf_op jit(solution)/shard_map/forward_waves/pallas_call | solution.py:563
  77.6 3.7 %collective-permute-start.8 = (bf16[16,32,128]{2,1,0:T(8,128)(2,1)S(1)}, bf16[16,32,128]{2,1,0:T(8,128)(2,1)S(1)}, u32[]{:S(2)}, u32[]{:S(2)}) collective-permute-start(bf16[16,32,128]{2,1,0:T(8,128)(2,1)S(1)} %get-tuple-element.90), channel_id=1, source_target_pairs={{0,1},{1,2},{2,3},{3,4},{4,5},{5,6},{6,7},{7,0},{8,9},{9,10},{10,1... | collective-permute-start | bytes 393224 | tf_op jit(solution)/shard_map/ppermute | solution.py:1084
  81.4 0.8 collective-permute-start.9
  82.1 3.8 %wave_slopes.1 = (f32[3,16,48,128]{3,2,1,0:T(8,128)S(1)}, f32[3,17,48,128]{3,2,1,0:T(8,128)S(1)}, f32[3,16,48,128]{3,2,1,0:T(8,128)S(1)}, f32[3,16,48,128]{3,2,1,0:T(8,128)S(1)}) custom-call(f32[16,64,128]{2,1,0:T(8,128)S(1)} %get-tuple-element.81.p1_ref, f32[16,64,128]{2,1,0:T(8,128)S(1)} %get-tuple-element.86.p2_ref, ...), custom_call_target="tpu_custom_call" | custom-call | bytes 18000000 | tf_op jit(solution)/shard_map/wave_slopes/pallas_call | solution.py:609
  86.4 1.6 %collective-permute-done.9.front_ref = bf16[16,32,128]{2,1,0:T(8,128)(2,1)S(1)} collective-permute-done((bf16[16,32,128]{2,1,0:T(8,128)(2,1)S(1)}, bf16[16,32,128]{2,1,0:T(8,128)(2,1)S(1)}, u32[]{:S(2)}, u32[]{:S(2)}) %collective-permute-start.9) | collective-permute-done | bytes 131104 | tf_op jit(solution)/shard_map/ppermute | solution.py:1084
  88.0 8.5 %adjoint_waves.1 = f32[32,72,128]{2,1,0:T(8,128)S(1)} custom-call(s32[3]{0:T(128)S(1)} %pad_add_fusion.at_ref, f32[16,64,128]{2,1,0:T(8,128)S(1)} %get-tuple-element.86.p2_ref, f32[16,48,128]{2,1,0:T(8,128)S(1)} %get-tuple-element.87.p3_ref, f32[16,32,128]{2,1,0:T(8,128)S(1)} %get-tuple-element.88.p4_ref, ...), custom_call_target="tpu_custom_call" | custom-call | tf_op jit(solution)/shard_map/adjoint_waves/pallas_call | solution.py:758
  96.5 20.9 %all_to_all.25 = f32[32,72,128]{2,1,0:T(8,128)S(1)} all-to-all(f32[32,72,128]{2,1,0:T(8,128)S(1)} %adjoint_waves.1), channel_id=1, replica_groups=mesh['shot'=16,'brick'=8] {'shot'}, dimensions={0} | all-to-all | bytes 2359296 | tf_op jit(solution)/shard_map/all_to_all | solution.py:1120
  118.0 0.7 collective-permute-start.11
  118.8 2.3 %second_grads.1.second_ref = f32[8,576]{1,0:T(8,128)S(1)} custom-call(bf16[2,2,36,128]{3,2,1,0:T(8,128)(2,1)S(1)} %chain.1.gmid_ref, bf16[34,192,128]{2,1,0:T(8,128)(2,1)S(1)} %get-tuple-element.109.s2), custom_call_target="tpu_custom_call" | custom-call | bytes 9000000 | tf_op jit(solution)/shard_map/second_grads/pallas_call | solution.py:856
  121.1 3.2 %collective-permute-done.10.glo_ref = bf16[2,2,36,128]{3,2,1,0:T(8,128)(2,1)S(1)} collective-permute-done((bf16[2,2,36,128]{3,2,1,0:T(8,128)(2,1)S(1)}, bf16[2,2,36,128]{3,2,1,0:T(8,128)(2,1)S(1)}, u32[]{:S(2)}, u32[]{:S(2)}) %collective-permute-start.10) | collective-permute-done | bytes 36896 | tf_op jit(solution)/shard_map/ppermute | solution.py:1084
  124.3 5.2 %first_grads.1 = (bf16[40,64,128]{2,1,0:T(8,128)(2,1)S(1)}, f32[128,128]{1,0:T(8,128)S(1)}) custom-call(s32[3]{0:T(128)S(1)} %pad_add_fusion.at_ref, bf16[2,2,36,128]{3,2,1,0:T(8,128)(2,1)S(1)} %collective-permute-done.10.glo_ref, bf16[2,2,36,128]{3,2,1,0:T(8,128)(2,1)S(1)} %chain.1.gmid_ref, bf16[2,2,36,128]{3,2,1,0:T(8,128)(2,1)S(1)} %collective-permute-done.11.ghi_ref, ...), custom_call_target="tpu_custom_call" | custom-call | tf_op jit(solution)/shard_map/first_grads/pallas_call | solution.py:934
  129.5 14.8 %all_to_all.26 = f32[128,1,128]{2,1,0:T(1,128)S(1)} all-to-all(f32[128,1,128]{2,1,0:T(1,128)S(1)} %bitcast.43), channel_id=1, replica_groups=mesh['shot'=16,'brick'=8] {'shot','brick'}, dimensions={0} | all-to-all | bytes 131072 | tf_op jit(solution)/shard_map/all_to_all | solution.py:1130
  144.5 0.7 broadcast_in_dim.5
  145.1 5.2 %all-to-all-start.3 = ((f32[128,1,128]{2,1,0:T(1,128)}), f32[128,1,128]{2,1,0:T(1,128)S(1)}, u32[]{:S(2)}, u32[]{:S(2)}) async-start(f32[128,1,128]{2,1,0:T(1,128)} %broadcast_in_dim.5), calls=%async_computation.3 | async-start | bytes 131072 | tf_op jit(solution)/shard_map/all_to_all | solution.py:1132
  150.3 3.4 %latent_grads.1 = f32[32,32,128]{2,1,0:T(8,128)S(1)} custom-call(bf16[40,64,128]{2,1,0:T(8,128)(2,1)S(1)} %get-tuple-element.112.inner_ref, bf16[128,1152]{1,0:T(8,128)(2,1)S(1)} %copy-done.11), custom_call_target="tpu_custom_call" | custom-call | bytes 12000000 | tf_op jit(solution)/shard_map/latent_grads/pallas_call | solution.py:972
  153.7 1.1 copy.55
  154.7 4.4 %all-to-all-done.3 = f32[128,1,128]{2,1,0:T(1,128)S(1)} async-done(((f32[128,1,128]{2,1,0:T(1,128)}), f32[128,1,128]{2,1,0:T(1,128)S(1)}, u32[]{:S(2)}, u32[]{:S(2)}) %all-to-all-start.3) | async-done | bytes 65568 | tf_op jit(solution)/shard_map/all_to_all | solution.py:1132
  159.7 0.8 copy.44
  160.5 0.8 copy.45
  (78 shorter events, 3.9 us)
Async XLA Ops:
  1.8 14.8 %copy-start.27 = (bf16[27,2,16]{0,2,1:T(8,128)(2,1)S(1)}, bf16[27,2,16]{0,2,1:T(8,128)(2,1)}, u32[]{:S(2)}) copy-start(bf16[27,2,16]{0,2,1:T(8,128)(2,1)} %param.15) | copy-start | bytes 5188
  1.8 15.9 %copy-start.24 = (bf16[27,16,16]{0,2,1:T(8,128)(2,1)S(1)}, bf16[27,16,16]{0,2,1:T(8,128)(2,1)}, u32[]{:S(2)}) copy-start(bf16[27,16,16]{0,2,1:T(8,128)(2,1)} %param.14) | copy-start | bytes 41476
  1.8 6.5 %collective-permute-start = (bf16[2,4,16,128]{3,2,1,0:T(8,128)(2,1)S(1)}, bf16[2,4,16,128]{3,2,1,0:T(8,128)(2,1)S(1)}, u32[]{:S(2)}, u32[]{:S(2)}) collective-permute-start(bf16[2,4,16,128]{3,2,1,0:T(8,128)(2,1)S(1)} %get-tuple-element.123), channel_id=1, source_target_pairs={{0,1},{1,2},{2,3},{3,4},{4,5},{5,6},{6,7},{7,0},{8,9},{9,10},{10,1... | collective-permute-start | bytes 98312 | tf_op jit(solution)/shard_map/ppermute | solution.py:1084
  4.9 13.1 %copy-start.18 = (s32[2,1536]{1,0:T(2,128)S(1)}, s32[2,1536]{1,0:T(2,128)}, u32[]{:S(2)}) copy-start(s32[2,1536]{1,0:T(2,128)} %constant.27.clone.codes_2_ref) | copy-start | bytes 36868
  4.9 13.1 %copy-start.20 = (s32[2,1152]{1,0:T(2,128)S(1)}, s32[2,1152]{1,0:T(2,128)}, u32[]{:S(2)}) copy-start(s32[2,1152]{1,0:T(2,128)} %constant.26.clone.codes_1_ref) | copy-start | bytes 27652
  4.9 5.4 %collective-permute-start.1 = (bf16[2,4,16,128]{3,2,1,0:T(8,128)(2,1)S(1)}, bf16[2,4,16,128]{3,2,1,0:T(8,128)(2,1)S(1)}, u32[]{:S(2)}, u32[]{:S(2)}) collective-permute-start(bf16[2,4,16,128]{3,2,1,0:T(8,128)(2,1)S(1)} %get-tuple-element.124), channel_id=1, source_target_pairs={{1,0},{2,1},{3,2},{4,3},{5,4},{6,5},{7,6},{0,7},{9,8},{10,9},{11,1... | collective-permute-start | bytes 98312 | tf_op jit(solution)/shard_map/ppermute | solution.py:1084
  10.4 9.5 %collective-permute-start.3 = (bf16[2,40,16,128]{3,2,1,0:T(8,128)(2,1)S(1)}, bf16[2,40,16,128]{3,2,1,0:T(8,128)(2,1)S(1)}, u32[]{:S(2)}, u32[]{:S(2)}) collective-permute-start(bf16[2,40,16,128]{3,2,1,0:T(8,128)(2,1)S(1)} %pad_maximum_fusion.mid_ref), channel_id=1, source_target_pairs={{8,0},{16,8},{24,16},{32,24},{40,32},{48,40},{56,48},{64,56},{72,6... | collective-permute-start | bytes 983048 | tf_op jit(solution)/shard_map/ppermute | solution.py:1084
  11.8 12.1 %collective-permute-start.2 = (bf16[2,40,16,128]{3,2,1,0:T(8,128)(2,1)S(1)}, bf16[2,40,16,128]{3,2,1,0:T(8,128)(2,1)S(1)}, u32[]{:S(2)}, u32[]{:S(2)}) collective-permute-start(bf16[2,40,16,128]{3,2,1,0:T(8,128)(2,1)S(1)} %pad_maximum_fusion.mid_ref), channel_id=1, source_target_pairs={{0,8},{8,16},{16,24},{24,32},{32,40},{40,48},{48,56},{56,64},{64,7... | collective-permute-start | bytes 983048 | tf_op jit(solution)/shard_map/ppermute | solution.py:1084
  11.8 20.5 %collective-permute-start.5 = (f32[16,24,128]{2,1,0:T(8,128)S(1)}, f32[16,24,128]{2,1,0:T(8,128)S(1)}, u32[]{:S(2)}, u32[]{:S(2)}) collective-permute-start(f32[16,24,128]{2,1,0:T(8,128)S(1)} %get-tuple-element.121), channel_id=1, source_target_pairs={{1,0},{2,1},{3,2},{4,3},{5,4},{6,5},{7,6},{0,7},{9,8},{10,9},{11,1... | collective-permute-start | bytes 589832 | tf_op jit(solution)/shard_map/ppermute | solution.py:1084
  15.4 16.9 %collective-permute-start.4 = (f32[16,24,128]{2,1,0:T(8,128)S(1)}, f32[16,24,128]{2,1,0:T(8,128)S(1)}, u32[]{:S(2)}, u32[]{:S(2)}) collective-permute-start(f32[16,24,128]{2,1,0:T(8,128)S(1)} %get-tuple-element.122), channel_id=1, source_target_pairs={{0,1},{1,2},{2,3},{3,4},{4,5},{5,6},{6,7},{7,0},{8,9},{9,10},{10,1... | collective-permute-start | bytes 589832 | tf_op jit(solution)/shard_map/ppermute | solution.py:1084
  16.8 0.6 copy-start.22
  19.9 13.6 %copy-start.3 = (bf16[2,40,16,128]{3,2,1,0:T(8,128)(2,1)}, bf16[2,40,16,128]{3,2,1,0:T(8,128)(2,1)S(1)}, u32[]{:S(2)}) copy-start(bf16[2,40,16,128]{3,2,1,0:T(8,128)(2,1)S(1)} %collective-permute-done.3.hi_ref) | copy-start | bytes 983044
  23.9 9.6 %copy-start.5 = (bf16[2,40,16,128]{3,2,1,0:T(8,128)(2,1)}, bf16[2,40,16,128]{3,2,1,0:T(8,128)(2,1)S(1)}, u32[]{:S(2)}) copy-start(bf16[2,40,16,128]{3,2,1,0:T(8,128)(2,1)S(1)} %collective-permute-done.2.lo_ref) | copy-start | bytes 983044
  30.9 0.8 copy-start.1
  31.7 0.6 copy-start.16
  32.3 1.2 copy-start.12
  32.3 1.2 copy-start.14
  33.5 4.6 %copy-start.25 = (f32[1,3,2048]{2,0,1:T(1,128)S(1)}, f32[1,3,2048]{2,0,1:T(1,128)}, u32[]{:S(2)}) copy-start(f32[1,3,2048]{2,0,1:T(1,128)} %param.17) | copy-start | bytes 73732
  33.5 4.6 %copy-start.26 = (s32[1,3,2048]{2,0,1:T(1,128)S(1)}, s32[1,3,2048]{2,0,1:T(1,128)}, u32[]{:S(2)}) copy-start(s32[1,3,2048]{2,0,1:T(1,128)} %param.19) | copy-start | bytes 73732
  33.5 20.9 %all-to-all-start = ((f32[16,2,2,32,128]{4,3,2,1,0:T(8,128)}), f32[16,2,2,32,128]{4,3,2,1,0:T(8,128)}, u32[]{:S(2)}, u32[]{:S(2)}) async-start(f32[16,2,2,32,128]{4,3,2,1,0:T(8,128)} %broadcast_in_dim.4), calls=%async_computation | async-start | bytes 2097152 | tf_op jit(solution)/shard_map/all_to_all | solution.py:1106
  38.1 9.2 %copy-start.23 = (bf16[27,2,16]{1,2,0:T(8,128)(2,1)S(1)}, bf16[27,2,16]{1,2,0:T(8,128)(2,1)}, u32[]{:S(2)}) copy-start(bf16[27,2,16]{1,2,0:T(8,128)(2,1)} %copy-done.22) | copy-start | bytes 5188
  38.1 9.2 %copy-start.19 = (s32[2,1152]{1,0:T(2,128)S(1)}, s32[2,1152]{1,0:T(2,128)}, u32[]{:S(2)}) copy-start(s32[2,1152]{1,0:T(2,128)} %constant.29.clone.codes_4_ref) | copy-start | bytes 27652
  38.2 9.2 %copy-start.21 = (s32[2,576]{1,0:T(2,128)S(1)}, s32[2,576]{1,0:T(2,128)}, u32[]{:S(2)}) copy-start(s32[2,576]{1,0:T(2,128)} %constant.28.clone.codes_3_ref) | copy-start | bytes 13828
  47.3 13.2 %copy-start = (bf16[384,256]{1,0:T(8,128)(2,1)S(1)}, bf16[384,256]{1,0:T(8,128)(2,1)}, u32[]{:S(2)}) copy-start(bf16[384,256]{1,0:T(8,128)(2,1)} %constant.30.clone.slope_ref) | copy-start | bytes 589828
  48.7 0.9 copy-start.8
  49.6 0.7 copy-start.10
  54.4 10.0 %copy-start.2 = (bf16[38,64,128]{2,1,0:T(8,128)(2,1)S(1)}, bf16[38,64,128]{2,1,0:T(8,128)(2,1)}, u32[]{:S(2)}) copy-start(bf16[38,64,128]{2,1,0:T(8,128)(2,1)} %copy-done.1) | copy-start | bytes 1867780
  54.4 10.0 %copy-start.4 = (bf16[2,40,16,128]{3,2,1,0:T(8,128)(2,1)S(1)}, bf16[2,40,16,128]{3,2,1,0:T(8,128)(2,1)}, u32[]{:S(2)}) copy-start(bf16[2,40,16,128]{3,2,1,0:T(8,128)(2,1)} %copy-done.3) | copy-start | bytes 983044
  54.4 10.0 %copy-start.6 = (bf16[2,40,16,128]{3,2,1,0:T(8,128)(2,1)S(1)}, bf16[2,40,16,128]{3,2,1,0:T(8,128)(2,1)}, u32[]{:S(2)}) copy-start(bf16[2,40,16,128]{3,2,1,0:T(8,128)(2,1)} %copy-done.5) | copy-start | bytes 983044
  56.0 10.9 %collective-permute-start.6 = (bf16[16,2,24,128]{3,2,1,0:T(8,128)(2,1)S(1)}, bf16[16,2,24,128]{3,2,1,0:T(8,128)(2,1)S(1)}, u32[]{:S(2)}, u32[]{:S(2)}) collective-permute-start(bf16[16,2,24,128]{3,2,1,0:T(8,128)(2,1)S(1)} %get-tuple-element.67), channel_id=1, source_target_pairs={{0,1},{1,2},{2,3},{3,4},{4,5},{5,6},{6,7},{7,0},{8,9},{9,10},{10,1... | collective-permute-start | bytes 589832 | tf_op jit(solution)/shard_map/ppermute | solution.py:1084
  60.0 9.5 %copy-start.7 = (bf16[768,128]{1,0:T(8,128)(2,1)S(1)}, bf16[768,128]{1,0:T(8,128)(2,1)}, u32[]{:S(2)}) copy-start(bf16[768,128]{1,0:T(8,128)(2,1)} %constant.31.clone.spread_ref) | copy-start | bytes 589828
  60.0 9.5 %collective-permute-start.7 = (bf16[16,2,24,128]{3,2,1,0:T(8,128)(2,1)S(1)}, bf16[16,2,24,128]{3,2,1,0:T(8,128)(2,1)S(1)}, u32[]{:S(2)}, u32[]{:S(2)}) collective-permute-start(bf16[16,2,24,128]{3,2,1,0:T(8,128)(2,1)S(1)} %get-tuple-element.68), channel_id=1, source_target_pairs={{1,0},{2,1},{3,2},{4,3},{5,4},{6,5},{7,6},{0,7},{9,8},{10,9},{11,1... | collective-permute-start | bytes 589832 | tf_op jit(solution)/shard_map/ppermute | solution.py:1084
  60.5 0.9 copy-start.13
  61.4 0.9 copy-start.15
  77.6 8.8 %collective-permute-start.8 = (bf16[16,32,128]{2,1,0:T(8,128)(2,1)S(1)}, bf16[16,32,128]{2,1,0:T(8,128)(2,1)S(1)}, u32[]{:S(2)}, u32[]{:S(2)}) collective-permute-start(bf16[16,32,128]{2,1,0:T(8,128)(2,1)S(1)} %get-tuple-element.90), channel_id=1, source_target_pairs={{0,1},{1,2},{2,3},{3,4},{4,5},{5,6},{6,7},{7,0},{8,9},{9,10},{10,1... | collective-permute-start | bytes 393224 | tf_op jit(solution)/shard_map/ppermute | solution.py:1084
  81.4 6.7 %collective-permute-start.9 = (bf16[16,32,128]{2,1,0:T(8,128)(2,1)S(1)}, bf16[16,32,128]{2,1,0:T(8,128)(2,1)S(1)}, u32[]{:S(2)}, u32[]{:S(2)}) collective-permute-start(bf16[16,32,128]{2,1,0:T(8,128)(2,1)S(1)} %get-tuple-element.91), channel_id=1, source_target_pairs={{1,0},{2,1},{3,2},{4,3},{5,4},{6,5},{7,6},{0,7},{9,8},{10,9},{11,1... | collective-permute-start | bytes 393224 | tf_op jit(solution)/shard_map/ppermute | solution.py:1084
  96.5 20.9 %copy-start.17 = (f32[2,2,36,128]{3,2,1,0:T(8,128)S(1)}, f32[2,2,36,128]{3,2,1,0:T(8,128)}, u32[]{:S(2)}) copy-start(f32[2,2,36,128]{3,2,1,0:T(8,128)} %copy-done.16) | copy-start | bytes 221188
  118.0 6.3 %copy-start.9 = (bf16[512,576]{1,0:T(8,128)(2,1)S(1)}, bf16[512,576]{1,0:T(8,128)(2,1)}, u32[]{:S(2)}) copy-start(bf16[512,576]{1,0:T(8,128)(2,1)} %copy-done.8) | copy-start | bytes 1769476
  118.0 3.1 %collective-permute-start.11 = (bf16[2,2,36,128]{3,2,1,0:T(8,128)(2,1)S(1)}, bf16[2,2,36,128]{3,2,1,0:T(8,128)(2,1)S(1)}, u32[]{:S(2)}, u32[]{:S(2)}) collective-permute-start(bf16[2,2,36,128]{3,2,1,0:T(8,128)(2,1)S(1)} %chain.1.gmid_ref), channel_id=1, source_target_pairs={{8,0},{16,8},{24,16},{32,24},{40,32},{48,40},{56,48},{64,56},{72,6... | collective-permute-start | bytes 110600 | tf_op jit(solution)/shard_map/ppermute | solution.py:1084
  118.7 5.5 %collective-permute-start.10 = (bf16[2,2,36,128]{3,2,1,0:T(8,128)(2,1)S(1)}, bf16[2,2,36,128]{3,2,1,0:T(8,128)(2,1)S(1)}, u32[]{:S(2)}, u32[]{:S(2)}) collective-permute-start(bf16[2,2,36,128]{3,2,1,0:T(8,128)(2,1)S(1)} %chain.1.gmid_ref), channel_id=1, source_target_pairs={{0,8},{8,16},{16,24},{24,32},{32,40},{40,48},{48,56},{56,64},{64,7... | collective-permute-start | bytes 110600 | tf_op jit(solution)/shard_map/ppermute | solution.py:1084
  121.1 29.2 %copy-start.11 = (bf16[128,1152]{1,0:T(8,128)(2,1)S(1)}, bf16[128,1152]{1,0:T(8,128)(2,1)}, u32[]{:S(2)}) copy-start(bf16[128,1152]{1,0:T(8,128)(2,1)} %copy-done.10) | copy-start | bytes 884740
  145.1 14.0 %all-to-all-start.3 = ((f32[128,1,128]{2,1,0:T(1,128)}), f32[128,1,128]{2,1,0:T(1,128)S(1)}, u32[]{:S(2)}, u32[]{:S(2)}) async-start(f32[128,1,128]{2,1,0:T(1,128)} %broadcast_in_dim.5), calls=%async_computation.3 | async-start | bytes 131072 | tf_op jit(solution)/shard_map/all_to_all | solution.py:1132

commit v7 on v6

--- a/solution.py
+++ b/solution.py
@@ -189,31 +189,25 @@
 
 def third_dimension_matrices():
     slope = np.zeros((nz, 2 * nz))
-    spread = np.zeros((2 * nz, nz))
+    spread = np.zeros((nz, nz))
     for t, ratio in enumerate(ratios, 1):
+        slope[t - 1, nz:] += ratio
         for face in range(nz):
-            for column, at in ((face, face), (nz + face, face if face < nz - 1 else -1)):
-                if 0 <= at + t < nz:
-                    slope[at + t, column] += ratio
-                if 0 <= at + 1 - t < nz:
-                    slope[at + 1 - t, column] -= ratio
+            if face + t < nz:
+                slope[face + t, face] += ratio
+            if face + 1 - t >= 0:
+                slope[face + 1 - t, face] -= ratio
         for cell in range(nz):
             if cell + t - 1 < nz:
                 spread[cell + t - 1, cell] += ratio
-            if cell - t >= -1:
-                spread[nz + (cell - t) % nz, cell] -= ratio
+            if cell - t >= 0:
+                spread[cell - t, cell] -= ratio
 
     def parts(matrix):
         high = matrix.astype(jnp.bfloat16)
-        return high, (matrix - high.astype(np.float64)).astype(jnp.bfloat16)
-
-    high, low = parts(slope)
-    slope = np.concatenate([high, high, low])
-    blocks = []
-    for half in (spread[:nz], spread[nz:]):
-        high, low = parts(half)
-        blocks += [high, high, low]
-    return slope, np.concatenate(blocks)
+        return np.concatenate([high, high, (matrix - high.astype(np.float64)).astype(jnp.bfloat16)])
+
+    return parts(slope), parts(spread)
 
 
 slope_matrix, spread_matrix = third_dimension_matrices()
@@ -232,13 +226,13 @@
     return both[:, :nz], both[:, nz:]
 
 
-def divergence_z(here, before, spread_ref):
-    high_h, low_h = halves(here)
-    high_b, low_b = halves(before)
-    return jnp.dot(
-        jnp.concatenate([high_h, low_h, high_h, high_b, low_b, high_b], axis=1),
-        spread_ref[...],
-        preferred_element_type=F32,
+def divergence_z(flux, first_part, spread_ref):
+    high, low = halves(flux)
+    return (
+        jnp.dot(
+            jnp.concatenate([high, low, high], axis=1), spread_ref[...], preferred_element_type=F32
+        )
+        - first_part
     )
 
 
@@ -351,7 +345,7 @@
         out[pl.ds(y, group), pl.ds(0, rows), :] = total.reshape(group, rows, nz)
         return carry
 
-    lax.fori_loop(0, ay // group, body, 0, unroll=2)
+    lax.fori_loop(0, ay // group, body, 0, unroll=4)
 
 
 def flux_pass(field, weights, fluxes, first, rows, also=None):
@@ -452,7 +446,9 @@
     p2_ref, p3_ref, p4_ref, image_ref, ahead_ref, behind_ref, modulus, wx, wy, wz, wzl,
     buoy, f2, f3, fx, fy, az, message,
 ):
+    half = 0.5 * tap_square
     last = lane_index() == nz - 1
+    first_taps = sum(jnp.where(lane_index() == t, half * ratios[t], 0.0) for t in range(4))
     weights = (wx, wy, wz, wzl)
     fluxes = (fx, fy, az)
     matrices = (slope_ref, spread_ref)
@@ -460,7 +456,6 @@
     for field in (buoy, f2, f3):
         clear_sides(field)
     low, high = halo_scale(at_ref)
-    half = 0.5 * tap_square
 
     def load(y, carry):
         for channel, ref, row, skip in ((0, modulus, y, 0), (1, buoy, y + 4, lead)):
@@ -482,7 +477,7 @@
         wx[y] = half * (value + buoy[y + 4, pl.ds(1, dom + 16), :])
         wy[y] = half * (buoy[y + 3, pl.ds(lead, dom), :] + inner)
         wz[y] = half * jnp.where(last, inner, inner + ahead)
-        wzl[y] = half * jnp.where(last, ahead, inner + ahead)
+        wzl[y] = inner[:, :1] * first_taps
         return carry
 
     lax.fori_loop(0, ay, weigh, 0, unroll=2)
@@ -538,7 +533,7 @@
         az[pl.ds(y, group), pl.ds(0, 64), :] = total.reshape(group, 64, nz)
         return carry
 
-    lax.fori_loop(0, ay // group, first_third, 0, unroll=2)
+    lax.fori_loop(0, ay // group, first_third, 0, unroll=4)
 
     def first_flux(y, carry):
         fx[y] = wx[y, pl.ds(lead + 4, 72), :] * sx_ref[y]
@@ -733,6 +728,7 @@
     cross_last(0, 0, slope_y(scaled, ay, 16, 48))
 
     first_row = at_ref[2]
+    first_lane = lane_index() == 0
 
     def blank(row, carry):
         column_ref[row] = jnp.zeros(column_ref.shape[1:], F32)
@@ -742,8 +738,8 @@
     lax.fori_loop(first_row + ay, 2 * shots, blank, 0)
 
     def place(y, carry):
-        before = pltpu.roll(qb[y, pl.ds(6, gx), :], 1, 1)
-        total = qh[y, pl.ds(6, gx), :] + before
+        here = qh[y, pl.ds(6, gx), :]
+        total = here + jnp.where(first_lane, qb[y, pl.ds(6, gx), :], pltpu.roll(here, 1, 1))
         total = total + qy[y, pl.ds(6, gx), :] + qy[y + 1, pl.ds(6, gx), :]
         total = total + qx[y, pl.ds(9, gx), :] + qx[y, pl.ds(10, gx), :]
         column_ref[first_row + y, pl.ds(0, gx), :] = grad_m[y, pl.ds(6, gx), :]
@@ -900,7 +896,7 @@
                 ).astype(BF16)
         return carry
 
-    lax.fori_loop(0, 5, hidden_grad, 0)
+    lax.fori_loop(0, 5, hidden_grad, 0, unroll=5)
     fetch.wait()
 
     def kernel_grad(x, first):

time: 164 us -> 163 us (level)
  no operation moved by 1% of the time
where the time goes in v7:
time: 163 us; the launch traced here: 160 us
  Pallas kernels  55.1 us (34%)
  blocking collectives  35.7 us (22%)
  starting transfers between devices  29.3 us (18%)
  waiting for transfers between devices  24.2 us (15%)
  local copies, waits for them, and re-layouts  13.8 us (8%)
  between operations  1.74 us (1%)
    all_to_all x1, blocking collectives, per_device(): got = lax.all_to_all(grads, 'shot', 0, 0, tiled=True)  20.9 us
    all_to_all x1, blocking collectives, per_device(): slices = lax.all_to_all(kernels, everyone, 0, 0, tiled=True)  14.8 us
    ppermute x6, starting transfers between devices, both_ways(): lax.ppermute(ahead, axis, forward)  11.4 us
    unnamed x66, local copies, waits for them, and re-layouts  10.3 us
    pallas_call x1, Pallas kernels, receiver_fields(): pl.pallas_call(receiver_kernel, out_shape=jax.ShapeDtypeStruct((4, ay * d...  9.12 us
    ppermute x6, waiting for transfers between devices, both_ways(): lax.ppermute(ahead, axis, forward)  8.6 us
    ppermute x6, starting transfers between devices, both_ways(): lax.ppermute(behind, axis, backward_)  8.35 us
    pallas_call x1, Pallas kernels, adjoint_waves(): pl.pallas_call(adjoint_kernel, out_shape=jax.ShapeDtypeStruct((2 * shots,...  8.23 us
  transfers between devices with their start and end apart: 14, of which 10 were waited for; matrix products, arithmetic and copies ran while one was open for 2% of the time, Pallas kernels for 20%

profile of v7, /device:TPU:32, one launch (start us, length us, event | category | flops | bytes accessed | tf_op | source)
XLA Modules:
  0.0 160.0 jit_solution(13263100120673305129)
XLA Ops:
  0.6 1.1 copy.57
  1.8 3.1 %collective-permute-start = (bf16[2,4,16,128]{3,2,1,0:T(8,128)(2,1)S(1)}, bf16[2,4,16,128]{3,2,1,0:T(8,128)(2,1)S(1)}, u32[]{:S(2)}, u32[]{:S(2)}) collective-permute-start(bf16[2,4,16,128]{3,2,1,0:T(8,128)(2,1)S(1)} %get-tuple-element.123), channel_id=1, source_target_pairs={{0,1},{1,2},{2,3},{3,4},{4,5},{5,6},{6,7},{7,0},{8,9},{9,10},{10,1... | collective-permute-start | bytes 98312 | tf_op jit(solution)/shard_map/ppermute | solution.py:1080
  4.9 1.4 collective-permute-start.1
  6.3 1.0 copy.56
  7.3 0.9 collective-permute-done
  8.3 2.0 %collective-permute-done.1 = bf16[2,4,16,128]{3,2,1,0:T(8,128)(2,1)S(1)} collective-permute-done((bf16[2,4,16,128]{3,2,1,0:T(8,128)(2,1)S(1)}, bf16[2,4,16,128]{3,2,1,0:T(8,128)(2,1)S(1)}, u32[]{:S(2)}, u32[]{:S(2)}) %collective-permute-start.1) | collective-permute-done | bytes 32800 | tf_op jit(solution)/shard_map/ppermute | solution.py:1080
  10.4 1.4 collective-permute-start.3
  11.8 3.6 %collective-permute-start.5 = (f32[16,24,128]{2,1,0:T(8,128)S(1)}, f32[16,24,128]{2,1,0:T(8,128)S(1)}, u32[]{:S(2)}, u32[]{:S(2)}) collective-permute-start(f32[16,24,128]{2,1,0:T(8,128)S(1)} %get-tuple-element.121), channel_id=1, source_target_pairs={{1,0},{2,1},{3,2},{4,3},{5,4},{6,5},{7,6},{0,7},{9,8},{10,9},{11,1... | collective-permute-start | bytes 589832 | tf_op jit(solution)/shard_map/ppermute | solution.py:1080
  16.8 0.6 copy-done.22
  18.0 1.0 forward_bands.1
  19.1 0.8 collective-permute-done.3.hi_ref
  19.9 4.0 %collective-permute-done.2.lo_ref = bf16[2,40,16,128]{3,2,1,0:T(8,128)(2,1)S(1)} collective-permute-done((bf16[2,40,16,128]{3,2,1,0:T(8,128)(2,1)S(1)}, bf16[2,40,16,128]{3,2,1,0:T(8,128)(2,1)S(1)}, u32[]{:S(2)}, u32[]{:S(2)}) %collective-permute-start.2) | collective-permute-done | bytes 327712 | tf_op jit(solution)/shard_map/ppermute | solution.py:1080
  23.9 6.9 %generator.1 = (f32[2,2,32,128]{3,2,1,0:T(8,128)S(1)}, f32[2,2,36,128]{3,2,1,0:T(8,128)S(1)}, bf16[38,64,128]{2,1,0:T(8,128)(2,1)S(1)}) custom-call(s32[3]{0:T(128)S(1)} %pad_add_fusion.at_ref, bf16[2,40,16,128]{3,2,1,0:T(8,128)(2,1)S(1)} %collective-permute-done.2.lo_ref, bf16[2,40,16,128]{3,2,1,0:T(8,128)(2,1)S(1)} %pad_maximum_fusion.mid_ref, ...), custom_call_target="tpu_custom_call" | custom-call | tf_op jit(solution)/shard_map/generator/pallas_call | solution.py:111
  30.9 0.8 copy-done.1
  31.7 0.6 copy-done.16
  32.3 1.1 broadcast_in_dim.4
  33.5 4.3 %all-to-all-start = ((f32[16,2,2,32,128]{4,3,2,1,0:T(8,128)}), f32[16,2,2,32,128]{4,3,2,1,0:T(8,128)}, u32[]{:S(2)}, u32[]{:S(2)}) async-start(f32[16,2,2,32,128]{4,3,2,1,0:T(8,128)} %broadcast_in_dim.4), calls=%async_computation | async-start | bytes 2097152 | tf_op jit(solution)/shard_map/all_to_all | solution.py:1102
  38.2 9.1 %receiver_fields.1.seen_ref = f32[4,1280,128]{2,1,0:T(8,128)S(1)} custom-call(s32[3]{0:T(128)S(1)} %pad_add_fusion.at_ref, s32[3,2048]{1,0:T(4,128)S(1)} %bitcast.42, f32[3,2048]{1,0:T(4,128)S(1)} %bitcast.41), custom_call_target="tpu_custom_call" | custom-call | bytes 27000000 | tf_op jit(solution)/shard_map/receiver_fields/pallas_call | solution.py:175
  47.4 1.3 backward_bands.1
  48.7 0.8 copy-done.7
  49.6 0.7 copy-done.10
  50.3 4.1 %all-to-all-done = f32[16,2,2,32,128]{4,3,2,1,0:T(8,128)} async-done(((f32[16,2,2,32,128]{4,3,2,1,0:T(8,128)}), f32[16,2,2,32,128]{4,3,2,1,0:T(8,128)}, u32[]{:S(2)}, u32[]{:S(2)}) %all-to-all-start) | async-done | bytes 1048608 | tf_op jit(solution)/shard_map/all_to_all | solution.py:1102
  54.4 1.6 take_window.1
  56.0 4.0 %collective-permute-start.6 = (bf16[16,2,24,128]{3,2,1,0:T(8,128)(2,1)S(1)}, bf16[16,2,24,128]{3,2,1,0:T(8,128)(2,1)S(1)}, u32[]{:S(2)}, u32[]{:S(2)}) collective-permute-start(bf16[16,2,24,128]{3,2,1,0:T(8,128)(2,1)S(1)} %get-tuple-element.67), channel_id=1, source_target_pairs={{0,1},{1,2},{2,3},{3,4},{4,5},{5,6},{6,7},{7,0},{8,9},{9,10},{10,1... | collective-permute-start | bytes 589832 | tf_op jit(solution)/shard_map/ppermute | solution.py:1080
  60.5 0.9 copy-done.13
  61.4 0.9 copy-done.15
  62.4 2.1 %source_slopes.1 = (f32[16,64,128]{2,1,0:T(8,128)S(1)}, f32[16,72,128]{2,1,0:T(8,128)S(1)}, f32[17,64,128]{2,1,0:T(8,128)S(1)}, f32[16,64,128]{2,1,0:T(8,128)S(1)}, f32[16,64,128]{2,1,0:T(8,128)S(1)}) custom-call(s32[3]{0:T(128)S(1)} %pad_add_fusion.at_ref, f32[16,32,128]{2,1,0:T(8,128)S(1)} %bitcast.38, f32[16,24,128]{2,1,0:T(8,128)S(1)} %copy-done.15, ...), custom_call_target="tpu_custom_call" | custom-call | bytes 9000000 | tf_op jit(solution)/shard_map/source_slopes/pallas_call | solution.py:432
  64.5 2.4 %spread_fields.1 = (bf16[34,192,128]{2,1,0:T(8,128)(2,1)S(1)}, bf16[34,192,128]{2,1,0:T(8,128)(2,1)S(1)}) custom-call(s32[3]{0:T(128)S(1)} %pad_add_fusion.at_ref, bf16[2,40,16,128]{3,2,1,0:T(8,128)(2,1)S(1)} %copy-done.6, bf16[2,40,16,128]{3,2,1,0:T(8,128)(2,1)S(1)} %pad_maximum_fusion.mid_ref, bf16[2,40,16,128]{3,2,1,0:T(8,128)(2,1)S(1)} %copy-done.4, ...), custom_call_target="tpu_custom_call" | custom-call | bytes 9000000 | tf_op jit(solution)/shard_map/spread_fields/pallas_call | solution.py:823
  66.9 2.6 %collective-permute-done.7.chi_ref = bf16[16,2,24,128]{3,2,1,0:T(8,128)(2,1)S(1)} collective-permute-done((bf16[16,2,24,128]{3,2,1,0:T(8,128)(2,1)S(1)}, bf16[16,2,24,128]{3,2,1,0:T(8,128)(2,1)S(1)}, u32[]{:S(2)}, u32[]{:S(2)}) %collective-permute-start.7) | collective-permute-done | bytes 196640 | tf_op jit(solution)/shard_map/ppermute | solution.py:1080
  69.5 7.9 %forward_waves.1 = (f32[16,64,128]{2,1,0:T(8,128)S(1)}, f32[16,48,128]{2,1,0:T(8,128)S(1)}, f32[16,32,128]{2,1,0:T(8,128)S(1)}, f32[3,16,48,128]{3,2,1,0:T(8,128...) custom-call(s32[3]{0:T(128)S(1)} %pad_add_fusion.at_ref, ...), custom_call_target="tpu_custom_call" | custom-call | tf_op jit(solution)/shard_map/forward_waves/pallas_call | solution.py:558
  77.3 3.7 %collective-permute-start.8 = (bf16[16,32,128]{2,1,0:T(8,128)(2,1)S(1)}, bf16[16,32,128]{2,1,0:T(8,128)(2,1)S(1)}, u32[]{:S(2)}, u32[]{:S(2)}) collective-permute-start(bf16[16,32,128]{2,1,0:T(8,128)(2,1)S(1)} %get-tuple-element.90), channel_id=1, source_target_pairs={{0,1},{1,2},{2,3},{3,4},{4,5},{5,6},{6,7},{7,0},{8,9},{9,10},{10,1... | collective-permute-start | bytes 393224 | tf_op jit(solution)/shard_map/ppermute | solution.py:1080
  81.1 0.8 collective-permute-start.9
  81.8 3.8 %wave_slopes.1 = (f32[3,16,48,128]{3,2,1,0:T(8,128)S(1)}, f32[3,17,48,128]{3,2,1,0:T(8,128)S(1)}, f32[3,16,48,128]{3,2,1,0:T(8,128)S(1)}, f32[3,16,48,128]{3,2,1,0:T(8,128)S(1)}) custom-call(f32[16,64,128]{2,1,0:T(8,128)S(1)} %get-tuple-element.81.p1_ref, f32[16,64,128]{2,1,0:T(8,128)S(1)} %get-tuple-element.86.p2_ref, ...), custom_call_target="tpu_custom_call" | custom-call | bytes 18000000 | tf_op jit(solution)/shard_map/wave_slopes/pallas_call | solution.py:604
  86.1 1.6 %collective-permute-done.9.front_ref = bf16[16,32,128]{2,1,0:T(8,128)(2,1)S(1)} collective-permute-done((bf16[16,32,128]{2,1,0:T(8,128)(2,1)S(1)}, bf16[16,32,128]{2,1,0:T(8,128)(2,1)S(1)}, u32[]{:S(2)}, u32[]{:S(2)}) %collective-permute-start.9) | collective-permute-done | bytes 131104 | tf_op jit(solution)/shard_map/ppermute | solution.py:1080
  87.8 8.2 %adjoint_waves.1 = f32[32,72,128]{2,1,0:T(8,128)S(1)} custom-call(s32[3]{0:T(128)S(1)} %pad_add_fusion.at_ref, f32[16,64,128]{2,1,0:T(8,128)S(1)} %get-tuple-element.86.p2_ref, f32[16,48,128]{2,1,0:T(8,128)S(1)} %get-tuple-element.87.p3_ref, f32[16,32,128]{2,1,0:T(8,128)S(1)} %get-tuple-element.88.p4_ref, ...), custom_call_target="tpu_custom_call" | custom-call | tf_op jit(solution)/shard_map/adjoint_waves/pallas_call | solution.py:754
  96.0 20.9 %all_to_all.25 = f32[32,72,128]{2,1,0:T(8,128)S(1)} all-to-all(f32[32,72,128]{2,1,0:T(8,128)S(1)} %adjoint_waves.1), channel_id=1, replica_groups=mesh['shot'=16,'brick'=8] {'shot'}, dimensions={0} | all-to-all | bytes 2359296 | tf_op jit(solution)/shard_map/all_to_all | solution.py:1116
  117.5 0.7 collective-permute-start.11
  118.2 2.3 %second_grads.1.second_ref = f32[8,576]{1,0:T(8,128)S(1)} custom-call(bf16[2,2,36,128]{3,2,1,0:T(8,128)(2,1)S(1)} %chain.1.gmid_ref, bf16[34,192,128]{2,1,0:T(8,128)(2,1)S(1)} %get-tuple-element.109.s2), custom_call_target="tpu_custom_call" | custom-call | bytes 9000000 | tf_op jit(solution)/shard_map/second_grads/pallas_call | solution.py:852
  120.6 3.2 %collective-permute-done.10.glo_ref = bf16[2,2,36,128]{3,2,1,0:T(8,128)(2,1)S(1)} collective-permute-done((bf16[2,2,36,128]{3,2,1,0:T(8,128)(2,1)S(1)}, bf16[2,2,36,128]{3,2,1,0:T(8,128)(2,1)S(1)}, u32[]{:S(2)}, u32[]{:S(2)}) %collective-permute-start.10) | collective-permute-done | bytes 36896 | tf_op jit(solution)/shard_map/ppermute | solution.py:1080
  123.8 4.4 %first_grads.1 = (bf16[40,64,128]{2,1,0:T(8,128)(2,1)S(1)}, f32[128,128]{1,0:T(8,128)S(1)}) custom-call(s32[3]{0:T(128)S(1)} %pad_add_fusion.at_ref, bf16[2,2,36,128]{3,2,1,0:T(8,128)(2,1)S(1)} %collective-permute-done.10.glo_ref, bf16[2,2,36,128]{3,2,1,0:T(8,128)(2,1)S(1)} %chain.1.gmid_ref, bf16[2,2,36,128]{3,2,1,0:T(8,128)(2,1)S(1)} %collective-permute-done.11.ghi_ref, ...), custom_call_target="tpu_custom_call" | custom-call | tf_op jit(solution)/shard_map/first_grads/pallas_call | solution.py:930
  128.2 14.8 %all_to_all.26 = f32[128,1,128]{2,1,0:T(1,128)S(1)} all-to-all(f32[128,1,128]{2,1,0:T(1,128)S(1)} %bitcast.43), channel_id=1, replica_groups=mesh['shot'=16,'brick'=8] {'shot','brick'}, dimensions={0} | all-to-all | bytes 131072 | tf_op jit(solution)/shard_map/all_to_all | solution.py:1126
  143.2 0.7 broadcast_in_dim.5
  143.8 5.2 %all-to-all-start.3 = ((f32[128,1,128]{2,1,0:T(1,128)}), f32[128,1,128]{2,1,0:T(1,128)S(1)}, u32[]{:S(2)}, u32[]{:S(2)}) async-start(f32[128,1,128]{2,1,0:T(1,128)} %broadcast_in_dim.5), calls=%async_computation.3 | async-start | bytes 131072 | tf_op jit(solution)/shard_map/all_to_all | solution.py:1128
  149.0 3.4 %latent_grads.1 = f32[32,32,128]{2,1,0:T(8,128)S(1)} custom-call(bf16[40,64,128]{2,1,0:T(8,128)(2,1)S(1)} %get-tuple-element.112.inner_ref, bf16[128,1152]{1,0:T(8,128)(2,1)S(1)} %copy-done.11), custom_call_target="tpu_custom_call" | custom-call | bytes 12000000 | tf_op jit(solution)/shard_map/latent_grads/pallas_call | solution.py:968
  152.4 1.1 copy.55
  153.4 4.4 %all-to-all-done.3 = f32[128,1,128]{2,1,0:T(1,128)S(1)} async-done(((f32[128,1,128]{2,1,0:T(1,128)}), f32[128,1,128]{2,1,0:T(1,128)S(1)}, u32[]{:S(2)}, u32[]{:S(2)}) %all-to-all-start.3) | async-done | bytes 65568 | tf_op jit(solution)/shard_map/all_to_all | solution.py:1128
  158.4 0.8 copy.44
  159.2 0.8 copy.45
  (78 shorter events, 4.0 us)
Async XLA Ops:
  1.8 14.8 %copy-start.27 = (bf16[27,2,16]{0,2,1:T(8,128)(2,1)S(1)}, bf16[27,2,16]{0,2,1:T(8,128)(2,1)}, u32[]{:S(2)}) copy-start(bf16[27,2,16]{0,2,1:T(8,128)(2,1)} %param.15) | copy-start | bytes 5188
  1.8 15.9 %copy-start.24 = (bf16[27,16,16]{0,2,1:T(8,128)(2,1)S(1)}, bf16[27,16,16]{0,2,1:T(8,128)(2,1)}, u32[]{:S(2)}) copy-start(bf16[27,16,16]{0,2,1:T(8,128)(2,1)} %param.14) | copy-start | bytes 41476
  1.8 6.5 %collective-permute-start = (bf16[2,4,16,128]{3,2,1,0:T(8,128)(2,1)S(1)}, bf16[2,4,16,128]{3,2,1,0:T(8,128)(2,1)S(1)}, u32[]{:S(2)}, u32[]{:S(2)}) collective-permute-start(bf16[2,4,16,128]{3,2,1,0:T(8,128)(2,1)S(1)} %get-tuple-element.123), channel_id=1, source_target_pairs={{0,1},{1,2},{2,3},{3,4},{4,5},{5,6},{6,7},{7,0},{8,9},{9,10},{10,1... | collective-permute-start | bytes 98312 | tf_op jit(solution)/shard_map/ppermute | solution.py:1080
  4.9 13.1 %copy-start.18 = (s32[2,1536]{1,0:T(2,128)S(1)}, s32[2,1536]{1,0:T(2,128)}, u32[]{:S(2)}) copy-start(s32[2,1536]{1,0:T(2,128)} %constant.27.clone.codes_2_ref) | copy-start | bytes 36868
  4.9 13.1 %copy-start.20 = (s32[2,1152]{1,0:T(2,128)S(1)}, s32[2,1152]{1,0:T(2,128)}, u32[]{:S(2)}) copy-start(s32[2,1152]{1,0:T(2,128)} %constant.26.clone.codes_1_ref) | copy-start | bytes 27652
  4.9 5.4 %collective-permute-start.1 = (bf16[2,4,16,128]{3,2,1,0:T(8,128)(2,1)S(1)}, bf16[2,4,16,128]{3,2,1,0:T(8,128)(2,1)S(1)}, u32[]{:S(2)}, u32[]{:S(2)}) collective-permute-start(bf16[2,4,16,128]{3,2,1,0:T(8,128)(2,1)S(1)} %get-tuple-element.124), channel_id=1, source_target_pairs={{1,0},{2,1},{3,2},{4,3},{5,4},{6,5},{7,6},{0,7},{9,8},{10,9},{11,1... | collective-permute-start | bytes 98312 | tf_op jit(solution)/shard_map/ppermute | solution.py:1080
  10.4 9.5 %collective-permute-start.3 = (bf16[2,40,16,128]{3,2,1,0:T(8,128)(2,1)S(1)}, bf16[2,40,16,128]{3,2,1,0:T(8,128)(2,1)S(1)}, u32[]{:S(2)}, u32[]{:S(2)}) collective-permute-start(bf16[2,40,16,128]{3,2,1,0:T(8,128)(2,1)S(1)} %pad_maximum_fusion.mid_ref), channel_id=1, source_target_pairs={{8,0},{16,8},{24,16},{32,24},{40,32},{48,40},{56,48},{64,56},{72,6... | collective-permute-start | bytes 983048 | tf_op jit(solution)/shard_map/ppermute | solution.py:1080
  11.8 12.1 %collective-permute-start.2 = (bf16[2,40,16,128]{3,2,1,0:T(8,128)(2,1)S(1)}, bf16[2,40,16,128]{3,2,1,0:T(8,128)(2,1)S(1)}, u32[]{:S(2)}, u32[]{:S(2)}) collective-permute-start(bf16[2,40,16,128]{3,2,1,0:T(8,128)(2,1)S(1)} %pad_maximum_fusion.mid_ref), channel_id=1, source_target_pairs={{0,8},{8,16},{16,24},{24,32},{32,40},{40,48},{48,56},{56,64},{64,7... | collective-permute-start | bytes 983048 | tf_op jit(solution)/shard_map/ppermute | solution.py:1080
  11.8 20.5 %collective-permute-start.5 = (f32[16,24,128]{2,1,0:T(8,128)S(1)}, f32[16,24,128]{2,1,0:T(8,128)S(1)}, u32[]{:S(2)}, u32[]{:S(2)}) collective-permute-start(f32[16,24,128]{2,1,0:T(8,128)S(1)} %get-tuple-element.121), channel_id=1, source_target_pairs={{1,0},{2,1},{3,2},{4,3},{5,4},{6,5},{7,6},{0,7},{9,8},{10,9},{11,1... | collective-permute-start | bytes 589832 | tf_op jit(solution)/shard_map/ppermute | solution.py:1080
  15.4 16.9 %collective-permute-start.4 = (f32[16,24,128]{2,1,0:T(8,128)S(1)}, f32[16,24,128]{2,1,0:T(8,128)S(1)}, u32[]{:S(2)}, u32[]{:S(2)}) collective-permute-start(f32[16,24,128]{2,1,0:T(8,128)S(1)} %get-tuple-element.122), channel_id=1, source_target_pairs={{0,1},{1,2},{2,3},{3,4},{4,5},{5,6},{6,7},{7,0},{8,9},{9,10},{10,1... | collective-permute-start | bytes 589832 | tf_op jit(solution)/shard_map/ppermute | solution.py:1080
  16.8 0.6 copy-start.22
  19.9 13.6 %copy-start.3 = (bf16[2,40,16,128]{3,2,1,0:T(8,128)(2,1)}, bf16[2,40,16,128]{3,2,1,0:T(8,128)(2,1)S(1)}, u32[]{:S(2)}) copy-start(bf16[2,40,16,128]{3,2,1,0:T(8,128)(2,1)S(1)} %collective-permute-done.3.hi_ref) | copy-start | bytes 983044
  23.9 9.6 %copy-start.5 = (bf16[2,40,16,128]{3,2,1,0:T(8,128)(2,1)}, bf16[2,40,16,128]{3,2,1,0:T(8,128)(2,1)S(1)}, u32[]{:S(2)}) copy-start(bf16[2,40,16,128]{3,2,1,0:T(8,128)(2,1)S(1)} %collective-permute-done.2.lo_ref) | copy-start | bytes 983044
  30.9 0.8 copy-start.1
  31.7 0.6 copy-start.16
  32.3 1.2 copy-start.12
  32.3 1.2 copy-start.14
  33.5 4.6 %copy-start.25 = (f32[1,3,2048]{2,0,1:T(1,128)S(1)}, f32[1,3,2048]{2,0,1:T(1,128)}, u32[]{:S(2)}) copy-start(f32[1,3,2048]{2,0,1:T(1,128)} %param.17) | copy-start | bytes 73732
  33.5 4.6 %copy-start.26 = (s32[1,3,2048]{2,0,1:T(1,128)S(1)}, s32[1,3,2048]{2,0,1:T(1,128)}, u32[]{:S(2)}) copy-start(s32[1,3,2048]{2,0,1:T(1,128)} %param.19) | copy-start | bytes 73732
  33.5 20.9 %all-to-all-start = ((f32[16,2,2,32,128]{4,3,2,1,0:T(8,128)}), f32[16,2,2,32,128]{4,3,2,1,0:T(8,128)}, u32[]{:S(2)}, u32[]{:S(2)}) async-start(f32[16,2,2,32,128]{4,3,2,1,0:T(8,128)} %broadcast_in_dim.4), calls=%async_computation | async-start | bytes 2097152 | tf_op jit(solution)/shard_map/all_to_all | solution.py:1102
  38.1 9.2 %copy-start.23 = (bf16[27,2,16]{1,2,0:T(8,128)(2,1)S(1)}, bf16[27,2,16]{1,2,0:T(8,128)(2,1)}, u32[]{:S(2)}) copy-start(bf16[27,2,16]{1,2,0:T(8,128)(2,1)} %copy-done.22) | copy-start | bytes 5188
  38.1 9.2 %copy-start.19 = (s32[2,1152]{1,0:T(2,128)S(1)}, s32[2,1152]{1,0:T(2,128)}, u32[]{:S(2)}) copy-start(s32[2,1152]{1,0:T(2,128)} %constant.29.clone.codes_4_ref) | copy-start | bytes 27652
  38.2 9.2 %copy-start.21 = (s32[2,576]{1,0:T(2,128)S(1)}, s32[2,576]{1,0:T(2,128)}, u32[]{:S(2)}) copy-start(s32[2,576]{1,0:T(2,128)} %constant.28.clone.codes_3_ref) | copy-start | bytes 13828
  47.3 13.2 %copy-start = (bf16[384,256]{1,0:T(8,128)(2,1)S(1)}, bf16[384,256]{1,0:T(8,128)(2,1)}, u32[]{:S(2)}) copy-start(bf16[384,256]{1,0:T(8,128)(2,1)} %constant.30.clone.slope_ref) | copy-start | bytes 589828
  48.7 0.9 copy-start.7
  49.6 0.7 copy-start.10
  54.4 10.0 %copy-start.2 = (bf16[38,64,128]{2,1,0:T(8,128)(2,1)S(1)}, bf16[38,64,128]{2,1,0:T(8,128)(2,1)}, u32[]{:S(2)}) copy-start(bf16[38,64,128]{2,1,0:T(8,128)(2,1)} %copy-done.1) | copy-start | bytes 1867780
  54.4 10.0 %copy-start.4 = (bf16[2,40,16,128]{3,2,1,0:T(8,128)(2,1)S(1)}, bf16[2,40,16,128]{3,2,1,0:T(8,128)(2,1)}, u32[]{:S(2)}) copy-start(bf16[2,40,16,128]{3,2,1,0:T(8,128)(2,1)} %copy-done.3) | copy-start | bytes 983044
  54.4 10.0 %copy-start.6 = (bf16[2,40,16,128]{3,2,1,0:T(8,128)(2,1)S(1)}, bf16[2,40,16,128]{3,2,1,0:T(8,128)(2,1)}, u32[]{:S(2)}) copy-start(bf16[2,40,16,128]{3,2,1,0:T(8,128)(2,1)} %copy-done.5) | copy-start | bytes 983044
  56.0 10.9 %collective-permute-start.6 = (bf16[16,2,24,128]{3,2,1,0:T(8,128)(2,1)S(1)}, bf16[16,2,24,128]{3,2,1,0:T(8,128)(2,1)S(1)}, u32[]{:S(2)}, u32[]{:S(2)}) collective-permute-start(bf16[16,2,24,128]{3,2,1,0:T(8,128)(2,1)S(1)} %get-tuple-element.67), channel_id=1, source_target_pairs={{0,1},{1,2},{2,3},{3,4},{4,5},{5,6},{6,7},{7,0},{8,9},{9,10},{10,1... | collective-permute-start | bytes 589832 | tf_op jit(solution)/shard_map/ppermute | solution.py:1080
  60.0 9.5 %copy-start.9 = (bf16[384,128]{1,0:T(8,128)(2,1)S(1)}, bf16[384,128]{1,0:T(8,128)(2,1)}, u32[]{:S(2)}) copy-start(bf16[384,128]{1,0:T(8,128)(2,1)} %constant.31.clone.spread_ref) | copy-start | bytes 294916
  60.0 9.5 %collective-permute-start.7 = (bf16[16,2,24,128]{3,2,1,0:T(8,128)(2,1)S(1)}, bf16[16,2,24,128]{3,2,1,0:T(8,128)(2,1)S(1)}, u32[]{:S(2)}, u32[]{:S(2)}) collective-permute-start(bf16[16,2,24,128]{3,2,1,0:T(8,128)(2,1)S(1)} %get-tuple-element.68), channel_id=1, source_target_pairs={{1,0},{2,1},{3,2},{4,3},{5,4},{6,5},{7,6},{0,7},{9,8},{10,9},{11,1... | collective-permute-start | bytes 589832 | tf_op jit(solution)/shard_map/ppermute | solution.py:1080
  60.5 0.9 copy-start.13
  61.4 0.9 copy-start.15
  77.3 8.8 %collective-permute-start.8 = (bf16[16,32,128]{2,1,0:T(8,128)(2,1)S(1)}, bf16[16,32,128]{2,1,0:T(8,128)(2,1)S(1)}, u32[]{:S(2)}, u32[]{:S(2)}) collective-permute-start(bf16[16,32,128]{2,1,0:T(8,128)(2,1)S(1)} %get-tuple-element.90), channel_id=1, source_target_pairs={{0,1},{1,2},{2,3},{3,4},{4,5},{5,6},{6,7},{7,0},{8,9},{9,10},{10,1... | collective-permute-start | bytes 393224 | tf_op jit(solution)/shard_map/ppermute | solution.py:1080
  81.1 6.7 %collective-permute-start.9 = (bf16[16,32,128]{2,1,0:T(8,128)(2,1)S(1)}, bf16[16,32,128]{2,1,0:T(8,128)(2,1)S(1)}, u32[]{:S(2)}, u32[]{:S(2)}) collective-permute-start(bf16[16,32,128]{2,1,0:T(8,128)(2,1)S(1)} %get-tuple-element.91), channel_id=1, source_target_pairs={{1,0},{2,1},{3,2},{4,3},{5,4},{6,5},{7,6},{0,7},{9,8},{10,9},{11,1... | collective-permute-start | bytes 393224 | tf_op jit(solution)/shard_map/ppermute | solution.py:1080
  96.0 20.9 %copy-start.17 = (f32[2,2,36,128]{3,2,1,0:T(8,128)S(1)}, f32[2,2,36,128]{3,2,1,0:T(8,128)}, u32[]{:S(2)}) copy-start(f32[2,2,36,128]{3,2,1,0:T(8,128)} %copy-done.16) | copy-start | bytes 221188
  117.5 6.3 %copy-start.8 = (bf16[512,576]{1,0:T(8,128)(2,1)S(1)}, bf16[512,576]{1,0:T(8,128)(2,1)}, u32[]{:S(2)}) copy-start(bf16[512,576]{1,0:T(8,128)(2,1)} %copy-done.7) | copy-start | bytes 1769476
  117.5 3.1 %collective-permute-start.11 = (bf16[2,2,36,128]{3,2,1,0:T(8,128)(2,1)S(1)}, bf16[2,2,36,128]{3,2,1,0:T(8,128)(2,1)S(1)}, u32[]{:S(2)}, u32[]{:S(2)}) collective-permute-start(bf16[2,2,36,128]{3,2,1,0:T(8,128)(2,1)S(1)} %chain.1.gmid_ref), channel_id=1, source_target_pairs={{8,0},{16,8},{24,16},{32,24},{40,32},{48,40},{56,48},{64,56},{72,6... | collective-permute-start | bytes 110600 | tf_op jit(solution)/shard_map/ppermute | solution.py:1080
  118.2 5.5 %collective-permute-start.10 = (bf16[2,2,36,128]{3,2,1,0:T(8,128)(2,1)S(1)}, bf16[2,2,36,128]{3,2,1,0:T(8,128)(2,1)S(1)}, u32[]{:S(2)}, u32[]{:S(2)}) collective-permute-start(bf16[2,2,36,128]{3,2,1,0:T(8,128)(2,1)S(1)} %chain.1.gmid_ref), channel_id=1, source_target_pairs={{0,8},{8,16},{16,24},{24,32},{32,40},{40,48},{48,56},{56,64},{64,7... | collective-permute-start | bytes 110600 | tf_op jit(solution)/shard_map/ppermute | solution.py:1080
  120.6 28.4 %copy-start.11 = (bf16[128,1152]{1,0:T(8,128)(2,1)S(1)}, bf16[128,1152]{1,0:T(8,128)(2,1)}, u32[]{:S(2)}) copy-start(bf16[128,1152]{1,0:T(8,128)(2,1)} %copy-done.10) | copy-start | bytes 884740
  143.8 14.0 %all-to-all-start.3 = ((f32[128,1,128]{2,1,0:T(1,128)}), f32[128,1,128]{2,1,0:T(1,128)S(1)}, u32[]{:S(2)}, u32[]{:S(2)}) async-start(f32[128,1,128]{2,1,0:T(1,128)} %broadcast_in_dim.5), calls=%async_computation.3 | async-start | bytes 131072 | tf_op jit(solution)/shard_map/all_to_all | solution.py:1128

commit v8 on v7

--- a/solution.py
+++ b/solution.py
@@ -71,10 +71,14 @@
     lax.fori_loop(0, bx + 8, spread, 0, unroll=4)
     last_block = (bx + 6) // 2 - 1
 
-    def first_conv(block, before):
-        before = jnp.tanh(before)
+    def multiply(block):
+        rows = s1[pl.ds(2 * block, 4)].reshape(4 * 288, nz)
+        return jnp.dot(w1_ref[...], rows, preferred_element_type=F32)
+
+    def finish(block, acc):
+        acc = jnp.tanh(acc)
         for xo in range(2):
-            x = jnp.maximum(2 * block - 2, 0) + xo
+            x = 2 * block + xo
             x_fine = ((x >= 3) | (brick > 0)) & ((x < bx + 3) | (brick < bricks - 1))
             for y in range(4):
                 fine = x_fine
@@ -83,15 +87,17 @@
                 if y == 3:
                     fine = fine & (shot < shots - 1)
                 start = (xo * 4 + y) * 16
-                value = jnp.where(fine, before[start : start + 16], 0.0).astype(BF16)
+                value = jnp.where(fine, acc[start : start + 16], 0.0).astype(BF16)
                 hid_ref[x, pl.ds(y * 16, 16), :] = value
                 wide = value.astype(F32)
                 for k in range(3):
                     s2[x, pl.ds(y * 48 + k * 16, 16), :] = lane_shift(wide, k).astype(BF16)
-        rows = s1[pl.ds(2 * jnp.minimum(block, last_block), 4)].reshape(4 * 288, nz)
-        return jnp.dot(w1_ref[...], rows, preferred_element_type=F32)
-
-    lax.fori_loop(0, last_block + 2, first_conv, jnp.zeros((128, nz), F32))
+
+    def first_conv(block, acc):
+        finish(block, acc)
+        return multiply(block + 1)
+
+    finish(last_block, lax.fori_loop(0, last_block, first_conv, multiply(0), unroll=3))
 
     for block in range(gx // 6):
         rows = s2[pl.ds(6 * block, 8)].reshape(8 * 192, nz)
@@ -272,13 +278,14 @@
     )
 
 
-def window_kernel(at_ref, column_ref, win_ref, ahead_ref, behind_ref, message):
-    first_row = at_ref[2]
+def window_kernel(at_ref, column_any, win_ref, ahead_ref, behind_ref, message, ready):
+    fetch = pltpu.make_async_copy(column_any.at[pl.ds(at_ref[2], ay)], win_ref, ready)
+    fetch.start()
+    fetch.wait()
 
     def body(y, carry):
         for channel in range(2):
-            value = column_ref[first_row + y, channel]
-            win_ref[y, channel] = value
+            value = win_ref[y, channel]
             rounded = value.astype(BF16).astype(F32)
             rest = value - rounded
             for slot, (ref, near, further) in enumerate(((ahead_ref, 28, 12), (behind_ref, 0, 4))):
@@ -300,9 +307,9 @@
             jax.ShapeDtypeStruct((ay, 2, 24, nz), BF16),
             jax.ShapeDtypeStruct((ay, 2, 24, nz), BF16),
         ),
-        in_specs=[scalars] + whole(1),
+        in_specs=[scalars, pl.BlockSpec(memory_space=pl.ANY)],
         out_specs=tuple(whole(3)),
-        scratch_shapes=[pltpu.VMEM((96, nz), F32)],
+        scratch_shapes=[pltpu.VMEM((96, nz), F32), pltpu.SemaphoreType.DMA],
         compiler_params=vmem,
         name="take_window",
     )(at, column)
@@ -845,7 +852,7 @@
             own[x].astype(BF16), s2[pl.ds(x, 3)].reshape(576, nz), contract_lanes, preferred_element_type=F32
         )
 
-    second_ref[...] = lax.fori_loop(0, bx, kernel_grad, jnp.zeros((8, 576), F32), unroll=4)
+    second_ref[...] = lax.fori_loop(0, bx, kernel_grad, jnp.zeros((8, 576), F32), unroll=8)
 
 
 def second_grads(grad_output, s2):
@@ -907,7 +914,7 @@
             preferred_element_type=F32,
         )
 
-    first = lax.fori_loop(0, bx, kernel_grad, jnp.zeros((32, 576), F32), unroll=4)
+    first = lax.fori_loop(0, bx, kernel_grad, jnp.zeros((32, 576), F32), unroll=8)
     second = second_ref[...]
     kernel_ref[...] = jnp.zeros(kernel_ref.shape, F32)
     for dx in range(3):

time: 163 us -> 162 us (level)
  Pallas kernels: 55.1 us -> 52.4 us
    ppermute x6, starting transfers between devices: 8.35 us -> 10.4 us  [both_ways(): lax.ppermute(behind, axis, backward_)]
    pallas_call x1, Pallas kernels: 6.95 us -> 4.89 us  [generator(): pl.pallas_call(generator_kernel, out_shape=(jax.ShapeDtypeStruct((2, 2, b...]
    ppermute x6, starting transfers between devices: 11.4 us -> 9.52 us  [both_ways(): lax.ppermute(ahead, axis, forward)]
  transfers between devices with their start and end apart: 14 -> 14, of which waited for: 10 -> 10; matrix products, arithmetic and copies ran while one was open for 2% -> 2% of each run, Pallas kernels for 20% -> 19%
where the time goes in v8:
time: 162 us; the launch traced here: 159 us
  Pallas kernels  52.4 us (32%)
  blocking collectives  36.9 us (23%)
  starting transfers between devices  29.4 us (18%)
  waiting for transfers between devices  24.8 us (15%)
  local copies, waits for them, and re-layouts  13.8 us (9%)
  between operations  1.74 us (1%)
    all_to_all x1, blocking collectives, per_device(): got = lax.all_to_all(grads, 'shot', 0, 0, tiled=True)  21.7 us
    all_to_all x1, blocking collectives, per_device(): slices = lax.all_to_all(kernels, everyone, 0, 0, tiled=True)  15.2 us
    ppermute x6, starting transfers between devices, both_ways(): lax.ppermute(behind, axis, backward_)  10.4 us
    unnamed x66, local copies, waits for them, and re-layouts  10.3 us
    ppermute x6, waiting for transfers between devices, both_ways(): lax.ppermute(ahead, axis, forward)  9.66 us
    ppermute x6, starting transfers between devices, both_ways(): lax.ppermute(ahead, axis, forward)  9.52 us
    pallas_call x1, Pallas kernels, receiver_fields(): pl.pallas_call(receiver_kernel, out_shape=jax.ShapeDtypeStruct((4, ay * d...  9.12 us
    pallas_call x1, Pallas kernels, adjoint_waves(): pl.pallas_call(adjoint_kernel, out_shape=jax.ShapeDtypeStruct((2 * shots,...  8.24 us
  transfers between devices with their start and end apart: 14, of which 10 were waited for; matrix products, arithmetic and copies ran while one was open for 2% of the time, Pallas kernels for 19%

profile of v8, /device:TPU:32, one launch (start us, length us, event | category | flops | bytes accessed | tf_op | source)
XLA Modules:
  0.0 159.2 jit_solution(548115701336752984)
XLA Ops:
  0.6 1.1 copy.57
  1.8 3.1 %collective-permute-start = (bf16[2,4,16,128]{3,2,1,0:T(8,128)(2,1)S(1)}, bf16[2,4,16,128]{3,2,1,0:T(8,128)(2,1)S(1)}, u32[]{:S(2)}, u32[]{:S(2)}) collective-permute-start(bf16[2,4,16,128]{3,2,1,0:T(8,128)(2,1)S(1)} %get-tuple-element.123), channel_id=1, source_target_pairs={{0,1},{1,2},{2,3},{3,4},{4,5},{5,6},{6,7},{7,0},{8,9},{9,10},{10,1... | collective-permute-start | bytes 98312 | tf_op jit(solution)/shard_map/ppermute | solution.py:1087
  4.9 1.4 collective-permute-start.1
  6.3 1.0 copy.56
  7.3 0.9 collective-permute-done
  8.3 2.0 %collective-permute-done.1 = bf16[2,4,16,128]{3,2,1,0:T(8,128)(2,1)S(1)} collective-permute-done((bf16[2,4,16,128]{3,2,1,0:T(8,128)(2,1)S(1)}, bf16[2,4,16,128]{3,2,1,0:T(8,128)(2,1)S(1)}, u32[]{:S(2)}, u32[]{:S(2)}) %collective-permute-start.1) | collective-permute-done | bytes 32800 | tf_op jit(solution)/shard_map/ppermute | solution.py:1087
  10.4 1.4 collective-permute-start.3
  11.8 3.6 %collective-permute-start.5 = (f32[16,24,128]{2,1,0:T(8,128)S(1)}, f32[16,24,128]{2,1,0:T(8,128)S(1)}, u32[]{:S(2)}, u32[]{:S(2)}) collective-permute-start(f32[16,24,128]{2,1,0:T(8,128)S(1)} %get-tuple-element.121), channel_id=1, source_target_pairs={{1,0},{2,1},{3,2},{4,3},{5,4},{6,5},{7,6},{0,7},{9,8},{10,9},{11,1... | collective-permute-start | bytes 589832 | tf_op jit(solution)/shard_map/ppermute | solution.py:1087
  18.0 1.0 forward_bands.1
  19.1 0.8 collective-permute-done.3.hi_ref
  19.9 4.0 %collective-permute-done.2.lo_ref = bf16[2,40,16,128]{3,2,1,0:T(8,128)(2,1)S(1)} collective-permute-done((bf16[2,40,16,128]{3,2,1,0:T(8,128)(2,1)S(1)}, bf16[2,40,16,128]{3,2,1,0:T(8,128)(2,1)S(1)}, u32[]{:S(2)}, u32[]{:S(2)}) %collective-permute-start.2) | collective-permute-done | bytes 327712 | tf_op jit(solution)/shard_map/ppermute | solution.py:1087
  23.9 4.9 %generator.1 = (f32[2,2,32,128]{3,2,1,0:T(8,128)S(1)}, f32[2,2,36,128]{3,2,1,0:T(8,128)S(1)}, bf16[38,64,128]{2,1,0:T(8,128)(2,1)S(1)}) custom-call(s32[3]{0:T(128)S(1)} %pad_add_fusion.at_ref, bf16[2,40,16,128]{3,2,1,0:T(8,128)(2,1)S(1)} %collective-permute-done.2.lo_ref, bf16[2,40,16,128]{3,2,1,0:T(8,128)(2,1)S(1)} %pad_maximum_fusion.mid_ref, ...), custom_call_target="tpu_custom_call" | custom-call | tf_op jit(solution)/shard_map/generator/pallas_call | solution.py:117
  28.8 0.8 copy-done.1
  30.3 1.1 collective-permute-done.4.plo_ref
  31.3 1.1 broadcast_in_dim.4
  32.5 4.3 %all-to-all-start = ((f32[16,2,2,32,128]{4,3,2,1,0:T(8,128)}), f32[16,2,2,32,128]{4,3,2,1,0:T(8,128)}, u32[]{:S(2)}, u32[]{:S(2)}) async-start(f32[16,2,2,32,128]{4,3,2,1,0:T(8,128)} %broadcast_in_dim.4), calls=%async_computation | async-start | bytes 2097152 | tf_op jit(solution)/shard_map/all_to_all | solution.py:1109
  37.1 9.1 %receiver_fields.1.seen_ref = f32[4,1280,128]{2,1,0:T(8,128)S(1)} custom-call(s32[3]{0:T(128)S(1)} %pad_add_fusion.at_ref, s32[3,2048]{1,0:T(4,128)S(1)} %bitcast.42, f32[3,2048]{1,0:T(4,128)S(1)} %bitcast.41), custom_call_target="tpu_custom_call" | custom-call | bytes 27000000 | tf_op jit(solution)/shard_map/receiver_fields/pallas_call | solution.py:181
  46.4 1.3 backward_bands.1
  47.7 0.8 copy-done.7
  48.6 0.7 copy-done.10
  49.3 4.1 %all-to-all-done = f32[16,2,2,32,128]{4,3,2,1,0:T(8,128)} async-done(((f32[16,2,2,32,128]{4,3,2,1,0:T(8,128)}), f32[16,2,2,32,128]{4,3,2,1,0:T(8,128)}, u32[]{:S(2)}, u32[]{:S(2)}) %all-to-all-start) | async-done | bytes 1048608 | tf_op jit(solution)/shard_map/all_to_all | solution.py:1109
  53.4 1.8 %take_window.1 = (f32[16,2,32,128]{3,2,1,0:T(8,128)S(1)}, bf16[16,2,24,128]{3,2,1,0:T(8,128)(2,1)S(1)}, bf16[16,2,24,128]{3,2,1,0:T(8,128)(2,1)S(1)}) custom-call(s32[3]{0:T(128)S(1)} %pad_add_fusion.at_ref, f32[32,2,32,128]{3,2,1,0:T(8,128)} %bitcast.8.column_any), custom_call_target="tpu_custom_call" | custom-call | tf_op jit(solution)/shard_map/take_window/pallas_call | solution.py:303
  55.2 3.0 %collective-permute-start.6 = (bf16[16,2,24,128]{3,2,1,0:T(8,128)(2,1)S(1)}, bf16[16,2,24,128]{3,2,1,0:T(8,128)(2,1)S(1)}, u32[]{:S(2)}, u32[]{:S(2)}) collective-permute-start(bf16[16,2,24,128]{3,2,1,0:T(8,128)(2,1)S(1)} %get-tuple-element.67), channel_id=1, source_target_pairs={{0,1},{1,2},{2,3},{3,4},{4,5},{5,6},{6,7},{7,0},{8,9},{9,10},{10,1... | collective-permute-start | bytes 589832 | tf_op jit(solution)/shard_map/ppermute | solution.py:1087
  58.2 1.5 collective-permute-start.7
  59.7 0.9 copy-done.13
  60.6 0.9 copy-done.15
  61.5 2.1 %source_slopes.1 = (f32[16,64,128]{2,1,0:T(8,128)S(1)}, f32[16,72,128]{2,1,0:T(8,128)S(1)}, f32[17,64,128]{2,1,0:T(8,128)S(1)}, f32[16,64,128]{2,1,0:T(8,128)S(1)}, f32[16,64,128]{2,1,0:T(8,128)S(1)}) custom-call(s32[3]{0:T(128)S(1)} %pad_add_fusion.at_ref, f32[16,32,128]{2,1,0:T(8,128)S(1)} %bitcast.38, f32[16,24,128]{2,1,0:T(8,128)S(1)} %copy-done.15, ...), custom_call_target="tpu_custom_call" | custom-call | bytes 9000000 | tf_op jit(solution)/shard_map/source_slopes/pallas_call | solution.py:439
  63.7 2.4 %spread_fields.1 = (bf16[34,192,128]{2,1,0:T(8,128)(2,1)S(1)}, bf16[34,192,128]{2,1,0:T(8,128)(2,1)S(1)}) custom-call(s32[3]{0:T(128)S(1)} %pad_add_fusion.at_ref, bf16[2,40,16,128]{3,2,1,0:T(8,128)(2,1)S(1)} %copy-done.6, bf16[2,40,16,128]{3,2,1,0:T(8,128)(2,1)S(1)} %pad_maximum_fusion.mid_ref, bf16[2,40,16,128]{3,2,1,0:T(8,128)(2,1)S(1)} %copy-done.4, ...), custom_call_target="tpu_custom_call" | custom-call | bytes 9000000 | tf_op jit(solution)/shard_map/spread_fields/pallas_call | solution.py:830
  66.1 2.6 %collective-permute-done.7.chi_ref = bf16[16,2,24,128]{3,2,1,0:T(8,128)(2,1)S(1)} collective-permute-done((bf16[16,2,24,128]{3,2,1,0:T(8,128)(2,1)S(1)}, bf16[16,2,24,128]{3,2,1,0:T(8,128)(2,1)S(1)}, u32[]{:S(2)}, u32[]{:S(2)}) %collective-permute-start.7) | collective-permute-done | bytes 196640 | tf_op jit(solution)/shard_map/ppermute | solution.py:1087
  68.7 7.9 %forward_waves.1 = (f32[16,64,128]{2,1,0:T(8,128)S(1)}, f32[16,48,128]{2,1,0:T(8,128)S(1)}, f32[16,32,128]{2,1,0:T(8,128)S(1)}, f32[3,16,48,128]{3,2,1,0:T(8,128...) custom-call(s32[3]{0:T(128)S(1)} %pad_add_fusion.at_ref, ...), custom_call_target="tpu_custom_call" | custom-call | tf_op jit(solution)/shard_map/forward_waves/pallas_call | solution.py:565
  76.5 2.9 %collective-permute-start.8 = (bf16[16,32,128]{2,1,0:T(8,128)(2,1)S(1)}, bf16[16,32,128]{2,1,0:T(8,128)(2,1)S(1)}, u32[]{:S(2)}, u32[]{:S(2)}) collective-permute-start(bf16[16,32,128]{2,1,0:T(8,128)(2,1)S(1)} %get-tuple-element.90), channel_id=1, source_target_pairs={{0,1},{1,2},{2,3},{3,4},{4,5},{5,6},{6,7},{7,0},{8,9},{9,10},{10,1... | collective-permute-start | bytes 393224 | tf_op jit(solution)/shard_map/ppermute | solution.py:1087
  79.4 1.8 %collective-permute-start.9 = (bf16[16,32,128]{2,1,0:T(8,128)(2,1)S(1)}, bf16[16,32,128]{2,1,0:T(8,128)(2,1)S(1)}, u32[]{:S(2)}, u32[]{:S(2)}) collective-permute-start(bf16[16,32,128]{2,1,0:T(8,128)(2,1)S(1)} %get-tuple-element.91), channel_id=1, source_target_pairs={{1,0},{2,1},{3,2},{4,3},{5,4},{6,5},{7,6},{0,7},{9,8},{10,9},{11,1... | collective-permute-start | bytes 393224 | tf_op jit(solution)/shard_map/ppermute | solution.py:1087
  81.2 3.8 %wave_slopes.1 = (f32[3,16,48,128]{3,2,1,0:T(8,128)S(1)}, f32[3,17,48,128]{3,2,1,0:T(8,128)S(1)}, f32[3,16,48,128]{3,2,1,0:T(8,128)S(1)}, f32[3,16,48,128]{3,2,1,0:T(8,128)S(1)}) custom-call(f32[16,64,128]{2,1,0:T(8,128)S(1)} %get-tuple-element.81.p1_ref, f32[16,64,128]{2,1,0:T(8,128)S(1)} %get-tuple-element.86.p2_ref, ...), custom_call_target="tpu_custom_call" | custom-call | bytes 18000000 | tf_op jit(solution)/shard_map/wave_slopes/pallas_call | solution.py:611
  85.1 1.2 collective-permute-done.9.front_ref
  86.3 8.2 %adjoint_waves.1 = f32[32,72,128]{2,1,0:T(8,128)S(1)} custom-call(s32[3]{0:T(128)S(1)} %pad_add_fusion.at_ref, f32[16,64,128]{2,1,0:T(8,128)S(1)} %get-tuple-element.86.p2_ref, f32[16,48,128]{2,1,0:T(8,128)S(1)} %get-tuple-element.87.p3_ref, f32[16,32,128]{2,1,0:T(8,128)S(1)} %get-tuple-element.88.p4_ref, ...), custom_call_target="tpu_custom_call" | custom-call | tf_op jit(solution)/shard_map/adjoint_waves/pallas_call | solution.py:761
  94.5 21.7 %all_to_all.25 = f32[32,72,128]{2,1,0:T(8,128)S(1)} all-to-all(f32[32,72,128]{2,1,0:T(8,128)S(1)} %adjoint_waves.1), channel_id=1, replica_groups=mesh['shot'=16,'brick'=8] {'shot'}, dimensions={0} | all-to-all | bytes 2359296 | tf_op jit(solution)/shard_map/all_to_all | solution.py:1123
  116.9 0.7 collective-permute-start.11
  117.6 1.9 %second_grads.1.second_ref = f32[8,576]{1,0:T(8,128)S(1)} custom-call(bf16[2,2,36,128]{3,2,1,0:T(8,128)(2,1)S(1)} %chain.1.gmid_ref, bf16[34,192,128]{2,1,0:T(8,128)(2,1)S(1)} %get-tuple-element.109.s2), custom_call_target="tpu_custom_call" | custom-call | bytes 9000000 | tf_op jit(solution)/shard_map/second_grads/pallas_call | solution.py:859
  119.5 3.7 %collective-permute-done.10.glo_ref = bf16[2,2,36,128]{3,2,1,0:T(8,128)(2,1)S(1)} collective-permute-done((bf16[2,2,36,128]{3,2,1,0:T(8,128)(2,1)S(1)}, bf16[2,2,36,128]{3,2,1,0:T(8,128)(2,1)S(1)}, u32[]{:S(2)}, u32[]{:S(2)}) %collective-permute-start.10) | collective-permute-done | bytes 36896 | tf_op jit(solution)/shard_map/ppermute | solution.py:1087
  123.1 4.0 %first_grads.1 = (bf16[40,64,128]{2,1,0:T(8,128)(2,1)S(1)}, f32[128,128]{1,0:T(8,128)S(1)}) custom-call(s32[3]{0:T(128)S(1)} %pad_add_fusion.at_ref, bf16[2,2,36,128]{3,2,1,0:T(8,128)(2,1)S(1)} %collective-permute-done.10.glo_ref, bf16[2,2,36,128]{3,2,1,0:T(8,128)(2,1)S(1)} %chain.1.gmid_ref, bf16[2,2,36,128]{3,2,1,0:T(8,128)(2,1)S(1)} %collective-permute-done.11.ghi_ref, ...), custom_call_target="tpu_custom_call" | custom-call | tf_op jit(solution)/shard_map/first_grads/pallas_call | solution.py:937
  127.1 15.2 %all_to_all.26 = f32[128,1,128]{2,1,0:T(1,128)S(1)} all-to-all(f32[128,1,128]{2,1,0:T(1,128)S(1)} %bitcast.43), channel_id=1, replica_groups=mesh['shot'=16,'brick'=8] {'shot','brick'}, dimensions={0} | all-to-all | bytes 131072 | tf_op jit(solution)/shard_map/all_to_all | solution.py:1133
  142.4 0.7 broadcast_in_dim.5
  143.0 5.2 %all-to-all-start.3 = ((f32[128,1,128]{2,1,0:T(1,128)}), f32[128,1,128]{2,1,0:T(1,128)S(1)}, u32[]{:S(2)}, u32[]{:S(2)}) async-start(f32[128,1,128]{2,1,0:T(1,128)} %broadcast_in_dim.5), calls=%async_computation.3 | async-start | bytes 131072 | tf_op jit(solution)/shard_map/all_to_all | solution.py:1135
  148.2 3.4 %latent_grads.1 = f32[32,32,128]{2,1,0:T(8,128)S(1)} custom-call(bf16[40,64,128]{2,1,0:T(8,128)(2,1)S(1)} %get-tuple-element.112.inner_ref, bf16[128,1152]{1,0:T(8,128)(2,1)S(1)} %copy-done.11), custom_call_target="tpu_custom_call" | custom-call | bytes 12000000 | tf_op jit(solution)/shard_map/latent_grads/pallas_call | solution.py:975
  151.6 1.1 copy.55
  152.6 4.4 %all-to-all-done.3 = f32[128,1,128]{2,1,0:T(1,128)S(1)} async-done(((f32[128,1,128]{2,1,0:T(1,128)}), f32[128,1,128]{2,1,0:T(1,128)S(1)}, u32[]{:S(2)}, u32[]{:S(2)}) %all-to-all-start.3) | async-done | bytes 65568 | tf_op jit(solution)/shard_map/all_to_all | solution.py:1135
  157.6 0.8 copy.44
  158.4 0.8 copy.45
  (78 shorter events, 4.3 us)
Async XLA Ops:
  1.8 14.8 %copy-start.27 = (bf16[27,2,16]{0,2,1:T(8,128)(2,1)S(1)}, bf16[27,2,16]{0,2,1:T(8,128)(2,1)}, u32[]{:S(2)}) copy-start(bf16[27,2,16]{0,2,1:T(8,128)(2,1)} %param.15) | copy-start | bytes 5188
  1.8 15.9 %copy-start.24 = (bf16[27,16,16]{0,2,1:T(8,128)(2,1)S(1)}, bf16[27,16,16]{0,2,1:T(8,128)(2,1)}, u32[]{:S(2)}) copy-start(bf16[27,16,16]{0,2,1:T(8,128)(2,1)} %param.14) | copy-start | bytes 41476
  1.8 6.5 %collective-permute-start = (bf16[2,4,16,128]{3,2,1,0:T(8,128)(2,1)S(1)}, bf16[2,4,16,128]{3,2,1,0:T(8,128)(2,1)S(1)}, u32[]{:S(2)}, u32[]{:S(2)}) collective-permute-start(bf16[2,4,16,128]{3,2,1,0:T(8,128)(2,1)S(1)} %get-tuple-element.123), channel_id=1, source_target_pairs={{0,1},{1,2},{2,3},{3,4},{4,5},{5,6},{6,7},{7,0},{8,9},{9,10},{10,1... | collective-permute-start | bytes 98312 | tf_op jit(solution)/shard_map/ppermute | solution.py:1087
  4.9 13.1 %copy-start.18 = (s32[2,1536]{1,0:T(2,128)S(1)}, s32[2,1536]{1,0:T(2,128)}, u32[]{:S(2)}) copy-start(s32[2,1536]{1,0:T(2,128)} %constant.27.clone.codes_2_ref) | copy-start | bytes 36868
  4.9 13.1 %copy-start.20 = (s32[2,1152]{1,0:T(2,128)S(1)}, s32[2,1152]{1,0:T(2,128)}, u32[]{:S(2)}) copy-start(s32[2,1152]{1,0:T(2,128)} %constant.26.clone.codes_1_ref) | copy-start | bytes 27652
  4.9 5.4 %collective-permute-start.1 = (bf16[2,4,16,128]{3,2,1,0:T(8,128)(2,1)S(1)}, bf16[2,4,16,128]{3,2,1,0:T(8,128)(2,1)S(1)}, u32[]{:S(2)}, u32[]{:S(2)}) collective-permute-start(bf16[2,4,16,128]{3,2,1,0:T(8,128)(2,1)S(1)} %get-tuple-element.124), channel_id=1, source_target_pairs={{1,0},{2,1},{3,2},{4,3},{5,4},{6,5},{7,6},{0,7},{9,8},{10,9},{11,1... | collective-permute-start | bytes 98312 | tf_op jit(solution)/shard_map/ppermute | solution.py:1087
  10.4 9.5 %collective-permute-start.3 = (bf16[2,40,16,128]{3,2,1,0:T(8,128)(2,1)S(1)}, bf16[2,40,16,128]{3,2,1,0:T(8,128)(2,1)S(1)}, u32[]{:S(2)}, u32[]{:S(2)}) collective-permute-start(bf16[2,40,16,128]{3,2,1,0:T(8,128)(2,1)S(1)} %pad_maximum_fusion.mid_ref), channel_id=1, source_target_pairs={{8,0},{16,8},{24,16},{32,24},{40,32},{48,40},{56,48},{64,56},{72,6... | collective-permute-start | bytes 983048 | tf_op jit(solution)/shard_map/ppermute | solution.py:1087
  11.8 12.1 %collective-permute-start.2 = (bf16[2,40,16,128]{3,2,1,0:T(8,128)(2,1)S(1)}, bf16[2,40,16,128]{3,2,1,0:T(8,128)(2,1)S(1)}, u32[]{:S(2)}, u32[]{:S(2)}) collective-permute-start(bf16[2,40,16,128]{3,2,1,0:T(8,128)(2,1)S(1)} %pad_maximum_fusion.mid_ref), channel_id=1, source_target_pairs={{0,8},{8,16},{16,24},{24,32},{32,40},{40,48},{48,56},{56,64},{64,7... | collective-permute-start | bytes 983048 | tf_op jit(solution)/shard_map/ppermute | solution.py:1087
  11.8 18.5 %collective-permute-start.5 = (f32[16,24,128]{2,1,0:T(8,128)S(1)}, f32[16,24,128]{2,1,0:T(8,128)S(1)}, u32[]{:S(2)}, u32[]{:S(2)}) collective-permute-start(f32[16,24,128]{2,1,0:T(8,128)S(1)} %get-tuple-element.121), channel_id=1, source_target_pairs={{1,0},{2,1},{3,2},{4,3},{5,4},{6,5},{7,6},{0,7},{9,8},{10,9},{11,1... | collective-permute-start | bytes 589832 | tf_op jit(solution)/shard_map/ppermute | solution.py:1087
  15.4 15.9 %collective-permute-start.4 = (f32[16,24,128]{2,1,0:T(8,128)S(1)}, f32[16,24,128]{2,1,0:T(8,128)S(1)}, u32[]{:S(2)}, u32[]{:S(2)}) collective-permute-start(f32[16,24,128]{2,1,0:T(8,128)S(1)} %get-tuple-element.122), channel_id=1, source_target_pairs={{0,1},{1,2},{2,3},{3,4},{4,5},{5,6},{6,7},{7,0},{8,9},{9,10},{10,1... | collective-permute-start | bytes 589832 | tf_op jit(solution)/shard_map/ppermute | solution.py:1087
  16.8 0.6 copy-start.22
  19.9 12.6 %copy-start.3 = (bf16[2,40,16,128]{3,2,1,0:T(8,128)(2,1)}, bf16[2,40,16,128]{3,2,1,0:T(8,128)(2,1)S(1)}, u32[]{:S(2)}) copy-start(bf16[2,40,16,128]{3,2,1,0:T(8,128)(2,1)S(1)} %collective-permute-done.3.hi_ref) | copy-start | bytes 983044
  23.9 8.6 %copy-start.5 = (bf16[2,40,16,128]{3,2,1,0:T(8,128)(2,1)}, bf16[2,40,16,128]{3,2,1,0:T(8,128)(2,1)S(1)}, u32[]{:S(2)}) copy-start(bf16[2,40,16,128]{3,2,1,0:T(8,128)(2,1)S(1)} %collective-permute-done.2.lo_ref) | copy-start | bytes 983044
  28.8 0.8 copy-start.1
  29.6 0.6 copy-start.16
  30.3 2.2 %copy-start.12 = (f32[16,24,128]{2,1,0:T(8,128)}, f32[16,24,128]{2,1,0:T(8,128)S(1)}, u32[]{:S(2)}) copy-start(f32[16,24,128]{2,1,0:T(8,128)S(1)} %collective-permute-done.5.phi_ref) | copy-start | bytes 589828
  31.3 1.2 copy-start.14
  32.5 4.6 %copy-start.25 = (f32[1,3,2048]{2,0,1:T(1,128)S(1)}, f32[1,3,2048]{2,0,1:T(1,128)}, u32[]{:S(2)}) copy-start(f32[1,3,2048]{2,0,1:T(1,128)} %param.17) | copy-start | bytes 73732
  32.5 4.6 %copy-start.26 = (s32[1,3,2048]{2,0,1:T(1,128)S(1)}, s32[1,3,2048]{2,0,1:T(1,128)}, u32[]{:S(2)}) copy-start(s32[1,3,2048]{2,0,1:T(1,128)} %param.19) | copy-start | bytes 73732
  32.5 20.9 %all-to-all-start = ((f32[16,2,2,32,128]{4,3,2,1,0:T(8,128)}), f32[16,2,2,32,128]{4,3,2,1,0:T(8,128)}, u32[]{:S(2)}, u32[]{:S(2)}) async-start(f32[16,2,2,32,128]{4,3,2,1,0:T(8,128)} %broadcast_in_dim.4), calls=%async_computation | async-start | bytes 2097152 | tf_op jit(solution)/shard_map/all_to_all | solution.py:1109
  37.1 9.2 %copy-start.23 = (bf16[27,2,16]{1,2,0:T(8,128)(2,1)S(1)}, bf16[27,2,16]{1,2,0:T(8,128)(2,1)}, u32[]{:S(2)}) copy-start(bf16[27,2,16]{1,2,0:T(8,128)(2,1)} %copy-done.22) | copy-start | bytes 5188
  37.1 9.2 %copy-start.19 = (s32[2,1152]{1,0:T(2,128)S(1)}, s32[2,1152]{1,0:T(2,128)}, u32[]{:S(2)}) copy-start(s32[2,1152]{1,0:T(2,128)} %constant.29.clone.codes_4_ref) | copy-start | bytes 27652
  37.1 9.2 %copy-start.21 = (s32[2,576]{1,0:T(2,128)S(1)}, s32[2,576]{1,0:T(2,128)}, u32[]{:S(2)}) copy-start(s32[2,576]{1,0:T(2,128)} %constant.28.clone.codes_3_ref) | copy-start | bytes 13828
  46.3 13.4 %copy-start = (bf16[384,256]{1,0:T(8,128)(2,1)S(1)}, bf16[384,256]{1,0:T(8,128)(2,1)}, u32[]{:S(2)}) copy-start(bf16[384,256]{1,0:T(8,128)(2,1)} %constant.30.clone.slope_ref) | copy-start | bytes 589828
  47.7 0.9 copy-start.7
  48.6 0.7 copy-start.10
  53.4 10.2 %copy-start.2 = (bf16[38,64,128]{2,1,0:T(8,128)(2,1)S(1)}, bf16[38,64,128]{2,1,0:T(8,128)(2,1)}, u32[]{:S(2)}) copy-start(bf16[38,64,128]{2,1,0:T(8,128)(2,1)} %copy-done.1) | copy-start | bytes 1867780
  53.4 10.2 %copy-start.4 = (bf16[2,40,16,128]{3,2,1,0:T(8,128)(2,1)S(1)}, bf16[2,40,16,128]{3,2,1,0:T(8,128)(2,1)}, u32[]{:S(2)}) copy-start(bf16[2,40,16,128]{3,2,1,0:T(8,128)(2,1)} %copy-done.3) | copy-start | bytes 983044
  53.4 10.3 %copy-start.6 = (bf16[2,40,16,128]{3,2,1,0:T(8,128)(2,1)S(1)}, bf16[2,40,16,128]{3,2,1,0:T(8,128)(2,1)}, u32[]{:S(2)}) copy-start(bf16[2,40,16,128]{3,2,1,0:T(8,128)(2,1)} %copy-done.5) | copy-start | bytes 983044
  55.2 10.9 %collective-permute-start.6 = (bf16[16,2,24,128]{3,2,1,0:T(8,128)(2,1)S(1)}, bf16[16,2,24,128]{3,2,1,0:T(8,128)(2,1)S(1)}, u32[]{:S(2)}, u32[]{:S(2)}) collective-permute-start(bf16[16,2,24,128]{3,2,1,0:T(8,128)(2,1)S(1)} %get-tuple-element.67), channel_id=1, source_target_pairs={{0,1},{1,2},{2,3},{3,4},{4,5},{5,6},{6,7},{7,0},{8,9},{9,10},{10,1... | collective-permute-start | bytes 589832 | tf_op jit(solution)/shard_map/ppermute | solution.py:1087
  58.2 10.5 %copy-start.9 = (bf16[384,128]{1,0:T(8,128)(2,1)S(1)}, bf16[384,128]{1,0:T(8,128)(2,1)}, u32[]{:S(2)}) copy-start(bf16[384,128]{1,0:T(8,128)(2,1)} %constant.31.clone.spread_ref) | copy-start | bytes 294916
  58.2 10.5 %collective-permute-start.7 = (bf16[16,2,24,128]{3,2,1,0:T(8,128)(2,1)S(1)}, bf16[16,2,24,128]{3,2,1,0:T(8,128)(2,1)S(1)}, u32[]{:S(2)}, u32[]{:S(2)}) collective-permute-start(bf16[16,2,24,128]{3,2,1,0:T(8,128)(2,1)S(1)} %get-tuple-element.68), channel_id=1, source_target_pairs={{1,0},{2,1},{3,2},{4,3},{5,4},{6,5},{7,6},{0,7},{9,8},{10,9},{11,1... | collective-permute-start | bytes 589832 | tf_op jit(solution)/shard_map/ppermute | solution.py:1087
  59.7 0.9 copy-start.13
  60.6 0.9 copy-start.15
  76.5 8.5 %collective-permute-start.8 = (bf16[16,32,128]{2,1,0:T(8,128)(2,1)S(1)}, bf16[16,32,128]{2,1,0:T(8,128)(2,1)S(1)}, u32[]{:S(2)}, u32[]{:S(2)}) collective-permute-start(bf16[16,32,128]{2,1,0:T(8,128)(2,1)S(1)} %get-tuple-element.90), channel_id=1, source_target_pairs={{0,1},{1,2},{2,3},{3,4},{4,5},{5,6},{6,7},{7,0},{8,9},{9,10},{10,1... | collective-permute-start | bytes 393224 | tf_op jit(solution)/shard_map/ppermute | solution.py:1087
  79.4 6.8 %collective-permute-start.9 = (bf16[16,32,128]{2,1,0:T(8,128)(2,1)S(1)}, bf16[16,32,128]{2,1,0:T(8,128)(2,1)S(1)}, u32[]{:S(2)}, u32[]{:S(2)}) collective-permute-start(bf16[16,32,128]{2,1,0:T(8,128)(2,1)S(1)} %get-tuple-element.91), channel_id=1, source_target_pairs={{1,0},{2,1},{3,2},{4,3},{5,4},{6,5},{7,6},{0,7},{9,8},{10,9},{11,1... | collective-permute-start | bytes 393224 | tf_op jit(solution)/shard_map/ppermute | solution.py:1087
  94.5 21.7 %copy-start.17 = (f32[2,2,36,128]{3,2,1,0:T(8,128)S(1)}, f32[2,2,36,128]{3,2,1,0:T(8,128)}, u32[]{:S(2)}) copy-start(f32[2,2,36,128]{3,2,1,0:T(8,128)} %copy-done.16) | copy-start | bytes 221188
  116.8 6.3 %copy-start.8 = (bf16[512,576]{1,0:T(8,128)(2,1)S(1)}, bf16[512,576]{1,0:T(8,128)(2,1)}, u32[]{:S(2)}) copy-start(bf16[512,576]{1,0:T(8,128)(2,1)} %copy-done.7) | copy-start | bytes 1769476
  116.9 2.6 %collective-permute-start.11 = (bf16[2,2,36,128]{3,2,1,0:T(8,128)(2,1)S(1)}, bf16[2,2,36,128]{3,2,1,0:T(8,128)(2,1)S(1)}, u32[]{:S(2)}, u32[]{:S(2)}) collective-permute-start(bf16[2,2,36,128]{3,2,1,0:T(8,128)(2,1)S(1)} %chain.1.gmid_ref), channel_id=1, source_target_pairs={{8,0},{16,8},{24,16},{32,24},{40,32},{48,40},{56,48},{64,56},{72,6... | collective-permute-start | bytes 110600 | tf_op jit(solution)/shard_map/ppermute | solution.py:1087
  117.6 5.5 %collective-permute-start.10 = (bf16[2,2,36,128]{3,2,1,0:T(8,128)(2,1)S(1)}, bf16[2,2,36,128]{3,2,1,0:T(8,128)(2,1)S(1)}, u32[]{:S(2)}, u32[]{:S(2)}) collective-permute-start(bf16[2,2,36,128]{3,2,1,0:T(8,128)(2,1)S(1)} %chain.1.gmid_ref), channel_id=1, source_target_pairs={{0,8},{8,16},{16,24},{24,32},{32,40},{40,48},{48,56},{56,64},{64,7... | collective-permute-start | bytes 110600 | tf_op jit(solution)/shard_map/ppermute | solution.py:1087
  119.4 28.8 %copy-start.11 = (bf16[128,1152]{1,0:T(8,128)(2,1)S(1)}, bf16[128,1152]{1,0:T(8,128)(2,1)}, u32[]{:S(2)}) copy-start(bf16[128,1152]{1,0:T(8,128)(2,1)} %copy-done.10) | copy-start | bytes 884740
  143.0 14.0 %all-to-all-start.3 = ((f32[128,1,128]{2,1,0:T(1,128)}), f32[128,1,128]{2,1,0:T(1,128)S(1)}, u32[]{:S(2)}, u32[]{:S(2)}) async-start(f32[128,1,128]{2,1,0:T(1,128)} %broadcast_in_dim.5), calls=%async_computation.3 | async-start | bytes 131072 | tf_op jit(solution)/shard_map/all_to_all | solution.py:1135

commit v9 on v8

--- a/solution.py
+++ b/solution.py
@@ -97,7 +97,7 @@
         finish(block, acc)
         return multiply(block + 1)
 
-    finish(last_block, lax.fori_loop(0, last_block, first_conv, multiply(0), unroll=3))
+    finish(last_block, lax.fori_loop(0, last_block, first_conv, multiply(0), unroll=6))
 
     for block in range(gx // 6):
         rows = s2[pl.ds(6 * block, 8)].reshape(8 * 192, nz)
@@ -725,7 +725,7 @@
         cross_third(0, 0)(y, *slopes_z(rows_of(scaled, y + 4, group, lead + 16, 48), slope_ref))
         return carry
 
-    lax.fori_loop(0, ay // group, last_third, 0)
+    lax.fori_loop(0, ay // group, last_third, 0, unroll=4)
 
     def last_slopes(y, carry):
         cross(0, 0)(y, *slopes_xy(scaled, y, 16, 48))

time: 162 us -> 161 us (level)
  no operation moved by 1% of the time
where the time goes in v9:
time: 161 us; the launch traced here: 159 us
  Pallas kernels  51.4 us (32%)
  blocking collectives  36.9 us (23%)
  starting transfers between devices  29.3 us (18%)
  waiting for transfers between devices  25.2 us (16%)
  local copies, waits for them, and re-layouts  13.8 us (9%)
  between operations  1.74 us (1%)
    all_to_all x1, blocking collectives, per_device(): got = lax.all_to_all(grads, 'shot', 0, 0, tiled=True)  21.7 us
    all_to_all x1, blocking collectives, per_device(): slices = lax.all_to_all(kernels, everyone, 0, 0, tiled=True)  15.2 us
    ppermute x6, starting transfers between devices, both_ways(): lax.ppermute(behind, axis, backward_)  11.3 us
    unnamed x66, local copies, waits for them, and re-layouts  10.3 us
    ppermute x6, waiting for transfers between devices, both_ways(): lax.ppermute(ahead, axis, forward)  10.1 us
    pallas_call x1, Pallas kernels, receiver_fields(): pl.pallas_call(receiver_kernel, out_shape=jax.ShapeDtypeStruct((4, ay * d...  9.12 us
    ppermute x6, starting transfers between devices, both_ways(): lax.ppermute(ahead, axis, forward)  8.43 us
    pallas_call x1, Pallas kernels, forward_waves(): pl.pallas_call(forward_kernel, out_shape=tuple((jax.ShapeDtypeStruct(shap...  7.86 us
  transfers between devices with their start and end apart: 14, of which 10 were waited for; matrix products, arithmetic and copies ran while one was open for 2% of the time, Pallas kernels for 19%

profile of v9, /device:TPU:32, one launch (start us, length us, event | category | flops | bytes accessed | tf_op | source)
XLA Modules:
  0.0 158.6 jit_solution(11760825810415848429)
XLA Ops:
  0.6 1.1 copy.57
  1.8 3.1 %collective-permute-start = (bf16[2,4,16,128]{3,2,1,0:T(8,128)(2,1)S(1)}, bf16[2,4,16,128]{3,2,1,0:T(8,128)(2,1)S(1)}, u32[]{:S(2)}, u32[]{:S(2)}) collective-permute-start(bf16[2,4,16,128]{3,2,1,0:T(8,128)(2,1)S(1)} %get-tuple-element.123), channel_id=1, source_target_pairs={{0,1},{1,2},{2,3},{3,4},{4,5},{5,6},{6,7},{7,0},{8,9},{9,10},{10,1... | collective-permute-start | bytes 98312 | tf_op jit(solution)/shard_map/ppermute | solution.py:1087
  4.9 1.4 collective-permute-start.1
  6.3 1.0 copy.56
  7.3 0.9 collective-permute-done
  8.3 2.0 %collective-permute-done.1 = bf16[2,4,16,128]{3,2,1,0:T(8,128)(2,1)S(1)} collective-permute-done((bf16[2,4,16,128]{3,2,1,0:T(8,128)(2,1)S(1)}, bf16[2,4,16,128]{3,2,1,0:T(8,128)(2,1)S(1)}, u32[]{:S(2)}, u32[]{:S(2)}) %collective-permute-start.1) | collective-permute-done | bytes 32800 | tf_op jit(solution)/shard_map/ppermute | solution.py:1087
  10.4 1.4 collective-permute-start.3
  11.8 3.6 %collective-permute-start.5 = (f32[16,24,128]{2,1,0:T(8,128)S(1)}, f32[16,24,128]{2,1,0:T(8,128)S(1)}, u32[]{:S(2)}, u32[]{:S(2)}) collective-permute-start(f32[16,24,128]{2,1,0:T(8,128)S(1)} %get-tuple-element.121), channel_id=1, source_target_pairs={{1,0},{2,1},{3,2},{4,3},{5,4},{6,5},{7,6},{0,7},{9,8},{10,9},{11,1... | collective-permute-start | bytes 589832 | tf_op jit(solution)/shard_map/ppermute | solution.py:1087
  18.0 1.0 forward_bands.1
  19.1 0.8 collective-permute-done.3.hi_ref
  19.9 4.0 %collective-permute-done.2.lo_ref = bf16[2,40,16,128]{3,2,1,0:T(8,128)(2,1)S(1)} collective-permute-done((bf16[2,40,16,128]{3,2,1,0:T(8,128)(2,1)S(1)}, bf16[2,40,16,128]{3,2,1,0:T(8,128)(2,1)S(1)}, u32[]{:S(2)}, u32[]{:S(2)}) %collective-permute-start.2) | collective-permute-done | bytes 327712 | tf_op jit(solution)/shard_map/ppermute | solution.py:1087
  23.9 4.4 %generator.1 = (f32[2,2,32,128]{3,2,1,0:T(8,128)S(1)}, f32[2,2,36,128]{3,2,1,0:T(8,128)S(1)}, bf16[38,64,128]{2,1,0:T(8,128)(2,1)S(1)}) custom-call(s32[3]{0:T(128)S(1)} %pad_add_fusion.at_ref, bf16[2,40,16,128]{3,2,1,0:T(8,128)(2,1)S(1)} %collective-permute-done.2.lo_ref, bf16[2,40,16,128]{3,2,1,0:T(8,128)(2,1)S(1)} %pad_maximum_fusion.mid_ref, ...), custom_call_target="tpu_custom_call" | custom-call | tf_op jit(solution)/shard_map/generator/pallas_call | solution.py:117
  28.4 0.8 copy-done.1
  29.8 1.5 collective-permute-done.4.plo_ref
  31.3 1.1 broadcast_in_dim.4
  32.5 4.3 %all-to-all-start = ((f32[16,2,2,32,128]{4,3,2,1,0:T(8,128)}), f32[16,2,2,32,128]{4,3,2,1,0:T(8,128)}, u32[]{:S(2)}, u32[]{:S(2)}) async-start(f32[16,2,2,32,128]{4,3,2,1,0:T(8,128)} %broadcast_in_dim.4), calls=%async_computation | async-start | bytes 2097152 | tf_op jit(solution)/shard_map/all_to_all | solution.py:1109
  37.1 9.1 %receiver_fields.1.seen_ref = f32[4,1280,128]{2,1,0:T(8,128)S(1)} custom-call(s32[3]{0:T(128)S(1)} %pad_add_fusion.at_ref, s32[3,2048]{1,0:T(4,128)S(1)} %bitcast.42, f32[3,2048]{1,0:T(4,128)S(1)} %bitcast.41), custom_call_target="tpu_custom_call" | custom-call | bytes 27000000 | tf_op jit(solution)/shard_map/receiver_fields/pallas_call | solution.py:181
  46.4 1.3 backward_bands.1
  47.7 0.8 copy-done.7
  48.6 0.7 copy-done.10
  49.3 4.1 %all-to-all-done = f32[16,2,2,32,128]{4,3,2,1,0:T(8,128)} async-done(((f32[16,2,2,32,128]{4,3,2,1,0:T(8,128)}), f32[16,2,2,32,128]{4,3,2,1,0:T(8,128)}, u32[]{:S(2)}, u32[]{:S(2)}) %all-to-all-start) | async-done | bytes 1048608 | tf_op jit(solution)/shard_map/all_to_all | solution.py:1109
  53.4 1.8 %take_window.1 = (f32[16,2,32,128]{3,2,1,0:T(8,128)S(1)}, bf16[16,2,24,128]{3,2,1,0:T(8,128)(2,1)S(1)}, bf16[16,2,24,128]{3,2,1,0:T(8,128)(2,1)S(1)}) custom-call(s32[3]{0:T(128)S(1)} %pad_add_fusion.at_ref, f32[32,2,32,128]{3,2,1,0:T(8,128)} %bitcast.8.column_any), custom_call_target="tpu_custom_call" | custom-call | tf_op jit(solution)/shard_map/take_window/pallas_call | solution.py:303
  55.2 2.5 %collective-permute-start.6 = (bf16[16,2,24,128]{3,2,1,0:T(8,128)(2,1)S(1)}, bf16[16,2,24,128]{3,2,1,0:T(8,128)(2,1)S(1)}, u32[]{:S(2)}, u32[]{:S(2)}) collective-permute-start(bf16[16,2,24,128]{3,2,1,0:T(8,128)(2,1)S(1)} %get-tuple-element.67), channel_id=1, source_target_pairs={{0,1},{1,2},{2,3},{3,4},{4,5},{5,6},{6,7},{7,0},{8,9},{9,10},{10,1... | collective-permute-start | bytes 589832 | tf_op jit(solution)/shard_map/ppermute | solution.py:1087
  57.7 1.9 %collective-permute-start.7 = (bf16[16,2,24,128]{3,2,1,0:T(8,128)(2,1)S(1)}, bf16[16,2,24,128]{3,2,1,0:T(8,128)(2,1)S(1)}, u32[]{:S(2)}, u32[]{:S(2)}) collective-permute-start(bf16[16,2,24,128]{3,2,1,0:T(8,128)(2,1)S(1)} %get-tuple-element.68), channel_id=1, source_target_pairs={{1,0},{2,1},{3,2},{4,3},{5,4},{6,5},{7,6},{0,7},{9,8},{10,9},{11,1... | collective-permute-start | bytes 589832 | tf_op jit(solution)/shard_map/ppermute | solution.py:1087
  59.7 0.9 copy-done.13
  60.6 0.9 copy-done.15
  61.5 2.1 %source_slopes.1 = (f32[16,64,128]{2,1,0:T(8,128)S(1)}, f32[16,72,128]{2,1,0:T(8,128)S(1)}, f32[17,64,128]{2,1,0:T(8,128)S(1)}, f32[16,64,128]{2,1,0:T(8,128)S(1)}, f32[16,64,128]{2,1,0:T(8,128)S(1)}) custom-call(s32[3]{0:T(128)S(1)} %pad_add_fusion.at_ref, f32[16,32,128]{2,1,0:T(8,128)S(1)} %bitcast.38, f32[16,24,128]{2,1,0:T(8,128)S(1)} %copy-done.15, ...), custom_call_target="tpu_custom_call" | custom-call | bytes 9000000 | tf_op jit(solution)/shard_map/source_slopes/pallas_call | solution.py:439
  63.7 2.4 %spread_fields.1 = (bf16[34,192,128]{2,1,0:T(8,128)(2,1)S(1)}, bf16[34,192,128]{2,1,0:T(8,128)(2,1)S(1)}) custom-call(s32[3]{0:T(128)S(1)} %pad_add_fusion.at_ref, bf16[2,40,16,128]{3,2,1,0:T(8,128)(2,1)S(1)} %copy-done.6, bf16[2,40,16,128]{3,2,1,0:T(8,128)(2,1)S(1)} %pad_maximum_fusion.mid_ref, bf16[2,40,16,128]{3,2,1,0:T(8,128)(2,1)S(1)} %copy-done.4, ...), custom_call_target="tpu_custom_call" | custom-call | bytes 9000000 | tf_op jit(solution)/shard_map/spread_fields/pallas_call | solution.py:830
  66.1 2.6 %collective-permute-done.7.chi_ref = bf16[16,2,24,128]{3,2,1,0:T(8,128)(2,1)S(1)} collective-permute-done((bf16[16,2,24,128]{3,2,1,0:T(8,128)(2,1)S(1)}, bf16[16,2,24,128]{3,2,1,0:T(8,128)(2,1)S(1)}, u32[]{:S(2)}, u32[]{:S(2)}) %collective-permute-start.7) | collective-permute-done | bytes 196640 | tf_op jit(solution)/shard_map/ppermute | solution.py:1087
  68.7 7.9 %forward_waves.1 = (f32[16,64,128]{2,1,0:T(8,128)S(1)}, f32[16,48,128]{2,1,0:T(8,128)S(1)}, f32[16,32,128]{2,1,0:T(8,128)S(1)}, f32[3,16,48,128]{3,2,1,0:T(8,128...) custom-call(s32[3]{0:T(128)S(1)} %pad_add_fusion.at_ref, ...), custom_call_target="tpu_custom_call" | custom-call | tf_op jit(solution)/shard_map/forward_waves/pallas_call | solution.py:565
  76.5 2.2 %collective-permute-start.8 = (bf16[16,32,128]{2,1,0:T(8,128)(2,1)S(1)}, bf16[16,32,128]{2,1,0:T(8,128)(2,1)S(1)}, u32[]{:S(2)}, u32[]{:S(2)}) collective-permute-start(bf16[16,32,128]{2,1,0:T(8,128)(2,1)S(1)} %get-tuple-element.90), channel_id=1, source_target_pairs={{0,1},{1,2},{2,3},{3,4},{4,5},{5,6},{6,7},{7,0},{8,9},{9,10},{10,1... | collective-permute-start | bytes 393224 | tf_op jit(solution)/shard_map/ppermute | solution.py:1087
  78.8 2.2 %collective-permute-start.9 = (bf16[16,32,128]{2,1,0:T(8,128)(2,1)S(1)}, bf16[16,32,128]{2,1,0:T(8,128)(2,1)S(1)}, u32[]{:S(2)}, u32[]{:S(2)}) collective-permute-start(bf16[16,32,128]{2,1,0:T(8,128)(2,1)S(1)} %get-tuple-element.91), channel_id=1, source_target_pairs={{1,0},{2,1},{3,2},{4,3},{5,4},{6,5},{7,6},{0,7},{9,8},{10,9},{11,1... | collective-permute-start | bytes 393224 | tf_op jit(solution)/shard_map/ppermute | solution.py:1087
  81.0 3.8 %wave_slopes.1 = (f32[3,16,48,128]{3,2,1,0:T(8,128)S(1)}, f32[3,17,48,128]{3,2,1,0:T(8,128)S(1)}, f32[3,16,48,128]{3,2,1,0:T(8,128)S(1)}, f32[3,16,48,128]{3,2,1,0:T(8,128)S(1)}) custom-call(f32[16,64,128]{2,1,0:T(8,128)S(1)} %get-tuple-element.81.p1_ref, f32[16,64,128]{2,1,0:T(8,128)S(1)} %get-tuple-element.86.p2_ref, ...), custom_call_target="tpu_custom_call" | custom-call | bytes 18000000 | tf_op jit(solution)/shard_map/wave_slopes/pallas_call | solution.py:611
  84.9 1.2 collective-permute-done.9.front_ref
  86.1 7.8 %adjoint_waves.1 = f32[32,72,128]{2,1,0:T(8,128)S(1)} custom-call(s32[3]{0:T(128)S(1)} %pad_add_fusion.at_ref, f32[16,64,128]{2,1,0:T(8,128)S(1)} %get-tuple-element.86.p2_ref, f32[16,48,128]{2,1,0:T(8,128)S(1)} %get-tuple-element.87.p3_ref, f32[16,32,128]{2,1,0:T(8,128)S(1)} %get-tuple-element.88.p4_ref, ...), custom_call_target="tpu_custom_call" | custom-call | tf_op jit(solution)/shard_map/adjoint_waves/pallas_call | solution.py:761
  93.9 21.7 %all_to_all.25 = f32[32,72,128]{2,1,0:T(8,128)S(1)} all-to-all(f32[32,72,128]{2,1,0:T(8,128)S(1)} %adjoint_waves.1), channel_id=1, replica_groups=mesh['shot'=16,'brick'=8] {'shot'}, dimensions={0} | all-to-all | bytes 2359296 | tf_op jit(solution)/shard_map/all_to_all | solution.py:1123
  116.2 0.7 collective-permute-start.11
  116.9 1.9 %second_grads.1.second_ref = f32[8,576]{1,0:T(8,128)S(1)} custom-call(bf16[2,2,36,128]{3,2,1,0:T(8,128)(2,1)S(1)} %chain.1.gmid_ref, bf16[34,192,128]{2,1,0:T(8,128)(2,1)S(1)} %get-tuple-element.109.s2), custom_call_target="tpu_custom_call" | custom-call | bytes 9000000 | tf_op jit(solution)/shard_map/second_grads/pallas_call | solution.py:859
  118.8 3.7 %collective-permute-done.10.glo_ref = bf16[2,2,36,128]{3,2,1,0:T(8,128)(2,1)S(1)} collective-permute-done((bf16[2,2,36,128]{3,2,1,0:T(8,128)(2,1)S(1)}, bf16[2,2,36,128]{3,2,1,0:T(8,128)(2,1)S(1)}, u32[]{:S(2)}, u32[]{:S(2)}) %collective-permute-start.10) | collective-permute-done | bytes 36896 | tf_op jit(solution)/shard_map/ppermute | solution.py:1087
  122.5 3.9 %first_grads.1 = (bf16[40,64,128]{2,1,0:T(8,128)(2,1)S(1)}, f32[128,128]{1,0:T(8,128)S(1)}) custom-call(s32[3]{0:T(128)S(1)} %pad_add_fusion.at_ref, bf16[2,2,36,128]{3,2,1,0:T(8,128)(2,1)S(1)} %collective-permute-done.10.glo_ref, bf16[2,2,36,128]{3,2,1,0:T(8,128)(2,1)S(1)} %chain.1.gmid_ref, bf16[2,2,36,128]{3,2,1,0:T(8,128)(2,1)S(1)} %collective-permute-done.11.ghi_ref, ...), custom_call_target="tpu_custom_call" | custom-call | tf_op jit(solution)/shard_map/first_grads/pallas_call | solution.py:937
  126.4 15.2 %all_to_all.26 = f32[128,1,128]{2,1,0:T(1,128)S(1)} all-to-all(f32[128,1,128]{2,1,0:T(1,128)S(1)} %bitcast.43), channel_id=1, replica_groups=mesh['shot'=16,'brick'=8] {'shot','brick'}, dimensions={0} | all-to-all | bytes 131072 | tf_op jit(solution)/shard_map/all_to_all | solution.py:1133
  141.7 0.7 broadcast_in_dim.5
  142.4 5.2 %all-to-all-start.3 = ((f32[128,1,128]{2,1,0:T(1,128)}), f32[128,1,128]{2,1,0:T(1,128)S(1)}, u32[]{:S(2)}, u32[]{:S(2)}) async-start(f32[128,1,128]{2,1,0:T(1,128)} %broadcast_in_dim.5), calls=%async_computation.3 | async-start | bytes 131072 | tf_op jit(solution)/shard_map/all_to_all | solution.py:1135
  147.6 3.4 %latent_grads.1 = f32[32,32,128]{2,1,0:T(8,128)S(1)} custom-call(bf16[40,64,128]{2,1,0:T(8,128)(2,1)S(1)} %get-tuple-element.112.inner_ref, bf16[128,1152]{1,0:T(8,128)(2,1)S(1)} %copy-done.11), custom_call_target="tpu_custom_call" | custom-call | bytes 12000000 | tf_op jit(solution)/shard_map/latent_grads/pallas_call | solution.py:975
  150.9 1.1 copy.55
  152.0 4.4 %all-to-all-done.3 = f32[128,1,128]{2,1,0:T(1,128)S(1)} async-done(((f32[128,1,128]{2,1,0:T(1,128)}), f32[128,1,128]{2,1,0:T(1,128)S(1)}, u32[]{:S(2)}, u32[]{:S(2)}) %all-to-all-start.3) | async-done | bytes 65568 | tf_op jit(solution)/shard_map/all_to_all | solution.py:1135
  156.9 0.8 copy.44
  157.8 0.8 copy.45
  (78 shorter events, 4.3 us)
Async XLA Ops:
  1.8 14.8 %copy-start.27 = (bf16[27,2,16]{0,2,1:T(8,128)(2,1)S(1)}, bf16[27,2,16]{0,2,1:T(8,128)(2,1)}, u32[]{:S(2)}) copy-start(bf16[27,2,16]{0,2,1:T(8,128)(2,1)} %param.15) | copy-start | bytes 5188
  1.8 15.9 %copy-start.24 = (bf16[27,16,16]{0,2,1:T(8,128)(2,1)S(1)}, bf16[27,16,16]{0,2,1:T(8,128)(2,1)}, u32[]{:S(2)}) copy-start(bf16[27,16,16]{0,2,1:T(8,128)(2,1)} %param.14) | copy-start | bytes 41476
  1.8 6.5 %collective-permute-start = (bf16[2,4,16,128]{3,2,1,0:T(8,128)(2,1)S(1)}, bf16[2,4,16,128]{3,2,1,0:T(8,128)(2,1)S(1)}, u32[]{:S(2)}, u32[]{:S(2)}) collective-permute-start(bf16[2,4,16,128]{3,2,1,0:T(8,128)(2,1)S(1)} %get-tuple-element.123), channel_id=1, source_target_pairs={{0,1},{1,2},{2,3},{3,4},{4,5},{5,6},{6,7},{7,0},{8,9},{9,10},{10,1... | collective-permute-start | bytes 98312 | tf_op jit(solution)/shard_map/ppermute | solution.py:1087
  4.9 13.1 %copy-start.18 = (s32[2,1536]{1,0:T(2,128)S(1)}, s32[2,1536]{1,0:T(2,128)}, u32[]{:S(2)}) copy-start(s32[2,1536]{1,0:T(2,128)} %constant.27.clone.codes_2_ref) | copy-start | bytes 36868
  4.9 13.1 %copy-start.20 = (s32[2,1152]{1,0:T(2,128)S(1)}, s32[2,1152]{1,0:T(2,128)}, u32[]{:S(2)}) copy-start(s32[2,1152]{1,0:T(2,128)} %constant.26.clone.codes_1_ref) | copy-start | bytes 27652
  4.9 5.4 %collective-permute-start.1 = (bf16[2,4,16,128]{3,2,1,0:T(8,128)(2,1)S(1)}, bf16[2,4,16,128]{3,2,1,0:T(8,128)(2,1)S(1)}, u32[]{:S(2)}, u32[]{:S(2)}) collective-permute-start(bf16[2,4,16,128]{3,2,1,0:T(8,128)(2,1)S(1)} %get-tuple-element.124), channel_id=1, source_target_pairs={{1,0},{2,1},{3,2},{4,3},{5,4},{6,5},{7,6},{0,7},{9,8},{10,9},{11,1... | collective-permute-start | bytes 98312 | tf_op jit(solution)/shard_map/ppermute | solution.py:1087
  10.4 9.5 %collective-permute-start.3 = (bf16[2,40,16,128]{3,2,1,0:T(8,128)(2,1)S(1)}, bf16[2,40,16,128]{3,2,1,0:T(8,128)(2,1)S(1)}, u32[]{:S(2)}, u32[]{:S(2)}) collective-permute-start(bf16[2,40,16,128]{3,2,1,0:T(8,128)(2,1)S(1)} %pad_maximum_fusion.mid_ref), channel_id=1, source_target_pairs={{8,0},{16,8},{24,16},{32,24},{40,32},{48,40},{56,48},{64,56},{72,6... | collective-permute-start | bytes 983048 | tf_op jit(solution)/shard_map/ppermute | solution.py:1087
  11.8 12.1 %collective-permute-start.2 = (bf16[2,40,16,128]{3,2,1,0:T(8,128)(2,1)S(1)}, bf16[2,40,16,128]{3,2,1,0:T(8,128)(2,1)S(1)}, u32[]{:S(2)}, u32[]{:S(2)}) collective-permute-start(bf16[2,40,16,128]{3,2,1,0:T(8,128)(2,1)S(1)} %pad_maximum_fusion.mid_ref), channel_id=1, source_target_pairs={{0,8},{8,16},{16,24},{24,32},{32,40},{40,48},{48,56},{56,64},{64,7... | collective-permute-start | bytes 983048 | tf_op jit(solution)/shard_map/ppermute | solution.py:1087
  11.8 18.0 %collective-permute-start.5 = (f32[16,24,128]{2,1,0:T(8,128)S(1)}, f32[16,24,128]{2,1,0:T(8,128)S(1)}, u32[]{:S(2)}, u32[]{:S(2)}) collective-permute-start(f32[16,24,128]{2,1,0:T(8,128)S(1)} %get-tuple-element.121), channel_id=1, source_target_pairs={{1,0},{2,1},{3,2},{4,3},{5,4},{6,5},{7,6},{0,7},{9,8},{10,9},{11,1... | collective-permute-start | bytes 589832 | tf_op jit(solution)/shard_map/ppermute | solution.py:1087
  15.4 15.9 %collective-permute-start.4 = (f32[16,24,128]{2,1,0:T(8,128)S(1)}, f32[16,24,128]{2,1,0:T(8,128)S(1)}, u32[]{:S(2)}, u32[]{:S(2)}) collective-permute-start(f32[16,24,128]{2,1,0:T(8,128)S(1)} %get-tuple-element.122), channel_id=1, source_target_pairs={{0,1},{1,2},{2,3},{3,4},{4,5},{5,6},{6,7},{7,0},{8,9},{9,10},{10,1... | collective-permute-start | bytes 589832 | tf_op jit(solution)/shard_map/ppermute | solution.py:1087
  16.8 0.6 copy-start.22
  19.9 12.6 %copy-start.3 = (bf16[2,40,16,128]{3,2,1,0:T(8,128)(2,1)}, bf16[2,40,16,128]{3,2,1,0:T(8,128)(2,1)S(1)}, u32[]{:S(2)}) copy-start(bf16[2,40,16,128]{3,2,1,0:T(8,128)(2,1)S(1)} %collective-permute-done.3.hi_ref) | copy-start | bytes 983044
  23.9 8.6 %copy-start.5 = (bf16[2,40,16,128]{3,2,1,0:T(8,128)(2,1)}, bf16[2,40,16,128]{3,2,1,0:T(8,128)(2,1)S(1)}, u32[]{:S(2)}) copy-start(bf16[2,40,16,128]{3,2,1,0:T(8,128)(2,1)S(1)} %collective-permute-done.2.lo_ref) | copy-start | bytes 983044
  28.3 0.8 copy-start.1
  29.2 0.6 copy-start.16
  29.8 2.7 %copy-start.12 = (f32[16,24,128]{2,1,0:T(8,128)}, f32[16,24,128]{2,1,0:T(8,128)S(1)}, u32[]{:S(2)}) copy-start(f32[16,24,128]{2,1,0:T(8,128)S(1)} %collective-permute-done.5.phi_ref) | copy-start | bytes 589828
  31.3 1.2 copy-start.14
  32.5 4.6 %copy-start.25 = (f32[1,3,2048]{2,0,1:T(1,128)S(1)}, f32[1,3,2048]{2,0,1:T(1,128)}, u32[]{:S(2)}) copy-start(f32[1,3,2048]{2,0,1:T(1,128)} %param.17) | copy-start | bytes 73732
  32.5 4.6 %copy-start.26 = (s32[1,3,2048]{2,0,1:T(1,128)S(1)}, s32[1,3,2048]{2,0,1:T(1,128)}, u32[]{:S(2)}) copy-start(s32[1,3,2048]{2,0,1:T(1,128)} %param.19) | copy-start | bytes 73732
  32.5 20.9 %all-to-all-start = ((f32[16,2,2,32,128]{4,3,2,1,0:T(8,128)}), f32[16,2,2,32,128]{4,3,2,1,0:T(8,128)}, u32[]{:S(2)}, u32[]{:S(2)}) async-start(f32[16,2,2,32,128]{4,3,2,1,0:T(8,128)} %broadcast_in_dim.4), calls=%async_computation | async-start | bytes 2097152 | tf_op jit(solution)/shard_map/all_to_all | solution.py:1109
  37.1 9.2 %copy-start.23 = (bf16[27,2,16]{1,2,0:T(8,128)(2,1)S(1)}, bf16[27,2,16]{1,2,0:T(8,128)(2,1)}, u32[]{:S(2)}) copy-start(bf16[27,2,16]{1,2,0:T(8,128)(2,1)} %copy-done.22) | copy-start | bytes 5188
  37.1 9.2 %copy-start.19 = (s32[2,1152]{1,0:T(2,128)S(1)}, s32[2,1152]{1,0:T(2,128)}, u32[]{:S(2)}) copy-start(s32[2,1152]{1,0:T(2,128)} %constant.29.clone.codes_4_ref) | copy-start | bytes 27652
  37.1 9.2 %copy-start.21 = (s32[2,576]{1,0:T(2,128)S(1)}, s32[2,576]{1,0:T(2,128)}, u32[]{:S(2)}) copy-start(s32[2,576]{1,0:T(2,128)} %constant.28.clone.codes_3_ref) | copy-start | bytes 13828
  46.3 13.4 %copy-start = (bf16[384,256]{1,0:T(8,128)(2,1)S(1)}, bf16[384,256]{1,0:T(8,128)(2,1)}, u32[]{:S(2)}) copy-start(bf16[384,256]{1,0:T(8,128)(2,1)} %constant.30.clone.slope_ref) | copy-start | bytes 589828
  47.7 0.9 copy-start.7
  48.6 0.7 copy-start.10
  53.4 10.2 %copy-start.2 = (bf16[38,64,128]{2,1,0:T(8,128)(2,1)S(1)}, bf16[38,64,128]{2,1,0:T(8,128)(2,1)}, u32[]{:S(2)}) copy-start(bf16[38,64,128]{2,1,0:T(8,128)(2,1)} %copy-done.1) | copy-start | bytes 1867780
  53.4 10.2 %copy-start.4 = (bf16[2,40,16,128]{3,2,1,0:T(8,128)(2,1)S(1)}, bf16[2,40,16,128]{3,2,1,0:T(8,128)(2,1)}, u32[]{:S(2)}) copy-start(bf16[2,40,16,128]{3,2,1,0:T(8,128)(2,1)} %copy-done.3) | copy-start | bytes 983044
  53.4 10.3 %copy-start.6 = (bf16[2,40,16,128]{3,2,1,0:T(8,128)(2,1)S(1)}, bf16[2,40,16,128]{3,2,1,0:T(8,128)(2,1)}, u32[]{:S(2)}) copy-start(bf16[2,40,16,128]{3,2,1,0:T(8,128)(2,1)} %copy-done.5) | copy-start | bytes 983044
  55.2 10.9 %collective-permute-start.6 = (bf16[16,2,24,128]{3,2,1,0:T(8,128)(2,1)S(1)}, bf16[16,2,24,128]{3,2,1,0:T(8,128)(2,1)S(1)}, u32[]{:S(2)}, u32[]{:S(2)}) collective-permute-start(bf16[16,2,24,128]{3,2,1,0:T(8,128)(2,1)S(1)} %get-tuple-element.67), channel_id=1, source_target_pairs={{0,1},{1,2},{2,3},{3,4},{4,5},{5,6},{6,7},{7,0},{8,9},{9,10},{10,1... | collective-permute-start | bytes 589832 | tf_op jit(solution)/shard_map/ppermute | solution.py:1087
  57.7 10.9 %copy-start.9 = (bf16[384,128]{1,0:T(8,128)(2,1)S(1)}, bf16[384,128]{1,0:T(8,128)(2,1)}, u32[]{:S(2)}) copy-start(bf16[384,128]{1,0:T(8,128)(2,1)} %constant.31.clone.spread_ref) | copy-start | bytes 294916
  57.7 10.9 %collective-permute-start.7 = (bf16[16,2,24,128]{3,2,1,0:T(8,128)(2,1)S(1)}, bf16[16,2,24,128]{3,2,1,0:T(8,128)(2,1)S(1)}, u32[]{:S(2)}, u32[]{:S(2)}) collective-permute-start(bf16[16,2,24,128]{3,2,1,0:T(8,128)(2,1)S(1)} %get-tuple-element.68), channel_id=1, source_target_pairs={{1,0},{2,1},{3,2},{4,3},{5,4},{6,5},{7,6},{0,7},{9,8},{10,9},{11,1... | collective-permute-start | bytes 589832 | tf_op jit(solution)/shard_map/ppermute | solution.py:1087
  59.7 0.9 copy-start.13
  60.6 0.9 copy-start.15
  76.5 8.3 %collective-permute-start.8 = (bf16[16,32,128]{2,1,0:T(8,128)(2,1)S(1)}, bf16[16,32,128]{2,1,0:T(8,128)(2,1)S(1)}, u32[]{:S(2)}, u32[]{:S(2)}) collective-permute-start(bf16[16,32,128]{2,1,0:T(8,128)(2,1)S(1)} %get-tuple-element.90), channel_id=1, source_target_pairs={{0,1},{1,2},{2,3},{3,4},{4,5},{5,6},{6,7},{7,0},{8,9},{9,10},{10,1... | collective-permute-start | bytes 393224 | tf_op jit(solution)/shard_map/ppermute | solution.py:1087
  78.8 7.3 %collective-permute-start.9 = (bf16[16,32,128]{2,1,0:T(8,128)(2,1)S(1)}, bf16[16,32,128]{2,1,0:T(8,128)(2,1)S(1)}, u32[]{:S(2)}, u32[]{:S(2)}) collective-permute-start(bf16[16,32,128]{2,1,0:T(8,128)(2,1)S(1)} %get-tuple-element.91), channel_id=1, source_target_pairs={{1,0},{2,1},{3,2},{4,3},{5,4},{6,5},{7,6},{0,7},{9,8},{10,9},{11,1... | collective-permute-start | bytes 393224 | tf_op jit(solution)/shard_map/ppermute | solution.py:1087
  93.8 21.7 %copy-start.17 = (f32[2,2,36,128]{3,2,1,0:T(8,128)S(1)}, f32[2,2,36,128]{3,2,1,0:T(8,128)}, u32[]{:S(2)}) copy-start(f32[2,2,36,128]{3,2,1,0:T(8,128)} %copy-done.16) | copy-start | bytes 221188
  116.2 6.3 %copy-start.8 = (bf16[512,576]{1,0:T(8,128)(2,1)S(1)}, bf16[512,576]{1,0:T(8,128)(2,1)}, u32[]{:S(2)}) copy-start(bf16[512,576]{1,0:T(8,128)(2,1)} %copy-done.7) | copy-start | bytes 1769476
  116.2 2.6 %collective-permute-start.11 = (bf16[2,2,36,128]{3,2,1,0:T(8,128)(2,1)S(1)}, bf16[2,2,36,128]{3,2,1,0:T(8,128)(2,1)S(1)}, u32[]{:S(2)}, u32[]{:S(2)}) collective-permute-start(bf16[2,2,36,128]{3,2,1,0:T(8,128)(2,1)S(1)} %chain.1.gmid_ref), channel_id=1, source_target_pairs={{8,0},{16,8},{24,16},{32,24},{40,32},{48,40},{56,48},{64,56},{72,6... | collective-permute-start | bytes 110600 | tf_op jit(solution)/shard_map/ppermute | solution.py:1087
  116.9 5.5 %collective-permute-start.10 = (bf16[2,2,36,128]{3,2,1,0:T(8,128)(2,1)S(1)}, bf16[2,2,36,128]{3,2,1,0:T(8,128)(2,1)S(1)}, u32[]{:S(2)}, u32[]{:S(2)}) collective-permute-start(bf16[2,2,36,128]{3,2,1,0:T(8,128)(2,1)S(1)} %chain.1.gmid_ref), channel_id=1, source_target_pairs={{0,8},{8,16},{16,24},{24,32},{32,40},{40,48},{48,56},{56,64},{64,7... | collective-permute-start | bytes 110600 | tf_op jit(solution)/shard_map/ppermute | solution.py:1087
  118.8 28.8 %copy-start.11 = (bf16[128,1152]{1,0:T(8,128)(2,1)S(1)}, bf16[128,1152]{1,0:T(8,128)(2,1)}, u32[]{:S(2)}) copy-start(bf16[128,1152]{1,0:T(8,128)(2,1)} %copy-done.10) | copy-start | bytes 884740
  142.4 14.0 %all-to-all-start.3 = ((f32[128,1,128]{2,1,0:T(1,128)}), f32[128,1,128]{2,1,0:T(1,128)S(1)}, u32[]{:S(2)}, u32[]{:S(2)}) async-start(f32[128,1,128]{2,1,0:T(1,128)} %broadcast_in_dim.5), calls=%async_computation.3 | async-start | bytes 131072 | tf_op jit(solution)/shard_map/all_to_all | solution.py:1135
